TPU v7x, 32 devices: a whole 2x2x4 slice. The times are simulated.
32 devices in a mesh: near: 4 (over x, core), far: 8 (over z, y).
Axes of the slice: x: 2, y: 2, z: 4, core: 2. Of those that a mesh axis runs over, the one named last changes fastest.
Arguments:
- w_reduce: bfloat16 [4, 8, 256, 1024], P('near', 'far'), may hold values from -6 to 6
- w_expand: bfloat16 [4, 8, 256, 1024], P('near', 'far'), may hold values from -6 to 6
- inputs: bfloat16 [4, 8, 2, 256, 1024], P('near', 'far'), may hold values from -6 to 6
- out_grads: bfloat16 [4, 8, 2, 256, 1024], P('near', 'far'), may hold values from -12 to 12
Outputs:
- new_reduce: float32 [4, 8, 256, 1024], P('near', 'far')
- new_expand: float32 [4, 8, 256, 1024], P('near', 'far')
All inputs are finite; a program needn't handle non-finite values.
Results may differ from a plain program's by a relative error of at most 0.0003.
Values sent between devices are 32-bit elements; how exact they have to be, the bound alone decides.
No kernel may reach another device: no remote copies, remote signals or barrier semaphores. Data moves between devices by JAX's collectives and lax.ppermute only.
A program may use at most 64 MiB of HBM per device.

v0:
```python
import functools
import math

import jax
import jax.numpy as jnp
from jax import lax
from jax.experimental import pallas as pl
from jax.experimental.pallas import tpu as pltpu
from jax.sharding import PartitionSpec as P


learn_rate = 1.0

ORDERS = (
    ((1, 2, 3), (2, 3, 1)),
    ((3, 1, 2), (1, 2, 3)),
    ((2, 3, 1), (3, 1, 2)),
    ((1, 2, 3), (2, 3, 1)),
)
BITS = 4
SMEM = pl.BlockSpec(memory_space=pltpu.SMEM)
VMEM = pl.BlockSpec(memory_space=pltpu.VMEM)
HBM = pl.BlockSpec(memory_space=pltpu.HBM)
SMALL = pltpu.CompilerParams(vmem_limit_bytes=2**20)
LARGE = pltpu.CompilerParams(vmem_limit_bytes=12 * 2**20)
f32, bf16 = jnp.float32, jnp.bfloat16


def bits_of(near, far):
    chip = ((near >> 1) & 1, far & 1, (far >> 1) & 1)
    return ((near & 1) ^ chip[0] ^ chip[1] ^ chip[2],) + chip


def from_partner(values, *bit_of_role):
    nears, fars = lax.axis_size("near"), lax.axis_size("far")
    pairs = []
    for near in range(nears):
        for far in range(fars):
            bit = bit_of_role[bits_of(near, far)[0]]
            to_near = near ^ 1 ^ (2 if bit == 1 else 0)
            to_far = far ^ (1 << (bit - 2)) if bit >= 2 else far
            pairs.append((near * fars + far, to_near * fars + to_far))
    return lax.ppermute(values, ("near", "far"), pairs)


def join_kernel(index, places_ref, own_ref, rest_ref, out_ref):
    rows = own_ref.shape[0]
    place = places_ref[index]
    out_ref[pl.ds(pl.multiple_of(place * rows, rows), rows), :] = own_ref[...]
    out_ref[pl.ds(pl.multiple_of((1 - place) * rows, rows), rows), :] = rest_ref[...]


def chain(keep, send, index, places):
    even, odd = ORDERS[index - 1]
    own = keep + from_partner(send, even[0], odd[0])
    own = own + from_partner(own, even[1], odd[1])
    own = own + from_partner(own, even[2], odd[2])
    rest = from_partner(own, even[0], odd[0])
    rows, columns = own.shape
    return pl.pallas_call(
        functools.partial(join_kernel, index),
        out_shape=jax.ShapeDtypeStruct((2 * rows, columns), f32),
        in_specs=[SMEM, VMEM, VMEM],
        out_specs=VMEM,
        compiler_params=SMALL,
    )(places, own, rest)


def meet_kernel(indices, places_ref, keep_ref, got_ref, *outs):
    rows = outs[0].shape[0]
    for k, index in enumerate(indices):
        low, high = pl.ds(2 * k * rows, rows), pl.ds((2 * k + 1) * rows, rows)
        stays_low = places_ref[index] == 0
        low, high = keep_ref[low, :] + got_ref[low, :], keep_ref[high, :] + got_ref[high, :]
        outs[2 * k][...] = jnp.where(stays_low, low, high)
        outs[2 * k + 1][...] = jnp.where(stays_low, high, low)


def sum_over_cube(keep, send, indices, places):
    rows, columns = keep.shape
    count = 2 * len(indices)
    got = pltpu.with_memory_space_constraint(from_partner(send, 0, 0), pltpu.VMEM)
    pieces = pl.pallas_call(
        functools.partial(meet_kernel, indices),
        out_shape=(jax.ShapeDtypeStruct((rows // count, columns), f32),) * count,
        in_specs=[SMEM, VMEM, VMEM],
        out_specs=(VMEM,) * count,
        compiler_params=SMALL,
    )(places, keep, got)
    parts = [chain(pieces[2 * k], pieces[2 * k + 1], index, places) for k, index in enumerate(indices)]
    return parts + [from_partner(part, 0, 0) for part in parts]


def place_of(index, count, role):
    per_role = count // 2
    return (role if index < per_role else 1 - role) * per_role + index % per_role


def store_kernel(places_ref, *refs):
    *parts, out_ref, sems = refs
    rows = parts[0].shape[0]
    copies = []
    for i, part in enumerate(parts):
        start = pl.multiple_of(place_of(i, len(parts), places_ref[0]) * rows, rows)
        copies.append(pltpu.make_async_copy(part, out_ref.at[pl.ds(start, rows), :], sems.at[i]))
        copies[-1].start()
    for copy in copies:
        copy.wait()


def store(parts, places):
    rows, columns = parts[0].shape
    return pl.pallas_call(
        store_kernel,
        out_shape=jax.ShapeDtypeStruct((rows * len(parts), columns), f32),
        in_specs=[SMEM] + [VMEM] * len(parts),
        out_specs=HBM,
        scratch_shapes=[pltpu.SemaphoreType.DMA((len(parts),))],
        compiler_params=SMALL,
    )(places, *parts)


def halves(values):
    high = values.astype(bf16)
    return high, (values - high.astype(f32)).astype(bf16)


def product(left, right, contract):
    total = None
    for i, a in enumerate(left):
        for j, b in enumerate(right):
            if i + j < 2:
                term = lax.dot_general(a, b, (contract, ((), ())), preferred_element_type=f32)
                total = term if total is None else total + term
    return total


def parts_of(values):
    return (values,) if values.dtype == bf16 else halves(values)


NN = ((1,), (0,))
NT = ((1,), (1,))


def expand_kernel(count, places_ref, x_in, g_in, *refs):
    if count:
        r_parts, e_parts, outs = refs[:count], refs[count : 2 * count], refs[2 * count :]
        keep_ref, send_ref, zh_ref, zl_ref, slope_ref, r_ref, e_ref = outs
        x_ref, g_ref = x_in, g_in
        rows = r_parts[0].shape[0]
        for parts, whole_ref in ((r_parts, r_ref), (e_parts, e_ref)):
            for i, part in enumerate(parts):
                start = pl.multiple_of(place_of(i, count, places_ref[0]) * rows, rows)
                whole_ref[pl.ds(start, rows), :] = part[...]
    else:
        r_in, e_in, keep_ref, send_ref, zh_ref, zl_ref, slope_ref, r_ref, e_ref, x_ref, g_ref, sems = refs
        copies = [
            pltpu.make_async_copy(source, target, sems.at[i])
            for i, (source, target) in enumerate(((r_in, r_ref), (x_in.at[0], x_ref), (e_in, e_ref), (g_in.at[0], g_ref)))
        ]
        for copy in copies:
            copy.start()
        copies[0].wait()
        copies[1].wait()
    width, columns = r_ref.shape
    reduce_scale = 1.0 / math.sqrt(columns)
    expand_scale = 1.0 / math.sqrt(width)
    feats = x_ref[...]
    pre = product(parts_of(r_ref[...]), (feats,), NT) * reduce_scale
    sig = jax.nn.sigmoid(pre)
    hidden = pre * sig
    slope_ref[...] = sig * (1.0 + pre * (1.0 - sig))
    hidden_t = halves(hidden)
    hidden_n = halves(hidden.T)
    if not count:
        copies[2].wait()
    e_parts = parts_of(e_ref[...])
    summed = feats.astype(f32) + product(hidden_n, e_parts, NN) * expand_scale
    if not count:
        copies[3].wait()
    sig = jax.nn.sigmoid(summed)
    grads = halves(g_ref[...].astype(f32) * (sig * (1.0 + summed * (1.0 - sig))))
    zh_ref[...] = grads[0]
    zl_ref[...] = grads[1]
    stepped = (e_ref[...].astype(f32) - learn_rate * expand_scale * product(hidden_t, grads, NN)) * (0.5**BITS)
    rows = width // 2
    even = places_ref[0] == 0
    keep_ref[...] = jnp.where(even, stepped[:rows], stepped[rows:])
    send_ref[...] = jnp.where(even, stepped[rows:], stepped[:rows])


def reduce_kernel(upcoming, places_ref, x_all, g_all, x_ref, r_ref, e_ref, zh_ref, zl_ref, slope_ref, keep_ref, send_ref, *refs):
    if upcoming is not None:
        next_x_ref, next_g_ref, sems = refs
        copies = (
            pltpu.make_async_copy(x_all.at[upcoming], next_x_ref, sems.at[0]),
            pltpu.make_async_copy(g_all.at[upcoming], next_g_ref, sems.at[1]),
        )
        for copy in copies:
            copy.start()
    width, columns = r_ref.shape
    reduce_scale = 1.0 / math.sqrt(columns)
    expand_scale = 1.0 / math.sqrt(width)
    grad_hidden = product(parts_of(e_ref[...]), (zh_ref[...], zl_ref[...]), NT) * expand_scale
    grad_pre = halves(grad_hidden * slope_ref[...])
    stepped = (r_ref[...].astype(f32) - learn_rate * reduce_scale * product(grad_pre, (x_ref[...],), NN)) * (0.5**BITS)
    rows = width // 2
    even = places_ref[0] == 0
    keep_ref[...] = jnp.where(even, stepped[:rows], stepped[rows:])
    send_ref[...] = jnp.where(even, stepped[rows:], stepped[:rows])
    if upcoming is not None:
        for copy in copies:
            copy.wait()


def shards(w_reduce, w_expand, inputs, out_grads):
    bits = bits_of(lax.axis_index("near"), lax.axis_index("far"))
    places = jnp.stack([bits[0]] + [jnp.where(bits[0] == 0, bits[even[0]], bits[odd[0]]) for even, odd in ORDERS]).astype(jnp.int32)
    held = [pltpu.with_memory_space_constraint(array[0, 0], pltpu.HBM) for array in (w_reduce, w_expand, inputs, out_grads)]
    reducing, expanding, inputs, out_grads = held
    iterations, rows, columns = inputs.shape
    width = reducing.shape[0]
    half = jax.ShapeDtypeStruct((width // 2, columns), f32)
    acts = jax.ShapeDtypeStruct((rows, columns), bf16)
    slopes = jax.ShapeDtypeStruct((width, rows), f32)
    for iteration in range(iterations):
        first, last = iteration == 0, iteration == iterations - 1
        weights = jax.ShapeDtypeStruct((width, columns), bf16 if first else f32)
        results = pl.pallas_call(
            functools.partial(expand_kernel, 0 if first else len(sums_r)),
            out_shape=(half, half, acts, acts, slopes, weights, weights) + ((acts,) if first else ()),
            in_specs=[SMEM] + ([HBM] * 4 if first else [VMEM] * (2 + len(sums_r) + len(sums_e))),
            out_specs=(VMEM,) * (8 if first else 7),
            scratch_shapes=[pltpu.VMEM((rows, columns), bf16), pltpu.SemaphoreType.DMA((4,))] if first else [],
            compiler_params=LARGE,
        )(places, *((inputs, out_grads, reducing, expanding) if first else (feats, grads, *sums_r, *sums_e)))
        keep_e, send_e, zh, zl, slope, reducing, expanding = results[:7]
        if first:
            feats = results[7]
        results = pl.pallas_call(
            functools.partial(reduce_kernel, None if last else iteration + 1),
            out_shape=(half, half) + (() if last else (acts, acts)),
            in_specs=[SMEM, HBM, HBM] + [VMEM] * 6,
            out_specs=(VMEM,) * (2 if last else 4),
            scratch_shapes=[] if last else [pltpu.SemaphoreType.DMA((2,))],
            compiler_params=LARGE,
        )(places, inputs, out_grads, feats, reducing, expanding, zh, zl, slope)
        keep_r, send_r = results[:2]
        if not last:
            feats, grads = results[2:]
        sums_e = sum_over_cube(keep_e, send_e, (1, 2), places)
        sums_r = sum_over_cube(keep_r, send_r, (3, 4), places)
    return (store(sums_r, places)[None, None], store(sums_e, places)[None, None])


def solution(mesh):
    in_specs = (
        P("near", "far", None, None),
        P("near", "far", None, None),
        P("near", "far", None, None, None),
        P("near", "far", None, None, None),
    )
    out_specs = (P("near", "far", None, None), P("near", "far", None, None))
    return jax.shard_map(shards, mesh=mesh, in_specs=in_specs, out_specs=out_specs, check_vma=False)
```

profile of v0, /device:TPU:0, one launch (start us, length us, event | category | flops | bytes accessed | tf_op | source)
XLA Modules:
  0.0 79.0 jit_solution(9083881142175073762)
XLA Ops:
  0.7 4.2 %shard_map.59 = (f32[128,1024]{1,0:T(8,128)S(1)}, f32[128,1024]{1,0:T(8,128)S(1)}, bf16[256,1024]{1,0:T(8,128)(2,1)S(1)}, bf16[256,1024]{1,0:T(8,128)(2,1)S(1)},...) custom-call(s32[5]{0:T(128)S(1)} %stack.20.places_ref, ...), custom_call_target="tpu_custom_call" | custom-call | tf_op jit(solution)/shard_map/pallas_call | solution.py:230
  5.0 2.7 %shard_map.60 = (f32[128,1024]{1,0:T(8,128)S(1)}, f32[128,1024]{1,0:T(8,128)S(1)}, bf16[256,1024]{1,0:T(8,128)(2,1)S(1)}, bf16[256,1024]{1,0:T(8,128)(2,1)S(1)}) custom-call(s32[5]{0:T(128)S(1)} %stack.20.places_ref, bf16[2,256,1024]{2,1,0:T(8,128)(2,1)} %bitcast.11, bf16[2,256,1024]{2,1,0:T(8,128)(2,1)} %bitcast.14, ...), custom_call_target="tpu_custom_call" | custom-call | tf_op jit(solution)/shard_map/pallas_call | solution.py:241
  8.3 1.5 %collective-permute-done.got_ref = f32[128,1024]{1,0:T(8,128)S(1)} collective-permute-done((f32[128,1024]{1,0:T(8,128)S(1)}, f32[128,1024]{1,0:T(8,128)S(1)}, u32[]{:S(2)}, u32[]{:S(2)}) %collective-permute-start) | collective-permute-done | bytes 524320 | tf_op jit(solution)/shard_map/ppermute | solution.py:43
  10.4 2.7 %collective-permute-start.5 = (f32[32,1024]{1,0:T(8,128)S(1)}, f32[32,1024]{1,0:T(8,128)S(1)}, u32[]{:S(2)}, u32[]{:S(2)}) collective-permute-start(f32[32,1024]{1,0:T(8,128)S(1)} %get-tuple-element.52), channel_id=1, source_target_pairs={{0,24},{1,8},{2,11},{3,27},{4,28},{5,12},{6,15},{7,31},{8,1},{9,17... | collective-permute-start | bytes 393224 | tf_op jit(solution)/shard_map/ppermute | solution.py:43
  13.0 1.5 %collective-permute-start.1 = (f32[32,1024]{1,0:T(8,128)S(1)}, f32[32,1024]{1,0:T(8,128)S(1)}, u32[]{:S(2)}, u32[]{:S(2)}) collective-permute-start(f32[32,1024]{1,0:T(8,128)S(1)} %get-tuple-element.50), channel_id=1, source_target_pairs={{0,9},{1,11},{2,8},{3,10},{4,13},{5,15},{6,12},{7,14},{8,2},{9,0},... | collective-permute-start | bytes 393224 | tf_op jit(solution)/shard_map/ppermute | solution.py:43
  15.1 1.4 %collective-permute-start.16 = (f32[32,1024]{1,0:T(8,128)S(1)}, f32[32,1024]{1,0:T(8,128)S(1)}, u32[]{:S(2)}, u32[]{:S(2)}) collective-permute-start(f32[32,1024]{1,0:T(8,128)S(1)} %get-tuple-element.58), channel_id=1, source_target_pairs={{0,10},{1,25},{2,26},{3,9},{4,14},{5,29},{6,30},{7,13},{8,16},{9,3... | collective-permute-start | bytes 393224 | tf_op jit(solution)/shard_map/ppermute | solution.py:43
  17.7 1.7 %collective-permute-start.2 = (f32[32,1024]{1,0:T(8,128)S(1)}, f32[32,1024]{1,0:T(8,128)S(1)}, u32[]{:S(2)}, u32[]{:S(2)}) collective-permute-start(f32[32,1024]{1,0:T(8,128)S(1)} %add.72), channel_id=1, source_target_pairs={{0,10},{1,25},{2,26},{3,9},{4,14},{5,29},{6,30},{7,13},{8,16},{9,3... | collective-permute-start | bytes 393224 | tf_op jit(solution)/shard_map/ppermute | solution.py:43
  19.7 1.5 %collective-permute-start.17 = (f32[32,1024]{1,0:T(8,128)S(1)}, f32[32,1024]{1,0:T(8,128)S(1)}, u32[]{:S(2)}, u32[]{:S(2)}) collective-permute-start(f32[32,1024]{1,0:T(8,128)S(1)} %add.81), channel_id=1, source_target_pairs={{0,24},{1,8},{2,11},{3,27},{4,28},{5,12},{6,15},{7,31},{8,1},{9,17... | collective-permute-start | bytes 393224 | tf_op jit(solution)/shard_map/ppermute | solution.py:43
  21.4 1.3 %collective-permute-start.13 = (f32[32,1024]{1,0:T(8,128)S(1)}, f32[32,1024]{1,0:T(8,128)S(1)}, u32[]{:S(2)}, u32[]{:S(2)}) collective-permute-start(f32[32,1024]{1,0:T(8,128)S(1)} %add.78), channel_id=1, source_target_pairs={{0,9},{1,11},{2,8},{3,10},{4,13},{5,15},{6,12},{7,14},{8,2},{9,0},... | collective-permute-start | bytes 393224 | tf_op jit(solution)/shard_map/ppermute | solution.py:43
  23.2 1.4 %collective-permute-start.3 = (f32[32,1024]{1,0:T(8,128)S(1)}, f32[32,1024]{1,0:T(8,128)S(1)}, u32[]{:S(2)}, u32[]{:S(2)}) collective-permute-start(f32[32,1024]{1,0:T(8,128)S(1)} %add.73), channel_id=1, source_target_pairs={{0,24},{1,8},{2,11},{3,27},{4,28},{5,12},{6,15},{7,31},{8,1},{9,17... | collective-permute-start | bytes 393224 | tf_op jit(solution)/shard_map/ppermute | solution.py:43
  25.2 1.4 %collective-permute-start.18 = (f32[32,1024]{1,0:T(8,128)S(1)}, f32[32,1024]{1,0:T(8,128)S(1)}, u32[]{:S(2)}, u32[]{:S(2)}) collective-permute-start(f32[32,1024]{1,0:T(8,128)S(1)} %add.82), channel_id=1, source_target_pairs={{0,9},{1,11},{2,8},{3,10},{4,13},{5,15},{6,12},{7,14},{8,2},{9,0},... | collective-permute-start | bytes 393224 | tf_op jit(solution)/shard_map/ppermute | solution.py:43
  27.5 1.0 %collective-permute-done.7 = f32[32,1024]{1,0:T(8,128)S(1)} collective-permute-done((f32[32,1024]{1,0:T(8,128)S(1)}, f32[32,1024]{1,0:T(8,128)S(1)}, u32[]{:S(2)}, u32[]{:S(2)}) %collective-permute-start.7) | collective-permute-done | bytes 131104 | tf_op jit(solution)/shard_map/ppermute | solution.py:43
  29.4 1.1 %collective-permute-start.4 = (f32[32,1024]{1,0:T(8,128)S(1)}, f32[32,1024]{1,0:T(8,128)S(1)}, u32[]{:S(2)}, u32[]{:S(2)}) collective-permute-start(f32[32,1024]{1,0:T(8,128)S(1)} %add.74.own_ref), channel_id=1, source_target_pairs={{0,9},{1,11},{2,8},{3,10},{4,13},{5,15},{6,12},{7,14},{8,2},{9,0},... | collective-permute-start | bytes 393224 | tf_op jit(solution)/shard_map/ppermute | solution.py:43
  31.0 1.5 %collective-permute-start.19 = (f32[32,1024]{1,0:T(8,128)S(1)}, f32[32,1024]{1,0:T(8,128)S(1)}, u32[]{:S(2)}, u32[]{:S(2)}) collective-permute-start(f32[32,1024]{1,0:T(8,128)S(1)} %add.83.own_ref), channel_id=1, source_target_pairs={{0,10},{1,25},{2,26},{3,9},{4,14},{5,29},{6,30},{7,13},{8,16},{9,3... | collective-permute-start | bytes 393224 | tf_op jit(solution)/shard_map/ppermute | solution.py:43
  34.4 1.6 %collective-permute-start.10 = (f32[64,1024]{1,0:T(8,128)S(1)}, f32[64,1024]{1,0:T(8,128)S(1)}, u32[]{:S(2)}, u32[]{:S(2)}) collective-permute-start(f32[64,1024]{1,0:T(8,128)S(1)} %shard_map.63.refs_1_), channel_id=1, source_target_pairs={{0,8},{1,9},{2,10},{3,11},{4,12},{5,13},{6,14},{7,15},{8,0},{9,1},... | collective-permute-start | bytes 786440 | tf_op jit(solution)/shard_map/ppermute | solution.py:43
  36.6 1.1 %collective-permute-start.9 = (f32[64,1024]{1,0:T(8,128)S(1)}, f32[64,1024]{1,0:T(8,128)S(1)}, u32[]{:S(2)}, u32[]{:S(2)}) collective-permute-start(f32[64,1024]{1,0:T(8,128)S(1)} %shard_map.62.refs_0_), channel_id=1, source_target_pairs={{0,8},{1,9},{2,10},{3,11},{4,12},{5,13},{6,14},{7,15},{8,0},{9,1},... | collective-permute-start | bytes 786440 | tf_op jit(solution)/shard_map/ppermute | solution.py:43
  40.3 1.0 %collective-permute-done.20.refs_6_ = f32[64,1024]{1,0:T(8,128)S(1)} collective-permute-done((f32[64,1024]{1,0:T(8,128)S(1)}, f32[64,1024]{1,0:T(8,128)S(1)}, u32[]{:S(2)}, u32[]{:S(2)}) %collective-permute-start.20) | collective-permute-done | bytes 262176 | tf_op jit(solution)/shard_map/ppermute | solution.py:43
  41.4 3.0 %shard_map.67 = (f32[128,1024]{1,0:T(8,128)S(1)}, f32[128,1024]{1,0:T(8,128)S(1)}, bf16[256,1024]{1,0:T(8,128)(2,1)S(1)}, bf16[256,1024]{1,0:T(8,128)(2,1)S(1)},...) custom-call(s32[5]{0:T(128)S(1)} %stack.20.places_ref, ...), custom_call_target="tpu_custom_call" | custom-call | tf_op jit(solution)/shard_map/pallas_call | solution.py:230
  44.4 2.0 %shard_map.68 = (f32[128,1024]{1,0:T(8,128)S(1)}, f32[128,1024]{1,0:T(8,128)S(1)}) custom-call(s32[5]{0:T(128)S(1)} %stack.20.places_ref, bf16[2,256,1024]{2,1,0:T(8,128)(2,1)} %bitcast.12, bf16[2,256,1024]{2,1,0:T(8,128)(2,1)} %bitcast.15, bf16[256,1024]{1,0:T(8,128)(2,1)S(1)} %get-tuple-element.45.x_in.x_ref, f32[256,1024]{1,0:T(8,128)S(1)} %get-tuple-element.59.r_ref, ...), custom_call_target="tpu_custom_call" | custom-call | tf_op jit(solution)/shard_map/pallas_call | solution.py:241
  47.0 1.4 %collective-permute-done.22.got_ref = f32[128,1024]{1,0:T(8,128)S(1)} collective-permute-done((f32[128,1024]{1,0:T(8,128)S(1)}, f32[128,1024]{1,0:T(8,128)S(1)}, u32[]{:S(2)}, u32[]{:S(2)}) %collective-permute-start.22) | collective-permute-done | bytes 524320 | tf_op jit(solution)/shard_map/ppermute | solution.py:43
  49.6 1.1 %collective-permute-start.23 = (f32[32,1024]{1,0:T(8,128)S(1)}, f32[32,1024]{1,0:T(8,128)S(1)}, u32[]{:S(2)}, u32[]{:S(2)}) collective-permute-start(f32[32,1024]{1,0:T(8,128)S(1)} %get-tuple-element.67), channel_id=1, source_target_pairs={{0,9},{1,11},{2,8},{3,10},{4,13},{5,15},{6,12},{7,14},{8,2},{9,0},... | collective-permute-start | bytes 393224 | tf_op jit(solution)/shard_map/ppermute | solution.py:43
  53.9 1.3 %collective-permute-done.23 = f32[32,1024]{1,0:T(8,128)S(1)} collective-permute-done((f32[32,1024]{1,0:T(8,128)S(1)}, f32[32,1024]{1,0:T(8,128)S(1)}, u32[]{:S(2)}, u32[]{:S(2)}) %collective-permute-start.23) | collective-permute-done | bytes 131104 | tf_op jit(solution)/shard_map/ppermute | solution.py:43
  55.2 1.1 %collective-permute-start.24 = (f32[32,1024]{1,0:T(8,128)S(1)}, f32[32,1024]{1,0:T(8,128)S(1)}, u32[]{:S(2)}, u32[]{:S(2)}) collective-permute-start(f32[32,1024]{1,0:T(8,128)S(1)} %add.84), channel_id=1, source_target_pairs={{0,10},{1,25},{2,26},{3,9},{4,14},{5,29},{6,30},{7,13},{8,16},{9,3... | collective-permute-start | bytes 393224 | tf_op jit(solution)/shard_map/ppermute | solution.py:43
  57.5 1.0 %collective-permute-start.35 = (f32[32,1024]{1,0:T(8,128)S(1)}, f32[32,1024]{1,0:T(8,128)S(1)}, u32[]{:S(2)}, u32[]{:S(2)}) collective-permute-start(f32[32,1024]{1,0:T(8,128)S(1)} %add.90), channel_id=1, source_target_pairs={{0,9},{1,11},{2,8},{3,10},{4,13},{5,15},{6,12},{7,14},{8,2},{9,0},... | collective-permute-start | bytes 393224 | tf_op jit(solution)/shard_map/ppermute | solution.py:43
  59.5 1.4 %collective-permute-done.24 = f32[32,1024]{1,0:T(8,128)S(1)} collective-permute-done((f32[32,1024]{1,0:T(8,128)S(1)}, f32[32,1024]{1,0:T(8,128)S(1)}, u32[]{:S(2)}, u32[]{:S(2)}) %collective-permute-start.24) | collective-permute-done | bytes 131104 | tf_op jit(solution)/shard_map/ppermute | solution.py:43
  62.0 1.1 %collective-permute-done.35 = f32[32,1024]{1,0:T(8,128)S(1)} collective-permute-done((f32[32,1024]{1,0:T(8,128)S(1)}, f32[32,1024]{1,0:T(8,128)S(1)}, u32[]{:S(2)}, u32[]{:S(2)}) %collective-permute-start.35) | collective-permute-done | bytes 131104 | tf_op jit(solution)/shard_map/ppermute | solution.py:43
  64.1 1.3 %collective-permute-start.30 = (f32[32,1024]{1,0:T(8,128)S(1)}, f32[32,1024]{1,0:T(8,128)S(1)}, u32[]{:S(2)}, u32[]{:S(2)}) collective-permute-start(f32[32,1024]{1,0:T(8,128)S(1)} %add.89.own_ref), channel_id=1, source_target_pairs={{0,24},{1,8},{2,11},{3,27},{4,28},{5,12},{6,15},{7,31},{8,1},{9,17... | collective-permute-start | bytes 393224 | tf_op jit(solution)/shard_map/ppermute | solution.py:43
  65.4 1.1 %collective-permute-done.25 = f32[32,1024]{1,0:T(8,128)S(1)} collective-permute-done((f32[32,1024]{1,0:T(8,128)S(1)}, f32[32,1024]{1,0:T(8,128)S(1)}, u32[]{:S(2)}, u32[]{:S(2)}) %collective-permute-start.25) | collective-permute-done | bytes 131104 | tf_op jit(solution)/shard_map/ppermute | solution.py:43
  67.5 1.1 %collective-permute-start.41 = (f32[32,1024]{1,0:T(8,128)S(1)}, f32[32,1024]{1,0:T(8,128)S(1)}, u32[]{:S(2)}, u32[]{:S(2)}) collective-permute-start(f32[32,1024]{1,0:T(8,128)S(1)} %add.95.own_ref), channel_id=1, source_target_pairs={{0,10},{1,25},{2,26},{3,9},{4,14},{5,29},{6,30},{7,13},{8,16},{9,3... | collective-permute-start | bytes 393224 | tf_op jit(solution)/shard_map/ppermute | solution.py:43
  70.4 2.7 %collective-permute-start.32 = (f32[64,1024]{1,0:T(8,128)S(1)}, f32[64,1024]{1,0:T(8,128)S(1)}, u32[]{:S(2)}, u32[]{:S(2)}) collective-permute-start(f32[64,1024]{1,0:T(8,128)S(1)} %shard_map.71.refs_1_), channel_id=1, source_target_pairs={{0,8},{1,9},{2,10},{3,11},{4,12},{5,13},{6,14},{7,15},{8,0},{9,1},... | collective-permute-start | bytes 786440 | tf_op jit(solution)/shard_map/ppermute | solution.py:43
  75.9 1.5 %shard_map.72 = f32[256,1024]{1,0:T(8,128)} custom-call(s32[5]{0:T(128)S(1)} %stack.20.places_ref, f32[64,1024]{1,0:T(8,128)S(1)} %shard_map.70.refs_0_, f32[64,1024]{1,0:T(8,128)S(1)} %shard_map.71.refs_1_, f32[64,1024]{1,0:T(8,128)S(1)} %collective-permute-done.31.refs_2_, f32[64,1024]{1,0:T(8,128)S(1)} %collective-permute-done.32.refs_3_), custom_call_target="tpu_custom_call" | custom-call | tf_op jit(solution)/shard_map/pallas_call | solution.py:113
  77.5 1.5 %shard_map.76 = f32[256,1024]{1,0:T(8,128)} custom-call(s32[5]{0:T(128)S(1)} %stack.20.places_ref, f32[64,1024]{1,0:T(8,128)S(1)} %shard_map.74.refs_0_, f32[64,1024]{1,0:T(8,128)S(1)} %shard_map.75.refs_1_, f32[64,1024]{1,0:T(8,128)S(1)} %collective-permute-done.42.refs_2_, f32[64,1024]{1,0:T(8,128)S(1)} %collective-permute-done.43.refs_3_), custom_call_target="tpu_custom_call" | custom-call | tf_op jit(solution)/shard_map/pallas_call | solution.py:113
  (99 shorter events, 26.8 us)
Async XLA Ops:
  8.2 6.3 %collective-permute-start.11 = (f32[128,1024]{1,0:T(8,128)S(1)}, f32[128,1024]{1,0:T(8,128)S(1)}, u32[]{:S(2)}, u32[]{:S(2)}) collective-permute-start(f32[128,1024]{1,0:T(8,128)S(1)} %get-tuple-element.54), channel_id=1, source_target_pairs={{0,8},{1,9},{2,10},{3,11},{4,12},{5,13},{6,14},{7,15},{8,0},{9,1},... | collective-permute-start | bytes 1572872 | tf_op jit(solution)/shard_map/ppermute | solution.py:43
  10.4 6.7 %collective-permute-start.5 = (f32[32,1024]{1,0:T(8,128)S(1)}, f32[32,1024]{1,0:T(8,128)S(1)}, u32[]{:S(2)}, u32[]{:S(2)}) collective-permute-start(f32[32,1024]{1,0:T(8,128)S(1)} %get-tuple-element.52), channel_id=1, source_target_pairs={{0,24},{1,8},{2,11},{3,27},{4,28},{5,12},{6,15},{7,31},{8,1},{9,17... | collective-permute-start | bytes 393224 | tf_op jit(solution)/shard_map/ppermute | solution.py:43
  16.5 4.9 %collective-permute-start.12 = (f32[32,1024]{1,0:T(8,128)S(1)}, f32[32,1024]{1,0:T(8,128)S(1)}, u32[]{:S(2)}, u32[]{:S(2)}) collective-permute-start(f32[32,1024]{1,0:T(8,128)S(1)} %get-tuple-element.56), channel_id=1, source_target_pairs={{0,24},{1,8},{2,11},{3,27},{4,28},{5,12},{6,15},{7,31},{8,1},{9,17... | collective-permute-start | bytes 393224 | tf_op jit(solution)/shard_map/ppermute | solution.py:43
  17.1 5.8 %collective-permute-start.6 = (f32[32,1024]{1,0:T(8,128)S(1)}, f32[32,1024]{1,0:T(8,128)S(1)}, u32[]{:S(2)}, u32[]{:S(2)}) collective-permute-start(f32[32,1024]{1,0:T(8,128)S(1)} %add.75), channel_id=1, source_target_pairs={{0,9},{1,11},{2,8},{3,10},{4,13},{5,15},{6,12},{7,14},{8,2},{9,0},... | collective-permute-start | bytes 393224 | tf_op jit(solution)/shard_map/ppermute | solution.py:43
  17.7 5.5 %collective-permute-start.2 = (f32[32,1024]{1,0:T(8,128)S(1)}, f32[32,1024]{1,0:T(8,128)S(1)}, u32[]{:S(2)}, u32[]{:S(2)}) collective-permute-start(f32[32,1024]{1,0:T(8,128)S(1)} %add.72), channel_id=1, source_target_pairs={{0,10},{1,25},{2,26},{3,9},{4,14},{5,29},{6,30},{7,13},{8,16},{9,3... | collective-permute-start | bytes 393224 | tf_op jit(solution)/shard_map/ppermute | solution.py:43
  19.7 5.5 %collective-permute-start.17 = (f32[32,1024]{1,0:T(8,128)S(1)}, f32[32,1024]{1,0:T(8,128)S(1)}, u32[]{:S(2)}, u32[]{:S(2)}) collective-permute-start(f32[32,1024]{1,0:T(8,128)S(1)} %add.81), channel_id=1, source_target_pairs={{0,24},{1,8},{2,11},{3,27},{4,28},{5,12},{6,15},{7,31},{8,1},{9,17... | collective-permute-start | bytes 393224 | tf_op jit(solution)/shard_map/ppermute | solution.py:43
  21.4 5.6 %collective-permute-start.13 = (f32[32,1024]{1,0:T(8,128)S(1)}, f32[32,1024]{1,0:T(8,128)S(1)}, u32[]{:S(2)}, u32[]{:S(2)}) collective-permute-start(f32[32,1024]{1,0:T(8,128)S(1)} %add.78), channel_id=1, source_target_pairs={{0,9},{1,11},{2,8},{3,10},{4,13},{5,15},{6,12},{7,14},{8,2},{9,0},... | collective-permute-start | bytes 393224 | tf_op jit(solution)/shard_map/ppermute | solution.py:43
  22.9 5.6 %collective-permute-start.7 = (f32[32,1024]{1,0:T(8,128)S(1)}, f32[32,1024]{1,0:T(8,128)S(1)}, u32[]{:S(2)}, u32[]{:S(2)}) collective-permute-start(f32[32,1024]{1,0:T(8,128)S(1)} %add.76), channel_id=1, source_target_pairs={{0,10},{1,25},{2,26},{3,9},{4,14},{5,29},{6,30},{7,13},{8,16},{9,3... | collective-permute-start | bytes 393224 | tf_op jit(solution)/shard_map/ppermute | solution.py:43
  23.2 6.1 %collective-permute-start.3 = (f32[32,1024]{1,0:T(8,128)S(1)}, f32[32,1024]{1,0:T(8,128)S(1)}, u32[]{:S(2)}, u32[]{:S(2)}) collective-permute-start(f32[32,1024]{1,0:T(8,128)S(1)} %add.73), channel_id=1, source_target_pairs={{0,24},{1,8},{2,11},{3,27},{4,28},{5,12},{6,15},{7,31},{8,1},{9,17... | collective-permute-start | bytes 393224 | tf_op jit(solution)/shard_map/ppermute | solution.py:43
  25.2 5.8 %collective-permute-start.18 = (f32[32,1024]{1,0:T(8,128)S(1)}, f32[32,1024]{1,0:T(8,128)S(1)}, u32[]{:S(2)}, u32[]{:S(2)}) collective-permute-start(f32[32,1024]{1,0:T(8,128)S(1)} %add.82), channel_id=1, source_target_pairs={{0,9},{1,11},{2,8},{3,10},{4,13},{5,15},{6,12},{7,14},{8,2},{9,0},... | collective-permute-start | bytes 393224 | tf_op jit(solution)/shard_map/ppermute | solution.py:43
  27.0 5.8 %collective-permute-start.14 = (f32[32,1024]{1,0:T(8,128)S(1)}, f32[32,1024]{1,0:T(8,128)S(1)}, u32[]{:S(2)}, u32[]{:S(2)}) collective-permute-start(f32[32,1024]{1,0:T(8,128)S(1)} %add.79), channel_id=1, source_target_pairs={{0,10},{1,25},{2,26},{3,9},{4,14},{5,29},{6,30},{7,13},{8,16},{9,3... | collective-permute-start | bytes 393224 | tf_op jit(solution)/shard_map/ppermute | solution.py:43
  28.5 5.3 %collective-permute-start.8 = (f32[32,1024]{1,0:T(8,128)S(1)}, f32[32,1024]{1,0:T(8,128)S(1)}, u32[]{:S(2)}, u32[]{:S(2)}) collective-permute-start(f32[32,1024]{1,0:T(8,128)S(1)} %add.77.own_ref), channel_id=1, source_target_pairs={{0,24},{1,8},{2,11},{3,27},{4,28},{5,12},{6,15},{7,31},{8,1},{9,17... | collective-permute-start | bytes 393224 | tf_op jit(solution)/shard_map/ppermute | solution.py:43
  29.4 6.6 %collective-permute-start.4 = (f32[32,1024]{1,0:T(8,128)S(1)}, f32[32,1024]{1,0:T(8,128)S(1)}, u32[]{:S(2)}, u32[]{:S(2)}) collective-permute-start(f32[32,1024]{1,0:T(8,128)S(1)} %add.74.own_ref), channel_id=1, source_target_pairs={{0,9},{1,11},{2,8},{3,10},{4,13},{5,15},{6,12},{7,14},{8,2},{9,0},... | collective-permute-start | bytes 393224 | tf_op jit(solution)/shard_map/ppermute | solution.py:43
  31.0 6.6 %collective-permute-start.19 = (f32[32,1024]{1,0:T(8,128)S(1)}, f32[32,1024]{1,0:T(8,128)S(1)}, u32[]{:S(2)}, u32[]{:S(2)}) collective-permute-start(f32[32,1024]{1,0:T(8,128)S(1)} %add.83.own_ref), channel_id=1, source_target_pairs={{0,10},{1,25},{2,26},{3,9},{4,14},{5,29},{6,30},{7,13},{8,16},{9,3... | collective-permute-start | bytes 393224 | tf_op jit(solution)/shard_map/ppermute | solution.py:43
  32.9 6.3 %collective-permute-start.15 = (f32[32,1024]{1,0:T(8,128)S(1)}, f32[32,1024]{1,0:T(8,128)S(1)}, u32[]{:S(2)}, u32[]{:S(2)}) collective-permute-start(f32[32,1024]{1,0:T(8,128)S(1)} %add.80.own_ref), channel_id=1, source_target_pairs={{0,24},{1,8},{2,11},{3,27},{4,28},{5,12},{6,15},{7,31},{8,1},{9,17... | collective-permute-start | bytes 393224 | tf_op jit(solution)/shard_map/ppermute | solution.py:43
  34.4 5.4 %collective-permute-start.10 = (f32[64,1024]{1,0:T(8,128)S(1)}, f32[64,1024]{1,0:T(8,128)S(1)}, u32[]{:S(2)}, u32[]{:S(2)}) collective-permute-start(f32[64,1024]{1,0:T(8,128)S(1)} %shard_map.63.refs_1_), channel_id=1, source_target_pairs={{0,8},{1,9},{2,10},{3,11},{4,12},{5,13},{6,14},{7,15},{8,0},{9,1},... | collective-permute-start | bytes 786440 | tf_op jit(solution)/shard_map/ppermute | solution.py:43
  49.6 5.6 %collective-permute-start.23 = (f32[32,1024]{1,0:T(8,128)S(1)}, f32[32,1024]{1,0:T(8,128)S(1)}, u32[]{:S(2)}, u32[]{:S(2)}) collective-permute-start(f32[32,1024]{1,0:T(8,128)S(1)} %get-tuple-element.67), channel_id=1, source_target_pairs={{0,9},{1,11},{2,8},{3,10},{4,13},{5,15},{6,12},{7,14},{8,2},{9,0},... | collective-permute-start | bytes 393224 | tf_op jit(solution)/shard_map/ppermute | solution.py:43
  51.3 5.0 %collective-permute-start.38 = (f32[32,1024]{1,0:T(8,128)S(1)}, f32[32,1024]{1,0:T(8,128)S(1)}, u32[]{:S(2)}, u32[]{:S(2)}) collective-permute-start(f32[32,1024]{1,0:T(8,128)S(1)} %get-tuple-element.75), channel_id=1, source_target_pairs={{0,10},{1,25},{2,26},{3,9},{4,14},{5,29},{6,30},{7,13},{8,16},{9,3... | collective-permute-start | bytes 393224 | tf_op jit(solution)/shard_map/ppermute | solution.py:43
  52.3 5.2 %collective-permute-start.34 = (f32[32,1024]{1,0:T(8,128)S(1)}, f32[32,1024]{1,0:T(8,128)S(1)}, u32[]{:S(2)}, u32[]{:S(2)}) collective-permute-start(f32[32,1024]{1,0:T(8,128)S(1)} %get-tuple-element.73), channel_id=1, source_target_pairs={{0,24},{1,8},{2,11},{3,27},{4,28},{5,12},{6,15},{7,31},{8,1},{9,17... | collective-permute-start | bytes 393224 | tf_op jit(solution)/shard_map/ppermute | solution.py:43
  53.5 5.1 %collective-permute-start.28 = (f32[32,1024]{1,0:T(8,128)S(1)}, f32[32,1024]{1,0:T(8,128)S(1)}, u32[]{:S(2)}, u32[]{:S(2)}) collective-permute-start(f32[32,1024]{1,0:T(8,128)S(1)} %add.87), channel_id=1, source_target_pairs={{0,9},{1,11},{2,8},{3,10},{4,13},{5,15},{6,12},{7,14},{8,2},{9,0},... | collective-permute-start | bytes 393224 | tf_op jit(solution)/shard_map/ppermute | solution.py:43
  55.2 5.8 %collective-permute-start.24 = (f32[32,1024]{1,0:T(8,128)S(1)}, f32[32,1024]{1,0:T(8,128)S(1)}, u32[]{:S(2)}, u32[]{:S(2)}) collective-permute-start(f32[32,1024]{1,0:T(8,128)S(1)} %add.84), channel_id=1, source_target_pairs={{0,10},{1,25},{2,26},{3,9},{4,14},{5,29},{6,30},{7,13},{8,16},{9,3... | collective-permute-start | bytes 393224 | tf_op jit(solution)/shard_map/ppermute | solution.py:43
  56.3 5.4 %collective-permute-start.39 = (f32[32,1024]{1,0:T(8,128)S(1)}, f32[32,1024]{1,0:T(8,128)S(1)}, u32[]{:S(2)}, u32[]{:S(2)}) collective-permute-start(f32[32,1024]{1,0:T(8,128)S(1)} %add.93), channel_id=1, source_target_pairs={{0,24},{1,8},{2,11},{3,27},{4,28},{5,12},{6,15},{7,31},{8,1},{9,17... | collective-permute-start | bytes 393224 | tf_op jit(solution)/shard_map/ppermute | solution.py:43
  57.5 5.7 %collective-permute-start.35 = (f32[32,1024]{1,0:T(8,128)S(1)}, f32[32,1024]{1,0:T(8,128)S(1)}, u32[]{:S(2)}, u32[]{:S(2)}) collective-permute-start(f32[32,1024]{1,0:T(8,128)S(1)} %add.90), channel_id=1, source_target_pairs={{0,9},{1,11},{2,8},{3,10},{4,13},{5,15},{6,12},{7,14},{8,2},{9,0},... | collective-permute-start | bytes 393224 | tf_op jit(solution)/shard_map/ppermute | solution.py:43
  58.6 5.4 %collective-permute-start.29 = (f32[32,1024]{1,0:T(8,128)S(1)}, f32[32,1024]{1,0:T(8,128)S(1)}, u32[]{:S(2)}, u32[]{:S(2)}) collective-permute-start(f32[32,1024]{1,0:T(8,128)S(1)} %add.88), channel_id=1, source_target_pairs={{0,10},{1,25},{2,26},{3,9},{4,14},{5,29},{6,30},{7,13},{8,16},{9,3... | collective-permute-start | bytes 393224 | tf_op jit(solution)/shard_map/ppermute | solution.py:43
  61.0 5.5 %collective-permute-start.25 = (f32[32,1024]{1,0:T(8,128)S(1)}, f32[32,1024]{1,0:T(8,128)S(1)}, u32[]{:S(2)}, u32[]{:S(2)}) collective-permute-start(f32[32,1024]{1,0:T(8,128)S(1)} %add.85), channel_id=1, source_target_pairs={{0,24},{1,8},{2,11},{3,27},{4,28},{5,12},{6,15},{7,31},{8,1},{9,17... | collective-permute-start | bytes 393224 | tf_op jit(solution)/shard_map/ppermute | solution.py:43
  61.7 5.7 %collective-permute-start.40 = (f32[32,1024]{1,0:T(8,128)S(1)}, f32[32,1024]{1,0:T(8,128)S(1)}, u32[]{:S(2)}, u32[]{:S(2)}) collective-permute-start(f32[32,1024]{1,0:T(8,128)S(1)} %add.94), channel_id=1, source_target_pairs={{0,9},{1,11},{2,8},{3,10},{4,13},{5,15},{6,12},{7,14},{8,2},{9,0},... | collective-permute-start | bytes 393224 | tf_op jit(solution)/shard_map/ppermute | solution.py:43
  63.2 5.4 %collective-permute-start.36 = (f32[32,1024]{1,0:T(8,128)S(1)}, f32[32,1024]{1,0:T(8,128)S(1)}, u32[]{:S(2)}, u32[]{:S(2)}) collective-permute-start(f32[32,1024]{1,0:T(8,128)S(1)} %add.91), channel_id=1, source_target_pairs={{0,10},{1,25},{2,26},{3,9},{4,14},{5,29},{6,30},{7,13},{8,16},{9,3... | collective-permute-start | bytes 393224 | tf_op jit(solution)/shard_map/ppermute | solution.py:43
  64.1 5.7 %collective-permute-start.30 = (f32[32,1024]{1,0:T(8,128)S(1)}, f32[32,1024]{1,0:T(8,128)S(1)}, u32[]{:S(2)}, u32[]{:S(2)}) collective-permute-start(f32[32,1024]{1,0:T(8,128)S(1)} %add.89.own_ref), channel_id=1, source_target_pairs={{0,24},{1,8},{2,11},{3,27},{4,28},{5,12},{6,15},{7,31},{8,1},{9,17... | collective-permute-start | bytes 393224 | tf_op jit(solution)/shard_map/ppermute | solution.py:43
  66.5 6.6 %collective-permute-start.26 = (f32[32,1024]{1,0:T(8,128)S(1)}, f32[32,1024]{1,0:T(8,128)S(1)}, u32[]{:S(2)}, u32[]{:S(2)}) collective-permute-start(f32[32,1024]{1,0:T(8,128)S(1)} %add.86.own_ref), channel_id=1, source_target_pairs={{0,9},{1,11},{2,8},{3,10},{4,13},{5,15},{6,12},{7,14},{8,2},{9,0},... | collective-permute-start | bytes 393224 | tf_op jit(solution)/shard_map/ppermute | solution.py:43
  67.5 6.6 %collective-permute-start.41 = (f32[32,1024]{1,0:T(8,128)S(1)}, f32[32,1024]{1,0:T(8,128)S(1)}, u32[]{:S(2)}, u32[]{:S(2)}) collective-permute-start(f32[32,1024]{1,0:T(8,128)S(1)} %add.95.own_ref), channel_id=1, source_target_pairs={{0,10},{1,25},{2,26},{3,9},{4,14},{5,29},{6,30},{7,13},{8,16},{9,3... | collective-permute-start | bytes 393224 | tf_op jit(solution)/shard_map/ppermute | solution.py:43
  68.6 6.3 %collective-permute-start.37 = (f32[32,1024]{1,0:T(8,128)S(1)}, f32[32,1024]{1,0:T(8,128)S(1)}, u32[]{:S(2)}, u32[]{:S(2)}) collective-permute-start(f32[32,1024]{1,0:T(8,128)S(1)} %add.92.own_ref), channel_id=1, source_target_pairs={{0,24},{1,8},{2,11},{3,27},{4,28},{5,12},{6,15},{7,31},{8,1},{9,17... | collective-permute-start | bytes 393224 | tf_op jit(solution)/shard_map/ppermute | solution.py:43
  70.4 5.5 %collective-permute-start.32 = (f32[64,1024]{1,0:T(8,128)S(1)}, f32[64,1024]{1,0:T(8,128)S(1)}, u32[]{:S(2)}, u32[]{:S(2)}) collective-permute-start(f32[64,1024]{1,0:T(8,128)S(1)} %shard_map.71.refs_1_), channel_id=1, source_target_pairs={{0,8},{1,9},{2,10},{3,11},{4,12},{5,13},{6,14},{7,15},{8,0},{9,1},... | collective-permute-start | bytes 786440 | tf_op jit(solution)/shard_map/ppermute | solution.py:43
  (12 other events, 35.7 us)
where the time goes:
time: 79.2 us; the launch traced here: 79 us
  starting transfers between devices  38.9 us (49%)
  Pallas kernels  21.9 us (28%)
  waiting for transfers between devices  16.7 us (21%)
  between operations  0.96 us (1%)
    ppermute x44, starting transfers between devices, from_partner(): return lax.ppermute(values, ('near', 'far'), pairs)  38.9 us
    ppermute x44, waiting for transfers between devices, from_partner(): return lax.ppermute(values, ('near', 'far'), pairs)  16.7 us
    pallas_call x2, Pallas kernels, shards(): pl.pallas_call(functools.partial(expand_kernel, 0 if first else len(sums_...  7.27 us
    pallas_call x2, Pallas kernels, shards(): pl.pallas_call(functools.partial(reduce_kernel, None if last else iterati...  4.7 us
    pallas_call x8, Pallas kernels, chain(): pl.pallas_call(functools.partial(join_kernel, index), out_shape=jax.Shape...  4.5 us
    pallas_call x2, Pallas kernels, store(): pl.pallas_call(store_kernel, out_shape=jax.ShapeDtypeStruct((rows * len(p...  3.08 us
    pallas_call x4, Pallas kernels, sum_over_cube(): pl.pallas_call(functools.partial(meet_kernel, indices), out_shape=(jax.Sh...  2.39 us
  transfers between devices with their start and end apart: 44, of which 26 were waited for; matrix products, arithmetic and copies ran while one was open for 0% of the time, Pallas kernels for 11%

commit v1 on v0

--- a/solution.py
+++ b/solution.py
@@ -18,7 +18,6 @@
     ((1, 2, 3), (2, 3, 1)),
 )
 BITS = 4
-SMEM = pl.BlockSpec(memory_space=pltpu.SMEM)
 VMEM = pl.BlockSpec(memory_space=pltpu.VMEM)
 HBM = pl.BlockSpec(memory_space=pltpu.HBM)
 SMALL = pltpu.CompilerParams(vmem_limit_bytes=2**20)
@@ -29,6 +28,11 @@
 def bits_of(near, far):
     chip = ((near >> 1) & 1, far & 1, (far >> 1) & 1)
     return ((near & 1) ^ chip[0] ^ chip[1] ^ chip[2],) + chip
+
+
+def places():
+    bits = bits_of(lax.axis_index("near"), lax.axis_index("far"))
+    return [bits[0]] + [jnp.where(bits[0] == 0, bits[even[0]], bits[odd[0]]) for even, odd in ORDERS]
 
 
 def from_partner(values, *bit_of_role):
@@ -43,14 +47,14 @@
     return lax.ppermute(values, ("near", "far"), pairs)
 
 
-def join_kernel(index, places_ref, own_ref, rest_ref, out_ref):
+def join_kernel(index, own_ref, rest_ref, out_ref):
     rows = own_ref.shape[0]
-    place = places_ref[index]
+    place = places()[index]
     out_ref[pl.ds(pl.multiple_of(place * rows, rows), rows), :] = own_ref[...]
     out_ref[pl.ds(pl.multiple_of((1 - place) * rows, rows), rows), :] = rest_ref[...]
 
 
-def chain(keep, send, index, places):
+def chain(keep, send, index):
     even, odd = ORDERS[index - 1]
     own = keep + from_partner(send, even[0], odd[0])
     own = own + from_partner(own, even[1], odd[1])
@@ -60,34 +64,35 @@
     return pl.pallas_call(
         functools.partial(join_kernel, index),
         out_shape=jax.ShapeDtypeStruct((2 * rows, columns), f32),
-        in_specs=[SMEM, VMEM, VMEM],
+        in_specs=[VMEM, VMEM],
         out_specs=VMEM,
         compiler_params=SMALL,
-    )(places, own, rest)
-
-
-def meet_kernel(indices, places_ref, keep_ref, got_ref, *outs):
+    )(own, rest)
+
+
+def meet_kernel(indices, keep_ref, got_ref, *outs):
     rows = outs[0].shape[0]
+    place = places()
     for k, index in enumerate(indices):
         low, high = pl.ds(2 * k * rows, rows), pl.ds((2 * k + 1) * rows, rows)
-        stays_low = places_ref[index] == 0
+        stays_low = place[index] == 0
         low, high = keep_ref[low, :] + got_ref[low, :], keep_ref[high, :] + got_ref[high, :]
         outs[2 * k][...] = jnp.where(stays_low, low, high)
         outs[2 * k + 1][...] = jnp.where(stays_low, high, low)
 
 
-def sum_over_cube(keep, send, indices, places):
+def sum_over_cube(keep, send, indices):
     rows, columns = keep.shape
     count = 2 * len(indices)
     got = pltpu.with_memory_space_constraint(from_partner(send, 0, 0), pltpu.VMEM)
     pieces = pl.pallas_call(
         functools.partial(meet_kernel, indices),
         out_shape=(jax.ShapeDtypeStruct((rows // count, columns), f32),) * count,
-        in_specs=[SMEM, VMEM, VMEM],
+        in_specs=[VMEM, VMEM],
         out_specs=(VMEM,) * count,
         compiler_params=SMALL,
-    )(places, keep, got)
-    parts = [chain(pieces[2 * k], pieces[2 * k + 1], index, places) for k, index in enumerate(indices)]
+    )(keep, got)
+    parts = [chain(pieces[2 * k], pieces[2 * k + 1], index) for k, index in enumerate(indices)]
     return parts + [from_partner(part, 0, 0) for part in parts]
 
 
@@ -96,28 +101,31 @@
     return (role if index < per_role else 1 - role) * per_role + index % per_role
 
 
-def store_kernel(places_ref, *refs):
-    *parts, out_ref, sems = refs
+def store_kernel(count, *refs):
+    parts, outs, sems = refs[: 2 * count], refs[2 * count : -1], refs[-1]
     rows = parts[0].shape[0]
+    role = places()[0]
     copies = []
     for i, part in enumerate(parts):
-        start = pl.multiple_of(place_of(i, len(parts), places_ref[0]) * rows, rows)
-        copies.append(pltpu.make_async_copy(part, out_ref.at[pl.ds(start, rows), :], sems.at[i]))
+        start = pl.multiple_of(place_of(i % count, count, role) * rows, rows)
+        copies.append(pltpu.make_async_copy(part, outs[i // count].at[pl.ds(start, rows), :], sems.at[i]))
         copies[-1].start()
     for copy in copies:
         copy.wait()
 
 
-def store(parts, places):
-    rows, columns = parts[0].shape
+def store(reducing, expanding):
+    rows, columns = reducing[0].shape
+    count = len(reducing)
     return pl.pallas_call(
-        store_kernel,
-        out_shape=jax.ShapeDtypeStruct((rows * len(parts), columns), f32),
-        in_specs=[SMEM] + [VMEM] * len(parts),
-        out_specs=HBM,
-        scratch_shapes=[pltpu.SemaphoreType.DMA((len(parts),))],
+        functools.partial(store_kernel, count),
+        out_shape=(jax.ShapeDtypeStruct((rows * count, columns), f32),) * 2,
+        in_specs=[VMEM] * (2 * count),
+        out_specs=(HBM, HBM),
+        scratch_shapes=[pltpu.SemaphoreType.DMA((2 * count,))],
         compiler_params=SMALL,
-    )(places, *parts)
+        name="store",
+    )(*reducing, *expanding)
 
 
 def halves(values):
@@ -143,15 +151,16 @@
 NT = ((1,), (1,))
 
 
-def expand_kernel(count, places_ref, x_in, g_in, *refs):
+def expand_kernel(count, x_in, g_in, *refs):
     if count:
         r_parts, e_parts, outs = refs[:count], refs[count : 2 * count], refs[2 * count :]
         keep_ref, send_ref, zh_ref, zl_ref, slope_ref, r_ref, e_ref = outs
         x_ref, g_ref = x_in, g_in
         rows = r_parts[0].shape[0]
+        role = places()[0]
         for parts, whole_ref in ((r_parts, r_ref), (e_parts, e_ref)):
             for i, part in enumerate(parts):
-                start = pl.multiple_of(place_of(i, count, places_ref[0]) * rows, rows)
+                start = pl.multiple_of(place_of(i, count, role) * rows, rows)
                 whole_ref[pl.ds(start, rows), :] = part[...]
     else:
         r_in, e_in, keep_ref, send_ref, zh_ref, zl_ref, slope_ref, r_ref, e_ref, x_ref, g_ref, sems = refs
@@ -185,12 +194,12 @@
     zl_ref[...] = grads[1]
     stepped = (e_ref[...].astype(f32) - learn_rate * expand_scale * product(hidden_t, grads, NN)) * (0.5**BITS)
     rows = width // 2
-    even = places_ref[0] == 0
+    even = places()[0] == 0
     keep_ref[...] = jnp.where(even, stepped[:rows], stepped[rows:])
     send_ref[...] = jnp.where(even, stepped[rows:], stepped[:rows])
 
 
-def reduce_kernel(upcoming, places_ref, x_all, g_all, x_ref, r_ref, e_ref, zh_ref, zl_ref, slope_ref, keep_ref, send_ref, *refs):
+def reduce_kernel(upcoming, x_all, g_all, x_ref, r_ref, e_ref, zh_ref, zl_ref, slope_ref, keep_ref, send_ref, *refs):
     if upcoming is not None:
         next_x_ref, next_g_ref, sems = refs
         copies = (
@@ -206,7 +215,7 @@
     grad_pre = halves(grad_hidden * slope_ref[...])
     stepped = (r_ref[...].astype(f32) - learn_rate * reduce_scale * product(grad_pre, (x_ref[...],), NN)) * (0.5**BITS)
     rows = width // 2
-    even = places_ref[0] == 0
+    even = places()[0] == 0
     keep_ref[...] = jnp.where(even, stepped[:rows], stepped[rows:])
     send_ref[...] = jnp.where(even, stepped[rows:], stepped[:rows])
     if upcoming is not None:
@@ -215,8 +224,6 @@
 
 
 def shards(w_reduce, w_expand, inputs, out_grads):
-    bits = bits_of(lax.axis_index("near"), lax.axis_index("far"))
-    places = jnp.stack([bits[0]] + [jnp.where(bits[0] == 0, bits[even[0]], bits[odd[0]]) for even, odd in ORDERS]).astype(jnp.int32)
     held = [pltpu.with_memory_space_constraint(array[0, 0], pltpu.HBM) for array in (w_reduce, w_expand, inputs, out_grads)]
     reducing, expanding, inputs, out_grads = held
     iterations, rows, columns = inputs.shape
@@ -230,28 +237,29 @@
         results = pl.pallas_call(
             functools.partial(expand_kernel, 0 if first else len(sums_r)),
             out_shape=(half, half, acts, acts, slopes, weights, weights) + ((acts,) if first else ()),
-            in_specs=[SMEM] + ([HBM] * 4 if first else [VMEM] * (2 + len(sums_r) + len(sums_e))),
+            in_specs=[HBM] * 4 if first else [VMEM] * (2 + len(sums_r) + len(sums_e)),
             out_specs=(VMEM,) * (8 if first else 7),
             scratch_shapes=[pltpu.VMEM((rows, columns), bf16), pltpu.SemaphoreType.DMA((4,))] if first else [],
             compiler_params=LARGE,
-        )(places, *((inputs, out_grads, reducing, expanding) if first else (feats, grads, *sums_r, *sums_e)))
+        )(*((inputs, out_grads, reducing, expanding) if first else (feats, grads, *sums_r, *sums_e)))
         keep_e, send_e, zh, zl, slope, reducing, expanding = results[:7]
         if first:
             feats = results[7]
         results = pl.pallas_call(
             functools.partial(reduce_kernel, None if last else iteration + 1),
             out_shape=(half, half) + (() if last else (acts, acts)),
-            in_specs=[SMEM, HBM, HBM] + [VMEM] * 6,
+            in_specs=[HBM, HBM] + [VMEM] * 6,
             out_specs=(VMEM,) * (2 if last else 4),
             scratch_shapes=[] if last else [pltpu.SemaphoreType.DMA((2,))],
             compiler_params=LARGE,
-        )(places, inputs, out_grads, feats, reducing, expanding, zh, zl, slope)
+        )(inputs, out_grads, feats, reducing, expanding, zh, zl, slope)
         keep_r, send_r = results[:2]
         if not last:
             feats, grads = results[2:]
-        sums_e = sum_over_cube(keep_e, send_e, (1, 2), places)
-        sums_r = sum_over_cube(keep_r, send_r, (3, 4), places)
-    return (store(sums_r, places)[None, None], store(sums_e, places)[None, None])
+        sums_e = sum_over_cube(keep_e, send_e, (1, 2))
+        sums_r = sum_over_cube(keep_r, send_r, (3, 4))
+    reducing, expanding = store(sums_r, sums_e)
+    return reducing[None, None], expanding[None, None]
 
 
 def solution(mesh):

time: 79.2 us -> 74 us (0.934)
  Pallas kernels: 21.9 us -> 11.7 us
  starting transfers between devices: 38.9 us -> 43.7 us
    ppermute x44, starting transfers between devices: 38.9 us -> 43.7 us  [from_partner(): return lax.ppermute(values, ('near', 'far'), pairs)]
    pallas_call x8, Pallas kernels: 4.5 us -> 0.23 us  [chain(): pl.pallas_call(functools.partial(join_kernel, index), out_shape=jax.Shape...]
    pallas_call x4, Pallas kernels: 2.39 us -> 0.25 us  [sum_over_cube(): pl.pallas_call(functools.partial(meet_kernel, indices), out_shape=(jax.Sh...]
    pallas_call x2 -> x1, Pallas kernels: 3.08 us -> 1.37 us  [store(): pl.pallas_call(functools.partial(store_kernel, count), out_shape=(jax.Sha...]
    pallas_call x2, Pallas kernels: 7.27 us -> 6.18 us  [shards(): pl.pallas_call(functools.partial(expand_kernel, 0 if first else len(sums_...]
    pallas_call x2, Pallas kernels: 4.7 us -> 3.65 us  [shards(): pl.pallas_call(functools.partial(reduce_kernel, None if last else iterati...]
  transfers between devices with their start and end apart: 44 -> 44, of which waited for: 26 -> 23; matrix products, arithmetic and copies ran while one was open for 0% -> 1% of each run, Pallas kernels for 11% -> 1%
where the time goes in v1:
time: 74 us; the launch traced here: 73.9 us
  starting transfers between devices  43.7 us (59%)
  waiting for transfers between devices  17.1 us (23%)
  Pallas kernels  11.7 us (16%)
  between operations  0.89 us (1%)
    ppermute x44, starting transfers between devices, from_partner(): return lax.ppermute(values, ('near', 'far'), pairs)  43.7 us
    ppermute x44, waiting for transfers between devices, from_partner(): return lax.ppermute(values, ('near', 'far'), pairs)  17.1 us
    pallas_call x2, Pallas kernels, shards(): pl.pallas_call(functools.partial(expand_kernel, 0 if first else len(sums_...  6.18 us
    pallas_call x2, Pallas kernels, shards(): pl.pallas_call(functools.partial(reduce_kernel, None if last else iterati...  3.65 us
  transfers between devices with their start and end apart: 44, of which 23 were waited for; matrix products, arithmetic and copies ran while one was open for 1% of the time, Pallas kernels for 1%

profile of v1, /device:TPU:0, one launch (start us, length us, event | category | flops | bytes accessed | tf_op | source)
XLA Modules:
  0.0 73.9 jit_solution(6859273553476080462)
XLA Ops:
  0.6 3.7 %shard_map.59 = (f32[128,1024]{1,0:T(8,128)S(1)}, f32[128,1024]{1,0:T(8,128)S(1)}, bf16[256,1024]{1,0:T(8,128)(2,1)S(1)}, bf16[256,1024]{1,0:T(8,128)(2,1)S(1)},...) custom-call(bf16[2,256,1024]{2,1,0:T(8,128)(2,1)} %bitcast.6, ...), custom_call_target="tpu_custom_call" | custom-call | tf_op jit(solution)/shard_map/pallas_call | solution.py:237
  4.3 2.2 %shard_map.60 = (f32[128,1024]{1,0:T(8,128)S(1)}, f32[128,1024]{1,0:T(8,128)S(1)}, bf16[256,1024]{1,0:T(8,128)(2,1)S(1)}, bf16[256,1024]{1,0:T(8,128)(2,1)S(1)}) custom-call(bf16[2,256,1024]{2,1,0:T(8,128)(2,1)} %bitcast.7, bf16[2,256,1024]{2,1,0:T(8,128)(2,1)} %bitcast.10, bf16[256,1024]{1,0:T(8,128)(2,1)S(1)} %get-tuple-element.41.x_ref, ...), custom_call_target="tpu_custom_call" | custom-call | tf_op jit(solution)/shard_map/pallas_call | solution.py:248
  7.2 1.5 %collective-permute-done.got_ref = f32[128,1024]{1,0:T(8,128)S(1)} collective-permute-done((f32[128,1024]{1,0:T(8,128)S(1)}, f32[128,1024]{1,0:T(8,128)S(1)}, u32[]{:S(2)}, u32[]{:S(2)}) %collective-permute-start) | collective-permute-done | bytes 524320 | tf_op jit(solution)/shard_map/ppermute | solution.py:47
  8.7 2.7 %collective-permute-start.5 = (f32[32,1024]{1,0:T(8,128)S(1)}, f32[32,1024]{1,0:T(8,128)S(1)}, u32[]{:S(2)}, u32[]{:S(2)}) collective-permute-start(f32[32,1024]{1,0:T(8,128)S(1)} %get-tuple-element.54), channel_id=1, source_target_pairs={{0,24},{1,8},{2,11},{3,27},{4,28},{5,12},{6,15},{7,31},{8,1},{9,17... | collective-permute-start | bytes 393224 | tf_op jit(solution)/shard_map/ppermute | solution.py:47
  11.3 1.5 %collective-permute-start.1 = (f32[32,1024]{1,0:T(8,128)S(1)}, f32[32,1024]{1,0:T(8,128)S(1)}, u32[]{:S(2)}, u32[]{:S(2)}) collective-permute-start(f32[32,1024]{1,0:T(8,128)S(1)} %get-tuple-element.52), channel_id=1, source_target_pairs={{0,9},{1,11},{2,8},{3,10},{4,13},{5,15},{6,12},{7,14},{8,2},{9,0},... | collective-permute-start | bytes 393224 | tf_op jit(solution)/shard_map/ppermute | solution.py:47
  12.9 1.4 %collective-permute-start.16 = (f32[32,1024]{1,0:T(8,128)S(1)}, f32[32,1024]{1,0:T(8,128)S(1)}, u32[]{:S(2)}, u32[]{:S(2)}) collective-permute-start(f32[32,1024]{1,0:T(8,128)S(1)} %get-tuple-element.60), channel_id=1, source_target_pairs={{0,10},{1,25},{2,26},{3,9},{4,14},{5,29},{6,30},{7,13},{8,16},{9,3... | collective-permute-start | bytes 393224 | tf_op jit(solution)/shard_map/ppermute | solution.py:47
  14.8 1.1 %collective-permute-start.6 = (f32[32,1024]{1,0:T(8,128)S(1)}, f32[32,1024]{1,0:T(8,128)S(1)}, u32[]{:S(2)}, u32[]{:S(2)}) collective-permute-start(f32[32,1024]{1,0:T(8,128)S(1)} %add.75), channel_id=1, source_target_pairs={{0,9},{1,11},{2,8},{3,10},{4,13},{5,15},{6,12},{7,14},{8,2},{9,0},... | collective-permute-start | bytes 393224 | tf_op jit(solution)/shard_map/ppermute | solution.py:47
  16.0 1.8 %collective-permute-start.2 = (f32[32,1024]{1,0:T(8,128)S(1)}, f32[32,1024]{1,0:T(8,128)S(1)}, u32[]{:S(2)}, u32[]{:S(2)}) collective-permute-start(f32[32,1024]{1,0:T(8,128)S(1)} %add.72), channel_id=1, source_target_pairs={{0,10},{1,25},{2,26},{3,9},{4,14},{5,29},{6,30},{7,13},{8,16},{9,3... | collective-permute-start | bytes 393224 | tf_op jit(solution)/shard_map/ppermute | solution.py:47
  17.9 2.2 %collective-permute-start.17 = (f32[32,1024]{1,0:T(8,128)S(1)}, f32[32,1024]{1,0:T(8,128)S(1)}, u32[]{:S(2)}, u32[]{:S(2)}) collective-permute-start(f32[32,1024]{1,0:T(8,128)S(1)} %add.81), channel_id=1, source_target_pairs={{0,24},{1,8},{2,11},{3,27},{4,28},{5,12},{6,15},{7,31},{8,1},{9,17... | collective-permute-start | bytes 393224 | tf_op jit(solution)/shard_map/ppermute | solution.py:47
  21.2 2.2 %collective-permute-start.3 = (f32[32,1024]{1,0:T(8,128)S(1)}, f32[32,1024]{1,0:T(8,128)S(1)}, u32[]{:S(2)}, u32[]{:S(2)}) collective-permute-start(f32[32,1024]{1,0:T(8,128)S(1)} %add.73), channel_id=1, source_target_pairs={{0,24},{1,8},{2,11},{3,27},{4,28},{5,12},{6,15},{7,31},{8,1},{9,17... | collective-permute-start | bytes 393224 | tf_op jit(solution)/shard_map/ppermute | solution.py:47
  23.5 2.0 %collective-permute-start.18 = (f32[32,1024]{1,0:T(8,128)S(1)}, f32[32,1024]{1,0:T(8,128)S(1)}, u32[]{:S(2)}, u32[]{:S(2)}) collective-permute-start(f32[32,1024]{1,0:T(8,128)S(1)} %add.82), channel_id=1, source_target_pairs={{0,9},{1,11},{2,8},{3,10},{4,13},{5,15},{6,12},{7,14},{8,2},{9,0},... | collective-permute-start | bytes 393224 | tf_op jit(solution)/shard_map/ppermute | solution.py:47
  27.2 1.6 %collective-permute-start.4 = (f32[32,1024]{1,0:T(8,128)S(1)}, f32[32,1024]{1,0:T(8,128)S(1)}, u32[]{:S(2)}, u32[]{:S(2)}) collective-permute-start(f32[32,1024]{1,0:T(8,128)S(1)} %add.74.own_ref), channel_id=1, source_target_pairs={{0,9},{1,11},{2,8},{3,10},{4,13},{5,15},{6,12},{7,14},{8,2},{9,0},... | collective-permute-start | bytes 393224 | tf_op jit(solution)/shard_map/ppermute | solution.py:47
  29.5 1.3 %collective-permute-start.19 = (f32[32,1024]{1,0:T(8,128)S(1)}, f32[32,1024]{1,0:T(8,128)S(1)}, u32[]{:S(2)}, u32[]{:S(2)}) collective-permute-start(f32[32,1024]{1,0:T(8,128)S(1)} %add.83.own_ref), channel_id=1, source_target_pairs={{0,10},{1,25},{2,26},{3,9},{4,14},{5,29},{6,30},{7,13},{8,16},{9,3... | collective-permute-start | bytes 393224 | tf_op jit(solution)/shard_map/ppermute | solution.py:47
  33.3 2.2 %collective-permute-start.9 = (f32[64,1024]{1,0:T(8,128)S(1)}, f32[64,1024]{1,0:T(8,128)S(1)}, u32[]{:S(2)}, u32[]{:S(2)}) collective-permute-start(f32[64,1024]{1,0:T(8,128)S(1)} %shard_map.62.refs_0_), channel_id=1, source_target_pairs={{0,8},{1,9},{2,10},{3,11},{4,12},{5,13},{6,14},{7,15},{8,0},{9,1},... | collective-permute-start | bytes 786440 | tf_op jit(solution)/shard_map/ppermute | solution.py:47
  35.6 1.6 %collective-permute-start.21 = (f32[64,1024]{1,0:T(8,128)S(1)}, f32[64,1024]{1,0:T(8,128)S(1)}, u32[]{:S(2)}, u32[]{:S(2)}) collective-permute-start(f32[64,1024]{1,0:T(8,128)S(1)} %shard_map.66.refs_5_), channel_id=1, source_target_pairs={{0,8},{1,9},{2,10},{3,11},{4,12},{5,13},{6,14},{7,15},{8,0},{9,1},... | collective-permute-start | bytes 786440 | tf_op jit(solution)/shard_map/ppermute | solution.py:47
  38.8 2.5 %shard_map.67 = (f32[128,1024]{1,0:T(8,128)S(1)}, f32[128,1024]{1,0:T(8,128)S(1)}, bf16[256,1024]{1,0:T(8,128)(2,1)S(1)}, bf16[256,1024]{1,0:T(8,128)(2,1)S(1)},...) custom-call(bf16[256,1024]{1,0:T(8,128)(2,1)S(1)} %get-tuple-element.47.x_in.x_ref, ...), custom_call_target="tpu_custom_call" | custom-call | tf_op jit(solution)/shard_map/pallas_call | solution.py:237
  41.3 1.5 %shard_map.68 = (f32[128,1024]{1,0:T(8,128)S(1)}, f32[128,1024]{1,0:T(8,128)S(1)}) custom-call(bf16[2,256,1024]{2,1,0:T(8,128)(2,1)} %bitcast.8, bf16[2,256,1024]{2,1,0:T(8,128)(2,1)} %bitcast.11, bf16[256,1024]{1,0:T(8,128)(2,1)S(1)} %get-tuple-element.47.x_in.x_ref, f32[256,1024]{1,0:T(8,128)S(1)} %get-tuple-element.61.r_ref, ...), custom_call_target="tpu_custom_call" | custom-call | tf_op jit(solution)/shard_map/pallas_call | solution.py:248
  43.4 1.4 %collective-permute-done.22.got_ref = f32[128,1024]{1,0:T(8,128)S(1)} collective-permute-done((f32[128,1024]{1,0:T(8,128)S(1)}, f32[128,1024]{1,0:T(8,128)S(1)}, u32[]{:S(2)}, u32[]{:S(2)}) %collective-permute-start.22) | collective-permute-done | bytes 524320 | tf_op jit(solution)/shard_map/ppermute | solution.py:47
  44.8 1.1 %collective-permute-start.27 = (f32[32,1024]{1,0:T(8,128)S(1)}, f32[32,1024]{1,0:T(8,128)S(1)}, u32[]{:S(2)}, u32[]{:S(2)}) collective-permute-start(f32[32,1024]{1,0:T(8,128)S(1)} %get-tuple-element.71), channel_id=1, source_target_pairs={{0,24},{1,8},{2,11},{3,27},{4,28},{5,12},{6,15},{7,31},{8,1},{9,17... | collective-permute-start | bytes 393224 | tf_op jit(solution)/shard_map/ppermute | solution.py:47
  47.0 1.3 %collective-permute-start.34 = (f32[32,1024]{1,0:T(8,128)S(1)}, f32[32,1024]{1,0:T(8,128)S(1)}, u32[]{:S(2)}, u32[]{:S(2)}) collective-permute-start(f32[32,1024]{1,0:T(8,128)S(1)} %get-tuple-element.75), channel_id=1, source_target_pairs={{0,24},{1,8},{2,11},{3,27},{4,28},{5,12},{6,15},{7,31},{8,1},{9,17... | collective-permute-start | bytes 393224 | tf_op jit(solution)/shard_map/ppermute | solution.py:47
  49.9 1.8 %collective-permute-done.23 = f32[32,1024]{1,0:T(8,128)S(1)} collective-permute-done((f32[32,1024]{1,0:T(8,128)S(1)}, f32[32,1024]{1,0:T(8,128)S(1)}, u32[]{:S(2)}, u32[]{:S(2)}) %collective-permute-start.23) | collective-permute-done | bytes 131104 | tf_op jit(solution)/shard_map/ppermute | solution.py:47
  52.8 1.2 %collective-permute-start.35 = (f32[32,1024]{1,0:T(8,128)S(1)}, f32[32,1024]{1,0:T(8,128)S(1)}, u32[]{:S(2)}, u32[]{:S(2)}) collective-permute-start(f32[32,1024]{1,0:T(8,128)S(1)} %add.90), channel_id=1, source_target_pairs={{0,9},{1,11},{2,8},{3,10},{4,13},{5,15},{6,12},{7,14},{8,2},{9,0},... | collective-permute-start | bytes 393224 | tf_op jit(solution)/shard_map/ppermute | solution.py:47
  54.1 1.1 %collective-permute-start.29 = (f32[32,1024]{1,0:T(8,128)S(1)}, f32[32,1024]{1,0:T(8,128)S(1)}, u32[]{:S(2)}, u32[]{:S(2)}) collective-permute-start(f32[32,1024]{1,0:T(8,128)S(1)} %add.88), channel_id=1, source_target_pairs={{0,10},{1,25},{2,26},{3,9},{4,14},{5,29},{6,30},{7,13},{8,16},{9,3... | collective-permute-start | bytes 393224 | tf_op jit(solution)/shard_map/ppermute | solution.py:47
  55.2 1.6 %collective-permute-done.24 = f32[32,1024]{1,0:T(8,128)S(1)} collective-permute-done((f32[32,1024]{1,0:T(8,128)S(1)}, f32[32,1024]{1,0:T(8,128)S(1)}, u32[]{:S(2)}, u32[]{:S(2)}) %collective-permute-start.24) | collective-permute-done | bytes 131104 | tf_op jit(solution)/shard_map/ppermute | solution.py:47
  57.1 2.1 %collective-permute-start.40 = (f32[32,1024]{1,0:T(8,128)S(1)}, f32[32,1024]{1,0:T(8,128)S(1)}, u32[]{:S(2)}, u32[]{:S(2)}) collective-permute-start(f32[32,1024]{1,0:T(8,128)S(1)} %add.94), channel_id=1, source_target_pairs={{0,9},{1,11},{2,8},{3,10},{4,13},{5,15},{6,12},{7,14},{8,2},{9,0},... | collective-permute-start | bytes 393224 | tf_op jit(solution)/shard_map/ppermute | solution.py:47
  59.8 1.5 %collective-permute-start.30 = (f32[32,1024]{1,0:T(8,128)S(1)}, f32[32,1024]{1,0:T(8,128)S(1)}, u32[]{:S(2)}, u32[]{:S(2)}) collective-permute-start(f32[32,1024]{1,0:T(8,128)S(1)} %add.89.own_ref), channel_id=1, source_target_pairs={{0,24},{1,8},{2,11},{3,27},{4,28},{5,12},{6,15},{7,31},{8,1},{9,17... | collective-permute-start | bytes 393224 | tf_op jit(solution)/shard_map/ppermute | solution.py:47
  63.8 1.2 %collective-permute-done.36 = f32[32,1024]{1,0:T(8,128)S(1)} collective-permute-done((f32[32,1024]{1,0:T(8,128)S(1)}, f32[32,1024]{1,0:T(8,128)S(1)}, u32[]{:S(2)}, u32[]{:S(2)}) %collective-permute-start.36) | collective-permute-done | bytes 131104 | tf_op jit(solution)/shard_map/ppermute | solution.py:47
  65.6 2.2 %collective-permute-start.32 = (f32[64,1024]{1,0:T(8,128)S(1)}, f32[64,1024]{1,0:T(8,128)S(1)}, u32[]{:S(2)}, u32[]{:S(2)}) collective-permute-start(f32[64,1024]{1,0:T(8,128)S(1)} %shard_map.71.refs_1_), channel_id=1, source_target_pairs={{0,8},{1,9},{2,10},{3,11},{4,12},{5,13},{6,14},{7,15},{8,0},{9,1},... | collective-permute-start | bytes 786440 | tf_op jit(solution)/shard_map/ppermute | solution.py:47
  67.9 1.5 %collective-permute-start.31 = (f32[64,1024]{1,0:T(8,128)S(1)}, f32[64,1024]{1,0:T(8,128)S(1)}, u32[]{:S(2)}, u32[]{:S(2)}) collective-permute-start(f32[64,1024]{1,0:T(8,128)S(1)} %shard_map.70.refs_0_), channel_id=1, source_target_pairs={{0,8},{1,9},{2,10},{3,11},{4,12},{5,13},{6,14},{7,15},{8,0},{9,1},... | collective-permute-start | bytes 786440 | tf_op jit(solution)/shard_map/ppermute | solution.py:47
  69.4 1.5 %collective-permute-start.43 = (f32[64,1024]{1,0:T(8,128)S(1)}, f32[64,1024]{1,0:T(8,128)S(1)}, u32[]{:S(2)}, u32[]{:S(2)}) collective-permute-start(f32[64,1024]{1,0:T(8,128)S(1)} %shard_map.74.refs_5_), channel_id=1, source_target_pairs={{0,8},{1,9},{2,10},{3,11},{4,12},{5,13},{6,14},{7,15},{8,0},{9,1},... | collective-permute-start | bytes 786440 | tf_op jit(solution)/shard_map/ppermute | solution.py:47
  71.0 1.0 %collective-permute-done.43.refs_7_ = f32[64,1024]{1,0:T(8,128)S(1)} collective-permute-done((f32[64,1024]{1,0:T(8,128)S(1)}, f32[64,1024]{1,0:T(8,128)S(1)}, u32[]{:S(2)}, u32[]{:S(2)}) %collective-permute-start.43) | collective-permute-done | bytes 262176 | tf_op jit(solution)/shard_map/ppermute | solution.py:47
  72.5 1.4 %store.1 = (f32[256,1024]{1,0:T(8,128)}, f32[256,1024]{1,0:T(8,128)}) custom-call(f32[64,1024]{1,0:T(8,128)S(1)} %shard_map.70.refs_0_, f32[64,1024]{1,0:T(8,128)S(1)} %shard_map.71.refs_1_, f32[64,1024]{1,0:T(8,128)S(1)} %collective-permute-done.31.refs_2_, f32[64,1024]{1,0:T(8,128)S(1)} %collective-permute-done.32.refs_3_, ...), custom_call_target="tpu_custom_call" | custom-call | tf_op jit(solution)/shard_map/store/pallas_call | solution.py:120
  (97 shorter events, 18.2 us)
Async XLA Ops:
  7.1 5.8 %collective-permute-start.11 = (f32[128,1024]{1,0:T(8,128)S(1)}, f32[128,1024]{1,0:T(8,128)S(1)}, u32[]{:S(2)}, u32[]{:S(2)}) collective-permute-start(f32[128,1024]{1,0:T(8,128)S(1)} %get-tuple-element.56), channel_id=1, source_target_pairs={{0,8},{1,9},{2,10},{3,11},{4,12},{5,13},{6,14},{7,15},{8,0},{9,1},... | collective-permute-start | bytes 1572872 | tf_op jit(solution)/shard_map/ppermute | solution.py:47
  8.7 6.1 %collective-permute-start.5 = (f32[32,1024]{1,0:T(8,128)S(1)}, f32[32,1024]{1,0:T(8,128)S(1)}, u32[]{:S(2)}, u32[]{:S(2)}) collective-permute-start(f32[32,1024]{1,0:T(8,128)S(1)} %get-tuple-element.54), channel_id=1, source_target_pairs={{0,24},{1,8},{2,11},{3,27},{4,28},{5,12},{6,15},{7,31},{8,1},{9,17... | collective-permute-start | bytes 393224 | tf_op jit(solution)/shard_map/ppermute | solution.py:47
  12.9 4.9 %collective-permute-start.16 = (f32[32,1024]{1,0:T(8,128)S(1)}, f32[32,1024]{1,0:T(8,128)S(1)}, u32[]{:S(2)}, u32[]{:S(2)}) collective-permute-start(f32[32,1024]{1,0:T(8,128)S(1)} %get-tuple-element.60), channel_id=1, source_target_pairs={{0,10},{1,25},{2,26},{3,9},{4,14},{5,29},{6,30},{7,13},{8,16},{9,3... | collective-permute-start | bytes 393224 | tf_op jit(solution)/shard_map/ppermute | solution.py:47
  14.3 5.7 %collective-permute-start.12 = (f32[32,1024]{1,0:T(8,128)S(1)}, f32[32,1024]{1,0:T(8,128)S(1)}, u32[]{:S(2)}, u32[]{:S(2)}) collective-permute-start(f32[32,1024]{1,0:T(8,128)S(1)} %get-tuple-element.58), channel_id=1, source_target_pairs={{0,24},{1,8},{2,11},{3,27},{4,28},{5,12},{6,15},{7,31},{8,1},{9,17... | collective-permute-start | bytes 393224 | tf_op jit(solution)/shard_map/ppermute | solution.py:47
  14.8 6.2 %collective-permute-start.6 = (f32[32,1024]{1,0:T(8,128)S(1)}, f32[32,1024]{1,0:T(8,128)S(1)}, u32[]{:S(2)}, u32[]{:S(2)}) collective-permute-start(f32[32,1024]{1,0:T(8,128)S(1)} %add.75), channel_id=1, source_target_pairs={{0,9},{1,11},{2,8},{3,10},{4,13},{5,15},{6,12},{7,14},{8,2},{9,0},... | collective-permute-start | bytes 393224 | tf_op jit(solution)/shard_map/ppermute | solution.py:47
  16.0 5.1 %collective-permute-start.2 = (f32[32,1024]{1,0:T(8,128)S(1)}, f32[32,1024]{1,0:T(8,128)S(1)}, u32[]{:S(2)}, u32[]{:S(2)}) collective-permute-start(f32[32,1024]{1,0:T(8,128)S(1)} %add.72), channel_id=1, source_target_pairs={{0,10},{1,25},{2,26},{3,9},{4,14},{5,29},{6,30},{7,13},{8,16},{9,3... | collective-permute-start | bytes 393224 | tf_op jit(solution)/shard_map/ppermute | solution.py:47
  17.9 5.6 %collective-permute-start.17 = (f32[32,1024]{1,0:T(8,128)S(1)}, f32[32,1024]{1,0:T(8,128)S(1)}, u32[]{:S(2)}, u32[]{:S(2)}) collective-permute-start(f32[32,1024]{1,0:T(8,128)S(1)} %add.81), channel_id=1, source_target_pairs={{0,24},{1,8},{2,11},{3,27},{4,28},{5,12},{6,15},{7,31},{8,1},{9,17... | collective-permute-start | bytes 393224 | tf_op jit(solution)/shard_map/ppermute | solution.py:47
  20.0 5.5 %collective-permute-start.13 = (f32[32,1024]{1,0:T(8,128)S(1)}, f32[32,1024]{1,0:T(8,128)S(1)}, u32[]{:S(2)}, u32[]{:S(2)}) collective-permute-start(f32[32,1024]{1,0:T(8,128)S(1)} %add.78), channel_id=1, source_target_pairs={{0,9},{1,11},{2,8},{3,10},{4,13},{5,15},{6,12},{7,14},{8,2},{9,0},... | collective-permute-start | bytes 393224 | tf_op jit(solution)/shard_map/ppermute | solution.py:47
  21.1 5.7 %collective-permute-start.7 = (f32[32,1024]{1,0:T(8,128)S(1)}, f32[32,1024]{1,0:T(8,128)S(1)}, u32[]{:S(2)}, u32[]{:S(2)}) collective-permute-start(f32[32,1024]{1,0:T(8,128)S(1)} %add.76), channel_id=1, source_target_pairs={{0,10},{1,25},{2,26},{3,9},{4,14},{5,29},{6,30},{7,13},{8,16},{9,3... | collective-permute-start | bytes 393224 | tf_op jit(solution)/shard_map/ppermute | solution.py:47
  21.2 6.0 %collective-permute-start.3 = (f32[32,1024]{1,0:T(8,128)S(1)}, f32[32,1024]{1,0:T(8,128)S(1)}, u32[]{:S(2)}, u32[]{:S(2)}) collective-permute-start(f32[32,1024]{1,0:T(8,128)S(1)} %add.73), channel_id=1, source_target_pairs={{0,24},{1,8},{2,11},{3,27},{4,28},{5,12},{6,15},{7,31},{8,1},{9,17... | collective-permute-start | bytes 393224 | tf_op jit(solution)/shard_map/ppermute | solution.py:47
  23.5 5.9 %collective-permute-start.18 = (f32[32,1024]{1,0:T(8,128)S(1)}, f32[32,1024]{1,0:T(8,128)S(1)}, u32[]{:S(2)}, u32[]{:S(2)}) collective-permute-start(f32[32,1024]{1,0:T(8,128)S(1)} %add.82), channel_id=1, source_target_pairs={{0,9},{1,11},{2,8},{3,10},{4,13},{5,15},{6,12},{7,14},{8,2},{9,0},... | collective-permute-start | bytes 393224 | tf_op jit(solution)/shard_map/ppermute | solution.py:47
  25.5 5.7 %collective-permute-start.14 = (f32[32,1024]{1,0:T(8,128)S(1)}, f32[32,1024]{1,0:T(8,128)S(1)}, u32[]{:S(2)}, u32[]{:S(2)}) collective-permute-start(f32[32,1024]{1,0:T(8,128)S(1)} %add.79), channel_id=1, source_target_pairs={{0,10},{1,25},{2,26},{3,9},{4,14},{5,29},{6,30},{7,13},{8,16},{9,3... | collective-permute-start | bytes 393224 | tf_op jit(solution)/shard_map/ppermute | solution.py:47
  26.8 5.7 %collective-permute-start.8 = (f32[32,1024]{1,0:T(8,128)S(1)}, f32[32,1024]{1,0:T(8,128)S(1)}, u32[]{:S(2)}, u32[]{:S(2)}) collective-permute-start(f32[32,1024]{1,0:T(8,128)S(1)} %add.77.own_ref), channel_id=1, source_target_pairs={{0,24},{1,8},{2,11},{3,27},{4,28},{5,12},{6,15},{7,31},{8,1},{9,17... | collective-permute-start | bytes 393224 | tf_op jit(solution)/shard_map/ppermute | solution.py:47
  27.2 6.1 %collective-permute-start.4 = (f32[32,1024]{1,0:T(8,128)S(1)}, f32[32,1024]{1,0:T(8,128)S(1)}, u32[]{:S(2)}, u32[]{:S(2)}) collective-permute-start(f32[32,1024]{1,0:T(8,128)S(1)} %add.74.own_ref), channel_id=1, source_target_pairs={{0,9},{1,11},{2,8},{3,10},{4,13},{5,15},{6,12},{7,14},{8,2},{9,0},... | collective-permute-start | bytes 393224 | tf_op jit(solution)/shard_map/ppermute | solution.py:47
  29.5 6.1 %collective-permute-start.19 = (f32[32,1024]{1,0:T(8,128)S(1)}, f32[32,1024]{1,0:T(8,128)S(1)}, u32[]{:S(2)}, u32[]{:S(2)}) collective-permute-start(f32[32,1024]{1,0:T(8,128)S(1)} %add.83.own_ref), channel_id=1, source_target_pairs={{0,10},{1,25},{2,26},{3,9},{4,14},{5,29},{6,30},{7,13},{8,16},{9,3... | collective-permute-start | bytes 393224 | tf_op jit(solution)/shard_map/ppermute | solution.py:47
  31.3 5.9 %collective-permute-start.15 = (f32[32,1024]{1,0:T(8,128)S(1)}, f32[32,1024]{1,0:T(8,128)S(1)}, u32[]{:S(2)}, u32[]{:S(2)}) collective-permute-start(f32[32,1024]{1,0:T(8,128)S(1)} %add.80.own_ref), channel_id=1, source_target_pairs={{0,24},{1,8},{2,11},{3,27},{4,28},{5,12},{6,15},{7,31},{8,1},{9,17... | collective-permute-start | bytes 393224 | tf_op jit(solution)/shard_map/ppermute | solution.py:47
  32.5 4.8 %collective-permute-start.10 = (f32[64,1024]{1,0:T(8,128)S(1)}, f32[64,1024]{1,0:T(8,128)S(1)}, u32[]{:S(2)}, u32[]{:S(2)}) collective-permute-start(f32[64,1024]{1,0:T(8,128)S(1)} %shard_map.63.refs_1_), channel_id=1, source_target_pairs={{0,8},{1,9},{2,10},{3,11},{4,12},{5,13},{6,14},{7,15},{8,0},{9,1},... | collective-permute-start | bytes 786440 | tf_op jit(solution)/shard_map/ppermute | solution.py:47
  45.9 5.8 %collective-permute-start.23 = (f32[32,1024]{1,0:T(8,128)S(1)}, f32[32,1024]{1,0:T(8,128)S(1)}, u32[]{:S(2)}, u32[]{:S(2)}) collective-permute-start(f32[32,1024]{1,0:T(8,128)S(1)} %get-tuple-element.69), channel_id=1, source_target_pairs={{0,9},{1,11},{2,8},{3,10},{4,13},{5,15},{6,12},{7,14},{8,2},{9,0},... | collective-permute-start | bytes 393224 | tf_op jit(solution)/shard_map/ppermute | solution.py:47
  46.9 4.9 %collective-permute-start.38 = (f32[32,1024]{1,0:T(8,128)S(1)}, f32[32,1024]{1,0:T(8,128)S(1)}, u32[]{:S(2)}, u32[]{:S(2)}) collective-permute-start(f32[32,1024]{1,0:T(8,128)S(1)} %get-tuple-element.77), channel_id=1, source_target_pairs={{0,10},{1,25},{2,26},{3,9},{4,14},{5,29},{6,30},{7,13},{8,16},{9,3... | collective-permute-start | bytes 393224 | tf_op jit(solution)/shard_map/ppermute | solution.py:47
  47.0 5.8 %collective-permute-start.34 = (f32[32,1024]{1,0:T(8,128)S(1)}, f32[32,1024]{1,0:T(8,128)S(1)}, u32[]{:S(2)}, u32[]{:S(2)}) collective-permute-start(f32[32,1024]{1,0:T(8,128)S(1)} %get-tuple-element.75), channel_id=1, source_target_pairs={{0,24},{1,8},{2,11},{3,27},{4,28},{5,12},{6,15},{7,31},{8,1},{9,17... | collective-permute-start | bytes 393224 | tf_op jit(solution)/shard_map/ppermute | solution.py:47
  51.7 5.1 %collective-permute-start.24 = (f32[32,1024]{1,0:T(8,128)S(1)}, f32[32,1024]{1,0:T(8,128)S(1)}, u32[]{:S(2)}, u32[]{:S(2)}) collective-permute-start(f32[32,1024]{1,0:T(8,128)S(1)} %add.84), channel_id=1, source_target_pairs={{0,10},{1,25},{2,26},{3,9},{4,14},{5,29},{6,30},{7,13},{8,16},{9,3... | collective-permute-start | bytes 393224 | tf_op jit(solution)/shard_map/ppermute | solution.py:47
  51.8 5.2 %collective-permute-start.39 = (f32[32,1024]{1,0:T(8,128)S(1)}, f32[32,1024]{1,0:T(8,128)S(1)}, u32[]{:S(2)}, u32[]{:S(2)}) collective-permute-start(f32[32,1024]{1,0:T(8,128)S(1)} %add.93), channel_id=1, source_target_pairs={{0,24},{1,8},{2,11},{3,27},{4,28},{5,12},{6,15},{7,31},{8,1},{9,17... | collective-permute-start | bytes 393224 | tf_op jit(solution)/shard_map/ppermute | solution.py:47
  52.8 6.4 %collective-permute-start.35 = (f32[32,1024]{1,0:T(8,128)S(1)}, f32[32,1024]{1,0:T(8,128)S(1)}, u32[]{:S(2)}, u32[]{:S(2)}) collective-permute-start(f32[32,1024]{1,0:T(8,128)S(1)} %add.90), channel_id=1, source_target_pairs={{0,9},{1,11},{2,8},{3,10},{4,13},{5,15},{6,12},{7,14},{8,2},{9,0},... | collective-permute-start | bytes 393224 | tf_op jit(solution)/shard_map/ppermute | solution.py:47
  54.1 5.7 %collective-permute-start.29 = (f32[32,1024]{1,0:T(8,128)S(1)}, f32[32,1024]{1,0:T(8,128)S(1)}, u32[]{:S(2)}, u32[]{:S(2)}) collective-permute-start(f32[32,1024]{1,0:T(8,128)S(1)} %add.88), channel_id=1, source_target_pairs={{0,10},{1,25},{2,26},{3,9},{4,14},{5,29},{6,30},{7,13},{8,16},{9,3... | collective-permute-start | bytes 393224 | tf_op jit(solution)/shard_map/ppermute | solution.py:47
  56.8 5.4 %collective-permute-start.25 = (f32[32,1024]{1,0:T(8,128)S(1)}, f32[32,1024]{1,0:T(8,128)S(1)}, u32[]{:S(2)}, u32[]{:S(2)}) collective-permute-start(f32[32,1024]{1,0:T(8,128)S(1)} %add.85), channel_id=1, source_target_pairs={{0,24},{1,8},{2,11},{3,27},{4,28},{5,12},{6,15},{7,31},{8,1},{9,17... | collective-permute-start | bytes 393224 | tf_op jit(solution)/shard_map/ppermute | solution.py:47
  57.1 6.1 %collective-permute-start.40 = (f32[32,1024]{1,0:T(8,128)S(1)}, f32[32,1024]{1,0:T(8,128)S(1)}, u32[]{:S(2)}, u32[]{:S(2)}) collective-permute-start(f32[32,1024]{1,0:T(8,128)S(1)} %add.94), channel_id=1, source_target_pairs={{0,9},{1,11},{2,8},{3,10},{4,13},{5,15},{6,12},{7,14},{8,2},{9,0},... | collective-permute-start | bytes 393224 | tf_op jit(solution)/shard_map/ppermute | solution.py:47
  59.2 5.8 %collective-permute-start.36 = (f32[32,1024]{1,0:T(8,128)S(1)}, f32[32,1024]{1,0:T(8,128)S(1)}, u32[]{:S(2)}, u32[]{:S(2)}) collective-permute-start(f32[32,1024]{1,0:T(8,128)S(1)} %add.91), channel_id=1, source_target_pairs={{0,10},{1,25},{2,26},{3,9},{4,14},{5,29},{6,30},{7,13},{8,16},{9,3... | collective-permute-start | bytes 393224 | tf_op jit(solution)/shard_map/ppermute | solution.py:47
  59.8 5.7 %collective-permute-start.30 = (f32[32,1024]{1,0:T(8,128)S(1)}, f32[32,1024]{1,0:T(8,128)S(1)}, u32[]{:S(2)}, u32[]{:S(2)}) collective-permute-start(f32[32,1024]{1,0:T(8,128)S(1)} %add.89.own_ref), channel_id=1, source_target_pairs={{0,24},{1,8},{2,11},{3,27},{4,28},{5,12},{6,15},{7,31},{8,1},{9,17... | collective-permute-start | bytes 393224 | tf_op jit(solution)/shard_map/ppermute | solution.py:47
  62.2 5.6 %collective-permute-start.26 = (f32[32,1024]{1,0:T(8,128)S(1)}, f32[32,1024]{1,0:T(8,128)S(1)}, u32[]{:S(2)}, u32[]{:S(2)}) collective-permute-start(f32[32,1024]{1,0:T(8,128)S(1)} %add.86.own_ref), channel_id=1, source_target_pairs={{0,9},{1,11},{2,8},{3,10},{4,13},{5,15},{6,12},{7,14},{8,2},{9,0},... | collective-permute-start | bytes 393224 | tf_op jit(solution)/shard_map/ppermute | solution.py:47
  63.2 6.1 %collective-permute-start.41 = (f32[32,1024]{1,0:T(8,128)S(1)}, f32[32,1024]{1,0:T(8,128)S(1)}, u32[]{:S(2)}, u32[]{:S(2)}) collective-permute-start(f32[32,1024]{1,0:T(8,128)S(1)} %add.95.own_ref), channel_id=1, source_target_pairs={{0,10},{1,25},{2,26},{3,9},{4,14},{5,29},{6,30},{7,13},{8,16},{9,3... | collective-permute-start | bytes 393224 | tf_op jit(solution)/shard_map/ppermute | solution.py:47
  65.1 5.8 %collective-permute-start.37 = (f32[32,1024]{1,0:T(8,128)S(1)}, f32[32,1024]{1,0:T(8,128)S(1)}, u32[]{:S(2)}, u32[]{:S(2)}) collective-permute-start(f32[32,1024]{1,0:T(8,128)S(1)} %add.92.own_ref), channel_id=1, source_target_pairs={{0,24},{1,8},{2,11},{3,27},{4,28},{5,12},{6,15},{7,31},{8,1},{9,17... | collective-permute-start | bytes 393224 | tf_op jit(solution)/shard_map/ppermute | solution.py:47
  65.6 5.4 %collective-permute-start.32 = (f32[64,1024]{1,0:T(8,128)S(1)}, f32[64,1024]{1,0:T(8,128)S(1)}, u32[]{:S(2)}, u32[]{:S(2)}) collective-permute-start(f32[64,1024]{1,0:T(8,128)S(1)} %shard_map.71.refs_1_), channel_id=1, source_target_pairs={{0,8},{1,9},{2,10},{3,11},{4,12},{5,13},{6,14},{7,15},{8,0},{9,1},... | collective-permute-start | bytes 786440 | tf_op jit(solution)/shard_map/ppermute | solution.py:47
  (12 other events, 37.4 us)

commit v2 on v1

--- a/solution.py
+++ b/solution.py
@@ -56,7 +56,8 @@
 
 def chain(keep, send, index):
     even, odd = ORDERS[index - 1]
-    own = keep + from_partner(send, even[0], odd[0])
+    got = from_partner(send, even[0], odd[0])
+    own = keep + got
     own = own + from_partner(own, even[1], odd[1])
     own = own + from_partner(own, even[2], odd[2])
     rest = from_partner(own, even[0], odd[0])
@@ -163,11 +164,10 @@
                 start = pl.multiple_of(place_of(i, count, role) * rows, rows)
                 whole_ref[pl.ds(start, rows), :] = part[...]
     else:
-        r_in, e_in, keep_ref, send_ref, zh_ref, zl_ref, slope_ref, r_ref, e_ref, x_ref, g_ref, sems = refs
-        copies = [
-            pltpu.make_async_copy(source, target, sems.at[i])
-            for i, (source, target) in enumerate(((r_in, r_ref), (x_in.at[0], x_ref), (e_in, e_ref), (g_in.at[0], g_ref)))
-        ]
+        r_in, e_in, keep_ref, send_ref, zh_ref, zl_ref, slope_ref, r_ref, e_ref, x_ref, *later, g_ref, sems = refs
+        moves = [(r_in, r_ref), (x_in.at[0], x_ref), (e_in, e_ref), (g_in.at[0], g_ref)]
+        moves += [(source.at[1 + i // 2], ref) for i, (source, ref) in enumerate(zip((x_in, g_in) * len(later), later))]
+        copies = [pltpu.make_async_copy(source, target, sems.at[i]) for i, (source, target) in enumerate(moves)]
         for copy in copies:
             copy.start()
         copies[0].wait()
@@ -197,17 +197,12 @@
     even = places()[0] == 0
     keep_ref[...] = jnp.where(even, stepped[:rows], stepped[rows:])
     send_ref[...] = jnp.where(even, stepped[rows:], stepped[:rows])
-
-
-def reduce_kernel(upcoming, x_all, g_all, x_ref, r_ref, e_ref, zh_ref, zl_ref, slope_ref, keep_ref, send_ref, *refs):
-    if upcoming is not None:
-        next_x_ref, next_g_ref, sems = refs
-        copies = (
-            pltpu.make_async_copy(x_all.at[upcoming], next_x_ref, sems.at[0]),
-            pltpu.make_async_copy(g_all.at[upcoming], next_g_ref, sems.at[1]),
-        )
-        for copy in copies:
-            copy.start()
+    if not count:
+        for copy in copies[4:]:
+            copy.wait()
+
+
+def reduce_kernel(x_ref, r_ref, e_ref, zh_ref, zl_ref, slope_ref, keep_ref, send_ref):
     width, columns = r_ref.shape
     reduce_scale = 1.0 / math.sqrt(columns)
     expand_scale = 1.0 / math.sqrt(width)
@@ -218,9 +213,6 @@
     even = places()[0] == 0
     keep_ref[...] = jnp.where(even, stepped[:rows], stepped[rows:])
     send_ref[...] = jnp.where(even, stepped[rows:], stepped[:rows])
-    if upcoming is not None:
-        for copy in copies:
-            copy.wait()
 
 
 def shards(w_reduce, w_expand, inputs, out_grads):
@@ -232,30 +224,22 @@
     acts = jax.ShapeDtypeStruct((rows, columns), bf16)
     slopes = jax.ShapeDtypeStruct((width, rows), f32)
     for iteration in range(iterations):
-        first, last = iteration == 0, iteration == iterations - 1
+        first = iteration == 0
         weights = jax.ShapeDtypeStruct((width, columns), bf16 if first else f32)
         results = pl.pallas_call(
             functools.partial(expand_kernel, 0 if first else len(sums_r)),
-            out_shape=(half, half, acts, acts, slopes, weights, weights) + ((acts,) if first else ()),
+            out_shape=(half, half, acts, acts, slopes, weights, weights) + ((acts,) * (2 * iterations - 1) if first else ()),
             in_specs=[HBM] * 4 if first else [VMEM] * (2 + len(sums_r) + len(sums_e)),
-            out_specs=(VMEM,) * (8 if first else 7),
-            scratch_shapes=[pltpu.VMEM((rows, columns), bf16), pltpu.SemaphoreType.DMA((4,))] if first else [],
+            out_specs=(VMEM,) * (7 + (2 * iterations - 1 if first else 0)),
+            scratch_shapes=[pltpu.VMEM((rows, columns), bf16), pltpu.SemaphoreType.DMA((2 * iterations + 2,))] if first else [],
             compiler_params=LARGE,
-        )(*((inputs, out_grads, reducing, expanding) if first else (feats, grads, *sums_r, *sums_e)))
+        )(*((inputs, out_grads, reducing, expanding) if first else (feats[iteration], grads[iteration], *sums_r, *sums_e)))
         keep_e, send_e, zh, zl, slope, reducing, expanding = results[:7]
         if first:
-            feats = results[7]
-        results = pl.pallas_call(
-            functools.partial(reduce_kernel, None if last else iteration + 1),
-            out_shape=(half, half) + (() if last else (acts, acts)),
-            in_specs=[HBM, HBM] + [VMEM] * 6,
-            out_specs=(VMEM,) * (2 if last else 4),
-            scratch_shapes=[] if last else [pltpu.SemaphoreType.DMA((2,))],
-            compiler_params=LARGE,
-        )(inputs, out_grads, feats, reducing, expanding, zh, zl, slope)
-        keep_r, send_r = results[:2]
-        if not last:
-            feats, grads = results[2:]
+            feats, grads = (results[7], *results[8::2]), (None, *results[9::2])
+        keep_r, send_r = pl.pallas_call(
+            reduce_kernel, out_shape=(half, half), in_specs=[VMEM] * 6, out_specs=(VMEM,) * 2, compiler_params=LARGE
+        )(feats[iteration], reducing, expanding, zh, zl, slope)
         sums_e = sum_over_cube(keep_e, send_e, (1, 2))
         sums_r = sum_over_cube(keep_r, send_r, (3, 4))
     reducing, expanding = store(sums_r, sums_e)

time: 74 us -> 71.7 us (0.969)
  waiting for transfers between devices: 17.1 us -> 11 us
  starting transfers between devices: 43.7 us -> 48.4 us
  Pallas kernels: 11.7 us -> 10.9 us
    ppermute x44, waiting for transfers between devices: 17.1 us -> 11 us  [from_partner(): return lax.ppermute(values, ('near', 'far'), pairs)]
    ppermute x44, starting transfers between devices: 43.7 us -> 48.4 us  [from_partner(): return lax.ppermute(values, ('near', 'far'), pairs)]
    pallas_call x2, Pallas kernels: 3.65 us -> 2.8 us  [shards(): pl.pallas_call(reduce_kernel, out_shape=(half, half), in_specs=[VMEM] * 6...]
  transfers between devices with their start and end apart: 44 -> 44, of which waited for: 23 -> 21; matrix products, arithmetic and copies ran while one was open for 1% -> 1% of each run, Pallas kernels for 1% -> 3%
where the time goes in v2:
time: 71.7 us; the launch traced here: 71.6 us
  starting transfers between devices  48.4 us (68%)
  waiting for transfers between devices  11 us (15%)
  Pallas kernels  10.9 us (15%)
  between operations  0.84 us (1%)
    ppermute x44, starting transfers between devices, from_partner(): return lax.ppermute(values, ('near', 'far'), pairs)  48.4 us
    ppermute x44, waiting for transfers between devices, from_partner(): return lax.ppermute(values, ('near', 'far'), pairs)  11 us
    pallas_call x2, Pallas kernels, shards(): pl.pallas_call(functools.partial(expand_kernel, 0 if first else len(sums_...  6.21 us
    pallas_call x2, Pallas kernels, shards(): pl.pallas_call(reduce_kernel, out_shape=(half, half), in_specs=[VMEM] * 6...  2.8 us
  transfers between devices with their start and end apart: 44, of which 21 were waited for; matrix products, arithmetic and copies ran while one was open for 1% of the time, Pallas kernels for 3%

profile of v2, /device:TPU:0, one launch (start us, length us, event | category | flops | bytes accessed | tf_op | source)
XLA Modules:
  0.0 71.6 jit_solution(16913991774686603811)
XLA Ops:
  0.6 3.7 %shard_map.59 = (f32[128,1024]{1,0:T(8,128)S(1)}, f32[128,1024]{1,0:T(8,128)S(1)}, bf16[256,1024]{1,0:T(8,128)(2,1)S(1)}, bf16[256,1024]{1,0:T(8,128)(2,1)S(1)},...) custom-call(bf16[2,256,1024]{2,1,0:T(8,128)(2,1)} %bitcast.6, ...), custom_call_target="tpu_custom_call" | custom-call | tf_op jit(solution)/shard_map/pallas_call | solution.py:229
  4.9 1.3 %shard_map.60 = (f32[128,1024]{1,0:T(8,128)S(1)}, f32[128,1024]{1,0:T(8,128)S(1)}) custom-call(bf16[256,1024]{1,0:T(8,128)(2,1)S(1)} %get-tuple-element.43.x_ref, bf16[256,1024]{1,0:T(8,128)(2,1)S(1)} %get-tuple-element.44.r_ref, bf16[256,1024]{1,0:T(8,128)(2,1)S(1)} %get-tuple-element.45.e_ref, bf16[256,1024]{1,0:T(8,128)(2,1)S(1)} %get-tuple-element.46.zh_ref, ...), custom_call_target="tpu_custom_call" | custom-call | tf_op jit(solution)/shard_map/pallas_call | solution.py:240
  6.5 2.7 %collective-permute-start.16 = (f32[32,1024]{1,0:T(8,128)S(1)}, f32[32,1024]{1,0:T(8,128)S(1)}, u32[]{:S(2)}, u32[]{:S(2)}) collective-permute-start(f32[32,1024]{1,0:T(8,128)S(1)} %get-tuple-element.60), channel_id=1, source_target_pairs={{0,10},{1,25},{2,26},{3,9},{4,14},{5,29},{6,30},{7,13},{8,16},{9,3... | collective-permute-start | bytes 393224 | tf_op jit(solution)/shard_map/ppermute | solution.py:47
  9.3 1.5 %collective-permute-start.12 = (f32[32,1024]{1,0:T(8,128)S(1)}, f32[32,1024]{1,0:T(8,128)S(1)}, u32[]{:S(2)}, u32[]{:S(2)}) collective-permute-start(f32[32,1024]{1,0:T(8,128)S(1)} %get-tuple-element.58), channel_id=1, source_target_pairs={{0,24},{1,8},{2,11},{3,27},{4,28},{5,12},{6,15},{7,31},{8,1},{9,17... | collective-permute-start | bytes 393224 | tf_op jit(solution)/shard_map/ppermute | solution.py:47
  11.1 1.5 %collective-permute-start.1 = (f32[32,1024]{1,0:T(8,128)S(1)}, f32[32,1024]{1,0:T(8,128)S(1)}, u32[]{:S(2)}, u32[]{:S(2)}) collective-permute-start(f32[32,1024]{1,0:T(8,128)S(1)} %get-tuple-element.52), channel_id=1, source_target_pairs={{0,9},{1,11},{2,8},{3,10},{4,13},{5,15},{6,12},{7,14},{8,2},{9,0},... | collective-permute-start | bytes 393224 | tf_op jit(solution)/shard_map/ppermute | solution.py:47
  12.7 1.3 %collective-permute-start.17 = (f32[32,1024]{1,0:T(8,128)S(1)}, f32[32,1024]{1,0:T(8,128)S(1)}, u32[]{:S(2)}, u32[]{:S(2)}) collective-permute-start(f32[32,1024]{1,0:T(8,128)S(1)} %add.81), channel_id=1, source_target_pairs={{0,24},{1,8},{2,11},{3,27},{4,28},{5,12},{6,15},{7,31},{8,1},{9,17... | collective-permute-start | bytes 393224 | tf_op jit(solution)/shard_map/ppermute | solution.py:47
  14.0 1.6 %collective-permute-start.13 = (f32[32,1024]{1,0:T(8,128)S(1)}, f32[32,1024]{1,0:T(8,128)S(1)}, u32[]{:S(2)}, u32[]{:S(2)}) collective-permute-start(f32[32,1024]{1,0:T(8,128)S(1)} %add.78), channel_id=1, source_target_pairs={{0,9},{1,11},{2,8},{3,10},{4,13},{5,15},{6,12},{7,14},{8,2},{9,0},... | collective-permute-start | bytes 393224 | tf_op jit(solution)/shard_map/ppermute | solution.py:47
  15.6 1.2 %collective-permute-start.6 = (f32[32,1024]{1,0:T(8,128)S(1)}, f32[32,1024]{1,0:T(8,128)S(1)}, u32[]{:S(2)}, u32[]{:S(2)}) collective-permute-start(f32[32,1024]{1,0:T(8,128)S(1)} %add.75), channel_id=1, source_target_pairs={{0,9},{1,11},{2,8},{3,10},{4,13},{5,15},{6,12},{7,14},{8,2},{9,0},... | collective-permute-start | bytes 393224 | tf_op jit(solution)/shard_map/ppermute | solution.py:47
  17.0 1.4 %collective-permute-start.2 = (f32[32,1024]{1,0:T(8,128)S(1)}, f32[32,1024]{1,0:T(8,128)S(1)}, u32[]{:S(2)}, u32[]{:S(2)}) collective-permute-start(f32[32,1024]{1,0:T(8,128)S(1)} %add.72), channel_id=1, source_target_pairs={{0,10},{1,25},{2,26},{3,9},{4,14},{5,29},{6,30},{7,13},{8,16},{9,3... | collective-permute-start | bytes 393224 | tf_op jit(solution)/shard_map/ppermute | solution.py:47
  18.4 1.4 %collective-permute-start.18 = (f32[32,1024]{1,0:T(8,128)S(1)}, f32[32,1024]{1,0:T(8,128)S(1)}, u32[]{:S(2)}, u32[]{:S(2)}) collective-permute-start(f32[32,1024]{1,0:T(8,128)S(1)} %add.82), channel_id=1, source_target_pairs={{0,9},{1,11},{2,8},{3,10},{4,13},{5,15},{6,12},{7,14},{8,2},{9,0},... | collective-permute-start | bytes 393224 | tf_op jit(solution)/shard_map/ppermute | solution.py:47
  19.8 1.0 %collective-permute-start.14 = (f32[32,1024]{1,0:T(8,128)S(1)}, f32[32,1024]{1,0:T(8,128)S(1)}, u32[]{:S(2)}, u32[]{:S(2)}) collective-permute-start(f32[32,1024]{1,0:T(8,128)S(1)} %add.79), channel_id=1, source_target_pairs={{0,10},{1,25},{2,26},{3,9},{4,14},{5,29},{6,30},{7,13},{8,16},{9,3... | collective-permute-start | bytes 393224 | tf_op jit(solution)/shard_map/ppermute | solution.py:47
  21.2 1.0 %collective-permute-start.7 = (f32[32,1024]{1,0:T(8,128)S(1)}, f32[32,1024]{1,0:T(8,128)S(1)}, u32[]{:S(2)}, u32[]{:S(2)}) collective-permute-start(f32[32,1024]{1,0:T(8,128)S(1)} %add.76), channel_id=1, source_target_pairs={{0,10},{1,25},{2,26},{3,9},{4,14},{5,29},{6,30},{7,13},{8,16},{9,3... | collective-permute-start | bytes 393224 | tf_op jit(solution)/shard_map/ppermute | solution.py:47
  22.4 1.6 %collective-permute-start.3 = (f32[32,1024]{1,0:T(8,128)S(1)}, f32[32,1024]{1,0:T(8,128)S(1)}, u32[]{:S(2)}, u32[]{:S(2)}) collective-permute-start(f32[32,1024]{1,0:T(8,128)S(1)} %add.73), channel_id=1, source_target_pairs={{0,24},{1,8},{2,11},{3,27},{4,28},{5,12},{6,15},{7,31},{8,1},{9,17... | collective-permute-start | bytes 393224 | tf_op jit(solution)/shard_map/ppermute | solution.py:47
  24.1 1.0 %collective-permute-start.19 = (f32[32,1024]{1,0:T(8,128)S(1)}, f32[32,1024]{1,0:T(8,128)S(1)}, u32[]{:S(2)}, u32[]{:S(2)}) collective-permute-start(f32[32,1024]{1,0:T(8,128)S(1)} %add.83.own_ref), channel_id=1, source_target_pairs={{0,10},{1,25},{2,26},{3,9},{4,14},{5,29},{6,30},{7,13},{8,16},{9,3... | collective-permute-start | bytes 393224 | tf_op jit(solution)/shard_map/ppermute | solution.py:47
  28.3 2.1 %collective-permute-start.4 = (f32[32,1024]{1,0:T(8,128)S(1)}, f32[32,1024]{1,0:T(8,128)S(1)}, u32[]{:S(2)}, u32[]{:S(2)}) collective-permute-start(f32[32,1024]{1,0:T(8,128)S(1)} %add.74.own_ref), channel_id=1, source_target_pairs={{0,9},{1,11},{2,8},{3,10},{4,13},{5,15},{6,12},{7,14},{8,2},{9,0},... | collective-permute-start | bytes 393224 | tf_op jit(solution)/shard_map/ppermute | solution.py:47
  30.4 2.0 %collective-permute-start.21 = (f32[64,1024]{1,0:T(8,128)S(1)}, f32[64,1024]{1,0:T(8,128)S(1)}, u32[]{:S(2)}, u32[]{:S(2)}) collective-permute-start(f32[64,1024]{1,0:T(8,128)S(1)} %shard_map.66.refs_5_), channel_id=1, source_target_pairs={{0,8},{1,9},{2,10},{3,11},{4,12},{5,13},{6,14},{7,15},{8,0},{9,1},... | collective-permute-start | bytes 786440 | tf_op jit(solution)/shard_map/ppermute | solution.py:47
  33.2 1.6 %collective-permute-start.10 = (f32[64,1024]{1,0:T(8,128)S(1)}, f32[64,1024]{1,0:T(8,128)S(1)}, u32[]{:S(2)}, u32[]{:S(2)}) collective-permute-start(f32[64,1024]{1,0:T(8,128)S(1)} %shard_map.63.refs_1_), channel_id=1, source_target_pairs={{0,8},{1,9},{2,10},{3,11},{4,12},{5,13},{6,14},{7,15},{8,0},{9,1},... | collective-permute-start | bytes 786440 | tf_op jit(solution)/shard_map/ppermute | solution.py:47
  36.4 2.5 %shard_map.67 = (f32[128,1024]{1,0:T(8,128)S(1)}, f32[128,1024]{1,0:T(8,128)S(1)}, bf16[256,1024]{1,0:T(8,128)(2,1)S(1)}, bf16[256,1024]{1,0:T(8,128)(2,1)S(1)},...) custom-call(bf16[256,1024]{1,0:T(8,128)(2,1)S(1)} %get-tuple-element.41.x_in.x_ref, ...), custom_call_target="tpu_custom_call" | custom-call | tf_op jit(solution)/shard_map/pallas_call | solution.py:229
  38.9 1.5 %shard_map.68 = (f32[128,1024]{1,0:T(8,128)S(1)}, f32[128,1024]{1,0:T(8,128)S(1)}) custom-call(bf16[256,1024]{1,0:T(8,128)(2,1)S(1)} %get-tuple-element.41.x_in.x_ref, f32[256,1024]{1,0:T(8,128)S(1)} %get-tuple-element.61.r_ref, f32[256,1024]{1,0:T(8,128)S(1)} %get-tuple-element.62.e_ref, bf16[256,1024]{1,0:T(8,128)(2,1)S(1)} %get-tuple-element.63.zh_ref, ...), custom_call_target="tpu_custom_call" | custom-call | tf_op jit(solution)/shard_map/pallas_call | solution.py:240
  40.9 1.4 %collective-permute-done.22.got_ref = f32[128,1024]{1,0:T(8,128)S(1)} collective-permute-done((f32[128,1024]{1,0:T(8,128)S(1)}, f32[128,1024]{1,0:T(8,128)S(1)}, u32[]{:S(2)}, u32[]{:S(2)}) %collective-permute-start.22) | collective-permute-done | bytes 524320 | tf_op jit(solution)/shard_map/ppermute | solution.py:47
  42.4 1.4 %collective-permute-start.27 = (f32[32,1024]{1,0:T(8,128)S(1)}, f32[32,1024]{1,0:T(8,128)S(1)}, u32[]{:S(2)}, u32[]{:S(2)}) collective-permute-start(f32[32,1024]{1,0:T(8,128)S(1)} %get-tuple-element.71), channel_id=1, source_target_pairs={{0,24},{1,8},{2,11},{3,27},{4,28},{5,12},{6,15},{7,31},{8,1},{9,17... | collective-permute-start | bytes 393224 | tf_op jit(solution)/shard_map/ppermute | solution.py:47
  44.3 2.1 %collective-permute-start.38 = (f32[32,1024]{1,0:T(8,128)S(1)}, f32[32,1024]{1,0:T(8,128)S(1)}, u32[]{:S(2)}, u32[]{:S(2)}) collective-permute-start(f32[32,1024]{1,0:T(8,128)S(1)} %get-tuple-element.77), channel_id=1, source_target_pairs={{0,10},{1,25},{2,26},{3,9},{4,14},{5,29},{6,30},{7,13},{8,16},{9,3... | collective-permute-start | bytes 393224 | tf_op jit(solution)/shard_map/ppermute | solution.py:47
  46.9 1.3 %collective-permute-start.28 = (f32[32,1024]{1,0:T(8,128)S(1)}, f32[32,1024]{1,0:T(8,128)S(1)}, u32[]{:S(2)}, u32[]{:S(2)}) collective-permute-start(f32[32,1024]{1,0:T(8,128)S(1)} %add.87), channel_id=1, source_target_pairs={{0,9},{1,11},{2,8},{3,10},{4,13},{5,15},{6,12},{7,14},{8,2},{9,0},... | collective-permute-start | bytes 393224 | tf_op jit(solution)/shard_map/ppermute | solution.py:47
  48.7 1.4 %collective-permute-start.24 = (f32[32,1024]{1,0:T(8,128)S(1)}, f32[32,1024]{1,0:T(8,128)S(1)}, u32[]{:S(2)}, u32[]{:S(2)}) collective-permute-start(f32[32,1024]{1,0:T(8,128)S(1)} %add.84), channel_id=1, source_target_pairs={{0,10},{1,25},{2,26},{3,9},{4,14},{5,29},{6,30},{7,13},{8,16},{9,3... | collective-permute-start | bytes 393224 | tf_op jit(solution)/shard_map/ppermute | solution.py:47
  50.1 1.7 %collective-permute-start.39 = (f32[32,1024]{1,0:T(8,128)S(1)}, f32[32,1024]{1,0:T(8,128)S(1)}, u32[]{:S(2)}, u32[]{:S(2)}) collective-permute-start(f32[32,1024]{1,0:T(8,128)S(1)} %add.93), channel_id=1, source_target_pairs={{0,24},{1,8},{2,11},{3,27},{4,28},{5,12},{6,15},{7,31},{8,1},{9,17... | collective-permute-start | bytes 393224 | tf_op jit(solution)/shard_map/ppermute | solution.py:47
  52.7 1.3 %collective-permute-start.29 = (f32[32,1024]{1,0:T(8,128)S(1)}, f32[32,1024]{1,0:T(8,128)S(1)}, u32[]{:S(2)}, u32[]{:S(2)}) collective-permute-start(f32[32,1024]{1,0:T(8,128)S(1)} %add.88), channel_id=1, source_target_pairs={{0,10},{1,25},{2,26},{3,9},{4,14},{5,29},{6,30},{7,13},{8,16},{9,3... | collective-permute-start | bytes 393224 | tf_op jit(solution)/shard_map/ppermute | solution.py:47
  55.3 1.4 %collective-permute-start.40 = (f32[32,1024]{1,0:T(8,128)S(1)}, f32[32,1024]{1,0:T(8,128)S(1)}, u32[]{:S(2)}, u32[]{:S(2)}) collective-permute-start(f32[32,1024]{1,0:T(8,128)S(1)} %add.94), channel_id=1, source_target_pairs={{0,9},{1,11},{2,8},{3,10},{4,13},{5,15},{6,12},{7,14},{8,2},{9,0},... | collective-permute-start | bytes 393224 | tf_op jit(solution)/shard_map/ppermute | solution.py:47
  56.7 1.4 %collective-permute-start.36 = (f32[32,1024]{1,0:T(8,128)S(1)}, f32[32,1024]{1,0:T(8,128)S(1)}, u32[]{:S(2)}, u32[]{:S(2)}) collective-permute-start(f32[32,1024]{1,0:T(8,128)S(1)} %add.91), channel_id=1, source_target_pairs={{0,10},{1,25},{2,26},{3,9},{4,14},{5,29},{6,30},{7,13},{8,16},{9,3... | collective-permute-start | bytes 393224 | tf_op jit(solution)/shard_map/ppermute | solution.py:47
  60.7 1.2 %collective-permute-start.41 = (f32[32,1024]{1,0:T(8,128)S(1)}, f32[32,1024]{1,0:T(8,128)S(1)}, u32[]{:S(2)}, u32[]{:S(2)}) collective-permute-start(f32[32,1024]{1,0:T(8,128)S(1)} %add.95.own_ref), channel_id=1, source_target_pairs={{0,10},{1,25},{2,26},{3,9},{4,14},{5,29},{6,30},{7,13},{8,16},{9,3... | collective-permute-start | bytes 393224 | tf_op jit(solution)/shard_map/ppermute | solution.py:47
  63.9 1.6 %collective-permute-start.32 = (f32[64,1024]{1,0:T(8,128)S(1)}, f32[64,1024]{1,0:T(8,128)S(1)}, u32[]{:S(2)}, u32[]{:S(2)}) collective-permute-start(f32[64,1024]{1,0:T(8,128)S(1)} %shard_map.71.refs_1_), channel_id=1, source_target_pairs={{0,8},{1,9},{2,10},{3,11},{4,12},{5,13},{6,14},{7,15},{8,0},{9,1},... | collective-permute-start | bytes 786440 | tf_op jit(solution)/shard_map/ppermute | solution.py:47
  66.4 2.0 %collective-permute-start.43 = (f32[64,1024]{1,0:T(8,128)S(1)}, f32[64,1024]{1,0:T(8,128)S(1)}, u32[]{:S(2)}, u32[]{:S(2)}) collective-permute-start(f32[64,1024]{1,0:T(8,128)S(1)} %shard_map.74.refs_5_), channel_id=1, source_target_pairs={{0,8},{1,9},{2,10},{3,11},{4,12},{5,13},{6,14},{7,15},{8,0},{9,1},... | collective-permute-start | bytes 786440 | tf_op jit(solution)/shard_map/ppermute | solution.py:47
  70.2 1.4 %store.1 = (f32[256,1024]{1,0:T(8,128)}, f32[256,1024]{1,0:T(8,128)}) custom-call(f32[64,1024]{1,0:T(8,128)S(1)} %shard_map.70.refs_0_, f32[64,1024]{1,0:T(8,128)S(1)} %shard_map.71.refs_1_, f32[64,1024]{1,0:T(8,128)S(1)} %collective-permute-done.31.refs_2_, f32[64,1024]{1,0:T(8,128)S(1)} %collective-permute-done.32.refs_3_, ...), custom_call_target="tpu_custom_call" | custom-call | tf_op jit(solution)/shard_map/store/pallas_call | solution.py:121
  (97 shorter events, 19.3 us)
Async XLA Ops:
  6.5 6.1 %collective-permute-start.16 = (f32[32,1024]{1,0:T(8,128)S(1)}, f32[32,1024]{1,0:T(8,128)S(1)}, u32[]{:S(2)}, u32[]{:S(2)}) collective-permute-start(f32[32,1024]{1,0:T(8,128)S(1)} %get-tuple-element.60), channel_id=1, source_target_pairs={{0,10},{1,25},{2,26},{3,9},{4,14},{5,29},{6,30},{7,13},{8,16},{9,3... | collective-permute-start | bytes 393224 | tf_op jit(solution)/shard_map/ppermute | solution.py:47
  9.3 4.7 %collective-permute-start.12 = (f32[32,1024]{1,0:T(8,128)S(1)}, f32[32,1024]{1,0:T(8,128)S(1)}, u32[]{:S(2)}, u32[]{:S(2)}) collective-permute-start(f32[32,1024]{1,0:T(8,128)S(1)} %get-tuple-element.58), channel_id=1, source_target_pairs={{0,24},{1,8},{2,11},{3,27},{4,28},{5,12},{6,15},{7,31},{8,1},{9,17... | collective-permute-start | bytes 393224 | tf_op jit(solution)/shard_map/ppermute | solution.py:47
  10.8 4.7 %collective-permute-start.5 = (f32[32,1024]{1,0:T(8,128)S(1)}, f32[32,1024]{1,0:T(8,128)S(1)}, u32[]{:S(2)}, u32[]{:S(2)}) collective-permute-start(f32[32,1024]{1,0:T(8,128)S(1)} %get-tuple-element.54), channel_id=1, source_target_pairs={{0,24},{1,8},{2,11},{3,27},{4,28},{5,12},{6,15},{7,31},{8,1},{9,17... | collective-permute-start | bytes 393224 | tf_op jit(solution)/shard_map/ppermute | solution.py:47
  11.1 5.8 %collective-permute-start.1 = (f32[32,1024]{1,0:T(8,128)S(1)}, f32[32,1024]{1,0:T(8,128)S(1)}, u32[]{:S(2)}, u32[]{:S(2)}) collective-permute-start(f32[32,1024]{1,0:T(8,128)S(1)} %get-tuple-element.52), channel_id=1, source_target_pairs={{0,9},{1,11},{2,8},{3,10},{4,13},{5,15},{6,12},{7,14},{8,2},{9,0},... | collective-permute-start | bytes 393224 | tf_op jit(solution)/shard_map/ppermute | solution.py:47
  12.7 5.7 %collective-permute-start.17 = (f32[32,1024]{1,0:T(8,128)S(1)}, f32[32,1024]{1,0:T(8,128)S(1)}, u32[]{:S(2)}, u32[]{:S(2)}) collective-permute-start(f32[32,1024]{1,0:T(8,128)S(1)} %add.81), channel_id=1, source_target_pairs={{0,24},{1,8},{2,11},{3,27},{4,28},{5,12},{6,15},{7,31},{8,1},{9,17... | collective-permute-start | bytes 393224 | tf_op jit(solution)/shard_map/ppermute | solution.py:47
  14.0 5.8 %collective-permute-start.13 = (f32[32,1024]{1,0:T(8,128)S(1)}, f32[32,1024]{1,0:T(8,128)S(1)}, u32[]{:S(2)}, u32[]{:S(2)}) collective-permute-start(f32[32,1024]{1,0:T(8,128)S(1)} %add.78), channel_id=1, source_target_pairs={{0,9},{1,11},{2,8},{3,10},{4,13},{5,15},{6,12},{7,14},{8,2},{9,0},... | collective-permute-start | bytes 393224 | tf_op jit(solution)/shard_map/ppermute | solution.py:47
  15.6 5.6 %collective-permute-start.6 = (f32[32,1024]{1,0:T(8,128)S(1)}, f32[32,1024]{1,0:T(8,128)S(1)}, u32[]{:S(2)}, u32[]{:S(2)}) collective-permute-start(f32[32,1024]{1,0:T(8,128)S(1)} %add.75), channel_id=1, source_target_pairs={{0,9},{1,11},{2,8},{3,10},{4,13},{5,15},{6,12},{7,14},{8,2},{9,0},... | collective-permute-start | bytes 393224 | tf_op jit(solution)/shard_map/ppermute | solution.py:47
  17.0 5.4 %collective-permute-start.2 = (f32[32,1024]{1,0:T(8,128)S(1)}, f32[32,1024]{1,0:T(8,128)S(1)}, u32[]{:S(2)}, u32[]{:S(2)}) collective-permute-start(f32[32,1024]{1,0:T(8,128)S(1)} %add.72), channel_id=1, source_target_pairs={{0,10},{1,25},{2,26},{3,9},{4,14},{5,29},{6,30},{7,13},{8,16},{9,3... | collective-permute-start | bytes 393224 | tf_op jit(solution)/shard_map/ppermute | solution.py:47
  18.4 5.7 %collective-permute-start.18 = (f32[32,1024]{1,0:T(8,128)S(1)}, f32[32,1024]{1,0:T(8,128)S(1)}, u32[]{:S(2)}, u32[]{:S(2)}) collective-permute-start(f32[32,1024]{1,0:T(8,128)S(1)} %add.82), channel_id=1, source_target_pairs={{0,9},{1,11},{2,8},{3,10},{4,13},{5,15},{6,12},{7,14},{8,2},{9,0},... | collective-permute-start | bytes 393224 | tf_op jit(solution)/shard_map/ppermute | solution.py:47
  19.8 5.7 %collective-permute-start.14 = (f32[32,1024]{1,0:T(8,128)S(1)}, f32[32,1024]{1,0:T(8,128)S(1)}, u32[]{:S(2)}, u32[]{:S(2)}) collective-permute-start(f32[32,1024]{1,0:T(8,128)S(1)} %add.79), channel_id=1, source_target_pairs={{0,10},{1,25},{2,26},{3,9},{4,14},{5,29},{6,30},{7,13},{8,16},{9,3... | collective-permute-start | bytes 393224 | tf_op jit(solution)/shard_map/ppermute | solution.py:47
  21.2 5.9 %collective-permute-start.7 = (f32[32,1024]{1,0:T(8,128)S(1)}, f32[32,1024]{1,0:T(8,128)S(1)}, u32[]{:S(2)}, u32[]{:S(2)}) collective-permute-start(f32[32,1024]{1,0:T(8,128)S(1)} %add.76), channel_id=1, source_target_pairs={{0,10},{1,25},{2,26},{3,9},{4,14},{5,29},{6,30},{7,13},{8,16},{9,3... | collective-permute-start | bytes 393224 | tf_op jit(solution)/shard_map/ppermute | solution.py:47
  22.4 5.9 %collective-permute-start.3 = (f32[32,1024]{1,0:T(8,128)S(1)}, f32[32,1024]{1,0:T(8,128)S(1)}, u32[]{:S(2)}, u32[]{:S(2)}) collective-permute-start(f32[32,1024]{1,0:T(8,128)S(1)} %add.73), channel_id=1, source_target_pairs={{0,24},{1,8},{2,11},{3,27},{4,28},{5,12},{6,15},{7,31},{8,1},{9,17... | collective-permute-start | bytes 393224 | tf_op jit(solution)/shard_map/ppermute | solution.py:47
  24.1 6.3 %collective-permute-start.19 = (f32[32,1024]{1,0:T(8,128)S(1)}, f32[32,1024]{1,0:T(8,128)S(1)}, u32[]{:S(2)}, u32[]{:S(2)}) collective-permute-start(f32[32,1024]{1,0:T(8,128)S(1)} %add.83.own_ref), channel_id=1, source_target_pairs={{0,10},{1,25},{2,26},{3,9},{4,14},{5,29},{6,30},{7,13},{8,16},{9,3... | collective-permute-start | bytes 393224 | tf_op jit(solution)/shard_map/ppermute | solution.py:47
  25.5 6.9 %collective-permute-start.15 = (f32[32,1024]{1,0:T(8,128)S(1)}, f32[32,1024]{1,0:T(8,128)S(1)}, u32[]{:S(2)}, u32[]{:S(2)}) collective-permute-start(f32[32,1024]{1,0:T(8,128)S(1)} %add.80.own_ref), channel_id=1, source_target_pairs={{0,24},{1,8},{2,11},{3,27},{4,28},{5,12},{6,15},{7,31},{8,1},{9,17... | collective-permute-start | bytes 393224 | tf_op jit(solution)/shard_map/ppermute | solution.py:47
  27.1 6.1 %collective-permute-start.8 = (f32[32,1024]{1,0:T(8,128)S(1)}, f32[32,1024]{1,0:T(8,128)S(1)}, u32[]{:S(2)}, u32[]{:S(2)}) collective-permute-start(f32[32,1024]{1,0:T(8,128)S(1)} %add.77.own_ref), channel_id=1, source_target_pairs={{0,24},{1,8},{2,11},{3,27},{4,28},{5,12},{6,15},{7,31},{8,1},{9,17... | collective-permute-start | bytes 393224 | tf_op jit(solution)/shard_map/ppermute | solution.py:47
  28.3 6.4 %collective-permute-start.4 = (f32[32,1024]{1,0:T(8,128)S(1)}, f32[32,1024]{1,0:T(8,128)S(1)}, u32[]{:S(2)}, u32[]{:S(2)}) collective-permute-start(f32[32,1024]{1,0:T(8,128)S(1)} %add.74.own_ref), channel_id=1, source_target_pairs={{0,9},{1,11},{2,8},{3,10},{4,13},{5,15},{6,12},{7,14},{8,2},{9,0},... | collective-permute-start | bytes 393224 | tf_op jit(solution)/shard_map/ppermute | solution.py:47
  43.8 4.9 %collective-permute-start.23 = (f32[32,1024]{1,0:T(8,128)S(1)}, f32[32,1024]{1,0:T(8,128)S(1)}, u32[]{:S(2)}, u32[]{:S(2)}) collective-permute-start(f32[32,1024]{1,0:T(8,128)S(1)} %get-tuple-element.69), channel_id=1, source_target_pairs={{0,9},{1,11},{2,8},{3,10},{4,13},{5,15},{6,12},{7,14},{8,2},{9,0},... | collective-permute-start | bytes 393224 | tf_op jit(solution)/shard_map/ppermute | solution.py:47
  44.3 5.8 %collective-permute-start.38 = (f32[32,1024]{1,0:T(8,128)S(1)}, f32[32,1024]{1,0:T(8,128)S(1)}, u32[]{:S(2)}, u32[]{:S(2)}) collective-permute-start(f32[32,1024]{1,0:T(8,128)S(1)} %get-tuple-element.77), channel_id=1, source_target_pairs={{0,10},{1,25},{2,26},{3,9},{4,14},{5,29},{6,30},{7,13},{8,16},{9,3... | collective-permute-start | bytes 393224 | tf_op jit(solution)/shard_map/ppermute | solution.py:47
  46.4 5.5 %collective-permute-start.34 = (f32[32,1024]{1,0:T(8,128)S(1)}, f32[32,1024]{1,0:T(8,128)S(1)}, u32[]{:S(2)}, u32[]{:S(2)}) collective-permute-start(f32[32,1024]{1,0:T(8,128)S(1)} %get-tuple-element.75), channel_id=1, source_target_pairs={{0,24},{1,8},{2,11},{3,27},{4,28},{5,12},{6,15},{7,31},{8,1},{9,17... | collective-permute-start | bytes 393224 | tf_op jit(solution)/shard_map/ppermute | solution.py:47
  46.9 5.8 %collective-permute-start.28 = (f32[32,1024]{1,0:T(8,128)S(1)}, f32[32,1024]{1,0:T(8,128)S(1)}, u32[]{:S(2)}, u32[]{:S(2)}) collective-permute-start(f32[32,1024]{1,0:T(8,128)S(1)} %add.87), channel_id=1, source_target_pairs={{0,9},{1,11},{2,8},{3,10},{4,13},{5,15},{6,12},{7,14},{8,2},{9,0},... | collective-permute-start | bytes 393224 | tf_op jit(solution)/shard_map/ppermute | solution.py:47
  48.7 5.3 %collective-permute-start.24 = (f32[32,1024]{1,0:T(8,128)S(1)}, f32[32,1024]{1,0:T(8,128)S(1)}, u32[]{:S(2)}, u32[]{:S(2)}) collective-permute-start(f32[32,1024]{1,0:T(8,128)S(1)} %add.84), channel_id=1, source_target_pairs={{0,10},{1,25},{2,26},{3,9},{4,14},{5,29},{6,30},{7,13},{8,16},{9,3... | collective-permute-start | bytes 393224 | tf_op jit(solution)/shard_map/ppermute | solution.py:47
  50.1 5.1 %collective-permute-start.39 = (f32[32,1024]{1,0:T(8,128)S(1)}, f32[32,1024]{1,0:T(8,128)S(1)}, u32[]{:S(2)}, u32[]{:S(2)}) collective-permute-start(f32[32,1024]{1,0:T(8,128)S(1)} %add.93), channel_id=1, source_target_pairs={{0,24},{1,8},{2,11},{3,27},{4,28},{5,12},{6,15},{7,31},{8,1},{9,17... | collective-permute-start | bytes 393224 | tf_op jit(solution)/shard_map/ppermute | solution.py:47
  51.9 4.8 %collective-permute-start.35 = (f32[32,1024]{1,0:T(8,128)S(1)}, f32[32,1024]{1,0:T(8,128)S(1)}, u32[]{:S(2)}, u32[]{:S(2)}) collective-permute-start(f32[32,1024]{1,0:T(8,128)S(1)} %add.90), channel_id=1, source_target_pairs={{0,9},{1,11},{2,8},{3,10},{4,13},{5,15},{6,12},{7,14},{8,2},{9,0},... | collective-permute-start | bytes 393224 | tf_op jit(solution)/shard_map/ppermute | solution.py:47
  52.7 5.7 %collective-permute-start.29 = (f32[32,1024]{1,0:T(8,128)S(1)}, f32[32,1024]{1,0:T(8,128)S(1)}, u32[]{:S(2)}, u32[]{:S(2)}) collective-permute-start(f32[32,1024]{1,0:T(8,128)S(1)} %add.88), channel_id=1, source_target_pairs={{0,10},{1,25},{2,26},{3,9},{4,14},{5,29},{6,30},{7,13},{8,16},{9,3... | collective-permute-start | bytes 393224 | tf_op jit(solution)/shard_map/ppermute | solution.py:47
  54.1 5.5 %collective-permute-start.25 = (f32[32,1024]{1,0:T(8,128)S(1)}, f32[32,1024]{1,0:T(8,128)S(1)}, u32[]{:S(2)}, u32[]{:S(2)}) collective-permute-start(f32[32,1024]{1,0:T(8,128)S(1)} %add.85), channel_id=1, source_target_pairs={{0,24},{1,8},{2,11},{3,27},{4,28},{5,12},{6,15},{7,31},{8,1},{9,17... | collective-permute-start | bytes 393224 | tf_op jit(solution)/shard_map/ppermute | solution.py:47
  55.3 5.4 %collective-permute-start.40 = (f32[32,1024]{1,0:T(8,128)S(1)}, f32[32,1024]{1,0:T(8,128)S(1)}, u32[]{:S(2)}, u32[]{:S(2)}) collective-permute-start(f32[32,1024]{1,0:T(8,128)S(1)} %add.94), channel_id=1, source_target_pairs={{0,9},{1,11},{2,8},{3,10},{4,13},{5,15},{6,12},{7,14},{8,2},{9,0},... | collective-permute-start | bytes 393224 | tf_op jit(solution)/shard_map/ppermute | solution.py:47
  56.7 5.7 %collective-permute-start.36 = (f32[32,1024]{1,0:T(8,128)S(1)}, f32[32,1024]{1,0:T(8,128)S(1)}, u32[]{:S(2)}, u32[]{:S(2)}) collective-permute-start(f32[32,1024]{1,0:T(8,128)S(1)} %add.91), channel_id=1, source_target_pairs={{0,10},{1,25},{2,26},{3,9},{4,14},{5,29},{6,30},{7,13},{8,16},{9,3... | collective-permute-start | bytes 393224 | tf_op jit(solution)/shard_map/ppermute | solution.py:47
  58.5 5.4 %collective-permute-start.30 = (f32[32,1024]{1,0:T(8,128)S(1)}, f32[32,1024]{1,0:T(8,128)S(1)}, u32[]{:S(2)}, u32[]{:S(2)}) collective-permute-start(f32[32,1024]{1,0:T(8,128)S(1)} %add.89.own_ref), channel_id=1, source_target_pairs={{0,24},{1,8},{2,11},{3,27},{4,28},{5,12},{6,15},{7,31},{8,1},{9,17... | collective-permute-start | bytes 393224 | tf_op jit(solution)/shard_map/ppermute | solution.py:47
  59.6 6.0 %collective-permute-start.26 = (f32[32,1024]{1,0:T(8,128)S(1)}, f32[32,1024]{1,0:T(8,128)S(1)}, u32[]{:S(2)}, u32[]{:S(2)}) collective-permute-start(f32[32,1024]{1,0:T(8,128)S(1)} %add.86.own_ref), channel_id=1, source_target_pairs={{0,9},{1,11},{2,8},{3,10},{4,13},{5,15},{6,12},{7,14},{8,2},{9,0},... | collective-permute-start | bytes 393224 | tf_op jit(solution)/shard_map/ppermute | solution.py:47
  60.7 5.7 %collective-permute-start.41 = (f32[32,1024]{1,0:T(8,128)S(1)}, f32[32,1024]{1,0:T(8,128)S(1)}, u32[]{:S(2)}, u32[]{:S(2)}) collective-permute-start(f32[32,1024]{1,0:T(8,128)S(1)} %add.95.own_ref), channel_id=1, source_target_pairs={{0,10},{1,25},{2,26},{3,9},{4,14},{5,29},{6,30},{7,13},{8,16},{9,3... | collective-permute-start | bytes 393224 | tf_op jit(solution)/shard_map/ppermute | solution.py:47
  62.4 6.0 %collective-permute-start.37 = (f32[32,1024]{1,0:T(8,128)S(1)}, f32[32,1024]{1,0:T(8,128)S(1)}, u32[]{:S(2)}, u32[]{:S(2)}) collective-permute-start(f32[32,1024]{1,0:T(8,128)S(1)} %add.92.own_ref), channel_id=1, source_target_pairs={{0,24},{1,8},{2,11},{3,27},{4,28},{5,12},{6,15},{7,31},{8,1},{9,17... | collective-permute-start | bytes 393224 | tf_op jit(solution)/shard_map/ppermute | solution.py:47
  63.9 5.1 %collective-permute-start.32 = (f32[64,1024]{1,0:T(8,128)S(1)}, f32[64,1024]{1,0:T(8,128)S(1)}, u32[]{:S(2)}, u32[]{:S(2)}) collective-permute-start(f32[64,1024]{1,0:T(8,128)S(1)} %shard_map.71.refs_1_), channel_id=1, source_target_pairs={{0,8},{1,9},{2,10},{3,11},{4,12},{5,13},{6,14},{7,15},{8,0},{9,1},... | collective-permute-start | bytes 786440 | tf_op jit(solution)/shard_map/ppermute | solution.py:47
  (12 other events, 36.4 us)

commit v3 on v2

--- a/solution.py
+++ b/solution.py
@@ -56,19 +56,23 @@
 
 def chain(keep, send, index):
     even, odd = ORDERS[index - 1]
-    got = from_partner(send, even[0], odd[0])
-    own = keep + got
-    own = own + from_partner(own, even[1], odd[1])
-    own = own + from_partner(own, even[2], odd[2])
-    rest = from_partner(own, even[0], odd[0])
+
+    def exchanged(values, step):
+        return from_partner(values, even[step % 3], odd[step % 3])
+
+    own = keep + exchanged(send, 0)
+    own = own + exchanged(own, 1)
+    own = own + exchanged(own, 2)
+    rest = exchanged(own, 3)
     rows, columns = own.shape
-    return pl.pallas_call(
+    joined = pl.pallas_call(
         functools.partial(join_kernel, index),
         out_shape=jax.ShapeDtypeStruct((2 * rows, columns), f32),
         in_specs=[VMEM, VMEM],
         out_specs=VMEM,
         compiler_params=SMALL,
     )(own, rest)
+    return joined, from_partner(joined, 0, 0)
 
 
 def meet_kernel(indices, keep_ref, got_ref, *outs):
@@ -94,7 +98,7 @@
         compiler_params=SMALL,
     )(keep, got)
     parts = [chain(pieces[2 * k], pieces[2 * k + 1], index) for k, index in enumerate(indices)]
-    return parts + [from_partner(part, 0, 0) for part in parts]
+    return [own for own, over in parts] + [over for own, over in parts]
 
 
 def place_of(index, count, role):

time: 71.7 us -> 71.7 us (level)
  no operation moved by 1% of the time
where the time goes in v3:
time: 71.7 us; the launch traced here: 71.6 us
  starting transfers between devices  48.4 us (68%)
  waiting for transfers between devices  11 us (15%)
  Pallas kernels  10.9 us (15%)
  between operations  0.84 us (1%)
    ppermute x44, starting transfers between devices, from_partner(): return lax.ppermute(values, ('near', 'far'), pairs)  48.4 us
    ppermute x44, waiting for transfers between devices, from_partner(): return lax.ppermute(values, ('near', 'far'), pairs)  11 us
    pallas_call x2, Pallas kernels, shards(): pl.pallas_call(functools.partial(expand_kernel, 0 if first else len(sums_...  6.21 us
    pallas_call x2, Pallas kernels, shards(): pl.pallas_call(reduce_kernel, out_shape=(half, half), in_specs=[VMEM] * 6...  2.8 us
  transfers between devices with their start and end apart: 44, of which 21 were waited for; matrix products, arithmetic and copies ran while one was open for 1% of the time, Pallas kernels for 3%

profile of v3, /device:TPU:0, one launch (start us, length us, event | category | flops | bytes accessed | tf_op | source)
XLA Modules:
  0.0 71.6 jit_solution(16913991774686603811)
XLA Ops:
  0.6 3.7 %shard_map.59 = (f32[128,1024]{1,0:T(8,128)S(1)}, f32[128,1024]{1,0:T(8,128)S(1)}, bf16[256,1024]{1,0:T(8,128)(2,1)S(1)}, bf16[256,1024]{1,0:T(8,128)(2,1)S(1)},...) custom-call(bf16[2,256,1024]{2,1,0:T(8,128)(2,1)} %bitcast.6, ...), custom_call_target="tpu_custom_call" | custom-call | tf_op jit(solution)/shard_map/pallas_call | solution.py:233
  4.9 1.3 %shard_map.60 = (f32[128,1024]{1,0:T(8,128)S(1)}, f32[128,1024]{1,0:T(8,128)S(1)}) custom-call(bf16[256,1024]{1,0:T(8,128)(2,1)S(1)} %get-tuple-element.43.x_ref, bf16[256,1024]{1,0:T(8,128)(2,1)S(1)} %get-tuple-element.44.r_ref, bf16[256,1024]{1,0:T(8,128)(2,1)S(1)} %get-tuple-element.45.e_ref, bf16[256,1024]{1,0:T(8,128)(2,1)S(1)} %get-tuple-element.46.zh_ref, ...), custom_call_target="tpu_custom_call" | custom-call | tf_op jit(solution)/shard_map/pallas_call | solution.py:244
  6.5 2.7 %collective-permute-start.16 = (f32[32,1024]{1,0:T(8,128)S(1)}, f32[32,1024]{1,0:T(8,128)S(1)}, u32[]{:S(2)}, u32[]{:S(2)}) collective-permute-start(f32[32,1024]{1,0:T(8,128)S(1)} %get-tuple-element.60), channel_id=1, source_target_pairs={{0,10},{1,25},{2,26},{3,9},{4,14},{5,29},{6,30},{7,13},{8,16},{9,3... | collective-permute-start | bytes 393224 | tf_op jit(solution)/shard_map/ppermute | solution.py:47
  9.3 1.5 %collective-permute-start.12 = (f32[32,1024]{1,0:T(8,128)S(1)}, f32[32,1024]{1,0:T(8,128)S(1)}, u32[]{:S(2)}, u32[]{:S(2)}) collective-permute-start(f32[32,1024]{1,0:T(8,128)S(1)} %get-tuple-element.58), channel_id=1, source_target_pairs={{0,24},{1,8},{2,11},{3,27},{4,28},{5,12},{6,15},{7,31},{8,1},{9,17... | collective-permute-start | bytes 393224 | tf_op jit(solution)/shard_map/ppermute | solution.py:47
  11.1 1.5 %collective-permute-start.1 = (f32[32,1024]{1,0:T(8,128)S(1)}, f32[32,1024]{1,0:T(8,128)S(1)}, u32[]{:S(2)}, u32[]{:S(2)}) collective-permute-start(f32[32,1024]{1,0:T(8,128)S(1)} %get-tuple-element.52), channel_id=1, source_target_pairs={{0,9},{1,11},{2,8},{3,10},{4,13},{5,15},{6,12},{7,14},{8,2},{9,0},... | collective-permute-start | bytes 393224 | tf_op jit(solution)/shard_map/ppermute | solution.py:47
  12.7 1.3 %collective-permute-start.17 = (f32[32,1024]{1,0:T(8,128)S(1)}, f32[32,1024]{1,0:T(8,128)S(1)}, u32[]{:S(2)}, u32[]{:S(2)}) collective-permute-start(f32[32,1024]{1,0:T(8,128)S(1)} %add.81), channel_id=1, source_target_pairs={{0,24},{1,8},{2,11},{3,27},{4,28},{5,12},{6,15},{7,31},{8,1},{9,17... | collective-permute-start | bytes 393224 | tf_op jit(solution)/shard_map/ppermute | solution.py:47
  14.0 1.6 %collective-permute-start.13 = (f32[32,1024]{1,0:T(8,128)S(1)}, f32[32,1024]{1,0:T(8,128)S(1)}, u32[]{:S(2)}, u32[]{:S(2)}) collective-permute-start(f32[32,1024]{1,0:T(8,128)S(1)} %add.78), channel_id=1, source_target_pairs={{0,9},{1,11},{2,8},{3,10},{4,13},{5,15},{6,12},{7,14},{8,2},{9,0},... | collective-permute-start | bytes 393224 | tf_op jit(solution)/shard_map/ppermute | solution.py:47
  15.6 1.2 %collective-permute-start.6 = (f32[32,1024]{1,0:T(8,128)S(1)}, f32[32,1024]{1,0:T(8,128)S(1)}, u32[]{:S(2)}, u32[]{:S(2)}) collective-permute-start(f32[32,1024]{1,0:T(8,128)S(1)} %add.75), channel_id=1, source_target_pairs={{0,9},{1,11},{2,8},{3,10},{4,13},{5,15},{6,12},{7,14},{8,2},{9,0},... | collective-permute-start | bytes 393224 | tf_op jit(solution)/shard_map/ppermute | solution.py:47
  17.0 1.4 %collective-permute-start.2 = (f32[32,1024]{1,0:T(8,128)S(1)}, f32[32,1024]{1,0:T(8,128)S(1)}, u32[]{:S(2)}, u32[]{:S(2)}) collective-permute-start(f32[32,1024]{1,0:T(8,128)S(1)} %add.72), channel_id=1, source_target_pairs={{0,10},{1,25},{2,26},{3,9},{4,14},{5,29},{6,30},{7,13},{8,16},{9,3... | collective-permute-start | bytes 393224 | tf_op jit(solution)/shard_map/ppermute | solution.py:47
  18.4 1.4 %collective-permute-start.18 = (f32[32,1024]{1,0:T(8,128)S(1)}, f32[32,1024]{1,0:T(8,128)S(1)}, u32[]{:S(2)}, u32[]{:S(2)}) collective-permute-start(f32[32,1024]{1,0:T(8,128)S(1)} %add.82), channel_id=1, source_target_pairs={{0,9},{1,11},{2,8},{3,10},{4,13},{5,15},{6,12},{7,14},{8,2},{9,0},... | collective-permute-start | bytes 393224 | tf_op jit(solution)/shard_map/ppermute | solution.py:47
  19.8 1.0 %collective-permute-start.14 = (f32[32,1024]{1,0:T(8,128)S(1)}, f32[32,1024]{1,0:T(8,128)S(1)}, u32[]{:S(2)}, u32[]{:S(2)}) collective-permute-start(f32[32,1024]{1,0:T(8,128)S(1)} %add.79), channel_id=1, source_target_pairs={{0,10},{1,25},{2,26},{3,9},{4,14},{5,29},{6,30},{7,13},{8,16},{9,3... | collective-permute-start | bytes 393224 | tf_op jit(solution)/shard_map/ppermute | solution.py:47
  21.2 1.0 %collective-permute-start.7 = (f32[32,1024]{1,0:T(8,128)S(1)}, f32[32,1024]{1,0:T(8,128)S(1)}, u32[]{:S(2)}, u32[]{:S(2)}) collective-permute-start(f32[32,1024]{1,0:T(8,128)S(1)} %add.76), channel_id=1, source_target_pairs={{0,10},{1,25},{2,26},{3,9},{4,14},{5,29},{6,30},{7,13},{8,16},{9,3... | collective-permute-start | bytes 393224 | tf_op jit(solution)/shard_map/ppermute | solution.py:47
  22.4 1.6 %collective-permute-start.3 = (f32[32,1024]{1,0:T(8,128)S(1)}, f32[32,1024]{1,0:T(8,128)S(1)}, u32[]{:S(2)}, u32[]{:S(2)}) collective-permute-start(f32[32,1024]{1,0:T(8,128)S(1)} %add.73), channel_id=1, source_target_pairs={{0,24},{1,8},{2,11},{3,27},{4,28},{5,12},{6,15},{7,31},{8,1},{9,17... | collective-permute-start | bytes 393224 | tf_op jit(solution)/shard_map/ppermute | solution.py:47
  24.1 1.0 %collective-permute-start.19 = (f32[32,1024]{1,0:T(8,128)S(1)}, f32[32,1024]{1,0:T(8,128)S(1)}, u32[]{:S(2)}, u32[]{:S(2)}) collective-permute-start(f32[32,1024]{1,0:T(8,128)S(1)} %add.83.own_ref), channel_id=1, source_target_pairs={{0,10},{1,25},{2,26},{3,9},{4,14},{5,29},{6,30},{7,13},{8,16},{9,3... | collective-permute-start | bytes 393224 | tf_op jit(solution)/shard_map/ppermute | solution.py:47
  28.3 2.1 %collective-permute-start.4 = (f32[32,1024]{1,0:T(8,128)S(1)}, f32[32,1024]{1,0:T(8,128)S(1)}, u32[]{:S(2)}, u32[]{:S(2)}) collective-permute-start(f32[32,1024]{1,0:T(8,128)S(1)} %add.74.own_ref), channel_id=1, source_target_pairs={{0,9},{1,11},{2,8},{3,10},{4,13},{5,15},{6,12},{7,14},{8,2},{9,0},... | collective-permute-start | bytes 393224 | tf_op jit(solution)/shard_map/ppermute | solution.py:47
  30.4 2.0 %collective-permute-start.21 = (f32[64,1024]{1,0:T(8,128)S(1)}, f32[64,1024]{1,0:T(8,128)S(1)}, u32[]{:S(2)}, u32[]{:S(2)}) collective-permute-start(f32[64,1024]{1,0:T(8,128)S(1)} %shard_map.66.refs_5_), channel_id=1, source_target_pairs={{0,8},{1,9},{2,10},{3,11},{4,12},{5,13},{6,14},{7,15},{8,0},{9,1},... | collective-permute-start | bytes 786440 | tf_op jit(solution)/shard_map/ppermute | solution.py:47
  33.2 1.6 %collective-permute-start.10 = (f32[64,1024]{1,0:T(8,128)S(1)}, f32[64,1024]{1,0:T(8,128)S(1)}, u32[]{:S(2)}, u32[]{:S(2)}) collective-permute-start(f32[64,1024]{1,0:T(8,128)S(1)} %shard_map.63.refs_1_), channel_id=1, source_target_pairs={{0,8},{1,9},{2,10},{3,11},{4,12},{5,13},{6,14},{7,15},{8,0},{9,1},... | collective-permute-start | bytes 786440 | tf_op jit(solution)/shard_map/ppermute | solution.py:47
  36.4 2.5 %shard_map.67 = (f32[128,1024]{1,0:T(8,128)S(1)}, f32[128,1024]{1,0:T(8,128)S(1)}, bf16[256,1024]{1,0:T(8,128)(2,1)S(1)}, bf16[256,1024]{1,0:T(8,128)(2,1)S(1)},...) custom-call(bf16[256,1024]{1,0:T(8,128)(2,1)S(1)} %get-tuple-element.41.x_in.x_ref, ...), custom_call_target="tpu_custom_call" | custom-call | tf_op jit(solution)/shard_map/pallas_call | solution.py:233
  38.9 1.5 %shard_map.68 = (f32[128,1024]{1,0:T(8,128)S(1)}, f32[128,1024]{1,0:T(8,128)S(1)}) custom-call(bf16[256,1024]{1,0:T(8,128)(2,1)S(1)} %get-tuple-element.41.x_in.x_ref, f32[256,1024]{1,0:T(8,128)S(1)} %get-tuple-element.61.r_ref, f32[256,1024]{1,0:T(8,128)S(1)} %get-tuple-element.62.e_ref, bf16[256,1024]{1,0:T(8,128)(2,1)S(1)} %get-tuple-element.63.zh_ref, ...), custom_call_target="tpu_custom_call" | custom-call | tf_op jit(solution)/shard_map/pallas_call | solution.py:244
  40.9 1.4 %collective-permute-done.22.got_ref = f32[128,1024]{1,0:T(8,128)S(1)} collective-permute-done((f32[128,1024]{1,0:T(8,128)S(1)}, f32[128,1024]{1,0:T(8,128)S(1)}, u32[]{:S(2)}, u32[]{:S(2)}) %collective-permute-start.22) | collective-permute-done | bytes 524320 | tf_op jit(solution)/shard_map/ppermute | solution.py:47
  42.4 1.4 %collective-permute-start.27 = (f32[32,1024]{1,0:T(8,128)S(1)}, f32[32,1024]{1,0:T(8,128)S(1)}, u32[]{:S(2)}, u32[]{:S(2)}) collective-permute-start(f32[32,1024]{1,0:T(8,128)S(1)} %get-tuple-element.71), channel_id=1, source_target_pairs={{0,24},{1,8},{2,11},{3,27},{4,28},{5,12},{6,15},{7,31},{8,1},{9,17... | collective-permute-start | bytes 393224 | tf_op jit(solution)/shard_map/ppermute | solution.py:47
  44.3 2.1 %collective-permute-start.38 = (f32[32,1024]{1,0:T(8,128)S(1)}, f32[32,1024]{1,0:T(8,128)S(1)}, u32[]{:S(2)}, u32[]{:S(2)}) collective-permute-start(f32[32,1024]{1,0:T(8,128)S(1)} %get-tuple-element.77), channel_id=1, source_target_pairs={{0,10},{1,25},{2,26},{3,9},{4,14},{5,29},{6,30},{7,13},{8,16},{9,3... | collective-permute-start | bytes 393224 | tf_op jit(solution)/shard_map/ppermute | solution.py:47
  46.9 1.3 %collective-permute-start.28 = (f32[32,1024]{1,0:T(8,128)S(1)}, f32[32,1024]{1,0:T(8,128)S(1)}, u32[]{:S(2)}, u32[]{:S(2)}) collective-permute-start(f32[32,1024]{1,0:T(8,128)S(1)} %add.87), channel_id=1, source_target_pairs={{0,9},{1,11},{2,8},{3,10},{4,13},{5,15},{6,12},{7,14},{8,2},{9,0},... | collective-permute-start | bytes 393224 | tf_op jit(solution)/shard_map/ppermute | solution.py:47
  48.7 1.4 %collective-permute-start.24 = (f32[32,1024]{1,0:T(8,128)S(1)}, f32[32,1024]{1,0:T(8,128)S(1)}, u32[]{:S(2)}, u32[]{:S(2)}) collective-permute-start(f32[32,1024]{1,0:T(8,128)S(1)} %add.84), channel_id=1, source_target_pairs={{0,10},{1,25},{2,26},{3,9},{4,14},{5,29},{6,30},{7,13},{8,16},{9,3... | collective-permute-start | bytes 393224 | tf_op jit(solution)/shard_map/ppermute | solution.py:47
  50.1 1.7 %collective-permute-start.39 = (f32[32,1024]{1,0:T(8,128)S(1)}, f32[32,1024]{1,0:T(8,128)S(1)}, u32[]{:S(2)}, u32[]{:S(2)}) collective-permute-start(f32[32,1024]{1,0:T(8,128)S(1)} %add.93), channel_id=1, source_target_pairs={{0,24},{1,8},{2,11},{3,27},{4,28},{5,12},{6,15},{7,31},{8,1},{9,17... | collective-permute-start | bytes 393224 | tf_op jit(solution)/shard_map/ppermute | solution.py:47
  52.7 1.3 %collective-permute-start.29 = (f32[32,1024]{1,0:T(8,128)S(1)}, f32[32,1024]{1,0:T(8,128)S(1)}, u32[]{:S(2)}, u32[]{:S(2)}) collective-permute-start(f32[32,1024]{1,0:T(8,128)S(1)} %add.88), channel_id=1, source_target_pairs={{0,10},{1,25},{2,26},{3,9},{4,14},{5,29},{6,30},{7,13},{8,16},{9,3... | collective-permute-start | bytes 393224 | tf_op jit(solution)/shard_map/ppermute | solution.py:47
  55.3 1.4 %collective-permute-start.40 = (f32[32,1024]{1,0:T(8,128)S(1)}, f32[32,1024]{1,0:T(8,128)S(1)}, u32[]{:S(2)}, u32[]{:S(2)}) collective-permute-start(f32[32,1024]{1,0:T(8,128)S(1)} %add.94), channel_id=1, source_target_pairs={{0,9},{1,11},{2,8},{3,10},{4,13},{5,15},{6,12},{7,14},{8,2},{9,0},... | collective-permute-start | bytes 393224 | tf_op jit(solution)/shard_map/ppermute | solution.py:47
  56.7 1.4 %collective-permute-start.36 = (f32[32,1024]{1,0:T(8,128)S(1)}, f32[32,1024]{1,0:T(8,128)S(1)}, u32[]{:S(2)}, u32[]{:S(2)}) collective-permute-start(f32[32,1024]{1,0:T(8,128)S(1)} %add.91), channel_id=1, source_target_pairs={{0,10},{1,25},{2,26},{3,9},{4,14},{5,29},{6,30},{7,13},{8,16},{9,3... | collective-permute-start | bytes 393224 | tf_op jit(solution)/shard_map/ppermute | solution.py:47
  60.7 1.2 %collective-permute-start.41 = (f32[32,1024]{1,0:T(8,128)S(1)}, f32[32,1024]{1,0:T(8,128)S(1)}, u32[]{:S(2)}, u32[]{:S(2)}) collective-permute-start(f32[32,1024]{1,0:T(8,128)S(1)} %add.95.own_ref), channel_id=1, source_target_pairs={{0,10},{1,25},{2,26},{3,9},{4,14},{5,29},{6,30},{7,13},{8,16},{9,3... | collective-permute-start | bytes 393224 | tf_op jit(solution)/shard_map/ppermute | solution.py:47
  63.9 1.6 %collective-permute-start.32 = (f32[64,1024]{1,0:T(8,128)S(1)}, f32[64,1024]{1,0:T(8,128)S(1)}, u32[]{:S(2)}, u32[]{:S(2)}) collective-permute-start(f32[64,1024]{1,0:T(8,128)S(1)} %shard_map.71.refs_1_), channel_id=1, source_target_pairs={{0,8},{1,9},{2,10},{3,11},{4,12},{5,13},{6,14},{7,15},{8,0},{9,1},... | collective-permute-start | bytes 786440 | tf_op jit(solution)/shard_map/ppermute | solution.py:47
  66.4 2.0 %collective-permute-start.43 = (f32[64,1024]{1,0:T(8,128)S(1)}, f32[64,1024]{1,0:T(8,128)S(1)}, u32[]{:S(2)}, u32[]{:S(2)}) collective-permute-start(f32[64,1024]{1,0:T(8,128)S(1)} %shard_map.74.refs_5_), channel_id=1, source_target_pairs={{0,8},{1,9},{2,10},{3,11},{4,12},{5,13},{6,14},{7,15},{8,0},{9,1},... | collective-permute-start | bytes 786440 | tf_op jit(solution)/shard_map/ppermute | solution.py:47
  70.2 1.4 %store.1 = (f32[256,1024]{1,0:T(8,128)}, f32[256,1024]{1,0:T(8,128)}) custom-call(f32[64,1024]{1,0:T(8,128)S(1)} %shard_map.70.refs_0_, f32[64,1024]{1,0:T(8,128)S(1)} %shard_map.71.refs_1_, f32[64,1024]{1,0:T(8,128)S(1)} %collective-permute-done.31.refs_2_, f32[64,1024]{1,0:T(8,128)S(1)} %collective-permute-done.32.refs_3_, ...), custom_call_target="tpu_custom_call" | custom-call | tf_op jit(solution)/shard_map/store/pallas_call | solution.py:125
  (97 shorter events, 19.3 us)
Async XLA Ops:
  6.5 6.1 %collective-permute-start.16 = (f32[32,1024]{1,0:T(8,128)S(1)}, f32[32,1024]{1,0:T(8,128)S(1)}, u32[]{:S(2)}, u32[]{:S(2)}) collective-permute-start(f32[32,1024]{1,0:T(8,128)S(1)} %get-tuple-element.60), channel_id=1, source_target_pairs={{0,10},{1,25},{2,26},{3,9},{4,14},{5,29},{6,30},{7,13},{8,16},{9,3... | collective-permute-start | bytes 393224 | tf_op jit(solution)/shard_map/ppermute | solution.py:47
  9.3 4.7 %collective-permute-start.12 = (f32[32,1024]{1,0:T(8,128)S(1)}, f32[32,1024]{1,0:T(8,128)S(1)}, u32[]{:S(2)}, u32[]{:S(2)}) collective-permute-start(f32[32,1024]{1,0:T(8,128)S(1)} %get-tuple-element.58), channel_id=1, source_target_pairs={{0,24},{1,8},{2,11},{3,27},{4,28},{5,12},{6,15},{7,31},{8,1},{9,17... | collective-permute-start | bytes 393224 | tf_op jit(solution)/shard_map/ppermute | solution.py:47
  10.8 4.7 %collective-permute-start.5 = (f32[32,1024]{1,0:T(8,128)S(1)}, f32[32,1024]{1,0:T(8,128)S(1)}, u32[]{:S(2)}, u32[]{:S(2)}) collective-permute-start(f32[32,1024]{1,0:T(8,128)S(1)} %get-tuple-element.54), channel_id=1, source_target_pairs={{0,24},{1,8},{2,11},{3,27},{4,28},{5,12},{6,15},{7,31},{8,1},{9,17... | collective-permute-start | bytes 393224 | tf_op jit(solution)/shard_map/ppermute | solution.py:47
  11.1 5.8 %collective-permute-start.1 = (f32[32,1024]{1,0:T(8,128)S(1)}, f32[32,1024]{1,0:T(8,128)S(1)}, u32[]{:S(2)}, u32[]{:S(2)}) collective-permute-start(f32[32,1024]{1,0:T(8,128)S(1)} %get-tuple-element.52), channel_id=1, source_target_pairs={{0,9},{1,11},{2,8},{3,10},{4,13},{5,15},{6,12},{7,14},{8,2},{9,0},... | collective-permute-start | bytes 393224 | tf_op jit(solution)/shard_map/ppermute | solution.py:47
  12.7 5.7 %collective-permute-start.17 = (f32[32,1024]{1,0:T(8,128)S(1)}, f32[32,1024]{1,0:T(8,128)S(1)}, u32[]{:S(2)}, u32[]{:S(2)}) collective-permute-start(f32[32,1024]{1,0:T(8,128)S(1)} %add.81), channel_id=1, source_target_pairs={{0,24},{1,8},{2,11},{3,27},{4,28},{5,12},{6,15},{7,31},{8,1},{9,17... | collective-permute-start | bytes 393224 | tf_op jit(solution)/shard_map/ppermute | solution.py:47
  14.0 5.8 %collective-permute-start.13 = (f32[32,1024]{1,0:T(8,128)S(1)}, f32[32,1024]{1,0:T(8,128)S(1)}, u32[]{:S(2)}, u32[]{:S(2)}) collective-permute-start(f32[32,1024]{1,0:T(8,128)S(1)} %add.78), channel_id=1, source_target_pairs={{0,9},{1,11},{2,8},{3,10},{4,13},{5,15},{6,12},{7,14},{8,2},{9,0},... | collective-permute-start | bytes 393224 | tf_op jit(solution)/shard_map/ppermute | solution.py:47
  15.6 5.6 %collective-permute-start.6 = (f32[32,1024]{1,0:T(8,128)S(1)}, f32[32,1024]{1,0:T(8,128)S(1)}, u32[]{:S(2)}, u32[]{:S(2)}) collective-permute-start(f32[32,1024]{1,0:T(8,128)S(1)} %add.75), channel_id=1, source_target_pairs={{0,9},{1,11},{2,8},{3,10},{4,13},{5,15},{6,12},{7,14},{8,2},{9,0},... | collective-permute-start | bytes 393224 | tf_op jit(solution)/shard_map/ppermute | solution.py:47
  17.0 5.4 %collective-permute-start.2 = (f32[32,1024]{1,0:T(8,128)S(1)}, f32[32,1024]{1,0:T(8,128)S(1)}, u32[]{:S(2)}, u32[]{:S(2)}) collective-permute-start(f32[32,1024]{1,0:T(8,128)S(1)} %add.72), channel_id=1, source_target_pairs={{0,10},{1,25},{2,26},{3,9},{4,14},{5,29},{6,30},{7,13},{8,16},{9,3... | collective-permute-start | bytes 393224 | tf_op jit(solution)/shard_map/ppermute | solution.py:47
  18.4 5.7 %collective-permute-start.18 = (f32[32,1024]{1,0:T(8,128)S(1)}, f32[32,1024]{1,0:T(8,128)S(1)}, u32[]{:S(2)}, u32[]{:S(2)}) collective-permute-start(f32[32,1024]{1,0:T(8,128)S(1)} %add.82), channel_id=1, source_target_pairs={{0,9},{1,11},{2,8},{3,10},{4,13},{5,15},{6,12},{7,14},{8,2},{9,0},... | collective-permute-start | bytes 393224 | tf_op jit(solution)/shard_map/ppermute | solution.py:47
  19.8 5.7 %collective-permute-start.14 = (f32[32,1024]{1,0:T(8,128)S(1)}, f32[32,1024]{1,0:T(8,128)S(1)}, u32[]{:S(2)}, u32[]{:S(2)}) collective-permute-start(f32[32,1024]{1,0:T(8,128)S(1)} %add.79), channel_id=1, source_target_pairs={{0,10},{1,25},{2,26},{3,9},{4,14},{5,29},{6,30},{7,13},{8,16},{9,3... | collective-permute-start | bytes 393224 | tf_op jit(solution)/shard_map/ppermute | solution.py:47
  21.2 5.9 %collective-permute-start.7 = (f32[32,1024]{1,0:T(8,128)S(1)}, f32[32,1024]{1,0:T(8,128)S(1)}, u32[]{:S(2)}, u32[]{:S(2)}) collective-permute-start(f32[32,1024]{1,0:T(8,128)S(1)} %add.76), channel_id=1, source_target_pairs={{0,10},{1,25},{2,26},{3,9},{4,14},{5,29},{6,30},{7,13},{8,16},{9,3... | collective-permute-start | bytes 393224 | tf_op jit(solution)/shard_map/ppermute | solution.py:47
  22.4 5.9 %collective-permute-start.3 = (f32[32,1024]{1,0:T(8,128)S(1)}, f32[32,1024]{1,0:T(8,128)S(1)}, u32[]{:S(2)}, u32[]{:S(2)}) collective-permute-start(f32[32,1024]{1,0:T(8,128)S(1)} %add.73), channel_id=1, source_target_pairs={{0,24},{1,8},{2,11},{3,27},{4,28},{5,12},{6,15},{7,31},{8,1},{9,17... | collective-permute-start | bytes 393224 | tf_op jit(solution)/shard_map/ppermute | solution.py:47
  24.1 6.3 %collective-permute-start.19 = (f32[32,1024]{1,0:T(8,128)S(1)}, f32[32,1024]{1,0:T(8,128)S(1)}, u32[]{:S(2)}, u32[]{:S(2)}) collective-permute-start(f32[32,1024]{1,0:T(8,128)S(1)} %add.83.own_ref), channel_id=1, source_target_pairs={{0,10},{1,25},{2,26},{3,9},{4,14},{5,29},{6,30},{7,13},{8,16},{9,3... | collective-permute-start | bytes 393224 | tf_op jit(solution)/shard_map/ppermute | solution.py:47
  25.5 6.9 %collective-permute-start.15 = (f32[32,1024]{1,0:T(8,128)S(1)}, f32[32,1024]{1,0:T(8,128)S(1)}, u32[]{:S(2)}, u32[]{:S(2)}) collective-permute-start(f32[32,1024]{1,0:T(8,128)S(1)} %add.80.own_ref), channel_id=1, source_target_pairs={{0,24},{1,8},{2,11},{3,27},{4,28},{5,12},{6,15},{7,31},{8,1},{9,17... | collective-permute-start | bytes 393224 | tf_op jit(solution)/shard_map/ppermute | solution.py:47
  27.1 6.1 %collective-permute-start.8 = (f32[32,1024]{1,0:T(8,128)S(1)}, f32[32,1024]{1,0:T(8,128)S(1)}, u32[]{:S(2)}, u32[]{:S(2)}) collective-permute-start(f32[32,1024]{1,0:T(8,128)S(1)} %add.77.own_ref), channel_id=1, source_target_pairs={{0,24},{1,8},{2,11},{3,27},{4,28},{5,12},{6,15},{7,31},{8,1},{9,17... | collective-permute-start | bytes 393224 | tf_op jit(solution)/shard_map/ppermute | solution.py:47
  28.3 6.4 %collective-permute-start.4 = (f32[32,1024]{1,0:T(8,128)S(1)}, f32[32,1024]{1,0:T(8,128)S(1)}, u32[]{:S(2)}, u32[]{:S(2)}) collective-permute-start(f32[32,1024]{1,0:T(8,128)S(1)} %add.74.own_ref), channel_id=1, source_target_pairs={{0,9},{1,11},{2,8},{3,10},{4,13},{5,15},{6,12},{7,14},{8,2},{9,0},... | collective-permute-start | bytes 393224 | tf_op jit(solution)/shard_map/ppermute | solution.py:47
  43.8 4.9 %collective-permute-start.23 = (f32[32,1024]{1,0:T(8,128)S(1)}, f32[32,1024]{1,0:T(8,128)S(1)}, u32[]{:S(2)}, u32[]{:S(2)}) collective-permute-start(f32[32,1024]{1,0:T(8,128)S(1)} %get-tuple-element.69), channel_id=1, source_target_pairs={{0,9},{1,11},{2,8},{3,10},{4,13},{5,15},{6,12},{7,14},{8,2},{9,0},... | collective-permute-start | bytes 393224 | tf_op jit(solution)/shard_map/ppermute | solution.py:47
  44.3 5.8 %collective-permute-start.38 = (f32[32,1024]{1,0:T(8,128)S(1)}, f32[32,1024]{1,0:T(8,128)S(1)}, u32[]{:S(2)}, u32[]{:S(2)}) collective-permute-start(f32[32,1024]{1,0:T(8,128)S(1)} %get-tuple-element.77), channel_id=1, source_target_pairs={{0,10},{1,25},{2,26},{3,9},{4,14},{5,29},{6,30},{7,13},{8,16},{9,3... | collective-permute-start | bytes 393224 | tf_op jit(solution)/shard_map/ppermute | solution.py:47
  46.4 5.5 %collective-permute-start.34 = (f32[32,1024]{1,0:T(8,128)S(1)}, f32[32,1024]{1,0:T(8,128)S(1)}, u32[]{:S(2)}, u32[]{:S(2)}) collective-permute-start(f32[32,1024]{1,0:T(8,128)S(1)} %get-tuple-element.75), channel_id=1, source_target_pairs={{0,24},{1,8},{2,11},{3,27},{4,28},{5,12},{6,15},{7,31},{8,1},{9,17... | collective-permute-start | bytes 393224 | tf_op jit(solution)/shard_map/ppermute | solution.py:47
  46.9 5.8 %collective-permute-start.28 = (f32[32,1024]{1,0:T(8,128)S(1)}, f32[32,1024]{1,0:T(8,128)S(1)}, u32[]{:S(2)}, u32[]{:S(2)}) collective-permute-start(f32[32,1024]{1,0:T(8,128)S(1)} %add.87), channel_id=1, source_target_pairs={{0,9},{1,11},{2,8},{3,10},{4,13},{5,15},{6,12},{7,14},{8,2},{9,0},... | collective-permute-start | bytes 393224 | tf_op jit(solution)/shard_map/ppermute | solution.py:47
  48.7 5.3 %collective-permute-start.24 = (f32[32,1024]{1,0:T(8,128)S(1)}, f32[32,1024]{1,0:T(8,128)S(1)}, u32[]{:S(2)}, u32[]{:S(2)}) collective-permute-start(f32[32,1024]{1,0:T(8,128)S(1)} %add.84), channel_id=1, source_target_pairs={{0,10},{1,25},{2,26},{3,9},{4,14},{5,29},{6,30},{7,13},{8,16},{9,3... | collective-permute-start | bytes 393224 | tf_op jit(solution)/shard_map/ppermute | solution.py:47
  50.1 5.1 %collective-permute-start.39 = (f32[32,1024]{1,0:T(8,128)S(1)}, f32[32,1024]{1,0:T(8,128)S(1)}, u32[]{:S(2)}, u32[]{:S(2)}) collective-permute-start(f32[32,1024]{1,0:T(8,128)S(1)} %add.93), channel_id=1, source_target_pairs={{0,24},{1,8},{2,11},{3,27},{4,28},{5,12},{6,15},{7,31},{8,1},{9,17... | collective-permute-start | bytes 393224 | tf_op jit(solution)/shard_map/ppermute | solution.py:47
  51.9 4.8 %collective-permute-start.35 = (f32[32,1024]{1,0:T(8,128)S(1)}, f32[32,1024]{1,0:T(8,128)S(1)}, u32[]{:S(2)}, u32[]{:S(2)}) collective-permute-start(f32[32,1024]{1,0:T(8,128)S(1)} %add.90), channel_id=1, source_target_pairs={{0,9},{1,11},{2,8},{3,10},{4,13},{5,15},{6,12},{7,14},{8,2},{9,0},... | collective-permute-start | bytes 393224 | tf_op jit(solution)/shard_map/ppermute | solution.py:47
  52.7 5.7 %collective-permute-start.29 = (f32[32,1024]{1,0:T(8,128)S(1)}, f32[32,1024]{1,0:T(8,128)S(1)}, u32[]{:S(2)}, u32[]{:S(2)}) collective-permute-start(f32[32,1024]{1,0:T(8,128)S(1)} %add.88), channel_id=1, source_target_pairs={{0,10},{1,25},{2,26},{3,9},{4,14},{5,29},{6,30},{7,13},{8,16},{9,3... | collective-permute-start | bytes 393224 | tf_op jit(solution)/shard_map/ppermute | solution.py:47
  54.1 5.5 %collective-permute-start.25 = (f32[32,1024]{1,0:T(8,128)S(1)}, f32[32,1024]{1,0:T(8,128)S(1)}, u32[]{:S(2)}, u32[]{:S(2)}) collective-permute-start(f32[32,1024]{1,0:T(8,128)S(1)} %add.85), channel_id=1, source_target_pairs={{0,24},{1,8},{2,11},{3,27},{4,28},{5,12},{6,15},{7,31},{8,1},{9,17... | collective-permute-start | bytes 393224 | tf_op jit(solution)/shard_map/ppermute | solution.py:47
  55.3 5.4 %collective-permute-start.40 = (f32[32,1024]{1,0:T(8,128)S(1)}, f32[32,1024]{1,0:T(8,128)S(1)}, u32[]{:S(2)}, u32[]{:S(2)}) collective-permute-start(f32[32,1024]{1,0:T(8,128)S(1)} %add.94), channel_id=1, source_target_pairs={{0,9},{1,11},{2,8},{3,10},{4,13},{5,15},{6,12},{7,14},{8,2},{9,0},... | collective-permute-start | bytes 393224 | tf_op jit(solution)/shard_map/ppermute | solution.py:47
  56.7 5.7 %collective-permute-start.36 = (f32[32,1024]{1,0:T(8,128)S(1)}, f32[32,1024]{1,0:T(8,128)S(1)}, u32[]{:S(2)}, u32[]{:S(2)}) collective-permute-start(f32[32,1024]{1,0:T(8,128)S(1)} %add.91), channel_id=1, source_target_pairs={{0,10},{1,25},{2,26},{3,9},{4,14},{5,29},{6,30},{7,13},{8,16},{9,3... | collective-permute-start | bytes 393224 | tf_op jit(solution)/shard_map/ppermute | solution.py:47
  58.5 5.4 %collective-permute-start.30 = (f32[32,1024]{1,0:T(8,128)S(1)}, f32[32,1024]{1,0:T(8,128)S(1)}, u32[]{:S(2)}, u32[]{:S(2)}) collective-permute-start(f32[32,1024]{1,0:T(8,128)S(1)} %add.89.own_ref), channel_id=1, source_target_pairs={{0,24},{1,8},{2,11},{3,27},{4,28},{5,12},{6,15},{7,31},{8,1},{9,17... | collective-permute-start | bytes 393224 | tf_op jit(solution)/shard_map/ppermute | solution.py:47
  59.6 6.0 %collective-permute-start.26 = (f32[32,1024]{1,0:T(8,128)S(1)}, f32[32,1024]{1,0:T(8,128)S(1)}, u32[]{:S(2)}, u32[]{:S(2)}) collective-permute-start(f32[32,1024]{1,0:T(8,128)S(1)} %add.86.own_ref), channel_id=1, source_target_pairs={{0,9},{1,11},{2,8},{3,10},{4,13},{5,15},{6,12},{7,14},{8,2},{9,0},... | collective-permute-start | bytes 393224 | tf_op jit(solution)/shard_map/ppermute | solution.py:47
  60.7 5.7 %collective-permute-start.41 = (f32[32,1024]{1,0:T(8,128)S(1)}, f32[32,1024]{1,0:T(8,128)S(1)}, u32[]{:S(2)}, u32[]{:S(2)}) collective-permute-start(f32[32,1024]{1,0:T(8,128)S(1)} %add.95.own_ref), channel_id=1, source_target_pairs={{0,10},{1,25},{2,26},{3,9},{4,14},{5,29},{6,30},{7,13},{8,16},{9,3... | collective-permute-start | bytes 393224 | tf_op jit(solution)/shard_map/ppermute | solution.py:47
  62.4 6.0 %collective-permute-start.37 = (f32[32,1024]{1,0:T(8,128)S(1)}, f32[32,1024]{1,0:T(8,128)S(1)}, u32[]{:S(2)}, u32[]{:S(2)}) collective-permute-start(f32[32,1024]{1,0:T(8,128)S(1)} %add.92.own_ref), channel_id=1, source_target_pairs={{0,24},{1,8},{2,11},{3,27},{4,28},{5,12},{6,15},{7,31},{8,1},{9,17... | collective-permute-start | bytes 393224 | tf_op jit(solution)/shard_map/ppermute | solution.py:47
  63.9 5.1 %collective-permute-start.32 = (f32[64,1024]{1,0:T(8,128)S(1)}, f32[64,1024]{1,0:T(8,128)S(1)}, u32[]{:S(2)}, u32[]{:S(2)}) collective-permute-start(f32[64,1024]{1,0:T(8,128)S(1)} %shard_map.71.refs_1_), channel_id=1, source_target_pairs={{0,8},{1,9},{2,10},{3,11},{4,12},{5,13},{6,14},{7,15},{8,0},{9,1},... | collective-permute-start | bytes 786440 | tf_op jit(solution)/shard_map/ppermute | solution.py:47
  (12 other events, 36.4 us)

commit v4 on v3

v4 whole, which is shorter than its diff:
```python
import functools
import math

import jax
import jax.numpy as jnp
from jax import lax
from jax.experimental import pallas as pl
from jax.experimental.pallas import tpu as pltpu
from jax.sharding import PartitionSpec as P


learn_rate = 1.0

ORDERS = (
    ((1, 3, 2), (3, 2, 1)),
    ((3, 2, 1), (2, 1, 3)),
    ((1, 3, 2), (2, 1, 3)),
    ((1, 3, 2), (3, 2, 1)),
)
EXPAND_CHAINS = ((1, 4), (2, 4))
REDUCE_CHAINS = ((3, 4), (4, 4))
BITS = 4
BLOCK = 256
VMEM = pl.BlockSpec(memory_space=pltpu.VMEM)
HBM = pl.BlockSpec(memory_space=pltpu.HBM)
SMALL = pltpu.CompilerParams(vmem_limit_bytes=2**20)
LARGE = pltpu.CompilerParams(vmem_limit_bytes=12 * 2**20)
f32, bf16 = jnp.float32, jnp.bfloat16


def bits_of(near, far):
    chip = ((near >> 1) & 1, far & 1, (far >> 1) & 1)
    return ((near & 1) ^ chip[0] ^ chip[1] ^ chip[2],) + chip


def places():
    bits = bits_of(lax.axis_index("near"), lax.axis_index("far"))
    return [bits[0]] + [jnp.where(bits[0] == 0, bits[even[0]], bits[odd[0]]) for even, odd in ORDERS]


def from_partner(values, *bit_of_role):
    nears, fars = lax.axis_size("near"), lax.axis_size("far")
    pairs = []
    for near in range(nears):
        for far in range(fars):
            bit = bit_of_role[bits_of(near, far)[0]]
            to_near = near ^ 1 ^ (2 if bit == 1 else 0)
            to_far = far ^ (1 << (bit - 2)) if bit >= 2 else far
            pairs.append((near * fars + far, to_near * fars + to_far))
    return lax.ppermute(values, ("near", "far"), pairs)


def join_kernel(index, own_ref, rest_ref, out_ref):
    rows = own_ref.shape[0]
    place = places()[index]
    out_ref[pl.ds(pl.multiple_of(place * rows, rows), rows), :] = own_ref[...]
    out_ref[pl.ds(pl.multiple_of((1 - place) * rows, rows), rows), :] = rest_ref[...]


def chain(keep, send, index):
    even, odd = ORDERS[index - 1]

    def exchanged(values, step):
        return from_partner(values, even[step % 3], odd[step % 3])

    own = keep + exchanged(send, 0)
    own = own + exchanged(own, 1)
    own = own + exchanged(own, 2)
    rest = exchanged(own, 3)
    rows, columns = own.shape
    joined = pl.pallas_call(
        functools.partial(join_kernel, index),
        out_shape=jax.ShapeDtypeStruct((2 * rows, columns), f32),
        in_specs=[VMEM, VMEM],
        out_specs=VMEM,
        compiler_params=SMALL,
    )(own, rest)
    return joined, from_partner(joined, 0, 0)


def spans(chains, rows):
    first = 0
    for index, eighths in chains:
        yield index, first, rows * eighths // 8
        first += rows * eighths // 8


def meet_kernel(chains, keep_ref, got_ref, *outs):
    place = places()
    for k, (index, first, rows) in enumerate(spans(chains, keep_ref.shape[0])):
        low, high = pl.ds(first, rows // 2), pl.ds(first + rows // 2, rows // 2)
        stays_low = place[index] == 0
        low, high = keep_ref[low, :] + got_ref[low, :], keep_ref[high, :] + got_ref[high, :]
        outs[2 * k][...] = jnp.where(stays_low, low, high)
        outs[2 * k + 1][...] = jnp.where(stays_low, high, low)


def sum_over_cube(keep, send, chains):
    rows, columns = keep.shape
    counts = [count // 2 for _, _, count in spans(chains, rows) for _ in range(2)]
    got = pltpu.with_memory_space_constraint(from_partner(send, 0, 0), pltpu.VMEM)
    pieces = pl.pallas_call(
        functools.partial(meet_kernel, chains),
        out_shape=[jax.ShapeDtypeStruct((count, columns), f32) for count in counts],
        in_specs=[VMEM, VMEM],
        out_specs=[VMEM] * len(counts),
        compiler_params=SMALL,
    )(keep, got)
    parts = [chain(pieces[2 * k], pieces[2 * k + 1], index) for k, (index, _) in enumerate(chains)]
    return [own for own, over in parts] + [over for own, over in parts]


def placed(parts, chains, role):
    rows = sum(part.shape[0] for part in parts) // 2
    firsts = [first for _, first, _ in spans(chains, rows)]
    for i, part in enumerate(parts):
        place = role if i < len(chains) else 1 - role
        yield part, pl.ds(pl.multiple_of(place * rows + firsts[i % len(chains)], 16), part.shape[0])


def store_kernel(*refs):
    *parts, reduce_ref, expand_ref, sems = refs
    role = places()[0]
    count = 2 * len(REDUCE_CHAINS)
    moves = [(part, reduce_ref.at[rows, :]) for part, rows in placed(parts[:count], REDUCE_CHAINS, role)]
    moves += [(part, expand_ref.at[rows, :]) for part, rows in placed(parts[count:], EXPAND_CHAINS, role)]
    copies = [pltpu.make_async_copy(source, target, sems.at[i]) for i, (source, target) in enumerate(moves)]
    for copy in copies:
        copy.start()
    for copy in copies:
        copy.wait()


def store(reducing, expanding):
    columns = reducing[0].shape[1]
    parts = [*reducing, *expanding]
    return pl.pallas_call(
        store_kernel,
        out_shape=[jax.ShapeDtypeStruct((sum(part.shape[0] for part in group), columns), f32) for group in (reducing, expanding)],
        in_specs=[VMEM] * len(parts),
        out_specs=[HBM, HBM],
        scratch_shapes=[pltpu.SemaphoreType.DMA((len(parts),))],
        compiler_params=SMALL,
        name="store",
    )(*parts)


def halves(values):
    high = values.astype(bf16)
    return high, (values - high.astype(f32)).astype(bf16)


def product(left, right, contract):
    total = None
    for i, a in enumerate(left):
        for j, b in enumerate(right):
            if i + j < 2:
                term = lax.dot_general(a, b, (contract, ((), ())), preferred_element_type=f32)
                total = term if total is None else total + term
    return total


def parts_of(values):
    return (values,) if values.dtype == bf16 else halves(values)


NN = ((1,), (0,))
NT = ((1,), (1,))


def in_columns(columns):
    return [pl.ds(start, BLOCK) for start in range(0, columns, BLOCK)]


def store_by_role(role, values, *refs):
    rows = values[0].shape[0] // 2
    for part, ref in zip(values, refs):
        ref[pl.ds(pl.multiple_of(role * rows, rows), rows), :] = part[:rows]
        ref[pl.ds(pl.multiple_of((1 - role) * rows, rows), rows), :] = part[rows:]


def step_columns(role, columns, weights_ref, step, keep_ref, send_ref):
    rows = keep_ref.shape[0]
    for i, (place, ref) in enumerate(((role, keep_ref), (1 - role, send_ref))):
        old = weights_ref[pl.ds(pl.multiple_of(place * rows, rows), rows), columns].astype(f32)
        ref[:, columns] = (old - step[i * rows : (i + 1) * rows]) * (0.5**BITS)


def expand_kernel(joined, x_in, g_in, *refs):
    role = places()[0]
    *refs, hidden_high_ref, hidden_low_ref = refs
    if joined:
        r_count, e_count = 2 * len(REDUCE_CHAINS), 2 * len(EXPAND_CHAINS)
        r_parts, e_parts, outs = refs[:r_count], refs[r_count : r_count + e_count], refs[r_count + e_count :]
        keep_ref, send_ref, zh_ref, zl_ref, slope_ref, r_ref, e_ref = outs
        x_ref, g_ref = x_in, g_in
        for parts, chains, whole_ref in ((r_parts, REDUCE_CHAINS, r_ref), (e_parts, EXPAND_CHAINS, e_ref)):
            for part, rows in placed(parts, chains, role):
                whole_ref[rows, :] = part[...]
    else:
        r_in, e_in, keep_ref, send_ref, zh_ref, zl_ref, slope_ref, r_ref, e_ref, x_ref, *later, g_ref, sems = refs
        moves = []
        for columns in in_columns(x_ref.shape[1]):
            moves += [(r_in.at[:, columns], r_ref.at[:, columns]), (x_in.at[0, :, columns], x_ref.at[:, columns])]
        early = len(moves)
        moves += [(e_in, e_ref), (g_in.at[0], g_ref)]
        moves += [(source.at[1 + i // 2], ref) for i, (source, ref) in enumerate(zip((x_in, g_in) * len(later), later))]
        copies = [pltpu.make_async_copy(source, target, sems.at[i]) for i, (source, target) in enumerate(moves)]
        for copy in copies:
            copy.start()
    width = r_ref.shape[0]
    blocks = in_columns(r_ref.shape[1])
    reduce_scale = 1.0 / math.sqrt(r_ref.shape[1])
    expand_scale = 1.0 / math.sqrt(width)
    pre = None
    for i, columns in enumerate(blocks):
        if not joined:
            copies[2 * i].wait()
            copies[2 * i + 1].wait()
        term = product(parts_of(r_ref[:, columns]), (x_ref[:, columns],), NT)
        pre = term if pre is None else pre + term
    pre = pre * reduce_scale
    sig = jax.nn.sigmoid(pre)
    hidden = pre * sig
    slope_ref[...] = sig * (1.0 + pre * (1.0 - sig))
    hidden_t = halves(hidden)
    store_by_role(role, hidden_t, hidden_high_ref, hidden_low_ref)
    hidden_n = tuple(part.T for part in hidden_t)
    if not joined:
        copies[early].wait()
        copies[early + 1].wait()

    def grads_of(columns):
        summed = x_ref[:, columns].astype(f32) + product(hidden_n, parts_of(e_ref[:, columns]), NN) * expand_scale
        sig = jax.nn.sigmoid(summed)
        grads = halves(g_ref[:, columns].astype(f32) * (sig * (1.0 + summed * (1.0 - sig))))
        zh_ref[:, columns], zl_ref[:, columns] = grads
        return grads

    grads = grads_of(blocks[0])
    for i, columns in enumerate(blocks):
        ahead = grads_of(blocks[i + 1]) if i + 1 < len(blocks) else None
        step = product((hidden_high_ref[...], hidden_low_ref[...]), grads, NN) * (learn_rate * expand_scale)
        step_columns(role, columns, e_ref, step, keep_ref, send_ref)
        grads = ahead
    if not joined:
        for copy in copies[early + 2 :]:
            copy.wait()


def reduce_kernel(x_ref, r_ref, e_ref, zh_ref, zl_ref, slope_ref, keep_ref, send_ref, high_ref, low_ref):
    role = places()[0]
    blocks = in_columns(r_ref.shape[1])
    reduce_scale = 1.0 / math.sqrt(r_ref.shape[1])
    expand_scale = 1.0 / math.sqrt(r_ref.shape[0])
    grad_hidden = None
    for columns in blocks:
        term = product(parts_of(e_ref[:, columns]), (zh_ref[:, columns], zl_ref[:, columns]), NT)
        grad_hidden = term if grad_hidden is None else grad_hidden + term
    store_by_role(role, halves(grad_hidden * expand_scale * slope_ref[...]), high_ref, low_ref)
    for columns in blocks:
        step = product((high_ref[...], low_ref[...]), (x_ref[:, columns],), NN) * (learn_rate * reduce_scale)
        step_columns(role, columns, r_ref, step, keep_ref, send_ref)


def shards(w_reduce, w_expand, inputs, out_grads):
    held = [pltpu.with_memory_space_constraint(array[0, 0], pltpu.HBM) for array in (w_reduce, w_expand, inputs, out_grads)]
    reducing, expanding, inputs, out_grads = held
    iterations, rows, columns = inputs.shape
    width = reducing.shape[0]
    half = jax.ShapeDtypeStruct((width // 2, columns), f32)
    acts = jax.ShapeDtypeStruct((rows, columns), bf16)
    slopes = jax.ShapeDtypeStruct((width, rows), f32)
    hidden_parts = [pltpu.VMEM((width, rows), bf16)] * 2
    for iteration in range(iterations):
        first = iteration == 0
        weights = jax.ShapeDtypeStruct((width, columns), bf16 if first else f32)
        results = pl.pallas_call(
            functools.partial(expand_kernel, not first),
            out_shape=(half, half, acts, acts, slopes, weights, weights) + ((acts,) * (2 * iterations - 1) if first else ()),
            in_specs=[HBM] * 4 if first else [VMEM] * (2 + len(sums_r) + len(sums_e)),
            out_specs=(VMEM,) * (7 + (2 * iterations - 1 if first else 0)),
            scratch_shapes=(
                [pltpu.VMEM((rows, columns), bf16), pltpu.SemaphoreType.DMA((2 * columns // BLOCK + 2 * iterations,))] if first else []
            )
            + hidden_parts,
            compiler_params=LARGE,
        )(*((inputs, out_grads, reducing, expanding) if first else (feats[iteration], grads[iteration], *sums_r, *sums_e)))
        keep_e, send_e, zh, zl, slope, reducing, expanding = results[:7]
        if first:
            feats, grads = (results[7], *results[8::2]), (None, *results[9::2])
        keep_r, send_r = pl.pallas_call(
            reduce_kernel,
            out_shape=(half, half),
            in_specs=[VMEM] * 6,
            out_specs=(VMEM,) * 2,
            scratch_shapes=hidden_parts,
            compiler_params=LARGE,
        )(feats[iteration], reducing, expanding, zh, zl, slope)
        sums_e = sum_over_cube(keep_e, send_e, EXPAND_CHAINS)
        sums_r = sum_over_cube(keep_r, send_r, REDUCE_CHAINS)
    reducing, expanding = store(sums_r, sums_e)
    return reducing[None, None], expanding[None, None]


def solution(mesh):
    in_specs = (
        P("near", "far", None, None),
        P("near", "far", None, None),
        P("near", "far", None, None, None),
        P("near", "far", None, None, None),
    )
    out_specs = (P("near", "far", None, None), P("near", "far", None, None))
    return jax.shard_map(shards, mesh=mesh, in_specs=in_specs, out_specs=out_specs, check_vma=False)
```

time: 71.7 us -> 70.4 us (0.982)
  starting transfers between devices: 48.4 us -> 43.8 us
  waiting for transfers between devices: 11 us -> 15.1 us
  Pallas kernels: 10.9 us -> 10.1 us
    ppermute x44, starting transfers between devices: 48.4 us -> 43.8 us  [from_partner(): return lax.ppermute(values, ('near', 'far'), pairs)]
    ppermute x44, waiting for transfers between devices: 11 us -> 15.1 us  [from_partner(): return lax.ppermute(values, ('near', 'far'), pairs)]
    pallas_call x7, Pallas kernels: 7.83 us -> 6.94 us  [the longest x2 5.33 us: shards(): pl.pallas_call(functools.partial(expand_kernel, not first), out_shape=(ha...]
  transfers between devices with their start and end apart: 44 -> 44, of which waited for: 21 -> 18; matrix products, arithmetic and copies ran while one was open for 1% -> 1% of each run, Pallas kernels for 3% -> 3%
where the time goes in v4:
time: 70.4 us; the launch traced here: 70.3 us
  starting transfers between devices  43.8 us (62%)
  waiting for transfers between devices  15.1 us (21%)
  Pallas kernels  10.1 us (14%)
  between operations  0.91 us (1%)
    ppermute x44, starting transfers between devices, from_partner(): return lax.ppermute(values, ('near', 'far'), pairs)  43.8 us
    ppermute x44, waiting for transfers between devices, from_partner(): return lax.ppermute(values, ('near', 'far'), pairs)  15.1 us
    pallas_call x2, Pallas kernels, shards(): pl.pallas_call(functools.partial(expand_kernel, not first), out_shape=(ha...  5.33 us
    pallas_call x2, Pallas kernels, shards(): pl.pallas_call(reduce_kernel, out_shape=(half, half), in_specs=[VMEM] * 6...  2.92 us
  transfers between devices with their start and end apart: 44, of which 18 were waited for; matrix products, arithmetic and copies ran while one was open for 1% of the time, Pallas kernels for 3%

profile of v4, /device:TPU:0, one launch (start us, length us, event | category | flops | bytes accessed | tf_op | source)
XLA Modules:
  0.0 70.3 jit_solution(366196970456101512)
XLA Ops:
  0.6 3.2 %shard_map.59 = (f32[128,1024]{1,0:T(8,128)S(1)}, f32[128,1024]{1,0:T(8,128)S(1)}, bf16[256,1024]{1,0:T(8,128)(2,1)S(1)}, bf16[256,1024]{1,0:T(8,128)(2,1)S(1)},...) custom-call(bf16[2,256,1024]{2,1,0:T(8,128)(2,1)} %bitcast.6, ...), custom_call_target="tpu_custom_call" | custom-call | tf_op jit(solution)/shard_map/pallas_call | solution.py:278
  4.4 1.4 %shard_map.60 = (f32[128,1024]{1,0:T(8,128)S(1)}, f32[128,1024]{1,0:T(8,128)S(1)}) custom-call(bf16[256,1024]{1,0:T(8,128)(2,1)S(1)} %get-tuple-element.43.x_ref, bf16[256,1024]{1,0:T(8,128)(2,1)S(1)} %get-tuple-element.44.r_ref, bf16[256,1024]{1,0:T(8,128)(2,1)S(1)} %get-tuple-element.45.e_ref, bf16[256,1024]{1,0:T(8,128)(2,1)S(1)} %get-tuple-element.46.zh_ref, ...), custom_call_target="tpu_custom_call" | custom-call | tf_op jit(solution)/shard_map/pallas_call | solution.py:292
  6.0 2.7 %collective-permute-start.16 = (f32[32,1024]{1,0:T(8,128)S(1)}, f32[32,1024]{1,0:T(8,128)S(1)}, u32[]{:S(2)}, u32[]{:S(2)}) collective-permute-start(f32[32,1024]{1,0:T(8,128)S(1)} %get-tuple-element.60), channel_id=1, source_target_pairs={{0,10},{1,8},{2,11},{3,9},{4,14},{5,12},{6,15},{7,13},{8,1},{9,3},... | collective-permute-start | bytes 393224 | tf_op jit(solution)/shard_map/ppermute | solution.py:50
  8.7 1.5 %collective-permute-start.12 = (f32[32,1024]{1,0:T(8,128)S(1)}, f32[32,1024]{1,0:T(8,128)S(1)}, u32[]{:S(2)}, u32[]{:S(2)}) collective-permute-start(f32[32,1024]{1,0:T(8,128)S(1)} %get-tuple-element.58), channel_id=1, source_target_pairs={{0,24},{1,11},{2,8},{3,27},{4,28},{5,15},{6,12},{7,31},{8,2},{9,17... | collective-permute-start | bytes 393224 | tf_op jit(solution)/shard_map/ppermute | solution.py:50
  10.6 1.5 %collective-permute-start.1 = (f32[32,1024]{1,0:T(8,128)S(1)}, f32[32,1024]{1,0:T(8,128)S(1)}, u32[]{:S(2)}, u32[]{:S(2)}) collective-permute-start(f32[32,1024]{1,0:T(8,128)S(1)} %get-tuple-element.52), channel_id=1, source_target_pairs={{0,24},{1,8},{2,11},{3,27},{4,28},{5,12},{6,15},{7,31},{8,1},{9,17... | collective-permute-start | bytes 393224 | tf_op jit(solution)/shard_map/ppermute | solution.py:50
  12.2 2.7 %collective-permute-start.17 = (f32[32,1024]{1,0:T(8,128)S(1)}, f32[32,1024]{1,0:T(8,128)S(1)}, u32[]{:S(2)}, u32[]{:S(2)}) collective-permute-start(f32[32,1024]{1,0:T(8,128)S(1)} %add.81), channel_id=1, source_target_pairs={{0,9},{1,25},{2,26},{3,10},{4,13},{5,29},{6,30},{7,14},{8,16},{9,0... | collective-permute-start | bytes 393224 | tf_op jit(solution)/shard_map/ppermute | solution.py:50
  15.5 1.3 %collective-permute-start.6 = (f32[32,1024]{1,0:T(8,128)S(1)}, f32[32,1024]{1,0:T(8,128)S(1)}, u32[]{:S(2)}, u32[]{:S(2)}) collective-permute-start(f32[32,1024]{1,0:T(8,128)S(1)} %add.75), channel_id=1, source_target_pairs={{0,10},{1,8},{2,11},{3,9},{4,14},{5,12},{6,15},{7,13},{8,1},{9,3},... | collective-permute-start | bytes 393224 | tf_op jit(solution)/shard_map/ppermute | solution.py:50
  17.4 1.4 %collective-permute-done.17 = f32[32,1024]{1,0:T(8,128)S(1)} collective-permute-done((f32[32,1024]{1,0:T(8,128)S(1)}, f32[32,1024]{1,0:T(8,128)S(1)}, u32[]{:S(2)}, u32[]{:S(2)}) %collective-permute-start.17) | collective-permute-done | bytes 131104 | tf_op jit(solution)/shard_map/ppermute | solution.py:50
  18.8 1.0 %collective-permute-start.18 = (f32[32,1024]{1,0:T(8,128)S(1)}, f32[32,1024]{1,0:T(8,128)S(1)}, u32[]{:S(2)}, u32[]{:S(2)}) collective-permute-start(f32[32,1024]{1,0:T(8,128)S(1)} %add.82), channel_id=1, source_target_pairs={{0,24},{1,11},{2,8},{3,27},{4,28},{5,15},{6,12},{7,31},{8,2},{9,17... | collective-permute-start | bytes 393224 | tf_op jit(solution)/shard_map/ppermute | solution.py:50
  19.8 1.4 %collective-permute-start.14 = (f32[32,1024]{1,0:T(8,128)S(1)}, f32[32,1024]{1,0:T(8,128)S(1)}, u32[]{:S(2)}, u32[]{:S(2)}) collective-permute-start(f32[32,1024]{1,0:T(8,128)S(1)} %add.79), channel_id=1, source_target_pairs={{0,9},{1,25},{2,26},{3,10},{4,13},{5,29},{6,30},{7,14},{8,16},{9,0... | collective-permute-start | bytes 393224 | tf_op jit(solution)/shard_map/ppermute | solution.py:50
  21.7 1.6 %collective-permute-done.2 = f32[32,1024]{1,0:T(8,128)S(1)} collective-permute-done((f32[32,1024]{1,0:T(8,128)S(1)}, f32[32,1024]{1,0:T(8,128)S(1)}, u32[]{:S(2)}, u32[]{:S(2)}) %collective-permute-start.2) | collective-permute-done | bytes 131104 | tf_op jit(solution)/shard_map/ppermute | solution.py:50
  23.3 1.6 %collective-permute-start.3 = (f32[32,1024]{1,0:T(8,128)S(1)}, f32[32,1024]{1,0:T(8,128)S(1)}, u32[]{:S(2)}, u32[]{:S(2)}) collective-permute-start(f32[32,1024]{1,0:T(8,128)S(1)} %add.73), channel_id=1, source_target_pairs={{0,9},{1,11},{2,8},{3,10},{4,13},{5,15},{6,12},{7,14},{8,2},{9,0},... | collective-permute-start | bytes 393224 | tf_op jit(solution)/shard_map/ppermute | solution.py:50
  25.0 1.1 %collective-permute-start.19 = (f32[32,1024]{1,0:T(8,128)S(1)}, f32[32,1024]{1,0:T(8,128)S(1)}, u32[]{:S(2)}, u32[]{:S(2)}) collective-permute-start(f32[32,1024]{1,0:T(8,128)S(1)} %add.83.own_ref), channel_id=1, source_target_pairs={{0,10},{1,8},{2,11},{3,9},{4,14},{5,12},{6,15},{7,13},{8,1},{9,3},... | collective-permute-start | bytes 393224 | tf_op jit(solution)/shard_map/ppermute | solution.py:50
  26.1 1.0 %collective-permute-start.15 = (f32[32,1024]{1,0:T(8,128)S(1)}, f32[32,1024]{1,0:T(8,128)S(1)}, u32[]{:S(2)}, u32[]{:S(2)}) collective-permute-start(f32[32,1024]{1,0:T(8,128)S(1)} %add.80.own_ref), channel_id=1, source_target_pairs={{0,24},{1,11},{2,8},{3,27},{4,28},{5,15},{6,12},{7,31},{8,2},{9,17... | collective-permute-start | bytes 393224 | tf_op jit(solution)/shard_map/ppermute | solution.py:50
  28.7 2.1 %collective-permute-start.4 = (f32[32,1024]{1,0:T(8,128)S(1)}, f32[32,1024]{1,0:T(8,128)S(1)}, u32[]{:S(2)}, u32[]{:S(2)}) collective-permute-start(f32[32,1024]{1,0:T(8,128)S(1)} %add.74.own_ref), channel_id=1, source_target_pairs={{0,24},{1,8},{2,11},{3,27},{4,28},{5,12},{6,15},{7,31},{8,1},{9,17... | collective-permute-start | bytes 393224 | tf_op jit(solution)/shard_map/ppermute | solution.py:50
  32.5 1.0 %collective-permute-done.4.rest_ref = f32[32,1024]{1,0:T(8,128)S(1)} collective-permute-done((f32[32,1024]{1,0:T(8,128)S(1)}, f32[32,1024]{1,0:T(8,128)S(1)}, u32[]{:S(2)}, u32[]{:S(2)}) %collective-permute-start.4) | collective-permute-done | bytes 131104 | tf_op jit(solution)/shard_map/ppermute | solution.py:50
  33.6 1.5 %collective-permute-done.9.refs_2_ = f32[64,1024]{1,0:T(8,128)S(1)} collective-permute-done((f32[64,1024]{1,0:T(8,128)S(1)}, f32[64,1024]{1,0:T(8,128)S(1)}, u32[]{:S(2)}, u32[]{:S(2)}) %collective-permute-start.9) | collective-permute-done | bytes 262176 | tf_op jit(solution)/shard_map/ppermute | solution.py:50
  35.1 2.1 %shard_map.67 = (f32[128,1024]{1,0:T(8,128)S(1)}, f32[128,1024]{1,0:T(8,128)S(1)}, bf16[256,1024]{1,0:T(8,128)(2,1)S(1)}, bf16[256,1024]{1,0:T(8,128)(2,1)S(1)},...) custom-call(bf16[256,1024]{1,0:T(8,128)(2,1)S(1)} %get-tuple-element.41.x_in.x_ref, ...), custom_call_target="tpu_custom_call" | custom-call | tf_op jit(solution)/shard_map/pallas_call | solution.py:278
  37.2 1.5 %shard_map.68 = (f32[128,1024]{1,0:T(8,128)S(1)}, f32[128,1024]{1,0:T(8,128)S(1)}) custom-call(bf16[256,1024]{1,0:T(8,128)(2,1)S(1)} %get-tuple-element.41.x_in.x_ref, f32[256,1024]{1,0:T(8,128)S(1)} %get-tuple-element.61.r_ref, f32[256,1024]{1,0:T(8,128)S(1)} %get-tuple-element.62.e_ref, bf16[256,1024]{1,0:T(8,128)(2,1)S(1)} %get-tuple-element.63.zh_ref, ...), custom_call_target="tpu_custom_call" | custom-call | tf_op jit(solution)/shard_map/pallas_call | solution.py:292
  39.4 1.4 %collective-permute-done.22.got_ref = f32[128,1024]{1,0:T(8,128)S(1)} collective-permute-done((f32[128,1024]{1,0:T(8,128)S(1)}, f32[128,1024]{1,0:T(8,128)S(1)}, u32[]{:S(2)}, u32[]{:S(2)}) %collective-permute-start.22) | collective-permute-done | bytes 524320 | tf_op jit(solution)/shard_map/ppermute | solution.py:50
  40.8 1.8 %collective-permute-start.27 = (f32[32,1024]{1,0:T(8,128)S(1)}, f32[32,1024]{1,0:T(8,128)S(1)}, u32[]{:S(2)}, u32[]{:S(2)}) collective-permute-start(f32[32,1024]{1,0:T(8,128)S(1)} %get-tuple-element.71), channel_id=1, source_target_pairs={{0,24},{1,11},{2,8},{3,27},{4,28},{5,15},{6,12},{7,31},{8,2},{9,17... | collective-permute-start | bytes 393224 | tf_op jit(solution)/shard_map/ppermute | solution.py:50
  42.8 3.1 %collective-permute-start.38 = (f32[32,1024]{1,0:T(8,128)S(1)}, f32[32,1024]{1,0:T(8,128)S(1)}, u32[]{:S(2)}, u32[]{:S(2)}) collective-permute-start(f32[32,1024]{1,0:T(8,128)S(1)} %get-tuple-element.77), channel_id=1, source_target_pairs={{0,10},{1,8},{2,11},{3,9},{4,14},{5,12},{6,15},{7,13},{8,1},{9,3},... | collective-permute-start | bytes 393224 | tf_op jit(solution)/shard_map/ppermute | solution.py:50
  45.9 2.8 %collective-permute-start.28 = (f32[32,1024]{1,0:T(8,128)S(1)}, f32[32,1024]{1,0:T(8,128)S(1)}, u32[]{:S(2)}, u32[]{:S(2)}) collective-permute-start(f32[32,1024]{1,0:T(8,128)S(1)} %add.87), channel_id=1, source_target_pairs={{0,10},{1,8},{2,11},{3,9},{4,14},{5,12},{6,15},{7,13},{8,1},{9,3},... | collective-permute-start | bytes 393224 | tf_op jit(solution)/shard_map/ppermute | solution.py:50
  48.8 1.4 %collective-permute-start.24 = (f32[32,1024]{1,0:T(8,128)S(1)}, f32[32,1024]{1,0:T(8,128)S(1)}, u32[]{:S(2)}, u32[]{:S(2)}) collective-permute-start(f32[32,1024]{1,0:T(8,128)S(1)} %add.84), channel_id=1, source_target_pairs={{0,10},{1,25},{2,26},{3,9},{4,14},{5,29},{6,30},{7,13},{8,16},{9,3... | collective-permute-start | bytes 393224 | tf_op jit(solution)/shard_map/ppermute | solution.py:50
  52.0 1.5 %collective-permute-start.29 = (f32[32,1024]{1,0:T(8,128)S(1)}, f32[32,1024]{1,0:T(8,128)S(1)}, u32[]{:S(2)}, u32[]{:S(2)}) collective-permute-start(f32[32,1024]{1,0:T(8,128)S(1)} %add.88), channel_id=1, source_target_pairs={{0,9},{1,25},{2,26},{3,10},{4,13},{5,29},{6,30},{7,14},{8,16},{9,0... | collective-permute-start | bytes 393224 | tf_op jit(solution)/shard_map/ppermute | solution.py:50
  55.3 1.7 %collective-permute-start.36 = (f32[32,1024]{1,0:T(8,128)S(1)}, f32[32,1024]{1,0:T(8,128)S(1)}, u32[]{:S(2)}, u32[]{:S(2)}) collective-permute-start(f32[32,1024]{1,0:T(8,128)S(1)} %add.91), channel_id=1, source_target_pairs={{0,9},{1,25},{2,26},{3,10},{4,13},{5,29},{6,30},{7,14},{8,16},{9,0... | collective-permute-start | bytes 393224 | tf_op jit(solution)/shard_map/ppermute | solution.py:50
  57.4 1.0 %collective-permute-start.30 = (f32[32,1024]{1,0:T(8,128)S(1)}, f32[32,1024]{1,0:T(8,128)S(1)}, u32[]{:S(2)}, u32[]{:S(2)}) collective-permute-start(f32[32,1024]{1,0:T(8,128)S(1)} %add.89.own_ref), channel_id=1, source_target_pairs={{0,24},{1,11},{2,8},{3,27},{4,28},{5,15},{6,12},{7,31},{8,2},{9,17... | collective-permute-start | bytes 393224 | tf_op jit(solution)/shard_map/ppermute | solution.py:50
  59.4 3.0 %collective-permute-start.41 = (f32[32,1024]{1,0:T(8,128)S(1)}, f32[32,1024]{1,0:T(8,128)S(1)}, u32[]{:S(2)}, u32[]{:S(2)}) collective-permute-start(f32[32,1024]{1,0:T(8,128)S(1)} %add.95.own_ref), channel_id=1, source_target_pairs={{0,10},{1,8},{2,11},{3,9},{4,14},{5,12},{6,15},{7,13},{8,1},{9,3},... | collective-permute-start | bytes 393224 | tf_op jit(solution)/shard_map/ppermute | solution.py:50
  63.4 1.2 %collective-permute-done.26.rest_ref = f32[32,1024]{1,0:T(8,128)S(1)} collective-permute-done((f32[32,1024]{1,0:T(8,128)S(1)}, f32[32,1024]{1,0:T(8,128)S(1)}, u32[]{:S(2)}, u32[]{:S(2)}) %collective-permute-start.26) | collective-permute-done | bytes 131104 | tf_op jit(solution)/shard_map/ppermute | solution.py:50
  64.7 1.3 %collective-permute-done.41.rest_ref = f32[32,1024]{1,0:T(8,128)S(1)} collective-permute-done((f32[32,1024]{1,0:T(8,128)S(1)}, f32[32,1024]{1,0:T(8,128)S(1)}, u32[]{:S(2)}, u32[]{:S(2)}) %collective-permute-start.41) | collective-permute-done | bytes 131104 | tf_op jit(solution)/shard_map/ppermute | solution.py:50
  67.8 1.1 %collective-permute-done.42.refs_6_ = f32[64,1024]{1,0:T(8,128)S(1)} collective-permute-done((f32[64,1024]{1,0:T(8,128)S(1)}, f32[64,1024]{1,0:T(8,128)S(1)}, u32[]{:S(2)}, u32[]{:S(2)}) %collective-permute-start.42) | collective-permute-done | bytes 262176 | tf_op jit(solution)/shard_map/ppermute | solution.py:50
  68.9 1.4 %store.1 = (f32[256,1024]{1,0:T(8,128)}, f32[256,1024]{1,0:T(8,128)}) custom-call(f32[64,1024]{1,0:T(8,128)S(1)} %shard_map.70.refs_0_, f32[64,1024]{1,0:T(8,128)S(1)} %shard_map.71.refs_1_, f32[64,1024]{1,0:T(8,128)S(1)} %collective-permute-done.31.refs_2_, f32[64,1024]{1,0:T(8,128)S(1)} %collective-permute-done.32.refs_3_, ...), custom_call_target="tpu_custom_call" | custom-call | tf_op jit(solution)/shard_map/store/pallas_call | solution.py:137
  (97 shorter events, 15.1 us)
Async XLA Ops:
  6.0 6.2 %collective-permute-start.16 = (f32[32,1024]{1,0:T(8,128)S(1)}, f32[32,1024]{1,0:T(8,128)S(1)}, u32[]{:S(2)}, u32[]{:S(2)}) collective-permute-start(f32[32,1024]{1,0:T(8,128)S(1)} %get-tuple-element.60), channel_id=1, source_target_pairs={{0,10},{1,8},{2,11},{3,9},{4,14},{5,12},{6,15},{7,13},{8,1},{9,3},... | collective-permute-start | bytes 393224 | tf_op jit(solution)/shard_map/ppermute | solution.py:50
  8.7 6.1 %collective-permute-start.12 = (f32[32,1024]{1,0:T(8,128)S(1)}, f32[32,1024]{1,0:T(8,128)S(1)}, u32[]{:S(2)}, u32[]{:S(2)}) collective-permute-start(f32[32,1024]{1,0:T(8,128)S(1)} %get-tuple-element.58), channel_id=1, source_target_pairs={{0,24},{1,11},{2,8},{3,27},{4,28},{5,15},{6,12},{7,31},{8,2},{9,17... | collective-permute-start | bytes 393224 | tf_op jit(solution)/shard_map/ppermute | solution.py:50
  10.3 5.1 %collective-permute-start.5 = (f32[32,1024]{1,0:T(8,128)S(1)}, f32[32,1024]{1,0:T(8,128)S(1)}, u32[]{:S(2)}, u32[]{:S(2)}) collective-permute-start(f32[32,1024]{1,0:T(8,128)S(1)} %get-tuple-element.54), channel_id=1, source_target_pairs={{0,24},{1,11},{2,8},{3,27},{4,28},{5,15},{6,12},{7,31},{8,2},{9,17... | collective-permute-start | bytes 393224 | tf_op jit(solution)/shard_map/ppermute | solution.py:50
  10.6 6.4 %collective-permute-start.1 = (f32[32,1024]{1,0:T(8,128)S(1)}, f32[32,1024]{1,0:T(8,128)S(1)}, u32[]{:S(2)}, u32[]{:S(2)}) collective-permute-start(f32[32,1024]{1,0:T(8,128)S(1)} %get-tuple-element.52), channel_id=1, source_target_pairs={{0,24},{1,8},{2,11},{3,27},{4,28},{5,12},{6,15},{7,31},{8,1},{9,17... | collective-permute-start | bytes 393224 | tf_op jit(solution)/shard_map/ppermute | solution.py:50
  12.2 6.6 %collective-permute-start.17 = (f32[32,1024]{1,0:T(8,128)S(1)}, f32[32,1024]{1,0:T(8,128)S(1)}, u32[]{:S(2)}, u32[]{:S(2)}) collective-permute-start(f32[32,1024]{1,0:T(8,128)S(1)} %add.81), channel_id=1, source_target_pairs={{0,9},{1,25},{2,26},{3,10},{4,13},{5,29},{6,30},{7,14},{8,16},{9,0... | collective-permute-start | bytes 393224 | tf_op jit(solution)/shard_map/ppermute | solution.py:50
  14.9 4.9 %collective-permute-start.13 = (f32[32,1024]{1,0:T(8,128)S(1)}, f32[32,1024]{1,0:T(8,128)S(1)}, u32[]{:S(2)}, u32[]{:S(2)}) collective-permute-start(f32[32,1024]{1,0:T(8,128)S(1)} %add.78), channel_id=1, source_target_pairs={{0,10},{1,8},{2,11},{3,9},{4,14},{5,12},{6,15},{7,13},{8,1},{9,3},... | collective-permute-start | bytes 393224 | tf_op jit(solution)/shard_map/ppermute | solution.py:50
  15.5 5.7 %collective-permute-start.6 = (f32[32,1024]{1,0:T(8,128)S(1)}, f32[32,1024]{1,0:T(8,128)S(1)}, u32[]{:S(2)}, u32[]{:S(2)}) collective-permute-start(f32[32,1024]{1,0:T(8,128)S(1)} %add.75), channel_id=1, source_target_pairs={{0,10},{1,8},{2,11},{3,9},{4,14},{5,12},{6,15},{7,13},{8,1},{9,3},... | collective-permute-start | bytes 393224 | tf_op jit(solution)/shard_map/ppermute | solution.py:50
  17.0 6.3 %collective-permute-start.2 = (f32[32,1024]{1,0:T(8,128)S(1)}, f32[32,1024]{1,0:T(8,128)S(1)}, u32[]{:S(2)}, u32[]{:S(2)}) collective-permute-start(f32[32,1024]{1,0:T(8,128)S(1)} %add.72), channel_id=1, source_target_pairs={{0,10},{1,25},{2,26},{3,9},{4,14},{5,29},{6,30},{7,13},{8,16},{9,3... | collective-permute-start | bytes 393224 | tf_op jit(solution)/shard_map/ppermute | solution.py:50
  18.8 6.2 %collective-permute-start.18 = (f32[32,1024]{1,0:T(8,128)S(1)}, f32[32,1024]{1,0:T(8,128)S(1)}, u32[]{:S(2)}, u32[]{:S(2)}) collective-permute-start(f32[32,1024]{1,0:T(8,128)S(1)} %add.82), channel_id=1, source_target_pairs={{0,24},{1,11},{2,8},{3,27},{4,28},{5,15},{6,12},{7,31},{8,2},{9,17... | collective-permute-start | bytes 393224 | tf_op jit(solution)/shard_map/ppermute | solution.py:50
  19.8 6.3 %collective-permute-start.14 = (f32[32,1024]{1,0:T(8,128)S(1)}, f32[32,1024]{1,0:T(8,128)S(1)}, u32[]{:S(2)}, u32[]{:S(2)}) collective-permute-start(f32[32,1024]{1,0:T(8,128)S(1)} %add.79), channel_id=1, source_target_pairs={{0,9},{1,25},{2,26},{3,10},{4,13},{5,29},{6,30},{7,14},{8,16},{9,0... | collective-permute-start | bytes 393224 | tf_op jit(solution)/shard_map/ppermute | solution.py:50
  21.2 5.9 %collective-permute-start.7 = (f32[32,1024]{1,0:T(8,128)S(1)}, f32[32,1024]{1,0:T(8,128)S(1)}, u32[]{:S(2)}, u32[]{:S(2)}) collective-permute-start(f32[32,1024]{1,0:T(8,128)S(1)} %add.76), channel_id=1, source_target_pairs={{0,9},{1,25},{2,26},{3,10},{4,13},{5,29},{6,30},{7,14},{8,16},{9,0... | collective-permute-start | bytes 393224 | tf_op jit(solution)/shard_map/ppermute | solution.py:50
  23.3 5.3 %collective-permute-start.3 = (f32[32,1024]{1,0:T(8,128)S(1)}, f32[32,1024]{1,0:T(8,128)S(1)}, u32[]{:S(2)}, u32[]{:S(2)}) collective-permute-start(f32[32,1024]{1,0:T(8,128)S(1)} %add.73), channel_id=1, source_target_pairs={{0,9},{1,11},{2,8},{3,10},{4,13},{5,15},{6,12},{7,14},{8,2},{9,0},... | collective-permute-start | bytes 393224 | tf_op jit(solution)/shard_map/ppermute | solution.py:50
  25.0 5.8 %collective-permute-start.19 = (f32[32,1024]{1,0:T(8,128)S(1)}, f32[32,1024]{1,0:T(8,128)S(1)}, u32[]{:S(2)}, u32[]{:S(2)}) collective-permute-start(f32[32,1024]{1,0:T(8,128)S(1)} %add.83.own_ref), channel_id=1, source_target_pairs={{0,10},{1,8},{2,11},{3,9},{4,14},{5,12},{6,15},{7,13},{8,1},{9,3},... | collective-permute-start | bytes 393224 | tf_op jit(solution)/shard_map/ppermute | solution.py:50
  26.1 4.9 %collective-permute-start.15 = (f32[32,1024]{1,0:T(8,128)S(1)}, f32[32,1024]{1,0:T(8,128)S(1)}, u32[]{:S(2)}, u32[]{:S(2)}) collective-permute-start(f32[32,1024]{1,0:T(8,128)S(1)} %add.80.own_ref), channel_id=1, source_target_pairs={{0,24},{1,11},{2,8},{3,27},{4,28},{5,15},{6,12},{7,31},{8,2},{9,17... | collective-permute-start | bytes 393224 | tf_op jit(solution)/shard_map/ppermute | solution.py:50
  27.1 4.8 %collective-permute-start.8 = (f32[32,1024]{1,0:T(8,128)S(1)}, f32[32,1024]{1,0:T(8,128)S(1)}, u32[]{:S(2)}, u32[]{:S(2)}) collective-permute-start(f32[32,1024]{1,0:T(8,128)S(1)} %add.77.own_ref), channel_id=1, source_target_pairs={{0,24},{1,11},{2,8},{3,27},{4,28},{5,15},{6,12},{7,31},{8,2},{9,17... | collective-permute-start | bytes 393224 | tf_op jit(solution)/shard_map/ppermute | solution.py:50
  28.7 4.8 %collective-permute-start.4 = (f32[32,1024]{1,0:T(8,128)S(1)}, f32[32,1024]{1,0:T(8,128)S(1)}, u32[]{:S(2)}, u32[]{:S(2)}) collective-permute-start(f32[32,1024]{1,0:T(8,128)S(1)} %add.74.own_ref), channel_id=1, source_target_pairs={{0,24},{1,8},{2,11},{3,27},{4,28},{5,12},{6,15},{7,31},{8,1},{9,17... | collective-permute-start | bytes 393224 | tf_op jit(solution)/shard_map/ppermute | solution.py:50
  40.8 5.1 %collective-permute-start.27 = (f32[32,1024]{1,0:T(8,128)S(1)}, f32[32,1024]{1,0:T(8,128)S(1)}, u32[]{:S(2)}, u32[]{:S(2)}) collective-permute-start(f32[32,1024]{1,0:T(8,128)S(1)} %get-tuple-element.71), channel_id=1, source_target_pairs={{0,24},{1,11},{2,8},{3,27},{4,28},{5,15},{6,12},{7,31},{8,2},{9,17... | collective-permute-start | bytes 393224 | tf_op jit(solution)/shard_map/ppermute | solution.py:50
  42.6 6.1 %collective-permute-start.23 = (f32[32,1024]{1,0:T(8,128)S(1)}, f32[32,1024]{1,0:T(8,128)S(1)}, u32[]{:S(2)}, u32[]{:S(2)}) collective-permute-start(f32[32,1024]{1,0:T(8,128)S(1)} %get-tuple-element.69), channel_id=1, source_target_pairs={{0,24},{1,8},{2,11},{3,27},{4,28},{5,12},{6,15},{7,31},{8,1},{9,17... | collective-permute-start | bytes 393224 | tf_op jit(solution)/shard_map/ppermute | solution.py:50
  42.8 7.4 %collective-permute-start.38 = (f32[32,1024]{1,0:T(8,128)S(1)}, f32[32,1024]{1,0:T(8,128)S(1)}, u32[]{:S(2)}, u32[]{:S(2)}) collective-permute-start(f32[32,1024]{1,0:T(8,128)S(1)} %get-tuple-element.77), channel_id=1, source_target_pairs={{0,10},{1,8},{2,11},{3,9},{4,14},{5,12},{6,15},{7,13},{8,1},{9,3},... | collective-permute-start | bytes 393224 | tf_op jit(solution)/shard_map/ppermute | solution.py:50
  45.8 4.8 %collective-permute-start.34 = (f32[32,1024]{1,0:T(8,128)S(1)}, f32[32,1024]{1,0:T(8,128)S(1)}, u32[]{:S(2)}, u32[]{:S(2)}) collective-permute-start(f32[32,1024]{1,0:T(8,128)S(1)} %get-tuple-element.75), channel_id=1, source_target_pairs={{0,24},{1,11},{2,8},{3,27},{4,28},{5,15},{6,12},{7,31},{8,2},{9,17... | collective-permute-start | bytes 393224 | tf_op jit(solution)/shard_map/ppermute | solution.py:50
  45.9 6.0 %collective-permute-start.28 = (f32[32,1024]{1,0:T(8,128)S(1)}, f32[32,1024]{1,0:T(8,128)S(1)}, u32[]{:S(2)}, u32[]{:S(2)}) collective-permute-start(f32[32,1024]{1,0:T(8,128)S(1)} %add.87), channel_id=1, source_target_pairs={{0,10},{1,8},{2,11},{3,9},{4,14},{5,12},{6,15},{7,13},{8,1},{9,3},... | collective-permute-start | bytes 393224 | tf_op jit(solution)/shard_map/ppermute | solution.py:50
  48.8 4.7 %collective-permute-start.24 = (f32[32,1024]{1,0:T(8,128)S(1)}, f32[32,1024]{1,0:T(8,128)S(1)}, u32[]{:S(2)}, u32[]{:S(2)}) collective-permute-start(f32[32,1024]{1,0:T(8,128)S(1)} %add.84), channel_id=1, source_target_pairs={{0,10},{1,25},{2,26},{3,9},{4,14},{5,29},{6,30},{7,13},{8,16},{9,3... | collective-permute-start | bytes 393224 | tf_op jit(solution)/shard_map/ppermute | solution.py:50
  50.2 4.6 %collective-permute-start.39 = (f32[32,1024]{1,0:T(8,128)S(1)}, f32[32,1024]{1,0:T(8,128)S(1)}, u32[]{:S(2)}, u32[]{:S(2)}) collective-permute-start(f32[32,1024]{1,0:T(8,128)S(1)} %add.93), channel_id=1, source_target_pairs={{0,9},{1,25},{2,26},{3,10},{4,13},{5,29},{6,30},{7,14},{8,16},{9,0... | collective-permute-start | bytes 393224 | tf_op jit(solution)/shard_map/ppermute | solution.py:50
  50.7 4.6 %collective-permute-start.35 = (f32[32,1024]{1,0:T(8,128)S(1)}, f32[32,1024]{1,0:T(8,128)S(1)}, u32[]{:S(2)}, u32[]{:S(2)}) collective-permute-start(f32[32,1024]{1,0:T(8,128)S(1)} %add.90), channel_id=1, source_target_pairs={{0,10},{1,8},{2,11},{3,9},{4,14},{5,12},{6,15},{7,13},{8,1},{9,3},... | collective-permute-start | bytes 393224 | tf_op jit(solution)/shard_map/ppermute | solution.py:50
  52.0 5.5 %collective-permute-start.29 = (f32[32,1024]{1,0:T(8,128)S(1)}, f32[32,1024]{1,0:T(8,128)S(1)}, u32[]{:S(2)}, u32[]{:S(2)}) collective-permute-start(f32[32,1024]{1,0:T(8,128)S(1)} %add.88), channel_id=1, source_target_pairs={{0,9},{1,25},{2,26},{3,10},{4,13},{5,29},{6,30},{7,14},{8,16},{9,0... | collective-permute-start | bytes 393224 | tf_op jit(solution)/shard_map/ppermute | solution.py:50
  53.5 5.3 %collective-permute-start.25 = (f32[32,1024]{1,0:T(8,128)S(1)}, f32[32,1024]{1,0:T(8,128)S(1)}, u32[]{:S(2)}, u32[]{:S(2)}) collective-permute-start(f32[32,1024]{1,0:T(8,128)S(1)} %add.85), channel_id=1, source_target_pairs={{0,9},{1,11},{2,8},{3,10},{4,13},{5,15},{6,12},{7,14},{8,2},{9,0},... | collective-permute-start | bytes 393224 | tf_op jit(solution)/shard_map/ppermute | solution.py:50
  54.8 4.6 %collective-permute-start.40 = (f32[32,1024]{1,0:T(8,128)S(1)}, f32[32,1024]{1,0:T(8,128)S(1)}, u32[]{:S(2)}, u32[]{:S(2)}) collective-permute-start(f32[32,1024]{1,0:T(8,128)S(1)} %add.94), channel_id=1, source_target_pairs={{0,24},{1,11},{2,8},{3,27},{4,28},{5,15},{6,12},{7,31},{8,2},{9,17... | collective-permute-start | bytes 393224 | tf_op jit(solution)/shard_map/ppermute | solution.py:50
  55.3 7.0 %collective-permute-start.36 = (f32[32,1024]{1,0:T(8,128)S(1)}, f32[32,1024]{1,0:T(8,128)S(1)}, u32[]{:S(2)}, u32[]{:S(2)}) collective-permute-start(f32[32,1024]{1,0:T(8,128)S(1)} %add.91), channel_id=1, source_target_pairs={{0,9},{1,25},{2,26},{3,10},{4,13},{5,29},{6,30},{7,14},{8,16},{9,0... | collective-permute-start | bytes 393224 | tf_op jit(solution)/shard_map/ppermute | solution.py:50
  57.4 5.7 %collective-permute-start.30 = (f32[32,1024]{1,0:T(8,128)S(1)}, f32[32,1024]{1,0:T(8,128)S(1)}, u32[]{:S(2)}, u32[]{:S(2)}) collective-permute-start(f32[32,1024]{1,0:T(8,128)S(1)} %add.89.own_ref), channel_id=1, source_target_pairs={{0,24},{1,11},{2,8},{3,27},{4,28},{5,15},{6,12},{7,31},{8,2},{9,17... | collective-permute-start | bytes 393224 | tf_op jit(solution)/shard_map/ppermute | solution.py:50
  58.8 5.7 %collective-permute-start.26 = (f32[32,1024]{1,0:T(8,128)S(1)}, f32[32,1024]{1,0:T(8,128)S(1)}, u32[]{:S(2)}, u32[]{:S(2)}) collective-permute-start(f32[32,1024]{1,0:T(8,128)S(1)} %add.86.own_ref), channel_id=1, source_target_pairs={{0,24},{1,8},{2,11},{3,27},{4,28},{5,12},{6,15},{7,31},{8,1},{9,17... | collective-permute-start | bytes 393224 | tf_op jit(solution)/shard_map/ppermute | solution.py:50
  59.4 6.7 %collective-permute-start.41 = (f32[32,1024]{1,0:T(8,128)S(1)}, f32[32,1024]{1,0:T(8,128)S(1)}, u32[]{:S(2)}, u32[]{:S(2)}) collective-permute-start(f32[32,1024]{1,0:T(8,128)S(1)} %add.95.own_ref), channel_id=1, source_target_pairs={{0,10},{1,8},{2,11},{3,9},{4,14},{5,12},{6,15},{7,13},{8,1},{9,3},... | collective-permute-start | bytes 393224 | tf_op jit(solution)/shard_map/ppermute | solution.py:50
  63.2 4.5 %collective-permute-start.32 = (f32[64,1024]{1,0:T(8,128)S(1)}, f32[64,1024]{1,0:T(8,128)S(1)}, u32[]{:S(2)}, u32[]{:S(2)}) collective-permute-start(f32[64,1024]{1,0:T(8,128)S(1)} %shard_map.71.refs_1_), channel_id=1, source_target_pairs={{0,8},{1,9},{2,10},{3,11},{4,12},{5,13},{6,14},{7,15},{8,0},{9,1},... | collective-permute-start | bytes 786440 | tf_op jit(solution)/shard_map/ppermute | solution.py:50
  (12 other events, 32.2 us)

commit v5 on v4

v5 whole, which is shorter than its diff:
```python
import functools
import math

import jax
import jax.numpy as jnp
from jax import lax
from jax.experimental import pallas as pl
from jax.experimental.pallas import tpu as pltpu
from jax.sharding import PartitionSpec as P


learn_rate = 1.0

ORDERS = (
    ((1, 3, 2), (3, 2, 1)),
    ((3, 2, 1), (2, 1, 3)),
    ((1, 3, 2), (2, 1, 3)),
    ((1, 3, 2), (3, 2, 1)),
)
REDUCE_CHAINS = ((1, 4), (2, 4))
EXPAND_CHAINS = ((3, 4), (4, 4))
BITS = 4
BLOCK = 256
VMEM = pl.BlockSpec(memory_space=pltpu.VMEM)
HBM = pl.BlockSpec(memory_space=pltpu.HBM)
SMALL = pltpu.CompilerParams(vmem_limit_bytes=2**20)
LARGE = pltpu.CompilerParams(vmem_limit_bytes=12 * 2**20)
f32, bf16 = jnp.float32, jnp.bfloat16


def bits_of(near, far):
    chip = ((near >> 1) & 1, far & 1, (far >> 1) & 1)
    return ((near & 1) ^ chip[0] ^ chip[1] ^ chip[2],) + chip


def places():
    bits = bits_of(lax.axis_index("near"), lax.axis_index("far"))
    return [bits[0]] + [jnp.where(bits[0] == 0, bits[even[0]], bits[odd[0]]) for even, odd in ORDERS]


def from_partner(values, *bit_of_role):
    nears, fars = lax.axis_size("near"), lax.axis_size("far")
    pairs = []
    for near in range(nears):
        for far in range(fars):
            bit = bit_of_role[bits_of(near, far)[0]]
            to_near = near ^ 1 ^ (2 if bit == 1 else 0)
            to_far = far ^ (1 << (bit - 2)) if bit >= 2 else far
            pairs.append((near * fars + far, to_near * fars + to_far))
    return lax.ppermute(values, ("near", "far"), pairs)


def join_kernel(index, own_ref, rest_ref, out_ref):
    rows = own_ref.shape[0]
    place = places()[index]
    out_ref[pl.ds(pl.multiple_of(place * rows, rows), rows), :] = own_ref[...]
    out_ref[pl.ds(pl.multiple_of((1 - place) * rows, rows), rows), :] = rest_ref[...]


def chain(keep, send, index):
    even, odd = ORDERS[index - 1]

    def exchanged(values, step):
        return from_partner(values, even[step % 3], odd[step % 3])

    own = keep + exchanged(send, 0)
    own = own + exchanged(own, 1)
    own = own + exchanged(own, 2)
    rest = exchanged(own, 3)
    rows, columns = own.shape
    joined = pl.pallas_call(
        functools.partial(join_kernel, index),
        out_shape=jax.ShapeDtypeStruct((2 * rows, columns), f32),
        in_specs=[VMEM, VMEM],
        out_specs=VMEM,
        compiler_params=SMALL,
    )(own, rest)
    return joined, from_partner(joined, 0, 0)


def spans(chains, rows):
    first = 0
    for index, eighths in chains:
        yield index, first, rows * eighths // 8
        first += rows * eighths // 8


def meet_kernel(chains, keep_ref, got_ref, *outs):
    place = places()
    for k, (index, first, rows) in enumerate(spans(chains, keep_ref.shape[0])):
        low, high = pl.ds(first, rows // 2), pl.ds(first + rows // 2, rows // 2)
        stays_low = place[index] == 0
        low, high = keep_ref[low, :] + got_ref[low, :], keep_ref[high, :] + got_ref[high, :]
        outs[2 * k][...] = jnp.where(stays_low, low, high)
        outs[2 * k + 1][...] = jnp.where(stays_low, high, low)


def sum_over_cube(keep, send, chains):
    rows, columns = keep.shape
    counts = [count // 2 for _, _, count in spans(chains, rows) for _ in range(2)]
    got = pltpu.with_memory_space_constraint(from_partner(send, 0, 0), pltpu.VMEM)
    pieces = pl.pallas_call(
        functools.partial(meet_kernel, chains),
        out_shape=[jax.ShapeDtypeStruct((count, columns), f32) for count in counts],
        in_specs=[VMEM, VMEM],
        out_specs=[VMEM] * len(counts),
        compiler_params=SMALL,
    )(keep, got)
    parts = [chain(pieces[2 * k], pieces[2 * k + 1], index) for k, (index, _) in enumerate(chains)]
    return [own for own, over in parts] + [over for own, over in parts]


def placed(parts, chains, role):
    rows = sum(part.shape[0] for part in parts) // 2
    firsts = [first for _, first, _ in spans(chains, rows)]
    for i, part in enumerate(parts):
        place = role if i < len(chains) else 1 - role
        yield part, pl.ds(pl.multiple_of(place * rows + firsts[i % len(chains)], 16), part.shape[0])


def store_kernel(chains, *refs):
    *parts, out_ref, sems = refs
    moves = [(part, out_ref.at[rows, :]) for part, rows in placed(parts, chains, places()[0])]
    copies = [pltpu.make_async_copy(source, target, sems.at[i]) for i, (source, target) in enumerate(moves)]
    for copy in copies:
        copy.start()
    for copy in copies:
        copy.wait()


def store(parts, chains):
    return pl.pallas_call(
        functools.partial(store_kernel, chains),
        out_shape=jax.ShapeDtypeStruct((sum(part.shape[0] for part in parts), parts[0].shape[1]), f32),
        in_specs=[VMEM] * len(parts),
        out_specs=HBM,
        scratch_shapes=[pltpu.SemaphoreType.DMA((len(parts),))],
        compiler_params=SMALL,
    )(*parts)


def halves(values):
    high = values.astype(bf16)
    return high, (values - high.astype(f32)).astype(bf16)


def product(left, right, contract):
    total = None
    for i, a in enumerate(left):
        for j, b in enumerate(right):
            if i + j < 2:
                term = lax.dot_general(a, b, (contract, ((), ())), preferred_element_type=f32)
                total = term if total is None else total + term
    return total


def parts_of(values):
    return (values,) if values.dtype == bf16 else halves(values)


NN = ((1,), (0,))
NT = ((1,), (1,))


def in_columns(columns):
    return [pl.ds(start, BLOCK) for start in range(0, columns, BLOCK)]


def store_by_role(role, values, *refs):
    rows = values[0].shape[0] // 2
    for part, ref in zip(values, refs):
        ref[pl.ds(pl.multiple_of(role * rows, rows), rows), :] = part[:rows]
        ref[pl.ds(pl.multiple_of((1 - role) * rows, rows), rows), :] = part[rows:]


def step_columns(role, columns, weights_ref, step, keep_ref, send_ref):
    rows = keep_ref.shape[0]
    for i, (place, ref) in enumerate(((role, keep_ref), (1 - role, send_ref))):
        old = weights_ref[pl.ds(pl.multiple_of(place * rows, rows), rows), columns].astype(f32)
        ref[:, columns] = (old - step[i * rows : (i + 1) * rows]) * (0.5**BITS)


def put_together(parts, chains, whole_ref):
    for part, rows in placed(parts, chains, places()[0]):
        whole_ref[rows, :] = part[...]


def start_copies(moves, sems):
    copies = [pltpu.make_async_copy(source, target, sems.at[i]) for i, (source, target) in enumerate(moves)]
    for copy in copies:
        copy.start()
    return copies


def hidden_of(r_ref, x_ref, outs, arrived):
    slope_ref, high_t_ref, low_t_ref, high_ref, low_ref = outs
    pre = None
    for i, columns in enumerate(in_columns(r_ref.shape[1])):
        arrived(i)
        term = product(parts_of(r_ref[:, columns]), (x_ref[:, columns],), NT)
        pre = term if pre is None else pre + term
    pre = pre * (1.0 / math.sqrt(r_ref.shape[1]))
    sig = jax.nn.sigmoid(pre)
    slope_ref[...] = sig * (1.0 + pre * (1.0 - sig))
    hidden = halves(pre * sig)
    store_by_role(places()[0], hidden, high_t_ref, low_t_ref)
    high_ref[...], low_ref[...] = (part.T for part in hidden)


def first_hidden_kernel(x_in, g_in, r_in, e_in, *refs):
    outs, (r_ref, e_ref), acts_refs, sems = refs[:5], refs[5:7], refs[7:-1], refs[-1]
    moves = []
    for columns in in_columns(r_ref.shape[1]):
        moves += [(r_in.at[:, columns], r_ref.at[:, columns]), (x_in.at[0, :, columns], acts_refs[0].at[:, columns])]
    early = len(moves)
    later = [(source.at[i // 2], ref) for i, (source, ref) in enumerate(zip((x_in, g_in) * len(acts_refs), acts_refs))]
    copies = start_copies(moves + [(e_in, e_ref)] + later[1:], sems)

    def arrived(i):
        copies[2 * i].wait()
        copies[2 * i + 1].wait()

    hidden_of(r_ref, acts_refs[0], outs, arrived)
    for copy in copies[early:]:
        copy.wait()


def hidden_kernel(x_ref, *refs):
    count = 2 * len(REDUCE_CHAINS)
    parts, outs, r_ref = refs[:count], refs[count:-1], refs[-1]
    put_together(parts, REDUCE_CHAINS, r_ref)
    hidden_of(r_ref, x_ref, outs, lambda i: None)


def reduce_kernel(joined, x_ref, g_ref, r_ref, slope_ref, hidden_high_ref, hidden_low_ref, *refs):
    if joined:
        *parts, keep_ref, send_ref, zh_ref, zl_ref, e_ref, high_ref, low_ref = refs
        put_together(parts, EXPAND_CHAINS, e_ref)
    else:
        e_ref, keep_ref, send_ref, zh_ref, zl_ref, high_ref, low_ref = refs
    role = places()[0]
    blocks = in_columns(r_ref.shape[1])
    reduce_scale = 1.0 / math.sqrt(r_ref.shape[1])
    expand_scale = 1.0 / math.sqrt(r_ref.shape[0])
    hidden = hidden_high_ref[...], hidden_low_ref[...]

    def grads_of(columns):
        weights = parts_of(e_ref[:, columns])
        summed = x_ref[:, columns].astype(f32) + product(hidden, weights, NN) * expand_scale
        sig = jax.nn.sigmoid(summed)
        grads = halves(g_ref[:, columns].astype(f32) * (sig * (1.0 + summed * (1.0 - sig))))
        zh_ref[:, columns], zl_ref[:, columns] = grads
        return weights, grads

    grad_hidden = None
    upcoming = grads_of(blocks[0])
    for i in range(len(blocks)):
        weights, grads = upcoming
        upcoming = grads_of(blocks[i + 1]) if i + 1 < len(blocks) else None
        term = product(weights, grads, NT)
        grad_hidden = term if grad_hidden is None else grad_hidden + term
    store_by_role(role, halves(grad_hidden * expand_scale * slope_ref[...]), high_ref, low_ref)
    for columns in blocks:
        step = product((high_ref[...], low_ref[...]), (x_ref[:, columns],), NN) * (learn_rate * reduce_scale)
        step_columns(role, columns, r_ref, step, keep_ref, send_ref)


def expand_kernel(e_ref, zh_ref, zl_ref, hidden_high_ref, hidden_low_ref, keep_ref, send_ref):
    role = places()[0]
    expand_scale = 1.0 / math.sqrt(e_ref.shape[0])
    for columns in in_columns(e_ref.shape[1]):
        grads = zh_ref[:, columns], zl_ref[:, columns]
        step = product((hidden_high_ref[...], hidden_low_ref[...]), grads, NN) * (learn_rate * expand_scale)
        step_columns(role, columns, e_ref, step, keep_ref, send_ref)


def shards(w_reduce, w_expand, inputs, out_grads):
    held = [pltpu.with_memory_space_constraint(array[0, 0], pltpu.HBM) for array in (inputs, out_grads, w_reduce, w_expand)]
    iterations, rows, columns = inputs.shape[2:]
    width = w_reduce.shape[2]
    half = jax.ShapeDtypeStruct((width // 2, columns), f32)
    acts = jax.ShapeDtypeStruct((rows, columns), bf16)
    hidden_shapes = (
        [jax.ShapeDtypeStruct((width, rows), f32)]
        + [jax.ShapeDtypeStruct((width, rows), bf16)] * 2
        + [jax.ShapeDtypeStruct((rows, width), bf16)] * 2
    )
    weights = jax.ShapeDtypeStruct((width, columns), f32)
    narrow = jax.ShapeDtypeStruct((width, columns), bf16)
    results = pl.pallas_call(
        first_hidden_kernel,
        out_shape=hidden_shapes + [narrow] * 2 + [acts] * (2 * iterations),
        in_specs=[HBM] * 4,
        out_specs=[VMEM] * (7 + 2 * iterations),
        scratch_shapes=[pltpu.SemaphoreType.DMA((2 * columns // BLOCK + 2 * iterations,))],
        compiler_params=LARGE,
        name="hidden_0",
    )(*held)
    hidden, (reducing, expanding), acts_of = results[:5], results[5:7], results[7:]
    for iteration in range(iterations):
        first, last = iteration == 0, iteration == iterations - 1
        feats, grads = acts_of[2 * iteration : 2 * iteration + 2]
        slope, high_t, low_t, high, low = hidden
        keep_r, send_r, zh, zl, *joined = pl.pallas_call(
            functools.partial(reduce_kernel, not first),
            out_shape=[half, half, acts, acts] + ([] if first else [weights]),
            in_specs=[VMEM] * (7 if first else 6 + len(expanding)),
            out_specs=[VMEM] * (4 if first else 5),
            scratch_shapes=[pltpu.VMEM((width, rows), bf16)] * 2,
            compiler_params=LARGE,
        )(feats, grads, reducing, slope, high, low, *([expanding] if first else expanding))
        keep_e, send_e = pl.pallas_call(
            expand_kernel, out_shape=[half, half], in_specs=[VMEM] * 5, out_specs=[VMEM] * 2, compiler_params=LARGE
        )(expanding if first else joined[0], zh, zl, high_t, low_t)
        sums_r = sum_over_cube(keep_r, send_r, REDUCE_CHAINS)
        expanding = sum_over_cube(keep_e, send_e, EXPAND_CHAINS)
        if last:
            new_reduce = store(sums_r, REDUCE_CHAINS)
        else:
            *hidden, reducing = pl.pallas_call(
                hidden_kernel,
                out_shape=hidden_shapes + [weights],
                in_specs=[VMEM] * (1 + len(sums_r)),
                out_specs=[VMEM] * 6,
                compiler_params=LARGE,
            )(acts_of[2 * iteration + 2], *sums_r)
    return new_reduce[None, None], store(expanding, EXPAND_CHAINS)[None, None]


def solution(mesh):
    in_specs = (
        P("near", "far", None, None),
        P("near", "far", None, None),
        P("near", "far", None, None, None),
        P("near", "far", None, None, None),
    )
    out_specs = (P("near", "far", None, None), P("near", "far", None, None))
    return jax.shard_map(shards, mesh=mesh, in_specs=in_specs, out_specs=out_specs, check_vma=False)
```

time: 70.4 us -> 71.2 us (1.011)
  waiting for transfers between devices: 15.1 us -> 17.4 us
  starting transfers between devices: 43.8 us -> 42.2 us
    ppermute x44, waiting for transfers between devices: 15.1 us -> 17.4 us  [from_partner(): return lax.ppermute(values, ('near', 'far'), pairs)]
    ppermute x44, starting transfers between devices: 43.8 us -> 42.2 us  [from_partner(): return lax.ppermute(values, ('near', 'far'), pairs)]
    pallas_call x5 -> x8, Pallas kernels: 9.62 us -> 9.53 us  [the longest x2 3.69 us: shards(): pl.pallas_call(functools.partial(reduce_kernel, not first), out_shape=[ha...]
  transfers between devices with their start and end apart: 44 -> 44, of which waited for: 18 -> 18; matrix products, arithmetic and copies ran while one was open for 1% -> 1% of each run, Pallas kernels for 3% -> 5%
where the time goes in v5:
time: 71.2 us; the launch traced here: 71 us
  starting transfers between devices  42.2 us (59%)
  waiting for transfers between devices  17.4 us (24%)
  Pallas kernels  10 us (14%)
  between operations  0.99 us (1%)
    ppermute x44, starting transfers between devices, from_partner(): return lax.ppermute(values, ('near', 'far'), pairs)  42.2 us
    ppermute x44, waiting for transfers between devices, from_partner(): return lax.ppermute(values, ('near', 'far'), pairs)  17.4 us
    pallas_call x2, Pallas kernels, shards(): pl.pallas_call(functools.partial(reduce_kernel, not first), out_shape=[ha...  3.69 us
    pallas_call x1, Pallas kernels, shards(): pl.pallas_call(first_hidden_kernel, out_shape=hidden_shapes + [narrow] *...  2.06 us
    pallas_call x2, Pallas kernels, store(): pl.pallas_call(functools.partial(store_kernel, chains), out_shape=jax.Sha...  2 us
  transfers between devices with their start and end apart: 44, of which 18 were waited for; matrix products, arithmetic and copies ran while one was open for 1% of the time, Pallas kernels for 5%

profile of v5, /device:TPU:0, one launch (start us, length us, event | category | flops | bytes accessed | tf_op | source)
XLA Modules:
  0.0 71.0 jit_solution(5970420820390399077)
XLA Ops:
  0.6 2.1 %hidden_0.1 = (f32[256,256]{1,0:T(8,128)S(1)}, bf16[256,256]{1,0:T(8,128)(2,1)S(1)}, bf16[256,256]{1,0:T(8,128)(2,1)S(1)}, bf16[256,256]{1,0:T(8,128)(2,1)S(1)},...) custom-call(bf16[2,256,1024]{2,1,0:T(8,128)(2,1)} %bitcast.6, ...), custom_call_target="tpu_custom_call" | custom-call | tf_op jit(solution)/shard_map/hidden_0/pallas_call | solution.py:290
  2.7 1.7 %shard_map.59 = (f32[128,1024]{1,0:T(8,128)S(1)}, f32[128,1024]{1,0:T(8,128)S(1)}, bf16[256,1024]{1,0:T(8,128)(2,1)S(1)}, bf16[256,1024]{1,0:T(8,128)(2,1)S(1)}) custom-call(bf16[256,1024]{1,0:T(8,128)(2,1)S(1)} %get-tuple-element.50.x_ref, bf16[256,1024]{1,0:T(8,128)(2,1)S(1)} %get-tuple-element.51.g_ref, bf16[256,1024]{1,0:T(8,128)(2,1)S(1)} %get-tuple-element.52.r_ref, ...), custom_call_target="tpu_custom_call" | custom-call | tf_op jit(solution)/shard_map/pallas_call | solution.py:304
  6.5 2.7 %collective-permute-start.5 = (f32[32,1024]{1,0:T(8,128)S(1)}, f32[32,1024]{1,0:T(8,128)S(1)}, u32[]{:S(2)}, u32[]{:S(2)}) collective-permute-start(f32[32,1024]{1,0:T(8,128)S(1)} %get-tuple-element.62), channel_id=1, source_target_pairs={{0,10},{1,8},{2,11},{3,9},{4,14},{5,12},{6,15},{7,13},{8,1},{9,3},... | collective-permute-start | bytes 393224 | tf_op jit(solution)/shard_map/ppermute | solution.py:50
  9.3 1.5 %collective-permute-start.1 = (f32[32,1024]{1,0:T(8,128)S(1)}, f32[32,1024]{1,0:T(8,128)S(1)}, u32[]{:S(2)}, u32[]{:S(2)}) collective-permute-start(f32[32,1024]{1,0:T(8,128)S(1)} %get-tuple-element.60), channel_id=1, source_target_pairs={{0,24},{1,11},{2,8},{3,27},{4,28},{5,15},{6,12},{7,31},{8,2},{9,17... | collective-permute-start | bytes 393224 | tf_op jit(solution)/shard_map/ppermute | solution.py:50
  11.1 1.5 %collective-permute-start.12 = (f32[32,1024]{1,0:T(8,128)S(1)}, f32[32,1024]{1,0:T(8,128)S(1)}, u32[]{:S(2)}, u32[]{:S(2)}) collective-permute-start(f32[32,1024]{1,0:T(8,128)S(1)} %get-tuple-element.74), channel_id=1, source_target_pairs={{0,24},{1,8},{2,11},{3,27},{4,28},{5,12},{6,15},{7,31},{8,1},{9,17... | collective-permute-start | bytes 393224 | tf_op jit(solution)/shard_map/ppermute | solution.py:50
  12.6 2.7 %collective-permute-start.6 = (f32[32,1024]{1,0:T(8,128)S(1)}, f32[32,1024]{1,0:T(8,128)S(1)}, u32[]{:S(2)}, u32[]{:S(2)}) collective-permute-start(f32[32,1024]{1,0:T(8,128)S(1)} %add.75), channel_id=1, source_target_pairs={{0,9},{1,25},{2,26},{3,10},{4,13},{5,29},{6,30},{7,14},{8,16},{9,0... | collective-permute-start | bytes 393224 | tf_op jit(solution)/shard_map/ppermute | solution.py:50
  15.9 1.4 %collective-permute-start.17 = (f32[32,1024]{1,0:T(8,128)S(1)}, f32[32,1024]{1,0:T(8,128)S(1)}, u32[]{:S(2)}, u32[]{:S(2)}) collective-permute-start(f32[32,1024]{1,0:T(8,128)S(1)} %add.81), channel_id=1, source_target_pairs={{0,10},{1,8},{2,11},{3,9},{4,14},{5,12},{6,15},{7,13},{8,1},{9,3},... | collective-permute-start | bytes 393224 | tf_op jit(solution)/shard_map/ppermute | solution.py:50
  17.8 1.4 %collective-permute-done.6 = f32[32,1024]{1,0:T(8,128)S(1)} collective-permute-done((f32[32,1024]{1,0:T(8,128)S(1)}, f32[32,1024]{1,0:T(8,128)S(1)}, u32[]{:S(2)}, u32[]{:S(2)}) %collective-permute-start.6) | collective-permute-done | bytes 131104 | tf_op jit(solution)/shard_map/ppermute | solution.py:50
  20.3 1.4 %collective-permute-start.3 = (f32[32,1024]{1,0:T(8,128)S(1)}, f32[32,1024]{1,0:T(8,128)S(1)}, u32[]{:S(2)}, u32[]{:S(2)}) collective-permute-start(f32[32,1024]{1,0:T(8,128)S(1)} %add.73), channel_id=1, source_target_pairs={{0,9},{1,25},{2,26},{3,10},{4,13},{5,29},{6,30},{7,14},{8,16},{9,0... | collective-permute-start | bytes 393224 | tf_op jit(solution)/shard_map/ppermute | solution.py:50
  22.2 1.6 %collective-permute-done.13 = f32[32,1024]{1,0:T(8,128)S(1)} collective-permute-done((f32[32,1024]{1,0:T(8,128)S(1)}, f32[32,1024]{1,0:T(8,128)S(1)}, u32[]{:S(2)}, u32[]{:S(2)}) %collective-permute-start.13) | collective-permute-done | bytes 131104 | tf_op jit(solution)/shard_map/ppermute | solution.py:50
  23.9 1.6 %collective-permute-start.14 = (f32[32,1024]{1,0:T(8,128)S(1)}, f32[32,1024]{1,0:T(8,128)S(1)}, u32[]{:S(2)}, u32[]{:S(2)}) collective-permute-start(f32[32,1024]{1,0:T(8,128)S(1)} %add.79), channel_id=1, source_target_pairs={{0,9},{1,11},{2,8},{3,10},{4,13},{5,15},{6,12},{7,14},{8,2},{9,0},... | collective-permute-start | bytes 393224 | tf_op jit(solution)/shard_map/ppermute | solution.py:50
  25.4 1.1 %collective-permute-start.8 = (f32[32,1024]{1,0:T(8,128)S(1)}, f32[32,1024]{1,0:T(8,128)S(1)}, u32[]{:S(2)}, u32[]{:S(2)}) collective-permute-start(f32[32,1024]{1,0:T(8,128)S(1)} %add.77.own_ref), channel_id=1, source_target_pairs={{0,10},{1,8},{2,11},{3,9},{4,14},{5,12},{6,15},{7,13},{8,1},{9,3},... | collective-permute-start | bytes 393224 | tf_op jit(solution)/shard_map/ppermute | solution.py:50
  26.6 1.0 %collective-permute-start.4 = (f32[32,1024]{1,0:T(8,128)S(1)}, f32[32,1024]{1,0:T(8,128)S(1)}, u32[]{:S(2)}, u32[]{:S(2)}) collective-permute-start(f32[32,1024]{1,0:T(8,128)S(1)} %add.74.own_ref), channel_id=1, source_target_pairs={{0,24},{1,11},{2,8},{3,27},{4,28},{5,15},{6,12},{7,31},{8,2},{9,17... | collective-permute-start | bytes 393224 | tf_op jit(solution)/shard_map/ppermute | solution.py:50
  29.2 2.1 %collective-permute-start.15 = (f32[32,1024]{1,0:T(8,128)S(1)}, f32[32,1024]{1,0:T(8,128)S(1)}, u32[]{:S(2)}, u32[]{:S(2)}) collective-permute-start(f32[32,1024]{1,0:T(8,128)S(1)} %add.80.own_ref), channel_id=1, source_target_pairs={{0,24},{1,8},{2,11},{3,27},{4,28},{5,12},{6,15},{7,31},{8,1},{9,17... | collective-permute-start | bytes 393224 | tf_op jit(solution)/shard_map/ppermute | solution.py:50
  35.6 2.0 %shard_map.68 = (f32[128,1024]{1,0:T(8,128)S(1)}, f32[128,1024]{1,0:T(8,128)S(1)}, bf16[256,1024]{1,0:T(8,128)(2,1)S(1)}, bf16[256,1024]{1,0:T(8,128)(2,1)S(1)}, f32[256,1024]{1,0:T(8,128)S(1)}) custom-call(bf16[256,1024]{1,0:T(8,128)(2,1)S(1)} %get-tuple-element.48.x_ref, bf16[256,1024]{1,0:T(8,128)(2,1)S(1)} %get-tuple-element.49.g_ref, ...), custom_call_target="tpu_custom_call" | custom-call | tf_op jit(solution)/shard_map/pallas_call | solution.py:304
  39.6 3.2 %collective-permute-start.27 = (f32[32,1024]{1,0:T(8,128)S(1)}, f32[32,1024]{1,0:T(8,128)S(1)}, u32[]{:S(2)}, u32[]{:S(2)}) collective-permute-start(f32[32,1024]{1,0:T(8,128)S(1)} %get-tuple-element.82), channel_id=1, source_target_pairs={{0,10},{1,8},{2,11},{3,9},{4,14},{5,12},{6,15},{7,13},{8,1},{9,3},... | collective-permute-start | bytes 393224 | tf_op jit(solution)/shard_map/ppermute | solution.py:50
  42.9 1.8 %collective-permute-start.38 = (f32[32,1024]{1,0:T(8,128)S(1)}, f32[32,1024]{1,0:T(8,128)S(1)}, u32[]{:S(2)}, u32[]{:S(2)}) collective-permute-start(f32[32,1024]{1,0:T(8,128)S(1)} %get-tuple-element.93), channel_id=1, source_target_pairs={{0,24},{1,11},{2,8},{3,27},{4,28},{5,15},{6,12},{7,31},{8,2},{9,17... | collective-permute-start | bytes 393224 | tf_op jit(solution)/shard_map/ppermute | solution.py:50
  44.8 1.9 %collective-permute-done.27 = f32[32,1024]{1,0:T(8,128)S(1)} collective-permute-done((f32[32,1024]{1,0:T(8,128)S(1)}, f32[32,1024]{1,0:T(8,128)S(1)}, u32[]{:S(2)}, u32[]{:S(2)}) %collective-permute-start.27) | collective-permute-done | bytes 131104 | tf_op jit(solution)/shard_map/ppermute | solution.py:50
  46.7 1.3 %collective-permute-start.28 = (f32[32,1024]{1,0:T(8,128)S(1)}, f32[32,1024]{1,0:T(8,128)S(1)}, u32[]{:S(2)}, u32[]{:S(2)}) collective-permute-start(f32[32,1024]{1,0:T(8,128)S(1)} %add.87), channel_id=1, source_target_pairs={{0,9},{1,25},{2,26},{3,10},{4,13},{5,29},{6,30},{7,14},{8,16},{9,0... | collective-permute-start | bytes 393224 | tf_op jit(solution)/shard_map/ppermute | solution.py:50
  48.1 1.0 %collective-permute-start.24 = (f32[32,1024]{1,0:T(8,128)S(1)}, f32[32,1024]{1,0:T(8,128)S(1)}, u32[]{:S(2)}, u32[]{:S(2)}) collective-permute-start(f32[32,1024]{1,0:T(8,128)S(1)} %add.84), channel_id=1, source_target_pairs={{0,10},{1,8},{2,11},{3,9},{4,14},{5,12},{6,15},{7,13},{8,1},{9,3},... | collective-permute-start | bytes 393224 | tf_op jit(solution)/shard_map/ppermute | solution.py:50
  50.0 1.4 %collective-permute-done.34 = f32[32,1024]{1,0:T(8,128)S(1)} collective-permute-done((f32[32,1024]{1,0:T(8,128)S(1)}, f32[32,1024]{1,0:T(8,128)S(1)}, u32[]{:S(2)}, u32[]{:S(2)}) %collective-permute-start.34) | collective-permute-done | bytes 131104 | tf_op jit(solution)/shard_map/ppermute | solution.py:50
  52.2 1.0 %collective-permute-start.29 = (f32[32,1024]{1,0:T(8,128)S(1)}, f32[32,1024]{1,0:T(8,128)S(1)}, u32[]{:S(2)}, u32[]{:S(2)}) collective-permute-start(f32[32,1024]{1,0:T(8,128)S(1)} %add.88), channel_id=1, source_target_pairs={{0,24},{1,11},{2,8},{3,27},{4,28},{5,15},{6,12},{7,31},{8,2},{9,17... | collective-permute-start | bytes 393224 | tf_op jit(solution)/shard_map/ppermute | solution.py:50
  53.2 1.2 %collective-permute-start.25 = (f32[32,1024]{1,0:T(8,128)S(1)}, f32[32,1024]{1,0:T(8,128)S(1)}, u32[]{:S(2)}, u32[]{:S(2)}) collective-permute-start(f32[32,1024]{1,0:T(8,128)S(1)} %add.85), channel_id=1, source_target_pairs={{0,9},{1,25},{2,26},{3,10},{4,13},{5,29},{6,30},{7,14},{8,16},{9,0... | collective-permute-start | bytes 393224 | tf_op jit(solution)/shard_map/ppermute | solution.py:50
  54.4 1.7 %collective-permute-start.40 = (f32[32,1024]{1,0:T(8,128)S(1)}, f32[32,1024]{1,0:T(8,128)S(1)}, u32[]{:S(2)}, u32[]{:S(2)}) collective-permute-start(f32[32,1024]{1,0:T(8,128)S(1)} %add.94), channel_id=1, source_target_pairs={{0,9},{1,25},{2,26},{3,10},{4,13},{5,29},{6,30},{7,14},{8,16},{9,0... | collective-permute-start | bytes 393224 | tf_op jit(solution)/shard_map/ppermute | solution.py:50
  56.1 1.1 %collective-permute-done.35 = f32[32,1024]{1,0:T(8,128)S(1)} collective-permute-done((f32[32,1024]{1,0:T(8,128)S(1)}, f32[32,1024]{1,0:T(8,128)S(1)}, u32[]{:S(2)}, u32[]{:S(2)}) %collective-permute-start.35) | collective-permute-done | bytes 131104 | tf_op jit(solution)/shard_map/ppermute | solution.py:50
  57.2 1.3 %collective-permute-start.36 = (f32[32,1024]{1,0:T(8,128)S(1)}, f32[32,1024]{1,0:T(8,128)S(1)}, u32[]{:S(2)}, u32[]{:S(2)}) collective-permute-start(f32[32,1024]{1,0:T(8,128)S(1)} %add.91), channel_id=1, source_target_pairs={{0,9},{1,11},{2,8},{3,10},{4,13},{5,15},{6,12},{7,14},{8,2},{9,0},... | collective-permute-start | bytes 393224 | tf_op jit(solution)/shard_map/ppermute | solution.py:50
  58.5 2.6 %collective-permute-start.30 = (f32[32,1024]{1,0:T(8,128)S(1)}, f32[32,1024]{1,0:T(8,128)S(1)}, u32[]{:S(2)}, u32[]{:S(2)}) collective-permute-start(f32[32,1024]{1,0:T(8,128)S(1)} %add.89.own_ref), channel_id=1, source_target_pairs={{0,10},{1,8},{2,11},{3,9},{4,14},{5,12},{6,15},{7,13},{8,1},{9,3},... | collective-permute-start | bytes 393224 | tf_op jit(solution)/shard_map/ppermute | solution.py:50
  61.2 1.8 %collective-permute-start.41 = (f32[32,1024]{1,0:T(8,128)S(1)}, f32[32,1024]{1,0:T(8,128)S(1)}, u32[]{:S(2)}, u32[]{:S(2)}) collective-permute-start(f32[32,1024]{1,0:T(8,128)S(1)} %add.95.own_ref), channel_id=1, source_target_pairs={{0,24},{1,11},{2,8},{3,27},{4,28},{5,15},{6,12},{7,31},{8,2},{9,17... | collective-permute-start | bytes 393224 | tf_op jit(solution)/shard_map/ppermute | solution.py:50
  63.9 1.2 %collective-permute-done.30.rest_ref = f32[32,1024]{1,0:T(8,128)S(1)} collective-permute-done((f32[32,1024]{1,0:T(8,128)S(1)}, f32[32,1024]{1,0:T(8,128)S(1)}, u32[]{:S(2)}, u32[]{:S(2)}) %collective-permute-start.30) | collective-permute-done | bytes 131104 | tf_op jit(solution)/shard_map/ppermute | solution.py:50
  65.9 1.1 %collective-permute-done.41.rest_ref = f32[32,1024]{1,0:T(8,128)S(1)} collective-permute-done((f32[32,1024]{1,0:T(8,128)S(1)}, f32[32,1024]{1,0:T(8,128)S(1)}, u32[]{:S(2)}, u32[]{:S(2)}) %collective-permute-start.41) | collective-permute-done | bytes 131104 | tf_op jit(solution)/shard_map/ppermute | solution.py:50
  67.1 1.3 %collective-permute-done.37.rest_ref = f32[32,1024]{1,0:T(8,128)S(1)} collective-permute-done((f32[32,1024]{1,0:T(8,128)S(1)}, f32[32,1024]{1,0:T(8,128)S(1)}, u32[]{:S(2)}, u32[]{:S(2)}) %collective-permute-start.37) | collective-permute-done | bytes 131104 | tf_op jit(solution)/shard_map/ppermute | solution.py:50
  68.5 1.0 %shard_map.72 = f32[256,1024]{1,0:T(8,128)} custom-call(f32[64,1024]{1,0:T(8,128)S(1)} %shard_map.70.refs_0_, f32[64,1024]{1,0:T(8,128)S(1)} %shard_map.71.refs_1_, f32[64,1024]{1,0:T(8,128)S(1)} %collective-permute-done.31.refs_2_, f32[64,1024]{1,0:T(8,128)S(1)} %collective-permute-done.32.refs_3_), custom_call_target="tpu_custom_call" | custom-call | tf_op jit(solution)/shard_map/pallas_call | solution.py:132
  (100 shorter events, 18.3 us)
Async XLA Ops:
  5.5 5.2 %collective-permute-start.11 = (f32[128,1024]{1,0:T(8,128)S(1)}, f32[128,1024]{1,0:T(8,128)S(1)}, u32[]{:S(2)}, u32[]{:S(2)}) collective-permute-start(f32[128,1024]{1,0:T(8,128)S(1)} %get-tuple-element.72), channel_id=1, source_target_pairs={{0,8},{1,9},{2,10},{3,11},{4,12},{5,13},{6,14},{7,15},{8,0},{9,1},... | collective-permute-start | bytes 1572872 | tf_op jit(solution)/shard_map/ppermute | solution.py:50
  6.5 6.1 %collective-permute-start.5 = (f32[32,1024]{1,0:T(8,128)S(1)}, f32[32,1024]{1,0:T(8,128)S(1)}, u32[]{:S(2)}, u32[]{:S(2)}) collective-permute-start(f32[32,1024]{1,0:T(8,128)S(1)} %get-tuple-element.62), channel_id=1, source_target_pairs={{0,10},{1,8},{2,11},{3,9},{4,14},{5,12},{6,15},{7,13},{8,1},{9,3},... | collective-permute-start | bytes 393224 | tf_op jit(solution)/shard_map/ppermute | solution.py:50
  9.3 6.1 %collective-permute-start.1 = (f32[32,1024]{1,0:T(8,128)S(1)}, f32[32,1024]{1,0:T(8,128)S(1)}, u32[]{:S(2)}, u32[]{:S(2)}) collective-permute-start(f32[32,1024]{1,0:T(8,128)S(1)} %get-tuple-element.60), channel_id=1, source_target_pairs={{0,24},{1,11},{2,8},{3,27},{4,28},{5,15},{6,12},{7,31},{8,2},{9,17... | collective-permute-start | bytes 393224 | tf_op jit(solution)/shard_map/ppermute | solution.py:50
  10.8 5.1 %collective-permute-start.16 = (f32[32,1024]{1,0:T(8,128)S(1)}, f32[32,1024]{1,0:T(8,128)S(1)}, u32[]{:S(2)}, u32[]{:S(2)}) collective-permute-start(f32[32,1024]{1,0:T(8,128)S(1)} %get-tuple-element.76), channel_id=1, source_target_pairs={{0,24},{1,11},{2,8},{3,27},{4,28},{5,15},{6,12},{7,31},{8,2},{9,17... | collective-permute-start | bytes 393224 | tf_op jit(solution)/shard_map/ppermute | solution.py:50
  11.1 6.4 %collective-permute-start.12 = (f32[32,1024]{1,0:T(8,128)S(1)}, f32[32,1024]{1,0:T(8,128)S(1)}, u32[]{:S(2)}, u32[]{:S(2)}) collective-permute-start(f32[32,1024]{1,0:T(8,128)S(1)} %get-tuple-element.74), channel_id=1, source_target_pairs={{0,24},{1,8},{2,11},{3,27},{4,28},{5,12},{6,15},{7,31},{8,1},{9,17... | collective-permute-start | bytes 393224 | tf_op jit(solution)/shard_map/ppermute | solution.py:50
  12.6 6.6 %collective-permute-start.6 = (f32[32,1024]{1,0:T(8,128)S(1)}, f32[32,1024]{1,0:T(8,128)S(1)}, u32[]{:S(2)}, u32[]{:S(2)}) collective-permute-start(f32[32,1024]{1,0:T(8,128)S(1)} %add.75), channel_id=1, source_target_pairs={{0,9},{1,25},{2,26},{3,10},{4,13},{5,29},{6,30},{7,14},{8,16},{9,0... | collective-permute-start | bytes 393224 | tf_op jit(solution)/shard_map/ppermute | solution.py:50
  15.4 4.9 %collective-permute-start.2 = (f32[32,1024]{1,0:T(8,128)S(1)}, f32[32,1024]{1,0:T(8,128)S(1)}, u32[]{:S(2)}, u32[]{:S(2)}) collective-permute-start(f32[32,1024]{1,0:T(8,128)S(1)} %add.72), channel_id=1, source_target_pairs={{0,10},{1,8},{2,11},{3,9},{4,14},{5,12},{6,15},{7,13},{8,1},{9,3},... | collective-permute-start | bytes 393224 | tf_op jit(solution)/shard_map/ppermute | solution.py:50
  15.9 5.7 %collective-permute-start.17 = (f32[32,1024]{1,0:T(8,128)S(1)}, f32[32,1024]{1,0:T(8,128)S(1)}, u32[]{:S(2)}, u32[]{:S(2)}) collective-permute-start(f32[32,1024]{1,0:T(8,128)S(1)} %add.81), channel_id=1, source_target_pairs={{0,10},{1,8},{2,11},{3,9},{4,14},{5,12},{6,15},{7,13},{8,1},{9,3},... | collective-permute-start | bytes 393224 | tf_op jit(solution)/shard_map/ppermute | solution.py:50
  17.6 6.3 %collective-permute-start.13 = (f32[32,1024]{1,0:T(8,128)S(1)}, f32[32,1024]{1,0:T(8,128)S(1)}, u32[]{:S(2)}, u32[]{:S(2)}) collective-permute-start(f32[32,1024]{1,0:T(8,128)S(1)} %add.78), channel_id=1, source_target_pairs={{0,10},{1,25},{2,26},{3,9},{4,14},{5,29},{6,30},{7,13},{8,16},{9,3... | collective-permute-start | bytes 393224 | tf_op jit(solution)/shard_map/ppermute | solution.py:50
  19.3 6.1 %collective-permute-start.7 = (f32[32,1024]{1,0:T(8,128)S(1)}, f32[32,1024]{1,0:T(8,128)S(1)}, u32[]{:S(2)}, u32[]{:S(2)}) collective-permute-start(f32[32,1024]{1,0:T(8,128)S(1)} %add.76), channel_id=1, source_target_pairs={{0,24},{1,11},{2,8},{3,27},{4,28},{5,15},{6,12},{7,31},{8,2},{9,17... | collective-permute-start | bytes 393224 | tf_op jit(solution)/shard_map/ppermute | solution.py:50
  20.3 6.3 %collective-permute-start.3 = (f32[32,1024]{1,0:T(8,128)S(1)}, f32[32,1024]{1,0:T(8,128)S(1)}, u32[]{:S(2)}, u32[]{:S(2)}) collective-permute-start(f32[32,1024]{1,0:T(8,128)S(1)} %add.73), channel_id=1, source_target_pairs={{0,9},{1,25},{2,26},{3,10},{4,13},{5,29},{6,30},{7,14},{8,16},{9,0... | collective-permute-start | bytes 393224 | tf_op jit(solution)/shard_map/ppermute | solution.py:50
  21.7 6.0 %collective-permute-start.18 = (f32[32,1024]{1,0:T(8,128)S(1)}, f32[32,1024]{1,0:T(8,128)S(1)}, u32[]{:S(2)}, u32[]{:S(2)}) collective-permute-start(f32[32,1024]{1,0:T(8,128)S(1)} %add.82), channel_id=1, source_target_pairs={{0,9},{1,25},{2,26},{3,10},{4,13},{5,29},{6,30},{7,14},{8,16},{9,0... | collective-permute-start | bytes 393224 | tf_op jit(solution)/shard_map/ppermute | solution.py:50
  23.9 5.3 %collective-permute-start.14 = (f32[32,1024]{1,0:T(8,128)S(1)}, f32[32,1024]{1,0:T(8,128)S(1)}, u32[]{:S(2)}, u32[]{:S(2)}) collective-permute-start(f32[32,1024]{1,0:T(8,128)S(1)} %add.79), channel_id=1, source_target_pairs={{0,9},{1,11},{2,8},{3,10},{4,13},{5,15},{6,12},{7,14},{8,2},{9,0},... | collective-permute-start | bytes 393224 | tf_op jit(solution)/shard_map/ppermute | solution.py:50
  25.4 5.8 %collective-permute-start.8 = (f32[32,1024]{1,0:T(8,128)S(1)}, f32[32,1024]{1,0:T(8,128)S(1)}, u32[]{:S(2)}, u32[]{:S(2)}) collective-permute-start(f32[32,1024]{1,0:T(8,128)S(1)} %add.77.own_ref), channel_id=1, source_target_pairs={{0,10},{1,8},{2,11},{3,9},{4,14},{5,12},{6,15},{7,13},{8,1},{9,3},... | collective-permute-start | bytes 393224 | tf_op jit(solution)/shard_map/ppermute | solution.py:50
  26.6 4.8 %collective-permute-start.4 = (f32[32,1024]{1,0:T(8,128)S(1)}, f32[32,1024]{1,0:T(8,128)S(1)}, u32[]{:S(2)}, u32[]{:S(2)}) collective-permute-start(f32[32,1024]{1,0:T(8,128)S(1)} %add.74.own_ref), channel_id=1, source_target_pairs={{0,24},{1,11},{2,8},{3,27},{4,28},{5,15},{6,12},{7,31},{8,2},{9,17... | collective-permute-start | bytes 393224 | tf_op jit(solution)/shard_map/ppermute | solution.py:50
  27.7 4.8 %collective-permute-start.19 = (f32[32,1024]{1,0:T(8,128)S(1)}, f32[32,1024]{1,0:T(8,128)S(1)}, u32[]{:S(2)}, u32[]{:S(2)}) collective-permute-start(f32[32,1024]{1,0:T(8,128)S(1)} %add.83.own_ref), channel_id=1, source_target_pairs={{0,24},{1,11},{2,8},{3,27},{4,28},{5,15},{6,12},{7,31},{8,2},{9,17... | collective-permute-start | bytes 393224 | tf_op jit(solution)/shard_map/ppermute | solution.py:50
  29.2 4.7 %collective-permute-start.15 = (f32[32,1024]{1,0:T(8,128)S(1)}, f32[32,1024]{1,0:T(8,128)S(1)}, u32[]{:S(2)}, u32[]{:S(2)}) collective-permute-start(f32[32,1024]{1,0:T(8,128)S(1)} %add.80.own_ref), channel_id=1, source_target_pairs={{0,24},{1,8},{2,11},{3,27},{4,28},{5,12},{6,15},{7,31},{8,1},{9,17... | collective-permute-start | bytes 393224 | tf_op jit(solution)/shard_map/ppermute | solution.py:50
  39.6 7.1 %collective-permute-start.27 = (f32[32,1024]{1,0:T(8,128)S(1)}, f32[32,1024]{1,0:T(8,128)S(1)}, u32[]{:S(2)}, u32[]{:S(2)}) collective-permute-start(f32[32,1024]{1,0:T(8,128)S(1)} %get-tuple-element.82), channel_id=1, source_target_pairs={{0,10},{1,8},{2,11},{3,9},{4,14},{5,12},{6,15},{7,13},{8,1},{9,3},... | collective-permute-start | bytes 393224 | tf_op jit(solution)/shard_map/ppermute | solution.py:50
  42.8 5.3 %collective-permute-start.23 = (f32[32,1024]{1,0:T(8,128)S(1)}, f32[32,1024]{1,0:T(8,128)S(1)}, u32[]{:S(2)}, u32[]{:S(2)}) collective-permute-start(f32[32,1024]{1,0:T(8,128)S(1)} %get-tuple-element.80), channel_id=1, source_target_pairs={{0,24},{1,11},{2,8},{3,27},{4,28},{5,15},{6,12},{7,31},{8,2},{9,17... | collective-permute-start | bytes 393224 | tf_op jit(solution)/shard_map/ppermute | solution.py:50
  42.9 6.2 %collective-permute-start.38 = (f32[32,1024]{1,0:T(8,128)S(1)}, f32[32,1024]{1,0:T(8,128)S(1)}, u32[]{:S(2)}, u32[]{:S(2)}) collective-permute-start(f32[32,1024]{1,0:T(8,128)S(1)} %get-tuple-element.93), channel_id=1, source_target_pairs={{0,24},{1,11},{2,8},{3,27},{4,28},{5,15},{6,12},{7,31},{8,2},{9,17... | collective-permute-start | bytes 393224 | tf_op jit(solution)/shard_map/ppermute | solution.py:50
  44.7 6.7 %collective-permute-start.34 = (f32[32,1024]{1,0:T(8,128)S(1)}, f32[32,1024]{1,0:T(8,128)S(1)}, u32[]{:S(2)}, u32[]{:S(2)}) collective-permute-start(f32[32,1024]{1,0:T(8,128)S(1)} %get-tuple-element.91), channel_id=1, source_target_pairs={{0,24},{1,8},{2,11},{3,27},{4,28},{5,12},{6,15},{7,31},{8,1},{9,17... | collective-permute-start | bytes 393224 | tf_op jit(solution)/shard_map/ppermute | solution.py:50
  46.7 5.4 %collective-permute-start.28 = (f32[32,1024]{1,0:T(8,128)S(1)}, f32[32,1024]{1,0:T(8,128)S(1)}, u32[]{:S(2)}, u32[]{:S(2)}) collective-permute-start(f32[32,1024]{1,0:T(8,128)S(1)} %add.87), channel_id=1, source_target_pairs={{0,9},{1,25},{2,26},{3,10},{4,13},{5,29},{6,30},{7,14},{8,16},{9,0... | collective-permute-start | bytes 393224 | tf_op jit(solution)/shard_map/ppermute | solution.py:50
  48.1 5.0 %collective-permute-start.24 = (f32[32,1024]{1,0:T(8,128)S(1)}, f32[32,1024]{1,0:T(8,128)S(1)}, u32[]{:S(2)}, u32[]{:S(2)}) collective-permute-start(f32[32,1024]{1,0:T(8,128)S(1)} %add.84), channel_id=1, source_target_pairs={{0,10},{1,8},{2,11},{3,9},{4,14},{5,12},{6,15},{7,13},{8,1},{9,3},... | collective-permute-start | bytes 393224 | tf_op jit(solution)/shard_map/ppermute | solution.py:50
  49.1 5.2 %collective-permute-start.39 = (f32[32,1024]{1,0:T(8,128)S(1)}, f32[32,1024]{1,0:T(8,128)S(1)}, u32[]{:S(2)}, u32[]{:S(2)}) collective-permute-start(f32[32,1024]{1,0:T(8,128)S(1)} %add.93), channel_id=1, source_target_pairs={{0,10},{1,8},{2,11},{3,9},{4,14},{5,12},{6,15},{7,13},{8,1},{9,3},... | collective-permute-start | bytes 393224 | tf_op jit(solution)/shard_map/ppermute | solution.py:50
  51.5 5.8 %collective-permute-start.35 = (f32[32,1024]{1,0:T(8,128)S(1)}, f32[32,1024]{1,0:T(8,128)S(1)}, u32[]{:S(2)}, u32[]{:S(2)}) collective-permute-start(f32[32,1024]{1,0:T(8,128)S(1)} %add.90), channel_id=1, source_target_pairs={{0,10},{1,25},{2,26},{3,9},{4,14},{5,29},{6,30},{7,13},{8,16},{9,3... | collective-permute-start | bytes 393224 | tf_op jit(solution)/shard_map/ppermute | solution.py:50
  52.2 6.4 %collective-permute-start.29 = (f32[32,1024]{1,0:T(8,128)S(1)}, f32[32,1024]{1,0:T(8,128)S(1)}, u32[]{:S(2)}, u32[]{:S(2)}) collective-permute-start(f32[32,1024]{1,0:T(8,128)S(1)} %add.88), channel_id=1, source_target_pairs={{0,24},{1,11},{2,8},{3,27},{4,28},{5,15},{6,12},{7,31},{8,2},{9,17... | collective-permute-start | bytes 393224 | tf_op jit(solution)/shard_map/ppermute | solution.py:50
  53.2 7.9 %collective-permute-start.25 = (f32[32,1024]{1,0:T(8,128)S(1)}, f32[32,1024]{1,0:T(8,128)S(1)}, u32[]{:S(2)}, u32[]{:S(2)}) collective-permute-start(f32[32,1024]{1,0:T(8,128)S(1)} %add.85), channel_id=1, source_target_pairs={{0,9},{1,25},{2,26},{3,10},{4,13},{5,29},{6,30},{7,14},{8,16},{9,0... | collective-permute-start | bytes 393224 | tf_op jit(solution)/shard_map/ppermute | solution.py:50
  54.4 6.8 %collective-permute-start.40 = (f32[32,1024]{1,0:T(8,128)S(1)}, f32[32,1024]{1,0:T(8,128)S(1)}, u32[]{:S(2)}, u32[]{:S(2)}) collective-permute-start(f32[32,1024]{1,0:T(8,128)S(1)} %add.94), channel_id=1, source_target_pairs={{0,9},{1,25},{2,26},{3,10},{4,13},{5,29},{6,30},{7,14},{8,16},{9,0... | collective-permute-start | bytes 393224 | tf_op jit(solution)/shard_map/ppermute | solution.py:50
  57.2 5.8 %collective-permute-start.36 = (f32[32,1024]{1,0:T(8,128)S(1)}, f32[32,1024]{1,0:T(8,128)S(1)}, u32[]{:S(2)}, u32[]{:S(2)}) collective-permute-start(f32[32,1024]{1,0:T(8,128)S(1)} %add.91), channel_id=1, source_target_pairs={{0,9},{1,11},{2,8},{3,10},{4,13},{5,15},{6,12},{7,14},{8,2},{9,0},... | collective-permute-start | bytes 393224 | tf_op jit(solution)/shard_map/ppermute | solution.py:50
  58.5 6.6 %collective-permute-start.30 = (f32[32,1024]{1,0:T(8,128)S(1)}, f32[32,1024]{1,0:T(8,128)S(1)}, u32[]{:S(2)}, u32[]{:S(2)}) collective-permute-start(f32[32,1024]{1,0:T(8,128)S(1)} %add.89.own_ref), channel_id=1, source_target_pairs={{0,10},{1,8},{2,11},{3,9},{4,14},{5,12},{6,15},{7,13},{8,1},{9,3},... | collective-permute-start | bytes 393224 | tf_op jit(solution)/shard_map/ppermute | solution.py:50
  61.2 5.7 %collective-permute-start.41 = (f32[32,1024]{1,0:T(8,128)S(1)}, f32[32,1024]{1,0:T(8,128)S(1)}, u32[]{:S(2)}, u32[]{:S(2)}) collective-permute-start(f32[32,1024]{1,0:T(8,128)S(1)} %add.95.own_ref), channel_id=1, source_target_pairs={{0,24},{1,11},{2,8},{3,27},{4,28},{5,15},{6,12},{7,31},{8,2},{9,17... | collective-permute-start | bytes 393224 | tf_op jit(solution)/shard_map/ppermute | solution.py:50
  63.0 5.3 %collective-permute-start.37 = (f32[32,1024]{1,0:T(8,128)S(1)}, f32[32,1024]{1,0:T(8,128)S(1)}, u32[]{:S(2)}, u32[]{:S(2)}) collective-permute-start(f32[32,1024]{1,0:T(8,128)S(1)} %add.92.own_ref), channel_id=1, source_target_pairs={{0,24},{1,8},{2,11},{3,27},{4,28},{5,12},{6,15},{7,31},{8,1},{9,17... | collective-permute-start | bytes 393224 | tf_op jit(solution)/shard_map/ppermute | solution.py:50
  (12 other events, 32.5 us)

commit v6 on v5

--- a/solution.py
+++ b/solution.py
@@ -13,9 +13,9 @@
 
 ORDERS = (
     ((1, 3, 2), (3, 2, 1)),
-    ((3, 2, 1), (2, 1, 3)),
-    ((1, 3, 2), (2, 1, 3)),
+    ((2, 3, 1), (2, 1, 3)),
     ((1, 3, 2), (3, 2, 1)),
+    ((1, 2, 3), (2, 1, 3)),
 )
 REDUCE_CHAINS = ((1, 4), (2, 4))
 EXPAND_CHAINS = ((3, 4), (4, 4))
@@ -110,33 +110,44 @@
     return [own for own, over in parts] + [over for own, over in parts]
 
 
-def placed(parts, chains, role):
-    rows = sum(part.shape[0] for part in parts) // 2
-    firsts = [first for _, first, _ in spans(chains, rows)]
-    for i, part in enumerate(parts):
-        place = role if i < len(chains) else 1 - role
-        yield part, pl.ds(pl.multiple_of(place * rows + firsts[i % len(chains)], 16), part.shape[0])
-
-
-def store_kernel(chains, *refs):
-    *parts, out_ref, sems = refs
-    moves = [(part, out_ref.at[rows, :]) for part, rows in placed(parts, chains, places()[0])]
+def row_span(chains, rows, i, role):
+    _, first, count = list(spans(chains, rows))[i % len(chains)]
+    place = role if i < len(chains) else 1 - role
+    return pl.ds(pl.multiple_of(place * rows + first, 16), count)
+
+
+def start_copies(moves, sems):
     copies = [pltpu.make_async_copy(source, target, sems.at[i]) for i, (source, target) in enumerate(moves)]
     for copy in copies:
         copy.start()
-    for copy in copies:
+    return copies
+
+
+def store_kernel(groups, *refs):
+    *refs, sems = refs
+    outs = refs[-len(groups) :]
+    moves = []
+    for (chains, rows, which), out_ref in zip(groups, outs):
+        parts, refs = refs[: len(which)], refs[len(which) :]
+        for i, part in zip(which, parts):
+            moves.append((part, out_ref.at[row_span(chains, rows, i, places()[0]), :]))
+    for copy in start_copies(moves, sems):
         copy.wait()
 
 
-def store(parts, chains):
+def store(groups, onto=()):
+    parts = [part for group in groups for part in group[0]]
+    columns = parts[0].shape[1]
+    counted = [(chains, rows, which) for _, chains, which, rows in groups]
     return pl.pallas_call(
-        functools.partial(store_kernel, chains),
-        out_shape=jax.ShapeDtypeStruct((sum(part.shape[0] for part in parts), parts[0].shape[1]), f32),
-        in_specs=[VMEM] * len(parts),
-        out_specs=HBM,
+        functools.partial(store_kernel, counted),
+        out_shape=[jax.ShapeDtypeStruct((2 * rows, columns), f32) for _, _, _, rows in groups],
+        in_specs=[VMEM] * len(parts) + [HBM] * len(onto),
+        out_specs=[HBM] * len(groups),
         scratch_shapes=[pltpu.SemaphoreType.DMA((len(parts),))],
+        input_output_aliases={len(parts) + i: i for i in range(len(onto))},
         compiler_params=SMALL,
-    )(*parts)
+    )(*parts, *onto)
 
 
 def halves(values):
@@ -181,15 +192,8 @@
 
 
 def put_together(parts, chains, whole_ref):
-    for part, rows in placed(parts, chains, places()[0]):
-        whole_ref[rows, :] = part[...]
-
-
-def start_copies(moves, sems):
-    copies = [pltpu.make_async_copy(source, target, sems.at[i]) for i, (source, target) in enumerate(moves)]
-    for copy in copies:
-        copy.start()
-    return copies
+    for i, part in enumerate(parts):
+        whole_ref[row_span(chains, whole_ref.shape[0] // 2, i, places()[0]), :] = part[...]
 
 
 def hidden_of(r_ref, x_ref, outs, arrived):
@@ -208,20 +212,18 @@
 
 
 def first_hidden_kernel(x_in, g_in, r_in, e_in, *refs):
-    outs, (r_ref, e_ref), acts_refs, sems = refs[:5], refs[5:7], refs[7:-1], refs[-1]
+    outs, (r_ref, e_ref, x_ref, g_ref, sems) = refs[:5], refs[5:]
     moves = []
     for columns in in_columns(r_ref.shape[1]):
-        moves += [(r_in.at[:, columns], r_ref.at[:, columns]), (x_in.at[0, :, columns], acts_refs[0].at[:, columns])]
-    early = len(moves)
-    later = [(source.at[i // 2], ref) for i, (source, ref) in enumerate(zip((x_in, g_in) * len(acts_refs), acts_refs))]
-    copies = start_copies(moves + [(e_in, e_ref)] + later[1:], sems)
+        moves += [(r_in.at[:, columns], r_ref.at[:, columns]), (x_in.at[0, :, columns], x_ref.at[:, columns])]
+    copies = start_copies(moves + [(e_in, e_ref), (g_in.at[0], g_ref)], sems)
 
     def arrived(i):
         copies[2 * i].wait()
         copies[2 * i + 1].wait()
 
-    hidden_of(r_ref, acts_refs[0], outs, arrived)
-    for copy in copies[early:]:
+    hidden_of(r_ref, x_ref, outs, arrived)
+    for copy in copies[len(moves) :]:
         copy.wait()
 
 
@@ -232,7 +234,12 @@
     hidden_of(r_ref, x_ref, outs, lambda i: None)
 
 
-def reduce_kernel(joined, x_ref, g_ref, r_ref, slope_ref, hidden_high_ref, hidden_low_ref, *refs):
+def reduce_kernel(joined, upcoming, x_ref, g_ref, r_ref, slope_ref, hidden_high_ref, hidden_low_ref, *refs):
+    copies = []
+    if upcoming is not None:
+        x_in, g_in, *refs, next_x_ref, next_g_ref, high_ref, low_ref, sems = refs
+        copies = start_copies([(x_in.at[upcoming], next_x_ref), (g_in.at[upcoming], next_g_ref)], sems)
+        refs = [*refs, high_ref, low_ref]
     if joined:
         *parts, keep_ref, send_ref, zh_ref, zl_ref, e_ref, high_ref, low_ref = refs
         put_together(parts, EXPAND_CHAINS, e_ref)
@@ -263,6 +270,8 @@
     for columns in blocks:
         step = product((high_ref[...], low_ref[...]), (x_ref[:, columns],), NN) * (learn_rate * reduce_scale)
         step_columns(role, columns, r_ref, step, keep_ref, send_ref)
+    for copy in copies:
+        copy.wait()
 
 
 def expand_kernel(e_ref, zh_ref, zl_ref, hidden_high_ref, hidden_low_ref, keep_ref, send_ref):
@@ -287,35 +296,43 @@
     )
     weights = jax.ShapeDtypeStruct((width, columns), f32)
     narrow = jax.ShapeDtypeStruct((width, columns), bf16)
-    results = pl.pallas_call(
+    *hidden, reducing, expanding, feats, grads = pl.pallas_call(
         first_hidden_kernel,
-        out_shape=hidden_shapes + [narrow] * 2 + [acts] * (2 * iterations),
+        out_shape=hidden_shapes + [narrow] * 2 + [acts] * 2,
         in_specs=[HBM] * 4,
-        out_specs=[VMEM] * (7 + 2 * iterations),
-        scratch_shapes=[pltpu.SemaphoreType.DMA((2 * columns // BLOCK + 2 * iterations,))],
+        out_specs=[VMEM] * 9,
+        scratch_shapes=[pltpu.SemaphoreType.DMA((2 * columns // BLOCK + 2,))],
         compiler_params=LARGE,
         name="hidden_0",
     )(*held)
-    hidden, (reducing, expanding), acts_of = results[:5], results[5:7], results[7:]
     for iteration in range(iterations):
         first, last = iteration == 0, iteration == iterations - 1
-        feats, grads = acts_of[2 * iteration : 2 * iteration + 2]
         slope, high_t, low_t, high, low = hidden
-        keep_r, send_r, zh, zl, *joined = pl.pallas_call(
-            functools.partial(reduce_kernel, not first),
-            out_shape=[half, half, acts, acts] + ([] if first else [weights]),
-            in_specs=[VMEM] * (7 if first else 6 + len(expanding)),
-            out_specs=[VMEM] * (4 if first else 5),
-            scratch_shapes=[pltpu.VMEM((width, rows), bf16)] * 2,
+        weights_in = [expanding] if first else expanding
+        keep_r, send_r, zh, zl, *more = pl.pallas_call(
+            functools.partial(reduce_kernel, not first, None if last else iteration + 1),
+            out_shape=[half, half, acts, acts] + ([] if first else [weights]) + ([] if last else [acts] * 2),
+            in_specs=[VMEM] * 6 + ([] if last else [HBM] * 2) + [VMEM] * len(weights_in),
+            out_specs=[VMEM] * (4 + (not first) + 2 * (not last)),
+            scratch_shapes=[pltpu.VMEM((width, rows), bf16)] * 2 + ([] if last else [pltpu.SemaphoreType.DMA((2,))]),
             compiler_params=LARGE,
-        )(feats, grads, reducing, slope, high, low, *([expanding] if first else expanding))
+        )(feats, grads, reducing, slope, high, low, *([] if last else held[:2]), *weights_in)
+        if not first:
+            expanding = more.pop(0)
+        if not last:
+            feats, grads = more
         keep_e, send_e = pl.pallas_call(
             expand_kernel, out_shape=[half, half], in_specs=[VMEM] * 5, out_specs=[VMEM] * 2, compiler_params=LARGE
-        )(expanding if first else joined[0], zh, zl, high_t, low_t)
+        )(expanding, zh, zl, high_t, low_t)
         sums_r = sum_over_cube(keep_r, send_r, REDUCE_CHAINS)
         expanding = sum_over_cube(keep_e, send_e, EXPAND_CHAINS)
         if last:
-            new_reduce = store(sums_r, REDUCE_CHAINS)
+            own = tuple(range(len(EXPAND_CHAINS)))
+            groups = [
+                (sums_r, REDUCE_CHAINS, tuple(range(len(sums_r))), width // 2),
+                ([expanding[i] for i in own], EXPAND_CHAINS, own, width // 2),
+            ]
+            new_reduce, new_expand = store(groups)
         else:
             *hidden, reducing = pl.pallas_call(
                 hidden_kernel,
@@ -323,8 +340,10 @@
                 in_specs=[VMEM] * (1 + len(sums_r)),
                 out_specs=[VMEM] * 6,
                 compiler_params=LARGE,
-            )(acts_of[2 * iteration + 2], *sums_r)
-    return new_reduce[None, None], store(expanding, EXPAND_CHAINS)[None, None]
+            )(feats, *sums_r)
+    over = tuple(range(len(EXPAND_CHAINS), len(expanding)))
+    (new_expand,) = store([([expanding[i] for i in over], EXPAND_CHAINS, over, width // 2)], [new_expand])
+    return new_reduce[None, None], new_expand[None, None]
 
 
 def solution(mesh):

time: 71.2 us -> 67.5 us (0.948)
  waiting for transfers between devices: 17.4 us -> 7.54 us
  starting transfers between devices: 42.2 us -> 47.8 us
    ppermute x44, waiting for transfers between devices: 17.4 us -> 7.54 us  [from_partner(): return lax.ppermute(values, ('near', 'far'), pairs)]
    ppermute x44, starting transfers between devices: 42.2 us -> 47.8 us  [from_partner(): return lax.ppermute(values, ('near', 'far'), pairs)]
  transfers between devices with their start and end apart: 44 -> 44, of which waited for: 18 -> 13; matrix products, arithmetic and copies ran while one was open for 1% -> 1% of each run, Pallas kernels for 5% -> 5%
where the time goes in v6:
time: 67.5 us; the launch traced here: 67.3 us
  starting transfers between devices  47.8 us (71%)
  Pallas kernels  10.6 us (16%)
  waiting for transfers between devices  7.54 us (11%)
  between operations  0.94 us (1%)
    ppermute x44, starting transfers between devices, from_partner(): return lax.ppermute(values, ('near', 'far'), pairs)  47.8 us
    ppermute x44, waiting for transfers between devices, from_partner(): return lax.ppermute(values, ('near', 'far'), pairs)  7.54 us
    pallas_call x2, Pallas kernels, shards(): pl.pallas_call(functools.partial(reduce_kernel, not first, None if last e...  4.32 us
    pallas_call x1, Pallas kernels, shards(): pl.pallas_call(first_hidden_kernel, out_shape=hidden_shapes + [narrow] *...  2.03 us
    pallas_call x2, Pallas kernels, store(): pl.pallas_call(functools.partial(store_kernel, counted), out_shape=[jax.S...  2 us
  transfers between devices with their start and end apart: 44, of which 13 were waited for; matrix products, arithmetic and copies ran while one was open for 1% of the time, Pallas kernels for 5%

profile of v6, /device:TPU:0, one launch (start us, length us, event | category | flops | bytes accessed | tf_op | source)
XLA Modules:
  0.0 67.3 jit_solution(5374020389388079551)
XLA Ops:
  0.6 2.0 %hidden_0.1 = (f32[256,256]{1,0:T(8,128)S(1)}, bf16[256,256]{1,0:T(8,128)(2,1)S(1)}, bf16[256,256]{1,0:T(8,128)(2,1)S(1)}, bf16[256,256]{1,0:T(8,128)(2,1)S(1)},...) custom-call(bf16[2,256,1024]{2,1,0:T(8,128)(2,1)} %bitcast.6, ...), custom_call_target="tpu_custom_call" | custom-call | tf_op jit(solution)/shard_map/hidden_0/pallas_call | solution.py:299
  2.7 2.3 %shard_map.59 = (f32[128,1024]{1,0:T(8,128)S(1)}, f32[128,1024]{1,0:T(8,128)S(1)}, bf16[256,1024]{1,0:T(8,128)(2,1)S(1)}, bf16[256,1024]{1,0:T(8,128)(2,1)S(1)},...) custom-call(bf16[256,1024]{1,0:T(8,128)(2,1)S(1)} %get-tuple-element.50.x_ref, ...), custom_call_target="tpu_custom_call" | custom-call | tf_op jit(solution)/shard_map/pallas_call | solution.py:312
  6.2 0.9 %collective-permute-done.got_ref = f32[128,1024]{1,0:T(8,128)S(1)} collective-permute-done((f32[128,1024]{1,0:T(8,128)S(1)}, f32[128,1024]{1,0:T(8,128)S(1)}, u32[]{:S(2)}, u32[]{:S(2)}) %collective-permute-start) | collective-permute-done | bytes 524320 | tf_op jit(solution)/shard_map/ppermute | solution.py:50
  7.1 2.7 %collective-permute-start.5 = (f32[32,1024]{1,0:T(8,128)S(1)}, f32[32,1024]{1,0:T(8,128)S(1)}, u32[]{:S(2)}, u32[]{:S(2)}) collective-permute-start(f32[32,1024]{1,0:T(8,128)S(1)} %get-tuple-element.64), channel_id=1, source_target_pairs={{0,9},{1,8},{2,11},{3,10},{4,13},{5,12},{6,15},{7,14},{8,1},{9,0},... | collective-permute-start | bytes 393224 | tf_op jit(solution)/shard_map/ppermute | solution.py:50
  9.8 1.5 %collective-permute-start.1 = (f32[32,1024]{1,0:T(8,128)S(1)}, f32[32,1024]{1,0:T(8,128)S(1)}, u32[]{:S(2)}, u32[]{:S(2)}) collective-permute-start(f32[32,1024]{1,0:T(8,128)S(1)} %get-tuple-element.62), channel_id=1, source_target_pairs={{0,24},{1,11},{2,8},{3,27},{4,28},{5,15},{6,12},{7,31},{8,2},{9,17... | collective-permute-start | bytes 393224 | tf_op jit(solution)/shard_map/ppermute | solution.py:50
  11.7 1.5 %collective-permute-start.12 = (f32[32,1024]{1,0:T(8,128)S(1)}, f32[32,1024]{1,0:T(8,128)S(1)}, u32[]{:S(2)}, u32[]{:S(2)}) collective-permute-start(f32[32,1024]{1,0:T(8,128)S(1)} %get-tuple-element.76), channel_id=1, source_target_pairs={{0,24},{1,11},{2,8},{3,27},{4,28},{5,15},{6,12},{7,31},{8,2},{9,17... | collective-permute-start | bytes 393224 | tf_op jit(solution)/shard_map/ppermute | solution.py:50
  13.7 2.3 %collective-permute-start.6 = (f32[32,1024]{1,0:T(8,128)S(1)}, f32[32,1024]{1,0:T(8,128)S(1)}, u32[]{:S(2)}, u32[]{:S(2)}) collective-permute-start(f32[32,1024]{1,0:T(8,128)S(1)} %add.75), channel_id=1, source_target_pairs={{0,10},{1,25},{2,26},{3,9},{4,14},{5,29},{6,30},{7,13},{8,16},{9,3... | collective-permute-start | bytes 393224 | tf_op jit(solution)/shard_map/ppermute | solution.py:50
  16.2 1.7 %collective-permute-start.17 = (f32[32,1024]{1,0:T(8,128)S(1)}, f32[32,1024]{1,0:T(8,128)S(1)}, u32[]{:S(2)}, u32[]{:S(2)}) collective-permute-start(f32[32,1024]{1,0:T(8,128)S(1)} %add.81), channel_id=1, source_target_pairs={{0,9},{1,25},{2,26},{3,10},{4,13},{5,29},{6,30},{7,14},{8,16},{9,0... | collective-permute-start | bytes 393224 | tf_op jit(solution)/shard_map/ppermute | solution.py:50
  17.9 1.5 %collective-permute-start.13 = (f32[32,1024]{1,0:T(8,128)S(1)}, f32[32,1024]{1,0:T(8,128)S(1)}, u32[]{:S(2)}, u32[]{:S(2)}) collective-permute-start(f32[32,1024]{1,0:T(8,128)S(1)} %add.78), channel_id=1, source_target_pairs={{0,10},{1,8},{2,11},{3,9},{4,14},{5,12},{6,15},{7,13},{8,1},{9,3},... | collective-permute-start | bytes 393224 | tf_op jit(solution)/shard_map/ppermute | solution.py:50
  19.4 1.4 %collective-permute-start.7 = (f32[32,1024]{1,0:T(8,128)S(1)}, f32[32,1024]{1,0:T(8,128)S(1)}, u32[]{:S(2)}, u32[]{:S(2)}) collective-permute-start(f32[32,1024]{1,0:T(8,128)S(1)} %add.76), channel_id=1, source_target_pairs={{0,24},{1,11},{2,8},{3,27},{4,28},{5,15},{6,12},{7,31},{8,2},{9,17... | collective-permute-start | bytes 393224 | tf_op jit(solution)/shard_map/ppermute | solution.py:50
  20.9 1.3 %collective-permute-start.3 = (f32[32,1024]{1,0:T(8,128)S(1)}, f32[32,1024]{1,0:T(8,128)S(1)}, u32[]{:S(2)}, u32[]{:S(2)}) collective-permute-start(f32[32,1024]{1,0:T(8,128)S(1)} %add.73), channel_id=1, source_target_pairs={{0,9},{1,25},{2,26},{3,10},{4,13},{5,29},{6,30},{7,14},{8,16},{9,0... | collective-permute-start | bytes 393224 | tf_op jit(solution)/shard_map/ppermute | solution.py:50
  22.2 1.6 %collective-permute-start.18 = (f32[32,1024]{1,0:T(8,128)S(1)}, f32[32,1024]{1,0:T(8,128)S(1)}, u32[]{:S(2)}, u32[]{:S(2)}) collective-permute-start(f32[32,1024]{1,0:T(8,128)S(1)} %add.82), channel_id=1, source_target_pairs={{0,10},{1,11},{2,8},{3,9},{4,14},{5,15},{6,12},{7,13},{8,2},{9,3},... | collective-permute-start | bytes 393224 | tf_op jit(solution)/shard_map/ppermute | solution.py:50
  23.8 1.0 %collective-permute-start.14 = (f32[32,1024]{1,0:T(8,128)S(1)}, f32[32,1024]{1,0:T(8,128)S(1)}, u32[]{:S(2)}, u32[]{:S(2)}) collective-permute-start(f32[32,1024]{1,0:T(8,128)S(1)} %add.79), channel_id=1, source_target_pairs={{0,9},{1,25},{2,26},{3,10},{4,13},{5,29},{6,30},{7,14},{8,16},{9,0... | collective-permute-start | bytes 393224 | tf_op jit(solution)/shard_map/ppermute | solution.py:50
  24.8 1.3 %collective-permute-start.8 = (f32[32,1024]{1,0:T(8,128)S(1)}, f32[32,1024]{1,0:T(8,128)S(1)}, u32[]{:S(2)}, u32[]{:S(2)}) collective-permute-start(f32[32,1024]{1,0:T(8,128)S(1)} %add.77.own_ref), channel_id=1, source_target_pairs={{0,9},{1,8},{2,11},{3,10},{4,13},{5,12},{6,15},{7,14},{8,1},{9,0},... | collective-permute-start | bytes 393224 | tf_op jit(solution)/shard_map/ppermute | solution.py:50
  27.8 1.2 %collective-permute-start.19 = (f32[32,1024]{1,0:T(8,128)S(1)}, f32[32,1024]{1,0:T(8,128)S(1)}, u32[]{:S(2)}, u32[]{:S(2)}) collective-permute-start(f32[32,1024]{1,0:T(8,128)S(1)} %add.83.own_ref), channel_id=1, source_target_pairs={{0,24},{1,8},{2,11},{3,27},{4,28},{5,12},{6,15},{7,31},{8,1},{9,17... | collective-permute-start | bytes 393224 | tf_op jit(solution)/shard_map/ppermute | solution.py:50
  29.1 2.1 %collective-permute-start.15 = (f32[32,1024]{1,0:T(8,128)S(1)}, f32[32,1024]{1,0:T(8,128)S(1)}, u32[]{:S(2)}, u32[]{:S(2)}) collective-permute-start(f32[32,1024]{1,0:T(8,128)S(1)} %add.80.own_ref), channel_id=1, source_target_pairs={{0,24},{1,11},{2,8},{3,27},{4,28},{5,15},{6,12},{7,31},{8,2},{9,17... | collective-permute-start | bytes 393224 | tf_op jit(solution)/shard_map/ppermute | solution.py:50
  35.5 2.0 %shard_map.68 = (f32[128,1024]{1,0:T(8,128)S(1)}, f32[128,1024]{1,0:T(8,128)S(1)}, bf16[256,1024]{1,0:T(8,128)(2,1)S(1)}, bf16[256,1024]{1,0:T(8,128)(2,1)S(1)}, f32[256,1024]{1,0:T(8,128)S(1)}) custom-call(bf16[256,1024]{1,0:T(8,128)(2,1)S(1)} %get-tuple-element.57.x_ref, bf16[256,1024]{1,0:T(8,128)(2,1)S(1)} %get-tuple-element.58.g_ref, ...), custom_call_target="tpu_custom_call" | custom-call | tf_op jit(solution)/shard_map/pallas_call | solution.py:312
  39.6 1.2 %collective-permute-start.27 = (f32[32,1024]{1,0:T(8,128)S(1)}, f32[32,1024]{1,0:T(8,128)S(1)}, u32[]{:S(2)}, u32[]{:S(2)}) collective-permute-start(f32[32,1024]{1,0:T(8,128)S(1)} %get-tuple-element.84), channel_id=1, source_target_pairs={{0,9},{1,8},{2,11},{3,10},{4,13},{5,12},{6,15},{7,14},{8,1},{9,0},... | collective-permute-start | bytes 393224 | tf_op jit(solution)/shard_map/ppermute | solution.py:50
  40.8 1.6 %collective-permute-start.23 = (f32[32,1024]{1,0:T(8,128)S(1)}, f32[32,1024]{1,0:T(8,128)S(1)}, u32[]{:S(2)}, u32[]{:S(2)}) collective-permute-start(f32[32,1024]{1,0:T(8,128)S(1)} %get-tuple-element.82), channel_id=1, source_target_pairs={{0,24},{1,11},{2,8},{3,27},{4,28},{5,15},{6,12},{7,31},{8,2},{9,17... | collective-permute-start | bytes 393224 | tf_op jit(solution)/shard_map/ppermute | solution.py:50
  42.7 1.6 %collective-permute-start.34 = (f32[32,1024]{1,0:T(8,128)S(1)}, f32[32,1024]{1,0:T(8,128)S(1)}, u32[]{:S(2)}, u32[]{:S(2)}) collective-permute-start(f32[32,1024]{1,0:T(8,128)S(1)} %get-tuple-element.93), channel_id=1, source_target_pairs={{0,24},{1,11},{2,8},{3,27},{4,28},{5,15},{6,12},{7,31},{8,2},{9,17... | collective-permute-start | bytes 393224 | tf_op jit(solution)/shard_map/ppermute | solution.py:50
  45.1 2.1 %collective-permute-start.28 = (f32[32,1024]{1,0:T(8,128)S(1)}, f32[32,1024]{1,0:T(8,128)S(1)}, u32[]{:S(2)}, u32[]{:S(2)}) collective-permute-start(f32[32,1024]{1,0:T(8,128)S(1)} %add.87), channel_id=1, source_target_pairs={{0,10},{1,25},{2,26},{3,9},{4,14},{5,29},{6,30},{7,13},{8,16},{9,3... | collective-permute-start | bytes 393224 | tf_op jit(solution)/shard_map/ppermute | solution.py:50
  47.3 1.6 %collective-permute-start.39 = (f32[32,1024]{1,0:T(8,128)S(1)}, f32[32,1024]{1,0:T(8,128)S(1)}, u32[]{:S(2)}, u32[]{:S(2)}) collective-permute-start(f32[32,1024]{1,0:T(8,128)S(1)} %add.93), channel_id=1, source_target_pairs={{0,9},{1,25},{2,26},{3,10},{4,13},{5,29},{6,30},{7,14},{8,16},{9,0... | collective-permute-start | bytes 393224 | tf_op jit(solution)/shard_map/ppermute | solution.py:50
  48.9 1.8 %collective-permute-start.35 = (f32[32,1024]{1,0:T(8,128)S(1)}, f32[32,1024]{1,0:T(8,128)S(1)}, u32[]{:S(2)}, u32[]{:S(2)}) collective-permute-start(f32[32,1024]{1,0:T(8,128)S(1)} %add.90), channel_id=1, source_target_pairs={{0,10},{1,8},{2,11},{3,9},{4,14},{5,12},{6,15},{7,13},{8,1},{9,3},... | collective-permute-start | bytes 393224 | tf_op jit(solution)/shard_map/ppermute | solution.py:50
  50.7 1.5 %collective-permute-start.29 = (f32[32,1024]{1,0:T(8,128)S(1)}, f32[32,1024]{1,0:T(8,128)S(1)}, u32[]{:S(2)}, u32[]{:S(2)}) collective-permute-start(f32[32,1024]{1,0:T(8,128)S(1)} %add.88), channel_id=1, source_target_pairs={{0,24},{1,11},{2,8},{3,27},{4,28},{5,15},{6,12},{7,31},{8,2},{9,17... | collective-permute-start | bytes 393224 | tf_op jit(solution)/shard_map/ppermute | solution.py:50
  52.2 0.9 %collective-permute-start.25 = (f32[32,1024]{1,0:T(8,128)S(1)}, f32[32,1024]{1,0:T(8,128)S(1)}, u32[]{:S(2)}, u32[]{:S(2)}) collective-permute-start(f32[32,1024]{1,0:T(8,128)S(1)} %add.85), channel_id=1, source_target_pairs={{0,9},{1,25},{2,26},{3,10},{4,13},{5,29},{6,30},{7,14},{8,16},{9,0... | collective-permute-start | bytes 393224 | tf_op jit(solution)/shard_map/ppermute | solution.py:50
  53.2 1.6 %collective-permute-start.40 = (f32[32,1024]{1,0:T(8,128)S(1)}, f32[32,1024]{1,0:T(8,128)S(1)}, u32[]{:S(2)}, u32[]{:S(2)}) collective-permute-start(f32[32,1024]{1,0:T(8,128)S(1)} %add.94), channel_id=1, source_target_pairs={{0,10},{1,11},{2,8},{3,9},{4,14},{5,15},{6,12},{7,13},{8,2},{9,3},... | collective-permute-start | bytes 393224 | tf_op jit(solution)/shard_map/ppermute | solution.py:50
  54.8 1.0 %collective-permute-start.36 = (f32[32,1024]{1,0:T(8,128)S(1)}, f32[32,1024]{1,0:T(8,128)S(1)}, u32[]{:S(2)}, u32[]{:S(2)}) collective-permute-start(f32[32,1024]{1,0:T(8,128)S(1)} %add.91), channel_id=1, source_target_pairs={{0,9},{1,25},{2,26},{3,10},{4,13},{5,29},{6,30},{7,14},{8,16},{9,0... | collective-permute-start | bytes 393224 | tf_op jit(solution)/shard_map/ppermute | solution.py:50
  55.9 1.2 %collective-permute-start.30 = (f32[32,1024]{1,0:T(8,128)S(1)}, f32[32,1024]{1,0:T(8,128)S(1)}, u32[]{:S(2)}, u32[]{:S(2)}) collective-permute-start(f32[32,1024]{1,0:T(8,128)S(1)} %add.89.own_ref), channel_id=1, source_target_pairs={{0,9},{1,8},{2,11},{3,10},{4,13},{5,12},{6,15},{7,14},{8,1},{9,0},... | collective-permute-start | bytes 393224 | tf_op jit(solution)/shard_map/ppermute | solution.py:50
  57.1 1.3 %collective-permute-start.26 = (f32[32,1024]{1,0:T(8,128)S(1)}, f32[32,1024]{1,0:T(8,128)S(1)}, u32[]{:S(2)}, u32[]{:S(2)}) collective-permute-start(f32[32,1024]{1,0:T(8,128)S(1)} %add.86.own_ref), channel_id=1, source_target_pairs={{0,24},{1,11},{2,8},{3,27},{4,28},{5,15},{6,12},{7,31},{8,2},{9,17... | collective-permute-start | bytes 393224 | tf_op jit(solution)/shard_map/ppermute | solution.py:50
  58.8 1.5 %collective-permute-start.41 = (f32[32,1024]{1,0:T(8,128)S(1)}, f32[32,1024]{1,0:T(8,128)S(1)}, u32[]{:S(2)}, u32[]{:S(2)}) collective-permute-start(f32[32,1024]{1,0:T(8,128)S(1)} %add.95.own_ref), channel_id=1, source_target_pairs={{0,24},{1,8},{2,11},{3,27},{4,28},{5,12},{6,15},{7,31},{8,1},{9,17... | collective-permute-start | bytes 393224 | tf_op jit(solution)/shard_map/ppermute | solution.py:50
  60.3 2.0 %collective-permute-start.37 = (f32[32,1024]{1,0:T(8,128)S(1)}, f32[32,1024]{1,0:T(8,128)S(1)}, u32[]{:S(2)}, u32[]{:S(2)}) collective-permute-start(f32[32,1024]{1,0:T(8,128)S(1)} %add.92.own_ref), channel_id=1, source_target_pairs={{0,24},{1,11},{2,8},{3,27},{4,28},{5,15},{6,12},{7,31},{8,2},{9,17... | collective-permute-start | bytes 393224 | tf_op jit(solution)/shard_map/ppermute | solution.py:50
  65.0 1.2 %shard_map.76 = (f32[256,1024]{1,0:T(8,128)}, f32[256,1024]{1,0:T(8,128)}) custom-call(f32[64,1024]{1,0:T(8,128)S(1)} %shard_map.70.refs_0_, f32[64,1024]{1,0:T(8,128)S(1)} %shard_map.71.refs_1_, f32[64,1024]{1,0:T(8,128)S(1)} %collective-permute-done.31.refs_2_, f32[64,1024]{1,0:T(8,128)S(1)} %collective-permute-done.32.refs_3_, ...), custom_call_target="tpu_custom_call" | custom-call | tf_op jit(solution)/shard_map/pallas_call | solution.py:142
  (100 shorter events, 16.1 us)
Async XLA Ops:
  6.1 5.2 %collective-permute-start.11 = (f32[128,1024]{1,0:T(8,128)S(1)}, f32[128,1024]{1,0:T(8,128)S(1)}, u32[]{:S(2)}, u32[]{:S(2)}) collective-permute-start(f32[128,1024]{1,0:T(8,128)S(1)} %get-tuple-element.74), channel_id=1, source_target_pairs={{0,8},{1,9},{2,10},{3,11},{4,12},{5,13},{6,14},{7,15},{8,0},{9,1},... | collective-permute-start | bytes 1572872 | tf_op jit(solution)/shard_map/ppermute | solution.py:50
  7.1 6.6 %collective-permute-start.5 = (f32[32,1024]{1,0:T(8,128)S(1)}, f32[32,1024]{1,0:T(8,128)S(1)}, u32[]{:S(2)}, u32[]{:S(2)}) collective-permute-start(f32[32,1024]{1,0:T(8,128)S(1)} %get-tuple-element.64), channel_id=1, source_target_pairs={{0,9},{1,8},{2,11},{3,10},{4,13},{5,12},{6,15},{7,14},{8,1},{9,0},... | collective-permute-start | bytes 393224 | tf_op jit(solution)/shard_map/ppermute | solution.py:50
  9.8 6.2 %collective-permute-start.1 = (f32[32,1024]{1,0:T(8,128)S(1)}, f32[32,1024]{1,0:T(8,128)S(1)}, u32[]{:S(2)}, u32[]{:S(2)}) collective-permute-start(f32[32,1024]{1,0:T(8,128)S(1)} %get-tuple-element.62), channel_id=1, source_target_pairs={{0,24},{1,11},{2,8},{3,27},{4,28},{5,15},{6,12},{7,31},{8,2},{9,17... | collective-permute-start | bytes 393224 | tf_op jit(solution)/shard_map/ppermute | solution.py:50
  11.3 4.8 %collective-permute-start.16 = (f32[32,1024]{1,0:T(8,128)S(1)}, f32[32,1024]{1,0:T(8,128)S(1)}, u32[]{:S(2)}, u32[]{:S(2)}) collective-permute-start(f32[32,1024]{1,0:T(8,128)S(1)} %get-tuple-element.78), channel_id=1, source_target_pairs={{0,24},{1,8},{2,11},{3,27},{4,28},{5,12},{6,15},{7,31},{8,1},{9,17... | collective-permute-start | bytes 393224 | tf_op jit(solution)/shard_map/ppermute | solution.py:50
  11.7 6.2 %collective-permute-start.12 = (f32[32,1024]{1,0:T(8,128)S(1)}, f32[32,1024]{1,0:T(8,128)S(1)}, u32[]{:S(2)}, u32[]{:S(2)}) collective-permute-start(f32[32,1024]{1,0:T(8,128)S(1)} %get-tuple-element.76), channel_id=1, source_target_pairs={{0,24},{1,11},{2,8},{3,27},{4,28},{5,15},{6,12},{7,31},{8,2},{9,17... | collective-permute-start | bytes 393224 | tf_op jit(solution)/shard_map/ppermute | solution.py:50
  13.7 5.7 %collective-permute-start.6 = (f32[32,1024]{1,0:T(8,128)S(1)}, f32[32,1024]{1,0:T(8,128)S(1)}, u32[]{:S(2)}, u32[]{:S(2)}) collective-permute-start(f32[32,1024]{1,0:T(8,128)S(1)} %add.75), channel_id=1, source_target_pairs={{0,10},{1,25},{2,26},{3,9},{4,14},{5,29},{6,30},{7,13},{8,16},{9,3... | collective-permute-start | bytes 393224 | tf_op jit(solution)/shard_map/ppermute | solution.py:50
  16.1 4.8 %collective-permute-start.2 = (f32[32,1024]{1,0:T(8,128)S(1)}, f32[32,1024]{1,0:T(8,128)S(1)}, u32[]{:S(2)}, u32[]{:S(2)}) collective-permute-start(f32[32,1024]{1,0:T(8,128)S(1)} %add.72), channel_id=1, source_target_pairs={{0,10},{1,8},{2,11},{3,9},{4,14},{5,12},{6,15},{7,13},{8,1},{9,3},... | collective-permute-start | bytes 393224 | tf_op jit(solution)/shard_map/ppermute | solution.py:50
  16.2 6.0 %collective-permute-start.17 = (f32[32,1024]{1,0:T(8,128)S(1)}, f32[32,1024]{1,0:T(8,128)S(1)}, u32[]{:S(2)}, u32[]{:S(2)}) collective-permute-start(f32[32,1024]{1,0:T(8,128)S(1)} %add.81), channel_id=1, source_target_pairs={{0,9},{1,25},{2,26},{3,10},{4,13},{5,29},{6,30},{7,14},{8,16},{9,0... | collective-permute-start | bytes 393224 | tf_op jit(solution)/shard_map/ppermute | solution.py:50
  17.9 5.8 %collective-permute-start.13 = (f32[32,1024]{1,0:T(8,128)S(1)}, f32[32,1024]{1,0:T(8,128)S(1)}, u32[]{:S(2)}, u32[]{:S(2)}) collective-permute-start(f32[32,1024]{1,0:T(8,128)S(1)} %add.78), channel_id=1, source_target_pairs={{0,10},{1,8},{2,11},{3,9},{4,14},{5,12},{6,15},{7,13},{8,1},{9,3},... | collective-permute-start | bytes 393224 | tf_op jit(solution)/shard_map/ppermute | solution.py:50
  19.4 5.4 %collective-permute-start.7 = (f32[32,1024]{1,0:T(8,128)S(1)}, f32[32,1024]{1,0:T(8,128)S(1)}, u32[]{:S(2)}, u32[]{:S(2)}) collective-permute-start(f32[32,1024]{1,0:T(8,128)S(1)} %add.76), channel_id=1, source_target_pairs={{0,24},{1,11},{2,8},{3,27},{4,28},{5,15},{6,12},{7,31},{8,2},{9,17... | collective-permute-start | bytes 393224 | tf_op jit(solution)/shard_map/ppermute | solution.py:50
  20.9 5.3 %collective-permute-start.3 = (f32[32,1024]{1,0:T(8,128)S(1)}, f32[32,1024]{1,0:T(8,128)S(1)}, u32[]{:S(2)}, u32[]{:S(2)}) collective-permute-start(f32[32,1024]{1,0:T(8,128)S(1)} %add.73), channel_id=1, source_target_pairs={{0,9},{1,25},{2,26},{3,10},{4,13},{5,29},{6,30},{7,14},{8,16},{9,0... | collective-permute-start | bytes 393224 | tf_op jit(solution)/shard_map/ppermute | solution.py:50
  22.2 5.6 %collective-permute-start.18 = (f32[32,1024]{1,0:T(8,128)S(1)}, f32[32,1024]{1,0:T(8,128)S(1)}, u32[]{:S(2)}, u32[]{:S(2)}) collective-permute-start(f32[32,1024]{1,0:T(8,128)S(1)} %add.82), channel_id=1, source_target_pairs={{0,10},{1,11},{2,8},{3,9},{4,14},{5,15},{6,12},{7,13},{8,2},{9,3},... | collective-permute-start | bytes 393224 | tf_op jit(solution)/shard_map/ppermute | solution.py:50
  23.8 5.3 %collective-permute-start.14 = (f32[32,1024]{1,0:T(8,128)S(1)}, f32[32,1024]{1,0:T(8,128)S(1)}, u32[]{:S(2)}, u32[]{:S(2)}) collective-permute-start(f32[32,1024]{1,0:T(8,128)S(1)} %add.79), channel_id=1, source_target_pairs={{0,9},{1,25},{2,26},{3,10},{4,13},{5,29},{6,30},{7,14},{8,16},{9,0... | collective-permute-start | bytes 393224 | tf_op jit(solution)/shard_map/ppermute | solution.py:50
  24.8 6.4 %collective-permute-start.8 = (f32[32,1024]{1,0:T(8,128)S(1)}, f32[32,1024]{1,0:T(8,128)S(1)}, u32[]{:S(2)}, u32[]{:S(2)}) collective-permute-start(f32[32,1024]{1,0:T(8,128)S(1)} %add.77.own_ref), channel_id=1, source_target_pairs={{0,9},{1,8},{2,11},{3,10},{4,13},{5,12},{6,15},{7,14},{8,1},{9,0},... | collective-permute-start | bytes 393224 | tf_op jit(solution)/shard_map/ppermute | solution.py:50
  26.2 5.2 %collective-permute-start.4 = (f32[32,1024]{1,0:T(8,128)S(1)}, f32[32,1024]{1,0:T(8,128)S(1)}, u32[]{:S(2)}, u32[]{:S(2)}) collective-permute-start(f32[32,1024]{1,0:T(8,128)S(1)} %add.74.own_ref), channel_id=1, source_target_pairs={{0,24},{1,11},{2,8},{3,27},{4,28},{5,15},{6,12},{7,31},{8,2},{9,17... | collective-permute-start | bytes 393224 | tf_op jit(solution)/shard_map/ppermute | solution.py:50
  27.8 4.5 %collective-permute-start.19 = (f32[32,1024]{1,0:T(8,128)S(1)}, f32[32,1024]{1,0:T(8,128)S(1)}, u32[]{:S(2)}, u32[]{:S(2)}) collective-permute-start(f32[32,1024]{1,0:T(8,128)S(1)} %add.83.own_ref), channel_id=1, source_target_pairs={{0,24},{1,8},{2,11},{3,27},{4,28},{5,12},{6,15},{7,31},{8,1},{9,17... | collective-permute-start | bytes 393224 | tf_op jit(solution)/shard_map/ppermute | solution.py:50
  29.1 4.8 %collective-permute-start.15 = (f32[32,1024]{1,0:T(8,128)S(1)}, f32[32,1024]{1,0:T(8,128)S(1)}, u32[]{:S(2)}, u32[]{:S(2)}) collective-permute-start(f32[32,1024]{1,0:T(8,128)S(1)} %add.80.own_ref), channel_id=1, source_target_pairs={{0,24},{1,11},{2,8},{3,27},{4,28},{5,15},{6,12},{7,31},{8,2},{9,17... | collective-permute-start | bytes 393224 | tf_op jit(solution)/shard_map/ppermute | solution.py:50
  39.6 5.5 %collective-permute-start.27 = (f32[32,1024]{1,0:T(8,128)S(1)}, f32[32,1024]{1,0:T(8,128)S(1)}, u32[]{:S(2)}, u32[]{:S(2)}) collective-permute-start(f32[32,1024]{1,0:T(8,128)S(1)} %get-tuple-element.84), channel_id=1, source_target_pairs={{0,9},{1,8},{2,11},{3,10},{4,13},{5,12},{6,15},{7,14},{8,1},{9,0},... | collective-permute-start | bytes 393224 | tf_op jit(solution)/shard_map/ppermute | solution.py:50
  40.8 6.3 %collective-permute-start.23 = (f32[32,1024]{1,0:T(8,128)S(1)}, f32[32,1024]{1,0:T(8,128)S(1)}, u32[]{:S(2)}, u32[]{:S(2)}) collective-permute-start(f32[32,1024]{1,0:T(8,128)S(1)} %get-tuple-element.82), channel_id=1, source_target_pairs={{0,24},{1,11},{2,8},{3,27},{4,28},{5,15},{6,12},{7,31},{8,2},{9,17... | collective-permute-start | bytes 393224 | tf_op jit(solution)/shard_map/ppermute | solution.py:50
  42.5 4.8 %collective-permute-start.38 = (f32[32,1024]{1,0:T(8,128)S(1)}, f32[32,1024]{1,0:T(8,128)S(1)}, u32[]{:S(2)}, u32[]{:S(2)}) collective-permute-start(f32[32,1024]{1,0:T(8,128)S(1)} %get-tuple-element.95), channel_id=1, source_target_pairs={{0,24},{1,8},{2,11},{3,27},{4,28},{5,12},{6,15},{7,31},{8,1},{9,17... | collective-permute-start | bytes 393224 | tf_op jit(solution)/shard_map/ppermute | solution.py:50
  42.7 6.2 %collective-permute-start.34 = (f32[32,1024]{1,0:T(8,128)S(1)}, f32[32,1024]{1,0:T(8,128)S(1)}, u32[]{:S(2)}, u32[]{:S(2)}) collective-permute-start(f32[32,1024]{1,0:T(8,128)S(1)} %get-tuple-element.93), channel_id=1, source_target_pairs={{0,24},{1,11},{2,8},{3,27},{4,28},{5,15},{6,12},{7,31},{8,2},{9,17... | collective-permute-start | bytes 393224 | tf_op jit(solution)/shard_map/ppermute | solution.py:50
  45.1 5.6 %collective-permute-start.28 = (f32[32,1024]{1,0:T(8,128)S(1)}, f32[32,1024]{1,0:T(8,128)S(1)}, u32[]{:S(2)}, u32[]{:S(2)}) collective-permute-start(f32[32,1024]{1,0:T(8,128)S(1)} %add.87), channel_id=1, source_target_pairs={{0,10},{1,25},{2,26},{3,9},{4,14},{5,29},{6,30},{7,13},{8,16},{9,3... | collective-permute-start | bytes 393224 | tf_op jit(solution)/shard_map/ppermute | solution.py:50
  47.2 5.1 %collective-permute-start.24 = (f32[32,1024]{1,0:T(8,128)S(1)}, f32[32,1024]{1,0:T(8,128)S(1)}, u32[]{:S(2)}, u32[]{:S(2)}) collective-permute-start(f32[32,1024]{1,0:T(8,128)S(1)} %add.84), channel_id=1, source_target_pairs={{0,10},{1,8},{2,11},{3,9},{4,14},{5,12},{6,15},{7,13},{8,1},{9,3},... | collective-permute-start | bytes 393224 | tf_op jit(solution)/shard_map/ppermute | solution.py:50
  47.3 5.9 %collective-permute-start.39 = (f32[32,1024]{1,0:T(8,128)S(1)}, f32[32,1024]{1,0:T(8,128)S(1)}, u32[]{:S(2)}, u32[]{:S(2)}) collective-permute-start(f32[32,1024]{1,0:T(8,128)S(1)} %add.93), channel_id=1, source_target_pairs={{0,9},{1,25},{2,26},{3,10},{4,13},{5,29},{6,30},{7,14},{8,16},{9,0... | collective-permute-start | bytes 393224 | tf_op jit(solution)/shard_map/ppermute | solution.py:50
  48.9 5.9 %collective-permute-start.35 = (f32[32,1024]{1,0:T(8,128)S(1)}, f32[32,1024]{1,0:T(8,128)S(1)}, u32[]{:S(2)}, u32[]{:S(2)}) collective-permute-start(f32[32,1024]{1,0:T(8,128)S(1)} %add.90), channel_id=1, source_target_pairs={{0,10},{1,8},{2,11},{3,9},{4,14},{5,12},{6,15},{7,13},{8,1},{9,3},... | collective-permute-start | bytes 393224 | tf_op jit(solution)/shard_map/ppermute | solution.py:50
  50.7 5.1 %collective-permute-start.29 = (f32[32,1024]{1,0:T(8,128)S(1)}, f32[32,1024]{1,0:T(8,128)S(1)}, u32[]{:S(2)}, u32[]{:S(2)}) collective-permute-start(f32[32,1024]{1,0:T(8,128)S(1)} %add.88), channel_id=1, source_target_pairs={{0,24},{1,11},{2,8},{3,27},{4,28},{5,15},{6,12},{7,31},{8,2},{9,17... | collective-permute-start | bytes 393224 | tf_op jit(solution)/shard_map/ppermute | solution.py:50
  52.2 4.9 %collective-permute-start.25 = (f32[32,1024]{1,0:T(8,128)S(1)}, f32[32,1024]{1,0:T(8,128)S(1)}, u32[]{:S(2)}, u32[]{:S(2)}) collective-permute-start(f32[32,1024]{1,0:T(8,128)S(1)} %add.85), channel_id=1, source_target_pairs={{0,9},{1,25},{2,26},{3,10},{4,13},{5,29},{6,30},{7,14},{8,16},{9,0... | collective-permute-start | bytes 393224 | tf_op jit(solution)/shard_map/ppermute | solution.py:50
  53.2 5.6 %collective-permute-start.40 = (f32[32,1024]{1,0:T(8,128)S(1)}, f32[32,1024]{1,0:T(8,128)S(1)}, u32[]{:S(2)}, u32[]{:S(2)}) collective-permute-start(f32[32,1024]{1,0:T(8,128)S(1)} %add.94), channel_id=1, source_target_pairs={{0,10},{1,11},{2,8},{3,9},{4,14},{5,15},{6,12},{7,13},{8,2},{9,3},... | collective-permute-start | bytes 393224 | tf_op jit(solution)/shard_map/ppermute | solution.py:50
  54.8 5.5 %collective-permute-start.36 = (f32[32,1024]{1,0:T(8,128)S(1)}, f32[32,1024]{1,0:T(8,128)S(1)}, u32[]{:S(2)}, u32[]{:S(2)}) collective-permute-start(f32[32,1024]{1,0:T(8,128)S(1)} %add.91), channel_id=1, source_target_pairs={{0,9},{1,25},{2,26},{3,10},{4,13},{5,29},{6,30},{7,14},{8,16},{9,0... | collective-permute-start | bytes 393224 | tf_op jit(solution)/shard_map/ppermute | solution.py:50
  55.9 6.3 %collective-permute-start.30 = (f32[32,1024]{1,0:T(8,128)S(1)}, f32[32,1024]{1,0:T(8,128)S(1)}, u32[]{:S(2)}, u32[]{:S(2)}) collective-permute-start(f32[32,1024]{1,0:T(8,128)S(1)} %add.89.own_ref), channel_id=1, source_target_pairs={{0,9},{1,8},{2,11},{3,10},{4,13},{5,12},{6,15},{7,14},{8,1},{9,0},... | collective-permute-start | bytes 393224 | tf_op jit(solution)/shard_map/ppermute | solution.py:50
  57.1 5.2 %collective-permute-start.26 = (f32[32,1024]{1,0:T(8,128)S(1)}, f32[32,1024]{1,0:T(8,128)S(1)}, u32[]{:S(2)}, u32[]{:S(2)}) collective-permute-start(f32[32,1024]{1,0:T(8,128)S(1)} %add.86.own_ref), channel_id=1, source_target_pairs={{0,24},{1,11},{2,8},{3,27},{4,28},{5,15},{6,12},{7,31},{8,2},{9,17... | collective-permute-start | bytes 393224 | tf_op jit(solution)/shard_map/ppermute | solution.py:50
  60.3 4.6 %collective-permute-start.37 = (f32[32,1024]{1,0:T(8,128)S(1)}, f32[32,1024]{1,0:T(8,128)S(1)}, u32[]{:S(2)}, u32[]{:S(2)}) collective-permute-start(f32[32,1024]{1,0:T(8,128)S(1)} %add.92.own_ref), channel_id=1, source_target_pairs={{0,24},{1,11},{2,8},{3,27},{4,28},{5,15},{6,12},{7,31},{8,2},{9,17... | collective-permute-start | bytes 393224 | tf_op jit(solution)/shard_map/ppermute | solution.py:50
  (12 other events, 32.3 us)

commit v7 on v6

--- a/solution.py
+++ b/solution.py
@@ -212,18 +212,20 @@
 
 
 def first_hidden_kernel(x_in, g_in, r_in, e_in, *refs):
-    outs, (r_ref, e_ref, x_ref, g_ref, sems) = refs[:5], refs[5:]
+    outs, (r_ref, e_ref), acts_refs, sems = refs[:5], refs[5:7], refs[7:-1], refs[-1]
     moves = []
     for columns in in_columns(r_ref.shape[1]):
-        moves += [(r_in.at[:, columns], r_ref.at[:, columns]), (x_in.at[0, :, columns], x_ref.at[:, columns])]
-    copies = start_copies(moves + [(e_in, e_ref), (g_in.at[0], g_ref)], sems)
+        moves += [(r_in.at[:, columns], r_ref.at[:, columns]), (x_in.at[0, :, columns], acts_refs[0].at[:, columns])]
+    early = len(moves)
+    later = [(source.at[i // 2], ref) for i, (source, ref) in enumerate(zip((x_in, g_in) * len(acts_refs), acts_refs))]
+    copies = start_copies(moves + [(e_in, e_ref)] + later[1:], sems)
 
     def arrived(i):
         copies[2 * i].wait()
         copies[2 * i + 1].wait()
 
-    hidden_of(r_ref, x_ref, outs, arrived)
-    for copy in copies[len(moves) :]:
+    hidden_of(r_ref, acts_refs[0], outs, arrived)
+    for copy in copies[early:]:
         copy.wait()
 
 
@@ -234,12 +236,7 @@
     hidden_of(r_ref, x_ref, outs, lambda i: None)
 
 
-def reduce_kernel(joined, upcoming, x_ref, g_ref, r_ref, slope_ref, hidden_high_ref, hidden_low_ref, *refs):
-    copies = []
-    if upcoming is not None:
-        x_in, g_in, *refs, next_x_ref, next_g_ref, high_ref, low_ref, sems = refs
-        copies = start_copies([(x_in.at[upcoming], next_x_ref), (g_in.at[upcoming], next_g_ref)], sems)
-        refs = [*refs, high_ref, low_ref]
+def reduce_kernel(joined, x_ref, g_ref, r_ref, slope_ref, hidden_high_ref, hidden_low_ref, *refs):
     if joined:
         *parts, keep_ref, send_ref, zh_ref, zl_ref, e_ref, high_ref, low_ref = refs
         put_together(parts, EXPAND_CHAINS, e_ref)
@@ -270,8 +267,6 @@
     for columns in blocks:
         step = product((high_ref[...], low_ref[...]), (x_ref[:, columns],), NN) * (learn_rate * reduce_scale)
         step_columns(role, columns, r_ref, step, keep_ref, send_ref)
-    for copy in copies:
-        copy.wait()
 
 
 def expand_kernel(e_ref, zh_ref, zl_ref, hidden_high_ref, hidden_low_ref, keep_ref, send_ref):
@@ -296,31 +291,31 @@
     )
     weights = jax.ShapeDtypeStruct((width, columns), f32)
     narrow = jax.ShapeDtypeStruct((width, columns), bf16)
-    *hidden, reducing, expanding, feats, grads = pl.pallas_call(
+    results = pl.pallas_call(
         first_hidden_kernel,
-        out_shape=hidden_shapes + [narrow] * 2 + [acts] * 2,
+        out_shape=hidden_shapes + [narrow] * 2 + [acts] * (2 * iterations),
         in_specs=[HBM] * 4,
-        out_specs=[VMEM] * 9,
-        scratch_shapes=[pltpu.SemaphoreType.DMA((2 * columns // BLOCK + 2,))],
+        out_specs=[VMEM] * (7 + 2 * iterations),
+        scratch_shapes=[pltpu.SemaphoreType.DMA((2 * columns // BLOCK + 2 * iterations,))],
         compiler_params=LARGE,
         name="hidden_0",
     )(*held)
+    hidden, (reducing, expanding), acts_of = results[:5], results[5:7], results[7:]
     for iteration in range(iterations):
         first, last = iteration == 0, iteration == iterations - 1
+        feats, grads = acts_of[2 * iteration : 2 * iteration + 2]
         slope, high_t, low_t, high, low = hidden
         weights_in = [expanding] if first else expanding
-        keep_r, send_r, zh, zl, *more = pl.pallas_call(
-            functools.partial(reduce_kernel, not first, None if last else iteration + 1),
-            out_shape=[half, half, acts, acts] + ([] if first else [weights]) + ([] if last else [acts] * 2),
-            in_specs=[VMEM] * 6 + ([] if last else [HBM] * 2) + [VMEM] * len(weights_in),
-            out_specs=[VMEM] * (4 + (not first) + 2 * (not last)),
-            scratch_shapes=[pltpu.VMEM((width, rows), bf16)] * 2 + ([] if last else [pltpu.SemaphoreType.DMA((2,))]),
+        keep_r, send_r, zh, zl, *joined = pl.pallas_call(
+            functools.partial(reduce_kernel, not first),
+            out_shape=[half, half, acts, acts] + ([] if first else [weights]),
+            in_specs=[VMEM] * (6 + len(weights_in)),
+            out_specs=[VMEM] * (4 if first else 5),
+            scratch_shapes=[pltpu.VMEM((width, rows), bf16)] * 2,
             compiler_params=LARGE,
-        )(feats, grads, reducing, slope, high, low, *([] if last else held[:2]), *weights_in)
-        if not first:
-            expanding = more.pop(0)
-        if not last:
-            feats, grads = more
+        )(feats, grads, reducing, slope, high, low, *weights_in)
+        if joined:
+            (expanding,) = joined
         keep_e, send_e = pl.pallas_call(
             expand_kernel, out_shape=[half, half], in_specs=[VMEM] * 5, out_specs=[VMEM] * 2, compiler_params=LARGE
         )(expanding, zh, zl, high_t, low_t)
@@ -340,7 +335,7 @@
                 in_specs=[VMEM] * (1 + len(sums_r)),
                 out_specs=[VMEM] * 6,
                 compiler_params=LARGE,
-            )(feats, *sums_r)
+            )(acts_of[2 * iteration + 2], *sums_r)
     over = tuple(range(len(EXPAND_CHAINS), len(expanding)))
     (new_expand,) = store([([expanding[i] for i in over], EXPAND_CHAINS, over, width // 2)], [new_expand])
     return new_reduce[None, None], new_expand[None, None]

time: 67.5 us -> 66.9 us (level)
  no operation moved by 1% of the time
where the time goes in v7:
time: 66.9 us; the launch traced here: 66.7 us
  starting transfers between devices  47.8 us (71%)
  Pallas kernels  10 us (15%)
  waiting for transfers between devices  7.52 us (11%)
  between operations  0.94 us (1%)
    ppermute x44, starting transfers between devices, from_partner(): return lax.ppermute(values, ('near', 'far'), pairs)  47.8 us
    ppermute x44, waiting for transfers between devices, from_partner(): return lax.ppermute(values, ('near', 'far'), pairs)  7.52 us
    pallas_call x2, Pallas kernels, shards(): pl.pallas_call(functools.partial(reduce_kernel, not first), out_shape=[ha...  3.69 us
    pallas_call x1, Pallas kernels, shards(): pl.pallas_call(first_hidden_kernel, out_shape=hidden_shapes + [narrow] *...  2.06 us
    pallas_call x2, Pallas kernels, store(): pl.pallas_call(functools.partial(store_kernel, counted), out_shape=[jax.S...  2 us
  transfers between devices with their start and end apart: 44, of which 13 were waited for; matrix products, arithmetic and copies ran while one was open for 1% of the time, Pallas kernels for 5%

profile of v7, /device:TPU:0, one launch (start us, length us, event | category | flops | bytes accessed | tf_op | source)
XLA Modules:
  0.0 66.7 jit_solution(1308472670055520636)
XLA Ops:
  0.6 2.1 %hidden_0.1 = (f32[256,256]{1,0:T(8,128)S(1)}, bf16[256,256]{1,0:T(8,128)(2,1)S(1)}, bf16[256,256]{1,0:T(8,128)(2,1)S(1)}, bf16[256,256]{1,0:T(8,128)(2,1)S(1)},...) custom-call(bf16[2,256,1024]{2,1,0:T(8,128)(2,1)} %bitcast.6, ...), custom_call_target="tpu_custom_call" | custom-call | tf_op jit(solution)/shard_map/hidden_0/pallas_call | solution.py:294
  2.7 1.7 %shard_map.59 = (f32[128,1024]{1,0:T(8,128)S(1)}, f32[128,1024]{1,0:T(8,128)S(1)}, bf16[256,1024]{1,0:T(8,128)(2,1)S(1)}, bf16[256,1024]{1,0:T(8,128)(2,1)S(1)}) custom-call(bf16[256,1024]{1,0:T(8,128)(2,1)S(1)} %get-tuple-element.52.x_ref, bf16[256,1024]{1,0:T(8,128)(2,1)S(1)} %get-tuple-element.53.g_ref, bf16[256,1024]{1,0:T(8,128)(2,1)S(1)} %get-tuple-element.54.r_ref, ...), custom_call_target="tpu_custom_call" | custom-call | tf_op jit(solution)/shard_map/pallas_call | solution.py:309
  5.6 0.9 %collective-permute-done.got_ref = f32[128,1024]{1,0:T(8,128)S(1)} collective-permute-done((f32[128,1024]{1,0:T(8,128)S(1)}, f32[128,1024]{1,0:T(8,128)S(1)}, u32[]{:S(2)}, u32[]{:S(2)}) %collective-permute-start) | collective-permute-done | bytes 524320 | tf_op jit(solution)/shard_map/ppermute | solution.py:50
  6.5 2.7 %collective-permute-start.5 = (f32[32,1024]{1,0:T(8,128)S(1)}, f32[32,1024]{1,0:T(8,128)S(1)}, u32[]{:S(2)}, u32[]{:S(2)}) collective-permute-start(f32[32,1024]{1,0:T(8,128)S(1)} %get-tuple-element.64), channel_id=1, source_target_pairs={{0,9},{1,8},{2,11},{3,10},{4,13},{5,12},{6,15},{7,14},{8,1},{9,0},... | collective-permute-start | bytes 393224 | tf_op jit(solution)/shard_map/ppermute | solution.py:50
  9.2 1.5 %collective-permute-start.1 = (f32[32,1024]{1,0:T(8,128)S(1)}, f32[32,1024]{1,0:T(8,128)S(1)}, u32[]{:S(2)}, u32[]{:S(2)}) collective-permute-start(f32[32,1024]{1,0:T(8,128)S(1)} %get-tuple-element.62), channel_id=1, source_target_pairs={{0,24},{1,11},{2,8},{3,27},{4,28},{5,15},{6,12},{7,31},{8,2},{9,17... | collective-permute-start | bytes 393224 | tf_op jit(solution)/shard_map/ppermute | solution.py:50
  11.1 1.5 %collective-permute-start.12 = (f32[32,1024]{1,0:T(8,128)S(1)}, f32[32,1024]{1,0:T(8,128)S(1)}, u32[]{:S(2)}, u32[]{:S(2)}) collective-permute-start(f32[32,1024]{1,0:T(8,128)S(1)} %get-tuple-element.76), channel_id=1, source_target_pairs={{0,24},{1,11},{2,8},{3,27},{4,28},{5,15},{6,12},{7,31},{8,2},{9,17... | collective-permute-start | bytes 393224 | tf_op jit(solution)/shard_map/ppermute | solution.py:50
  13.1 2.3 %collective-permute-start.6 = (f32[32,1024]{1,0:T(8,128)S(1)}, f32[32,1024]{1,0:T(8,128)S(1)}, u32[]{:S(2)}, u32[]{:S(2)}) collective-permute-start(f32[32,1024]{1,0:T(8,128)S(1)} %add.75), channel_id=1, source_target_pairs={{0,10},{1,25},{2,26},{3,9},{4,14},{5,29},{6,30},{7,13},{8,16},{9,3... | collective-permute-start | bytes 393224 | tf_op jit(solution)/shard_map/ppermute | solution.py:50
  15.6 1.7 %collective-permute-start.17 = (f32[32,1024]{1,0:T(8,128)S(1)}, f32[32,1024]{1,0:T(8,128)S(1)}, u32[]{:S(2)}, u32[]{:S(2)}) collective-permute-start(f32[32,1024]{1,0:T(8,128)S(1)} %add.81), channel_id=1, source_target_pairs={{0,9},{1,25},{2,26},{3,10},{4,13},{5,29},{6,30},{7,14},{8,16},{9,0... | collective-permute-start | bytes 393224 | tf_op jit(solution)/shard_map/ppermute | solution.py:50
  17.3 1.5 %collective-permute-start.13 = (f32[32,1024]{1,0:T(8,128)S(1)}, f32[32,1024]{1,0:T(8,128)S(1)}, u32[]{:S(2)}, u32[]{:S(2)}) collective-permute-start(f32[32,1024]{1,0:T(8,128)S(1)} %add.78), channel_id=1, source_target_pairs={{0,10},{1,8},{2,11},{3,9},{4,14},{5,12},{6,15},{7,13},{8,1},{9,3},... | collective-permute-start | bytes 393224 | tf_op jit(solution)/shard_map/ppermute | solution.py:50
  18.8 1.4 %collective-permute-start.7 = (f32[32,1024]{1,0:T(8,128)S(1)}, f32[32,1024]{1,0:T(8,128)S(1)}, u32[]{:S(2)}, u32[]{:S(2)}) collective-permute-start(f32[32,1024]{1,0:T(8,128)S(1)} %add.76), channel_id=1, source_target_pairs={{0,24},{1,11},{2,8},{3,27},{4,28},{5,15},{6,12},{7,31},{8,2},{9,17... | collective-permute-start | bytes 393224 | tf_op jit(solution)/shard_map/ppermute | solution.py:50
  20.3 1.3 %collective-permute-start.3 = (f32[32,1024]{1,0:T(8,128)S(1)}, f32[32,1024]{1,0:T(8,128)S(1)}, u32[]{:S(2)}, u32[]{:S(2)}) collective-permute-start(f32[32,1024]{1,0:T(8,128)S(1)} %add.73), channel_id=1, source_target_pairs={{0,9},{1,25},{2,26},{3,10},{4,13},{5,29},{6,30},{7,14},{8,16},{9,0... | collective-permute-start | bytes 393224 | tf_op jit(solution)/shard_map/ppermute | solution.py:50
  21.6 1.6 %collective-permute-start.18 = (f32[32,1024]{1,0:T(8,128)S(1)}, f32[32,1024]{1,0:T(8,128)S(1)}, u32[]{:S(2)}, u32[]{:S(2)}) collective-permute-start(f32[32,1024]{1,0:T(8,128)S(1)} %add.82), channel_id=1, source_target_pairs={{0,10},{1,11},{2,8},{3,9},{4,14},{5,15},{6,12},{7,13},{8,2},{9,3},... | collective-permute-start | bytes 393224 | tf_op jit(solution)/shard_map/ppermute | solution.py:50
  23.2 1.0 %collective-permute-start.14 = (f32[32,1024]{1,0:T(8,128)S(1)}, f32[32,1024]{1,0:T(8,128)S(1)}, u32[]{:S(2)}, u32[]{:S(2)}) collective-permute-start(f32[32,1024]{1,0:T(8,128)S(1)} %add.79), channel_id=1, source_target_pairs={{0,9},{1,25},{2,26},{3,10},{4,13},{5,29},{6,30},{7,14},{8,16},{9,0... | collective-permute-start | bytes 393224 | tf_op jit(solution)/shard_map/ppermute | solution.py:50
  24.2 1.3 %collective-permute-start.8 = (f32[32,1024]{1,0:T(8,128)S(1)}, f32[32,1024]{1,0:T(8,128)S(1)}, u32[]{:S(2)}, u32[]{:S(2)}) collective-permute-start(f32[32,1024]{1,0:T(8,128)S(1)} %add.77.own_ref), channel_id=1, source_target_pairs={{0,9},{1,8},{2,11},{3,10},{4,13},{5,12},{6,15},{7,14},{8,1},{9,0},... | collective-permute-start | bytes 393224 | tf_op jit(solution)/shard_map/ppermute | solution.py:50
  25.6 0.9 %collective-permute-start.4 = (f32[32,1024]{1,0:T(8,128)S(1)}, f32[32,1024]{1,0:T(8,128)S(1)}, u32[]{:S(2)}, u32[]{:S(2)}) collective-permute-start(f32[32,1024]{1,0:T(8,128)S(1)} %add.74.own_ref), channel_id=1, source_target_pairs={{0,24},{1,11},{2,8},{3,27},{4,28},{5,15},{6,12},{7,31},{8,2},{9,17... | collective-permute-start | bytes 393224 | tf_op jit(solution)/shard_map/ppermute | solution.py:50
  27.2 1.2 %collective-permute-start.19 = (f32[32,1024]{1,0:T(8,128)S(1)}, f32[32,1024]{1,0:T(8,128)S(1)}, u32[]{:S(2)}, u32[]{:S(2)}) collective-permute-start(f32[32,1024]{1,0:T(8,128)S(1)} %add.83.own_ref), channel_id=1, source_target_pairs={{0,24},{1,8},{2,11},{3,27},{4,28},{5,12},{6,15},{7,31},{8,1},{9,17... | collective-permute-start | bytes 393224 | tf_op jit(solution)/shard_map/ppermute | solution.py:50
  28.5 2.2 %collective-permute-start.15 = (f32[32,1024]{1,0:T(8,128)S(1)}, f32[32,1024]{1,0:T(8,128)S(1)}, u32[]{:S(2)}, u32[]{:S(2)}) collective-permute-start(f32[32,1024]{1,0:T(8,128)S(1)} %add.80.own_ref), channel_id=1, source_target_pairs={{0,24},{1,11},{2,8},{3,27},{4,28},{5,15},{6,12},{7,31},{8,2},{9,17... | collective-permute-start | bytes 393224 | tf_op jit(solution)/shard_map/ppermute | solution.py:50
  34.9 2.0 %shard_map.68 = (f32[128,1024]{1,0:T(8,128)S(1)}, f32[128,1024]{1,0:T(8,128)S(1)}, bf16[256,1024]{1,0:T(8,128)(2,1)S(1)}, bf16[256,1024]{1,0:T(8,128)(2,1)S(1)}, f32[256,1024]{1,0:T(8,128)S(1)}) custom-call(bf16[256,1024]{1,0:T(8,128)(2,1)S(1)} %get-tuple-element.50.x_ref, bf16[256,1024]{1,0:T(8,128)(2,1)S(1)} %get-tuple-element.51.g_ref, ...), custom_call_target="tpu_custom_call" | custom-call | tf_op jit(solution)/shard_map/pallas_call | solution.py:309
  39.0 1.2 %collective-permute-start.27 = (f32[32,1024]{1,0:T(8,128)S(1)}, f32[32,1024]{1,0:T(8,128)S(1)}, u32[]{:S(2)}, u32[]{:S(2)}) collective-permute-start(f32[32,1024]{1,0:T(8,128)S(1)} %get-tuple-element.84), channel_id=1, source_target_pairs={{0,9},{1,8},{2,11},{3,10},{4,13},{5,12},{6,15},{7,14},{8,1},{9,0},... | collective-permute-start | bytes 393224 | tf_op jit(solution)/shard_map/ppermute | solution.py:50
  40.2 1.6 %collective-permute-start.23 = (f32[32,1024]{1,0:T(8,128)S(1)}, f32[32,1024]{1,0:T(8,128)S(1)}, u32[]{:S(2)}, u32[]{:S(2)}) collective-permute-start(f32[32,1024]{1,0:T(8,128)S(1)} %get-tuple-element.82), channel_id=1, source_target_pairs={{0,24},{1,11},{2,8},{3,27},{4,28},{5,15},{6,12},{7,31},{8,2},{9,17... | collective-permute-start | bytes 393224 | tf_op jit(solution)/shard_map/ppermute | solution.py:50
  42.1 1.6 %collective-permute-start.34 = (f32[32,1024]{1,0:T(8,128)S(1)}, f32[32,1024]{1,0:T(8,128)S(1)}, u32[]{:S(2)}, u32[]{:S(2)}) collective-permute-start(f32[32,1024]{1,0:T(8,128)S(1)} %get-tuple-element.93), channel_id=1, source_target_pairs={{0,24},{1,11},{2,8},{3,27},{4,28},{5,15},{6,12},{7,31},{8,2},{9,17... | collective-permute-start | bytes 393224 | tf_op jit(solution)/shard_map/ppermute | solution.py:50
  44.5 2.0 %collective-permute-start.28 = (f32[32,1024]{1,0:T(8,128)S(1)}, f32[32,1024]{1,0:T(8,128)S(1)}, u32[]{:S(2)}, u32[]{:S(2)}) collective-permute-start(f32[32,1024]{1,0:T(8,128)S(1)} %add.87), channel_id=1, source_target_pairs={{0,10},{1,25},{2,26},{3,9},{4,14},{5,29},{6,30},{7,13},{8,16},{9,3... | collective-permute-start | bytes 393224 | tf_op jit(solution)/shard_map/ppermute | solution.py:50
  46.7 1.6 %collective-permute-start.39 = (f32[32,1024]{1,0:T(8,128)S(1)}, f32[32,1024]{1,0:T(8,128)S(1)}, u32[]{:S(2)}, u32[]{:S(2)}) collective-permute-start(f32[32,1024]{1,0:T(8,128)S(1)} %add.93), channel_id=1, source_target_pairs={{0,9},{1,25},{2,26},{3,10},{4,13},{5,29},{6,30},{7,14},{8,16},{9,0... | collective-permute-start | bytes 393224 | tf_op jit(solution)/shard_map/ppermute | solution.py:50
  48.3 1.8 %collective-permute-start.35 = (f32[32,1024]{1,0:T(8,128)S(1)}, f32[32,1024]{1,0:T(8,128)S(1)}, u32[]{:S(2)}, u32[]{:S(2)}) collective-permute-start(f32[32,1024]{1,0:T(8,128)S(1)} %add.90), channel_id=1, source_target_pairs={{0,10},{1,8},{2,11},{3,9},{4,14},{5,12},{6,15},{7,13},{8,1},{9,3},... | collective-permute-start | bytes 393224 | tf_op jit(solution)/shard_map/ppermute | solution.py:50
  50.1 1.5 %collective-permute-start.29 = (f32[32,1024]{1,0:T(8,128)S(1)}, f32[32,1024]{1,0:T(8,128)S(1)}, u32[]{:S(2)}, u32[]{:S(2)}) collective-permute-start(f32[32,1024]{1,0:T(8,128)S(1)} %add.88), channel_id=1, source_target_pairs={{0,24},{1,11},{2,8},{3,27},{4,28},{5,15},{6,12},{7,31},{8,2},{9,17... | collective-permute-start | bytes 393224 | tf_op jit(solution)/shard_map/ppermute | solution.py:50
  52.6 1.6 %collective-permute-start.40 = (f32[32,1024]{1,0:T(8,128)S(1)}, f32[32,1024]{1,0:T(8,128)S(1)}, u32[]{:S(2)}, u32[]{:S(2)}) collective-permute-start(f32[32,1024]{1,0:T(8,128)S(1)} %add.94), channel_id=1, source_target_pairs={{0,10},{1,11},{2,8},{3,9},{4,14},{5,15},{6,12},{7,13},{8,2},{9,3},... | collective-permute-start | bytes 393224 | tf_op jit(solution)/shard_map/ppermute | solution.py:50
  54.2 1.0 %collective-permute-start.36 = (f32[32,1024]{1,0:T(8,128)S(1)}, f32[32,1024]{1,0:T(8,128)S(1)}, u32[]{:S(2)}, u32[]{:S(2)}) collective-permute-start(f32[32,1024]{1,0:T(8,128)S(1)} %add.91), channel_id=1, source_target_pairs={{0,9},{1,25},{2,26},{3,10},{4,13},{5,29},{6,30},{7,14},{8,16},{9,0... | collective-permute-start | bytes 393224 | tf_op jit(solution)/shard_map/ppermute | solution.py:50
  55.4 1.1 %collective-permute-start.30 = (f32[32,1024]{1,0:T(8,128)S(1)}, f32[32,1024]{1,0:T(8,128)S(1)}, u32[]{:S(2)}, u32[]{:S(2)}) collective-permute-start(f32[32,1024]{1,0:T(8,128)S(1)} %add.89.own_ref), channel_id=1, source_target_pairs={{0,9},{1,8},{2,11},{3,10},{4,13},{5,12},{6,15},{7,14},{8,1},{9,0},... | collective-permute-start | bytes 393224 | tf_op jit(solution)/shard_map/ppermute | solution.py:50
  56.5 1.4 %collective-permute-start.26 = (f32[32,1024]{1,0:T(8,128)S(1)}, f32[32,1024]{1,0:T(8,128)S(1)}, u32[]{:S(2)}, u32[]{:S(2)}) collective-permute-start(f32[32,1024]{1,0:T(8,128)S(1)} %add.86.own_ref), channel_id=1, source_target_pairs={{0,24},{1,11},{2,8},{3,27},{4,28},{5,15},{6,12},{7,31},{8,2},{9,17... | collective-permute-start | bytes 393224 | tf_op jit(solution)/shard_map/ppermute | solution.py:50
  58.1 1.6 %collective-permute-start.41 = (f32[32,1024]{1,0:T(8,128)S(1)}, f32[32,1024]{1,0:T(8,128)S(1)}, u32[]{:S(2)}, u32[]{:S(2)}) collective-permute-start(f32[32,1024]{1,0:T(8,128)S(1)} %add.95.own_ref), channel_id=1, source_target_pairs={{0,24},{1,8},{2,11},{3,27},{4,28},{5,12},{6,15},{7,31},{8,1},{9,17... | collective-permute-start | bytes 393224 | tf_op jit(solution)/shard_map/ppermute | solution.py:50
  59.7 1.9 %collective-permute-start.37 = (f32[32,1024]{1,0:T(8,128)S(1)}, f32[32,1024]{1,0:T(8,128)S(1)}, u32[]{:S(2)}, u32[]{:S(2)}) collective-permute-start(f32[32,1024]{1,0:T(8,128)S(1)} %add.92.own_ref), channel_id=1, source_target_pairs={{0,24},{1,11},{2,8},{3,27},{4,28},{5,15},{6,12},{7,31},{8,2},{9,17... | collective-permute-start | bytes 393224 | tf_op jit(solution)/shard_map/ppermute | solution.py:50
  64.4 1.2 %shard_map.76 = (f32[256,1024]{1,0:T(8,128)}, f32[256,1024]{1,0:T(8,128)}) custom-call(f32[64,1024]{1,0:T(8,128)S(1)} %shard_map.70.refs_0_, f32[64,1024]{1,0:T(8,128)S(1)} %shard_map.71.refs_1_, f32[64,1024]{1,0:T(8,128)S(1)} %collective-permute-done.31.refs_2_, f32[64,1024]{1,0:T(8,128)S(1)} %collective-permute-done.32.refs_3_, ...), custom_call_target="tpu_custom_call" | custom-call | tf_op jit(solution)/shard_map/pallas_call | solution.py:142
  (100 shorter events, 16.1 us)
Async XLA Ops:
  5.5 5.2 %collective-permute-start.11 = (f32[128,1024]{1,0:T(8,128)S(1)}, f32[128,1024]{1,0:T(8,128)S(1)}, u32[]{:S(2)}, u32[]{:S(2)}) collective-permute-start(f32[128,1024]{1,0:T(8,128)S(1)} %get-tuple-element.74), channel_id=1, source_target_pairs={{0,8},{1,9},{2,10},{3,11},{4,12},{5,13},{6,14},{7,15},{8,0},{9,1},... | collective-permute-start | bytes 1572872 | tf_op jit(solution)/shard_map/ppermute | solution.py:50
  6.5 6.6 %collective-permute-start.5 = (f32[32,1024]{1,0:T(8,128)S(1)}, f32[32,1024]{1,0:T(8,128)S(1)}, u32[]{:S(2)}, u32[]{:S(2)}) collective-permute-start(f32[32,1024]{1,0:T(8,128)S(1)} %get-tuple-element.64), channel_id=1, source_target_pairs={{0,9},{1,8},{2,11},{3,10},{4,13},{5,12},{6,15},{7,14},{8,1},{9,0},... | collective-permute-start | bytes 393224 | tf_op jit(solution)/shard_map/ppermute | solution.py:50
  9.2 6.2 %collective-permute-start.1 = (f32[32,1024]{1,0:T(8,128)S(1)}, f32[32,1024]{1,0:T(8,128)S(1)}, u32[]{:S(2)}, u32[]{:S(2)}) collective-permute-start(f32[32,1024]{1,0:T(8,128)S(1)} %get-tuple-element.62), channel_id=1, source_target_pairs={{0,24},{1,11},{2,8},{3,27},{4,28},{5,15},{6,12},{7,31},{8,2},{9,17... | collective-permute-start | bytes 393224 | tf_op jit(solution)/shard_map/ppermute | solution.py:50
  10.7 4.8 %collective-permute-start.16 = (f32[32,1024]{1,0:T(8,128)S(1)}, f32[32,1024]{1,0:T(8,128)S(1)}, u32[]{:S(2)}, u32[]{:S(2)}) collective-permute-start(f32[32,1024]{1,0:T(8,128)S(1)} %get-tuple-element.78), channel_id=1, source_target_pairs={{0,24},{1,8},{2,11},{3,27},{4,28},{5,12},{6,15},{7,31},{8,1},{9,17... | collective-permute-start | bytes 393224 | tf_op jit(solution)/shard_map/ppermute | solution.py:50
  11.1 6.2 %collective-permute-start.12 = (f32[32,1024]{1,0:T(8,128)S(1)}, f32[32,1024]{1,0:T(8,128)S(1)}, u32[]{:S(2)}, u32[]{:S(2)}) collective-permute-start(f32[32,1024]{1,0:T(8,128)S(1)} %get-tuple-element.76), channel_id=1, source_target_pairs={{0,24},{1,11},{2,8},{3,27},{4,28},{5,15},{6,12},{7,31},{8,2},{9,17... | collective-permute-start | bytes 393224 | tf_op jit(solution)/shard_map/ppermute | solution.py:50
  13.1 5.7 %collective-permute-start.6 = (f32[32,1024]{1,0:T(8,128)S(1)}, f32[32,1024]{1,0:T(8,128)S(1)}, u32[]{:S(2)}, u32[]{:S(2)}) collective-permute-start(f32[32,1024]{1,0:T(8,128)S(1)} %add.75), channel_id=1, source_target_pairs={{0,10},{1,25},{2,26},{3,9},{4,14},{5,29},{6,30},{7,13},{8,16},{9,3... | collective-permute-start | bytes 393224 | tf_op jit(solution)/shard_map/ppermute | solution.py:50
  15.5 4.8 %collective-permute-start.2 = (f32[32,1024]{1,0:T(8,128)S(1)}, f32[32,1024]{1,0:T(8,128)S(1)}, u32[]{:S(2)}, u32[]{:S(2)}) collective-permute-start(f32[32,1024]{1,0:T(8,128)S(1)} %add.72), channel_id=1, source_target_pairs={{0,10},{1,8},{2,11},{3,9},{4,14},{5,12},{6,15},{7,13},{8,1},{9,3},... | collective-permute-start | bytes 393224 | tf_op jit(solution)/shard_map/ppermute | solution.py:50
  15.6 6.0 %collective-permute-start.17 = (f32[32,1024]{1,0:T(8,128)S(1)}, f32[32,1024]{1,0:T(8,128)S(1)}, u32[]{:S(2)}, u32[]{:S(2)}) collective-permute-start(f32[32,1024]{1,0:T(8,128)S(1)} %add.81), channel_id=1, source_target_pairs={{0,9},{1,25},{2,26},{3,10},{4,13},{5,29},{6,30},{7,14},{8,16},{9,0... | collective-permute-start | bytes 393224 | tf_op jit(solution)/shard_map/ppermute | solution.py:50
  17.3 5.8 %collective-permute-start.13 = (f32[32,1024]{1,0:T(8,128)S(1)}, f32[32,1024]{1,0:T(8,128)S(1)}, u32[]{:S(2)}, u32[]{:S(2)}) collective-permute-start(f32[32,1024]{1,0:T(8,128)S(1)} %add.78), channel_id=1, source_target_pairs={{0,10},{1,8},{2,11},{3,9},{4,14},{5,12},{6,15},{7,13},{8,1},{9,3},... | collective-permute-start | bytes 393224 | tf_op jit(solution)/shard_map/ppermute | solution.py:50
  18.8 5.4 %collective-permute-start.7 = (f32[32,1024]{1,0:T(8,128)S(1)}, f32[32,1024]{1,0:T(8,128)S(1)}, u32[]{:S(2)}, u32[]{:S(2)}) collective-permute-start(f32[32,1024]{1,0:T(8,128)S(1)} %add.76), channel_id=1, source_target_pairs={{0,24},{1,11},{2,8},{3,27},{4,28},{5,15},{6,12},{7,31},{8,2},{9,17... | collective-permute-start | bytes 393224 | tf_op jit(solution)/shard_map/ppermute | solution.py:50
  20.3 5.3 %collective-permute-start.3 = (f32[32,1024]{1,0:T(8,128)S(1)}, f32[32,1024]{1,0:T(8,128)S(1)}, u32[]{:S(2)}, u32[]{:S(2)}) collective-permute-start(f32[32,1024]{1,0:T(8,128)S(1)} %add.73), channel_id=1, source_target_pairs={{0,9},{1,25},{2,26},{3,10},{4,13},{5,29},{6,30},{7,14},{8,16},{9,0... | collective-permute-start | bytes 393224 | tf_op jit(solution)/shard_map/ppermute | solution.py:50
  21.6 5.6 %collective-permute-start.18 = (f32[32,1024]{1,0:T(8,128)S(1)}, f32[32,1024]{1,0:T(8,128)S(1)}, u32[]{:S(2)}, u32[]{:S(2)}) collective-permute-start(f32[32,1024]{1,0:T(8,128)S(1)} %add.82), channel_id=1, source_target_pairs={{0,10},{1,11},{2,8},{3,9},{4,14},{5,15},{6,12},{7,13},{8,2},{9,3},... | collective-permute-start | bytes 393224 | tf_op jit(solution)/shard_map/ppermute | solution.py:50
  23.2 5.3 %collective-permute-start.14 = (f32[32,1024]{1,0:T(8,128)S(1)}, f32[32,1024]{1,0:T(8,128)S(1)}, u32[]{:S(2)}, u32[]{:S(2)}) collective-permute-start(f32[32,1024]{1,0:T(8,128)S(1)} %add.79), channel_id=1, source_target_pairs={{0,9},{1,25},{2,26},{3,10},{4,13},{5,29},{6,30},{7,14},{8,16},{9,0... | collective-permute-start | bytes 393224 | tf_op jit(solution)/shard_map/ppermute | solution.py:50
  24.2 6.4 %collective-permute-start.8 = (f32[32,1024]{1,0:T(8,128)S(1)}, f32[32,1024]{1,0:T(8,128)S(1)}, u32[]{:S(2)}, u32[]{:S(2)}) collective-permute-start(f32[32,1024]{1,0:T(8,128)S(1)} %add.77.own_ref), channel_id=1, source_target_pairs={{0,9},{1,8},{2,11},{3,10},{4,13},{5,12},{6,15},{7,14},{8,1},{9,0},... | collective-permute-start | bytes 393224 | tf_op jit(solution)/shard_map/ppermute | solution.py:50
  25.6 5.2 %collective-permute-start.4 = (f32[32,1024]{1,0:T(8,128)S(1)}, f32[32,1024]{1,0:T(8,128)S(1)}, u32[]{:S(2)}, u32[]{:S(2)}) collective-permute-start(f32[32,1024]{1,0:T(8,128)S(1)} %add.74.own_ref), channel_id=1, source_target_pairs={{0,24},{1,11},{2,8},{3,27},{4,28},{5,15},{6,12},{7,31},{8,2},{9,17... | collective-permute-start | bytes 393224 | tf_op jit(solution)/shard_map/ppermute | solution.py:50
  27.2 4.5 %collective-permute-start.19 = (f32[32,1024]{1,0:T(8,128)S(1)}, f32[32,1024]{1,0:T(8,128)S(1)}, u32[]{:S(2)}, u32[]{:S(2)}) collective-permute-start(f32[32,1024]{1,0:T(8,128)S(1)} %add.83.own_ref), channel_id=1, source_target_pairs={{0,24},{1,8},{2,11},{3,27},{4,28},{5,12},{6,15},{7,31},{8,1},{9,17... | collective-permute-start | bytes 393224 | tf_op jit(solution)/shard_map/ppermute | solution.py:50
  28.5 4.8 %collective-permute-start.15 = (f32[32,1024]{1,0:T(8,128)S(1)}, f32[32,1024]{1,0:T(8,128)S(1)}, u32[]{:S(2)}, u32[]{:S(2)}) collective-permute-start(f32[32,1024]{1,0:T(8,128)S(1)} %add.80.own_ref), channel_id=1, source_target_pairs={{0,24},{1,11},{2,8},{3,27},{4,28},{5,15},{6,12},{7,31},{8,2},{9,17... | collective-permute-start | bytes 393224 | tf_op jit(solution)/shard_map/ppermute | solution.py:50
  39.0 5.5 %collective-permute-start.27 = (f32[32,1024]{1,0:T(8,128)S(1)}, f32[32,1024]{1,0:T(8,128)S(1)}, u32[]{:S(2)}, u32[]{:S(2)}) collective-permute-start(f32[32,1024]{1,0:T(8,128)S(1)} %get-tuple-element.84), channel_id=1, source_target_pairs={{0,9},{1,8},{2,11},{3,10},{4,13},{5,12},{6,15},{7,14},{8,1},{9,0},... | collective-permute-start | bytes 393224 | tf_op jit(solution)/shard_map/ppermute | solution.py:50
  40.2 6.3 %collective-permute-start.23 = (f32[32,1024]{1,0:T(8,128)S(1)}, f32[32,1024]{1,0:T(8,128)S(1)}, u32[]{:S(2)}, u32[]{:S(2)}) collective-permute-start(f32[32,1024]{1,0:T(8,128)S(1)} %get-tuple-element.82), channel_id=1, source_target_pairs={{0,24},{1,11},{2,8},{3,27},{4,28},{5,15},{6,12},{7,31},{8,2},{9,17... | collective-permute-start | bytes 393224 | tf_op jit(solution)/shard_map/ppermute | solution.py:50
  41.9 4.8 %collective-permute-start.38 = (f32[32,1024]{1,0:T(8,128)S(1)}, f32[32,1024]{1,0:T(8,128)S(1)}, u32[]{:S(2)}, u32[]{:S(2)}) collective-permute-start(f32[32,1024]{1,0:T(8,128)S(1)} %get-tuple-element.95), channel_id=1, source_target_pairs={{0,24},{1,8},{2,11},{3,27},{4,28},{5,12},{6,15},{7,31},{8,1},{9,17... | collective-permute-start | bytes 393224 | tf_op jit(solution)/shard_map/ppermute | solution.py:50
  42.1 6.2 %collective-permute-start.34 = (f32[32,1024]{1,0:T(8,128)S(1)}, f32[32,1024]{1,0:T(8,128)S(1)}, u32[]{:S(2)}, u32[]{:S(2)}) collective-permute-start(f32[32,1024]{1,0:T(8,128)S(1)} %get-tuple-element.93), channel_id=1, source_target_pairs={{0,24},{1,11},{2,8},{3,27},{4,28},{5,15},{6,12},{7,31},{8,2},{9,17... | collective-permute-start | bytes 393224 | tf_op jit(solution)/shard_map/ppermute | solution.py:50
  44.5 5.6 %collective-permute-start.28 = (f32[32,1024]{1,0:T(8,128)S(1)}, f32[32,1024]{1,0:T(8,128)S(1)}, u32[]{:S(2)}, u32[]{:S(2)}) collective-permute-start(f32[32,1024]{1,0:T(8,128)S(1)} %add.87), channel_id=1, source_target_pairs={{0,10},{1,25},{2,26},{3,9},{4,14},{5,29},{6,30},{7,13},{8,16},{9,3... | collective-permute-start | bytes 393224 | tf_op jit(solution)/shard_map/ppermute | solution.py:50
  46.6 5.1 %collective-permute-start.24 = (f32[32,1024]{1,0:T(8,128)S(1)}, f32[32,1024]{1,0:T(8,128)S(1)}, u32[]{:S(2)}, u32[]{:S(2)}) collective-permute-start(f32[32,1024]{1,0:T(8,128)S(1)} %add.84), channel_id=1, source_target_pairs={{0,10},{1,8},{2,11},{3,9},{4,14},{5,12},{6,15},{7,13},{8,1},{9,3},... | collective-permute-start | bytes 393224 | tf_op jit(solution)/shard_map/ppermute | solution.py:50
  46.7 5.9 %collective-permute-start.39 = (f32[32,1024]{1,0:T(8,128)S(1)}, f32[32,1024]{1,0:T(8,128)S(1)}, u32[]{:S(2)}, u32[]{:S(2)}) collective-permute-start(f32[32,1024]{1,0:T(8,128)S(1)} %add.93), channel_id=1, source_target_pairs={{0,9},{1,25},{2,26},{3,10},{4,13},{5,29},{6,30},{7,14},{8,16},{9,0... | collective-permute-start | bytes 393224 | tf_op jit(solution)/shard_map/ppermute | solution.py:50
  48.3 5.9 %collective-permute-start.35 = (f32[32,1024]{1,0:T(8,128)S(1)}, f32[32,1024]{1,0:T(8,128)S(1)}, u32[]{:S(2)}, u32[]{:S(2)}) collective-permute-start(f32[32,1024]{1,0:T(8,128)S(1)} %add.90), channel_id=1, source_target_pairs={{0,10},{1,8},{2,11},{3,9},{4,14},{5,12},{6,15},{7,13},{8,1},{9,3},... | collective-permute-start | bytes 393224 | tf_op jit(solution)/shard_map/ppermute | solution.py:50
  50.1 5.2 %collective-permute-start.29 = (f32[32,1024]{1,0:T(8,128)S(1)}, f32[32,1024]{1,0:T(8,128)S(1)}, u32[]{:S(2)}, u32[]{:S(2)}) collective-permute-start(f32[32,1024]{1,0:T(8,128)S(1)} %add.88), channel_id=1, source_target_pairs={{0,24},{1,11},{2,8},{3,27},{4,28},{5,15},{6,12},{7,31},{8,2},{9,17... | collective-permute-start | bytes 393224 | tf_op jit(solution)/shard_map/ppermute | solution.py:50
  51.7 4.8 %collective-permute-start.25 = (f32[32,1024]{1,0:T(8,128)S(1)}, f32[32,1024]{1,0:T(8,128)S(1)}, u32[]{:S(2)}, u32[]{:S(2)}) collective-permute-start(f32[32,1024]{1,0:T(8,128)S(1)} %add.85), channel_id=1, source_target_pairs={{0,9},{1,25},{2,26},{3,10},{4,13},{5,29},{6,30},{7,14},{8,16},{9,0... | collective-permute-start | bytes 393224 | tf_op jit(solution)/shard_map/ppermute | solution.py:50
  52.6 5.5 %collective-permute-start.40 = (f32[32,1024]{1,0:T(8,128)S(1)}, f32[32,1024]{1,0:T(8,128)S(1)}, u32[]{:S(2)}, u32[]{:S(2)}) collective-permute-start(f32[32,1024]{1,0:T(8,128)S(1)} %add.94), channel_id=1, source_target_pairs={{0,10},{1,11},{2,8},{3,9},{4,14},{5,15},{6,12},{7,13},{8,2},{9,3},... | collective-permute-start | bytes 393224 | tf_op jit(solution)/shard_map/ppermute | solution.py:50
  54.2 5.5 %collective-permute-start.36 = (f32[32,1024]{1,0:T(8,128)S(1)}, f32[32,1024]{1,0:T(8,128)S(1)}, u32[]{:S(2)}, u32[]{:S(2)}) collective-permute-start(f32[32,1024]{1,0:T(8,128)S(1)} %add.91), channel_id=1, source_target_pairs={{0,9},{1,25},{2,26},{3,10},{4,13},{5,29},{6,30},{7,14},{8,16},{9,0... | collective-permute-start | bytes 393224 | tf_op jit(solution)/shard_map/ppermute | solution.py:50
  55.4 6.2 %collective-permute-start.30 = (f32[32,1024]{1,0:T(8,128)S(1)}, f32[32,1024]{1,0:T(8,128)S(1)}, u32[]{:S(2)}, u32[]{:S(2)}) collective-permute-start(f32[32,1024]{1,0:T(8,128)S(1)} %add.89.own_ref), channel_id=1, source_target_pairs={{0,9},{1,8},{2,11},{3,10},{4,13},{5,12},{6,15},{7,14},{8,1},{9,0},... | collective-permute-start | bytes 393224 | tf_op jit(solution)/shard_map/ppermute | solution.py:50
  56.5 5.3 %collective-permute-start.26 = (f32[32,1024]{1,0:T(8,128)S(1)}, f32[32,1024]{1,0:T(8,128)S(1)}, u32[]{:S(2)}, u32[]{:S(2)}) collective-permute-start(f32[32,1024]{1,0:T(8,128)S(1)} %add.86.own_ref), channel_id=1, source_target_pairs={{0,24},{1,11},{2,8},{3,27},{4,28},{5,15},{6,12},{7,31},{8,2},{9,17... | collective-permute-start | bytes 393224 | tf_op jit(solution)/shard_map/ppermute | solution.py:50
  59.7 4.6 %collective-permute-start.37 = (f32[32,1024]{1,0:T(8,128)S(1)}, f32[32,1024]{1,0:T(8,128)S(1)}, u32[]{:S(2)}, u32[]{:S(2)}) collective-permute-start(f32[32,1024]{1,0:T(8,128)S(1)} %add.92.own_ref), channel_id=1, source_target_pairs={{0,24},{1,11},{2,8},{3,27},{4,28},{5,15},{6,12},{7,31},{8,2},{9,17... | collective-permute-start | bytes 393224 | tf_op jit(solution)/shard_map/ppermute | solution.py:50
  (12 other events, 32.3 us)

commit v8 on v7

--- a/solution.py
+++ b/solution.py
@@ -12,13 +12,15 @@
 learn_rate = 1.0
 
 ORDERS = (
-    ((1, 3, 2), (3, 2, 1)),
-    ((2, 3, 1), (2, 1, 3)),
-    ((1, 3, 2), (3, 2, 1)),
-    ((1, 2, 3), (2, 1, 3)),
+    ((2, 3, 1), (3, 1, 2)),
+    ((1, 3, 2), (1, 2, 3)),
+    ((2, 3, 1), (3, 1, 2)),
+    ((2, 1, 3), (1, 2, 3)),
 )
 REDUCE_CHAINS = ((1, 4), (2, 4))
 EXPAND_CHAINS = ((3, 4), (4, 4))
+REDUCE_GROUPS = tuple((chain,) for chain in REDUCE_CHAINS)
+EXPAND_GROUPS = (EXPAND_CHAINS,)
 BITS = 4
 BLOCK = 256
 VMEM = pl.BlockSpec(memory_space=pltpu.VMEM)
@@ -57,13 +59,24 @@
     out_ref[pl.ds(pl.multiple_of((1 - place) * rows, rows), rows), :] = rest_ref[...]
 
 
+def add_kernel(left_ref, right_ref, out_ref):
+    out_ref[...] = left_ref[...] + right_ref[...]
+
+
 def chain(keep, send, index):
     even, odd = ORDERS[index - 1]
 
     def exchanged(values, step):
         return from_partner(values, even[step % 3], odd[step % 3])
 
-    own = keep + exchanged(send, 0)
+    got = exchanged(send, 0)
+    own = pl.pallas_call(
+        add_kernel,
+        out_shape=jax.ShapeDtypeStruct(keep.shape, f32),
+        in_specs=[VMEM, VMEM],
+        out_specs=VMEM,
+        compiler_params=SMALL,
+    )(keep, got)
     own = own + exchanged(own, 1)
     own = own + exchanged(own, 2)
     rest = exchanged(own, 3)
@@ -87,26 +100,31 @@
 
 def meet_kernel(chains, keep_ref, got_ref, *outs):
     place = places()
-    for k, (index, first, rows) in enumerate(spans(chains, keep_ref.shape[0])):
-        low, high = pl.ds(first, rows // 2), pl.ds(first + rows // 2, rows // 2)
+    first = 0
+    for k, (index, _) in enumerate(chains):
+        rows = outs[2 * k].shape[0]
+        low, high = pl.ds(first, rows), pl.ds(first + rows, rows)
         stays_low = place[index] == 0
         low, high = keep_ref[low, :] + got_ref[low, :], keep_ref[high, :] + got_ref[high, :]
         outs[2 * k][...] = jnp.where(stays_low, low, high)
         outs[2 * k + 1][...] = jnp.where(stays_low, high, low)
-
-
-def sum_over_cube(keep, send, chains):
-    rows, columns = keep.shape
-    counts = [count // 2 for _, _, count in spans(chains, rows) for _ in range(2)]
-    got = pltpu.with_memory_space_constraint(from_partner(send, 0, 0), pltpu.VMEM)
-    pieces = pl.pallas_call(
-        functools.partial(meet_kernel, chains),
-        out_shape=[jax.ShapeDtypeStruct((count, columns), f32) for count in counts],
-        in_specs=[VMEM, VMEM],
-        out_specs=[VMEM] * len(counts),
-        compiler_params=SMALL,
-    )(keep, got)
-    parts = [chain(pieces[2 * k], pieces[2 * k + 1], index) for k, (index, _) in enumerate(chains)]
+        first += 2 * rows
+
+
+def sum_over_cube(keeps, sends, groups, rows):
+    columns = keeps[0].shape[1]
+    parts = []
+    for chains, keep, send in zip(groups, keeps, sends):
+        counts = [rows * eighths // 16 for _, eighths in chains for _ in range(2)]
+        got = pltpu.with_memory_space_constraint(from_partner(send, 0, 0), pltpu.VMEM)
+        pieces = pl.pallas_call(
+            functools.partial(meet_kernel, chains),
+            out_shape=[jax.ShapeDtypeStruct((count, columns), f32) for count in counts],
+            in_specs=[VMEM, VMEM],
+            out_specs=[VMEM] * len(counts),
+            compiler_params=SMALL,
+        )(keep, got)
+        parts += [chain(pieces[2 * k], pieces[2 * k + 1], index) for k, (index, _) in enumerate(chains)]
     return [own for own, over in parts] + [over for own, over in parts]
 
 
@@ -184,11 +202,15 @@
         ref[pl.ds(pl.multiple_of((1 - role) * rows, rows), rows), :] = part[rows:]
 
 
-def step_columns(role, columns, weights_ref, step, keep_ref, send_ref):
-    rows = keep_ref.shape[0]
-    for i, (place, ref) in enumerate(((role, keep_ref), (1 - role, send_ref))):
+def step_columns(role, columns, weights_ref, step, keep_refs, send_refs):
+    rows = weights_ref.shape[0] // 2
+    for i, (place, refs) in enumerate(((role, keep_refs), (1 - role, send_refs))):
         old = weights_ref[pl.ds(pl.multiple_of(place * rows, rows), rows), columns].astype(f32)
-        ref[:, columns] = (old - step[i * rows : (i + 1) * rows]) * (0.5**BITS)
+        stepped = (old - step[i * rows : (i + 1) * rows]) * (0.5**BITS)
+        first = 0
+        for ref in refs:
+            ref[:, columns] = stepped[first : first + ref.shape[0]]
+            first += ref.shape[0]
 
 
 def put_together(parts, chains, whole_ref):
@@ -238,10 +260,13 @@
 
 def reduce_kernel(joined, x_ref, g_ref, r_ref, slope_ref, hidden_high_ref, hidden_low_ref, *refs):
     if joined:
-        *parts, keep_ref, send_ref, zh_ref, zl_ref, e_ref, high_ref, low_ref = refs
-        put_together(parts, EXPAND_CHAINS, e_ref)
+        *refs, zh_ref, zl_ref, e_ref, high_ref, low_ref = refs
+        count = 2 * len(EXPAND_CHAINS)
+        put_together(refs[:count], EXPAND_CHAINS, e_ref)
+        refs = refs[count:]
     else:
-        e_ref, keep_ref, send_ref, zh_ref, zl_ref, high_ref, low_ref = refs
+        e_ref, *refs, zh_ref, zl_ref, high_ref, low_ref = refs
+    keep_refs, send_refs = refs[: len(REDUCE_GROUPS)], refs[len(REDUCE_GROUPS) :]
     role = places()[0]
     blocks = in_columns(r_ref.shape[1])
     reduce_scale = 1.0 / math.sqrt(r_ref.shape[1])
@@ -266,23 +291,27 @@
     store_by_role(role, halves(grad_hidden * expand_scale * slope_ref[...]), high_ref, low_ref)
     for columns in blocks:
         step = product((high_ref[...], low_ref[...]), (x_ref[:, columns],), NN) * (learn_rate * reduce_scale)
-        step_columns(role, columns, r_ref, step, keep_ref, send_ref)
-
-
-def expand_kernel(e_ref, zh_ref, zl_ref, hidden_high_ref, hidden_low_ref, keep_ref, send_ref):
+        step_columns(role, columns, r_ref, step, keep_refs, send_refs)
+
+
+def expand_kernel(e_ref, zh_ref, zl_ref, hidden_high_ref, hidden_low_ref, *refs):
+    keep_refs, send_refs = refs[: len(EXPAND_GROUPS)], refs[len(EXPAND_GROUPS) :]
     role = places()[0]
     expand_scale = 1.0 / math.sqrt(e_ref.shape[0])
     for columns in in_columns(e_ref.shape[1]):
         grads = zh_ref[:, columns], zl_ref[:, columns]
         step = product((hidden_high_ref[...], hidden_low_ref[...]), grads, NN) * (learn_rate * expand_scale)
-        step_columns(role, columns, e_ref, step, keep_ref, send_ref)
+        step_columns(role, columns, e_ref, step, keep_refs, send_refs)
 
 
 def shards(w_reduce, w_expand, inputs, out_grads):
     held = [pltpu.with_memory_space_constraint(array[0, 0], pltpu.HBM) for array in (inputs, out_grads, w_reduce, w_expand)]
     iterations, rows, columns = inputs.shape[2:]
     width = w_reduce.shape[2]
-    half = jax.ShapeDtypeStruct((width // 2, columns), f32)
+    halves_r, halves_e = (
+        [jax.ShapeDtypeStruct((width // 2 * sum(eighths for _, eighths in chains) // 8, columns), f32) for chains in groups] * 2
+        for groups in (REDUCE_GROUPS, EXPAND_GROUPS)
+    )
     acts = jax.ShapeDtypeStruct((rows, columns), bf16)
     hidden_shapes = (
         [jax.ShapeDtypeStruct((width, rows), f32)]
@@ -306,21 +335,27 @@
         feats, grads = acts_of[2 * iteration : 2 * iteration + 2]
         slope, high_t, low_t, high, low = hidden
         weights_in = [expanding] if first else expanding
-        keep_r, send_r, zh, zl, *joined = pl.pallas_call(
+        results = pl.pallas_call(
             functools.partial(reduce_kernel, not first),
-            out_shape=[half, half, acts, acts] + ([] if first else [weights]),
+            out_shape=halves_r + [acts] * 2 + ([] if first else [weights]),
             in_specs=[VMEM] * (6 + len(weights_in)),
-            out_specs=[VMEM] * (4 if first else 5),
+            out_specs=[VMEM] * (len(halves_r) + (2 if first else 3)),
             scratch_shapes=[pltpu.VMEM((width, rows), bf16)] * 2,
             compiler_params=LARGE,
         )(feats, grads, reducing, slope, high, low, *weights_in)
+        stepped_r, (zh, zl, *joined) = results[: len(halves_r)], results[len(halves_r) :]
         if joined:
             (expanding,) = joined
-        keep_e, send_e = pl.pallas_call(
-            expand_kernel, out_shape=[half, half], in_specs=[VMEM] * 5, out_specs=[VMEM] * 2, compiler_params=LARGE
+        stepped_e = pl.pallas_call(
+            expand_kernel,
+            out_shape=halves_e,
+            in_specs=[VMEM] * 5,
+            out_specs=[VMEM] * len(halves_e),
+            compiler_params=LARGE,
         )(expanding, zh, zl, high_t, low_t)
-        sums_r = sum_over_cube(keep_r, send_r, REDUCE_CHAINS)
-        expanding = sum_over_cube(keep_e, send_e, EXPAND_CHAINS)
+        r, e = len(REDUCE_GROUPS), len(EXPAND_GROUPS)
+        sums_r = sum_over_cube(stepped_r[:r], stepped_r[r:], REDUCE_GROUPS, width // 2)
+        expanding = sum_over_cube(stepped_e[:e], stepped_e[e:], EXPAND_GROUPS, width // 2)
         if last:
             own = tuple(range(len(EXPAND_CHAINS)))
             groups = [

time: 66.9 us -> 68.4 us (1.022)
  waiting for transfers between devices: 7.52 us -> 14.9 us
  starting transfers between devices: 47.8 us -> 42.1 us
    ppermute x44 -> x46, waiting for transfers between devices: 7.52 us -> 14.9 us  [from_partner(): return lax.ppermute(values, ('near', 'far'), pairs)]
    ppermute x44 -> x46, starting transfers between devices: 47.8 us -> 42.1 us  [from_partner(): return lax.ppermute(values, ('near', 'far'), pairs)]
    pallas_call x4 -> x12, Pallas kernels: 4.83 us -> 4.95 us  [the longest x2 3.68 us: shards(): pl.pallas_call(functools.partial(reduce_kernel, not first), out_shape=hal...]
  transfers between devices with their start and end apart: 44 -> 46, of which waited for: 13 -> 20; matrix products, arithmetic and copies ran while one was open for 1% -> 0% of each run, Pallas kernels for 5% -> 4%
where the time goes in v8:
time: 68.4 us; the launch traced here: 68.2 us
  starting transfers between devices  42.1 us (62%)
  waiting for transfers between devices  14.9 us (22%)
  Pallas kernels  10.1 us (15%)
  between operations  0.9 us (1%)
    ppermute x46, starting transfers between devices, from_partner(): return lax.ppermute(values, ('near', 'far'), pairs)  42.1 us
    ppermute x46, waiting for transfers between devices, from_partner(): return lax.ppermute(values, ('near', 'far'), pairs)  14.9 us
    pallas_call x2, Pallas kernels, shards(): pl.pallas_call(functools.partial(reduce_kernel, not first), out_shape=hal...  3.68 us
    pallas_call x1, Pallas kernels, shards(): pl.pallas_call(first_hidden_kernel, out_shape=hidden_shapes + [narrow] *...  2.06 us
    pallas_call x2, Pallas kernels, store(): pl.pallas_call(functools.partial(store_kernel, counted), out_shape=[jax.S...  1.99 us
  transfers between devices with their start and end apart: 46, of which 20 were waited for; matrix products, arithmetic and copies ran while one was open for 0% of the time, Pallas kernels for 4%

profile of v8, /device:TPU:0, one launch (start us, length us, event | category | flops | bytes accessed | tf_op | source)
XLA Modules:
  0.0 68.2 jit_solution(1880689998724433221)
XLA Ops:
  0.6 2.1 %hidden_0.1 = (f32[256,256]{1,0:T(8,128)S(1)}, bf16[256,256]{1,0:T(8,128)(2,1)S(1)}, bf16[256,256]{1,0:T(8,128)(2,1)S(1)}, bf16[256,256]{1,0:T(8,128)(2,1)S(1)},...) custom-call(bf16[2,256,1024]{2,1,0:T(8,128)(2,1)} %bitcast.6, ...), custom_call_target="tpu_custom_call" | custom-call | tf_op jit(solution)/shard_map/hidden_0/pallas_call | solution.py:323
  2.7 1.7 %shard_map.59 = (f32[64,1024]{1,0:T(8,128)S(1)}, f32[64,1024]{1,0:T(8,128)S(1)}, f32[64,1024]{1,0:T(8,128)S(1)}, f32[64,1024]{1,0:T(8,128)S(1)}, bf16[256,1024]{...) custom-call(bf16[256,1024]{1,0:T(8,128)(2,1)S(1)} %get-tuple-element.56.x_ref, ...), custom_call_target="tpu_custom_call" | custom-call | tf_op jit(solution)/shard_map/pallas_call | solution.py:338
  6.0 1.4 %collective-permute-done.got_ref = f32[64,1024]{1,0:T(8,128)S(1)} collective-permute-done((f32[64,1024]{1,0:T(8,128)S(1)}, f32[64,1024]{1,0:T(8,128)S(1)}, u32[]{:S(2)}, u32[]{:S(2)}) %collective-permute-start) | collective-permute-done | bytes 262176 | tf_op jit(solution)/shard_map/ppermute | solution.py:52
  7.5 2.7 %collective-permute-start.1 = (f32[32,1024]{1,0:T(8,128)S(1)}, f32[32,1024]{1,0:T(8,128)S(1)}, u32[]{:S(2)}, u32[]{:S(2)}) collective-permute-start(f32[32,1024]{1,0:T(8,128)S(1)} %get-tuple-element.66), channel_id=1, source_target_pairs={{0,9},{1,11},{2,8},{3,10},{4,13},{5,15},{6,12},{7,14},{8,2},{9,0},... | collective-permute-start | bytes 393224 | tf_op jit(solution)/shard_map/ppermute | solution.py:52
  10.2 1.5 %collective-permute-start.6 = (f32[32,1024]{1,0:T(8,128)S(1)}, f32[32,1024]{1,0:T(8,128)S(1)}, u32[]{:S(2)}, u32[]{:S(2)}) collective-permute-start(f32[32,1024]{1,0:T(8,128)S(1)} %get-tuple-element.70), channel_id=1, source_target_pairs={{0,24},{1,25},{2,26},{3,27},{4,28},{5,29},{6,30},{7,31},{8,16},{9,... | collective-permute-start | bytes 393224 | tf_op jit(solution)/shard_map/ppermute | solution.py:52
  12.1 1.5 %collective-permute-start.13 = (f32[32,1024]{1,0:T(8,128)S(1)}, f32[32,1024]{1,0:T(8,128)S(1)}, u32[]{:S(2)}, u32[]{:S(2)}) collective-permute-start(f32[32,1024]{1,0:T(8,128)S(1)} %get-tuple-element.82), channel_id=1, source_target_pairs={{0,9},{1,11},{2,8},{3,10},{4,13},{5,15},{6,12},{7,14},{8,2},{9,0},... | collective-permute-start | bytes 393224 | tf_op jit(solution)/shard_map/ppermute | solution.py:52
  13.6 1.4 %collective-permute-start.2 = (f32[32,1024]{1,0:T(8,128)S(1)}, f32[32,1024]{1,0:T(8,128)S(1)}, u32[]{:S(2)}, u32[]{:S(2)}) collective-permute-start(f32[32,1024]{1,0:T(8,128)S(1)} %shard_map.61), channel_id=1, source_target_pairs={{0,10},{1,25},{2,26},{3,9},{4,14},{5,29},{6,30},{7,13},{8,16},{9,3... | collective-permute-start | bytes 393224 | tf_op jit(solution)/shard_map/ppermute | solution.py:52
  15.6 2.4 %collective-permute-start.7 = (f32[32,1024]{1,0:T(8,128)S(1)}, f32[32,1024]{1,0:T(8,128)S(1)}, u32[]{:S(2)}, u32[]{:S(2)}) collective-permute-start(f32[32,1024]{1,0:T(8,128)S(1)} %shard_map.64), channel_id=1, source_target_pairs={{0,10},{1,8},{2,11},{3,9},{4,14},{5,12},{6,15},{7,13},{8,1},{9,3},... | collective-permute-start | bytes 393224 | tf_op jit(solution)/shard_map/ppermute | solution.py:52
  18.0 1.0 %collective-permute-start.18 = (f32[32,1024]{1,0:T(8,128)S(1)}, f32[32,1024]{1,0:T(8,128)S(1)}, u32[]{:S(2)}, u32[]{:S(2)}) collective-permute-start(f32[32,1024]{1,0:T(8,128)S(1)} %shard_map.71), channel_id=1, source_target_pairs={{0,24},{1,8},{2,11},{3,27},{4,28},{5,12},{6,15},{7,31},{8,1},{9,17... | collective-permute-start | bytes 393224 | tf_op jit(solution)/shard_map/ppermute | solution.py:52
  21.4 1.7 %collective-permute-done.18 = f32[32,1024]{1,0:T(8,128)S(1)} collective-permute-done((f32[32,1024]{1,0:T(8,128)S(1)}, f32[32,1024]{1,0:T(8,128)S(1)}, u32[]{:S(2)}, u32[]{:S(2)}) %collective-permute-start.18) | collective-permute-done | bytes 131104 | tf_op jit(solution)/shard_map/ppermute | solution.py:52
  23.5 1.8 %collective-permute-start.15 = (f32[32,1024]{1,0:T(8,128)S(1)}, f32[32,1024]{1,0:T(8,128)S(1)}, u32[]{:S(2)}, u32[]{:S(2)}) collective-permute-start(f32[32,1024]{1,0:T(8,128)S(1)} %add.52), channel_id=1, source_target_pairs={{0,24},{1,8},{2,11},{3,27},{4,28},{5,12},{6,15},{7,31},{8,1},{9,17... | collective-permute-start | bytes 393224 | tf_op jit(solution)/shard_map/ppermute | solution.py:52
  25.8 1.7 %collective-permute-start.9 = (f32[32,1024]{1,0:T(8,128)S(1)}, f32[32,1024]{1,0:T(8,128)S(1)}, u32[]{:S(2)}, u32[]{:S(2)}) collective-permute-start(f32[32,1024]{1,0:T(8,128)S(1)} %add.51.own_ref), channel_id=1, source_target_pairs={{0,24},{1,25},{2,26},{3,27},{4,28},{5,29},{6,30},{7,31},{8,16},{9,... | collective-permute-start | bytes 393224 | tf_op jit(solution)/shard_map/ppermute | solution.py:52
  27.4 1.2 %collective-permute-done.19 = f32[32,1024]{1,0:T(8,128)S(1)} collective-permute-done((f32[32,1024]{1,0:T(8,128)S(1)}, f32[32,1024]{1,0:T(8,128)S(1)}, u32[]{:S(2)}, u32[]{:S(2)}) %collective-permute-start.19) | collective-permute-done | bytes 131104 | tf_op jit(solution)/shard_map/ppermute | solution.py:52
  28.9 1.6 %collective-permute-start.16 = (f32[32,1024]{1,0:T(8,128)S(1)}, f32[32,1024]{1,0:T(8,128)S(1)}, u32[]{:S(2)}, u32[]{:S(2)}) collective-permute-start(f32[32,1024]{1,0:T(8,128)S(1)} %add.53.own_ref), channel_id=1, source_target_pairs={{0,9},{1,11},{2,8},{3,10},{4,13},{5,15},{6,12},{7,14},{8,2},{9,0},... | collective-permute-start | bytes 393224 | tf_op jit(solution)/shard_map/ppermute | solution.py:52
  31.5 1.5 %collective-permute-done.20.rest_ref = f32[32,1024]{1,0:T(8,128)S(1)} collective-permute-done((f32[32,1024]{1,0:T(8,128)S(1)}, f32[32,1024]{1,0:T(8,128)S(1)}, u32[]{:S(2)}, u32[]{:S(2)}) %collective-permute-start.20) | collective-permute-done | bytes 131104 | tf_op jit(solution)/shard_map/ppermute | solution.py:52
  33.2 1.2 %collective-permute-done.16.rest_ref = f32[32,1024]{1,0:T(8,128)S(1)} collective-permute-done((f32[32,1024]{1,0:T(8,128)S(1)}, f32[32,1024]{1,0:T(8,128)S(1)}, u32[]{:S(2)}, u32[]{:S(2)}) %collective-permute-start.16) | collective-permute-done | bytes 131104 | tf_op jit(solution)/shard_map/ppermute | solution.py:52
  36.2 2.0 %shard_map.73 = (f32[64,1024]{1,0:T(8,128)S(1)}, f32[64,1024]{1,0:T(8,128)S(1)}, f32[64,1024]{1,0:T(8,128)S(1)}, f32[64,1024]{1,0:T(8,128)S(1)}, bf16[256,1024]{...) custom-call(bf16[256,1024]{1,0:T(8,128)(2,1)S(1)} %get-tuple-element.54.x_ref, ...), custom_call_target="tpu_custom_call" | custom-call | tf_op jit(solution)/shard_map/pallas_call | solution.py:338
  39.7 1.4 %collective-permute-done.23.got_ref = f32[64,1024]{1,0:T(8,128)S(1)} collective-permute-done((f32[64,1024]{1,0:T(8,128)S(1)}, f32[64,1024]{1,0:T(8,128)S(1)}, u32[]{:S(2)}, u32[]{:S(2)}) %collective-permute-start.23) | collective-permute-done | bytes 262176 | tf_op jit(solution)/shard_map/ppermute | solution.py:52
  41.7 2.3 %collective-permute-start.29 = (f32[32,1024]{1,0:T(8,128)S(1)}, f32[32,1024]{1,0:T(8,128)S(1)}, u32[]{:S(2)}, u32[]{:S(2)}) collective-permute-start(f32[32,1024]{1,0:T(8,128)S(1)} %get-tuple-element.92), channel_id=1, source_target_pairs={{0,24},{1,25},{2,26},{3,27},{4,28},{5,29},{6,30},{7,31},{8,16},{9,... | collective-permute-start | bytes 393224 | tf_op jit(solution)/shard_map/ppermute | solution.py:52
  44.5 1.3 %collective-permute-start.36 = (f32[32,1024]{1,0:T(8,128)S(1)}, f32[32,1024]{1,0:T(8,128)S(1)}, u32[]{:S(2)}, u32[]{:S(2)}) collective-permute-start(f32[32,1024]{1,0:T(8,128)S(1)} %get-tuple-element.101), channel_id=1, source_target_pairs={{0,9},{1,11},{2,8},{3,10},{4,13},{5,15},{6,12},{7,14},{8,2},{9,0},... | collective-permute-start | bytes 393224 | tf_op jit(solution)/shard_map/ppermute | solution.py:52
  46.6 1.2 %collective-permute-done.29.right_ref = f32[32,1024]{1,0:T(8,128)S(1)} collective-permute-done((f32[32,1024]{1,0:T(8,128)S(1)}, f32[32,1024]{1,0:T(8,128)S(1)}, u32[]{:S(2)}, u32[]{:S(2)}) %collective-permute-start.29) | collective-permute-done | bytes 131104 | tf_op jit(solution)/shard_map/ppermute | solution.py:52
  47.9 1.4 %collective-permute-start.30 = (f32[32,1024]{1,0:T(8,128)S(1)}, f32[32,1024]{1,0:T(8,128)S(1)}, u32[]{:S(2)}, u32[]{:S(2)}) collective-permute-start(f32[32,1024]{1,0:T(8,128)S(1)} %shard_map.78), channel_id=1, source_target_pairs={{0,10},{1,8},{2,11},{3,9},{4,14},{5,12},{6,15},{7,13},{8,1},{9,3},... | collective-permute-start | bytes 393224 | tf_op jit(solution)/shard_map/ppermute | solution.py:52
  49.3 1.0 %collective-permute-start.41 = (f32[32,1024]{1,0:T(8,128)S(1)}, f32[32,1024]{1,0:T(8,128)S(1)}, u32[]{:S(2)}, u32[]{:S(2)}) collective-permute-start(f32[32,1024]{1,0:T(8,128)S(1)} %shard_map.84), channel_id=1, source_target_pairs={{0,24},{1,8},{2,11},{3,27},{4,28},{5,12},{6,15},{7,31},{8,1},{9,17... | collective-permute-start | bytes 393224 | tf_op jit(solution)/shard_map/ppermute | solution.py:52
  50.2 1.8 %collective-permute-start.37 = (f32[32,1024]{1,0:T(8,128)S(1)}, f32[32,1024]{1,0:T(8,128)S(1)}, u32[]{:S(2)}, u32[]{:S(2)}) collective-permute-start(f32[32,1024]{1,0:T(8,128)S(1)} %shard_map.82), channel_id=1, source_target_pairs={{0,10},{1,25},{2,26},{3,9},{4,14},{5,29},{6,30},{7,13},{8,16},{9,3... | collective-permute-start | bytes 393224 | tf_op jit(solution)/shard_map/ppermute | solution.py:52
  52.3 1.7 %collective-permute-start.31 = (f32[32,1024]{1,0:T(8,128)S(1)}, f32[32,1024]{1,0:T(8,128)S(1)}, u32[]{:S(2)}, u32[]{:S(2)}) collective-permute-start(f32[32,1024]{1,0:T(8,128)S(1)} %add.58), channel_id=1, source_target_pairs={{0,9},{1,11},{2,8},{3,10},{4,13},{5,15},{6,12},{7,14},{8,2},{9,0},... | collective-permute-start | bytes 393224 | tf_op jit(solution)/shard_map/ppermute | solution.py:52
  54.1 1.5 %collective-permute-start.42 = (f32[32,1024]{1,0:T(8,128)S(1)}, f32[32,1024]{1,0:T(8,128)S(1)}, u32[]{:S(2)}, u32[]{:S(2)}) collective-permute-start(f32[32,1024]{1,0:T(8,128)S(1)} %add.62), channel_id=1, source_target_pairs={{0,10},{1,11},{2,8},{3,9},{4,14},{5,15},{6,12},{7,13},{8,2},{9,3},... | collective-permute-start | bytes 393224 | tf_op jit(solution)/shard_map/ppermute | solution.py:52
  55.6 0.9 %collective-permute-start.38 = (f32[32,1024]{1,0:T(8,128)S(1)}, f32[32,1024]{1,0:T(8,128)S(1)}, u32[]{:S(2)}, u32[]{:S(2)}) collective-permute-start(f32[32,1024]{1,0:T(8,128)S(1)} %add.60), channel_id=1, source_target_pairs={{0,24},{1,8},{2,11},{3,27},{4,28},{5,12},{6,15},{7,31},{8,1},{9,17... | collective-permute-start | bytes 393224 | tf_op jit(solution)/shard_map/ppermute | solution.py:52
  56.6 0.9 %collective-permute-start.27 = (f32[32,1024]{1,0:T(8,128)S(1)}, f32[32,1024]{1,0:T(8,128)S(1)}, u32[]{:S(2)}, u32[]{:S(2)}) collective-permute-start(f32[32,1024]{1,0:T(8,128)S(1)} %add.57.own_ref), channel_id=1, source_target_pairs={{0,9},{1,11},{2,8},{3,10},{4,13},{5,15},{6,12},{7,14},{8,2},{9,0},... | collective-permute-start | bytes 393224 | tf_op jit(solution)/shard_map/ppermute | solution.py:52
  58.0 1.7 %collective-permute-start.32 = (f32[32,1024]{1,0:T(8,128)S(1)}, f32[32,1024]{1,0:T(8,128)S(1)}, u32[]{:S(2)}, u32[]{:S(2)}) collective-permute-start(f32[32,1024]{1,0:T(8,128)S(1)} %add.59.own_ref), channel_id=1, source_target_pairs={{0,24},{1,25},{2,26},{3,27},{4,28},{5,29},{6,30},{7,31},{8,16},{9,... | collective-permute-start | bytes 393224 | tf_op jit(solution)/shard_map/ppermute | solution.py:52
  59.9 1.0 %collective-permute-start.43 = (f32[32,1024]{1,0:T(8,128)S(1)}, f32[32,1024]{1,0:T(8,128)S(1)}, u32[]{:S(2)}, u32[]{:S(2)}) collective-permute-start(f32[32,1024]{1,0:T(8,128)S(1)} %add.63.own_ref), channel_id=1, source_target_pairs={{0,9},{1,25},{2,26},{3,10},{4,13},{5,29},{6,30},{7,14},{8,16},{9,0... | collective-permute-start | bytes 393224 | tf_op jit(solution)/shard_map/ppermute | solution.py:52
  64.4 1.1 %collective-permute-start.45 = (f32[64,1024]{1,0:T(8,128)S(1)}, f32[64,1024]{1,0:T(8,128)S(1)}, u32[]{:S(2)}, u32[]{:S(2)}) collective-permute-start(f32[64,1024]{1,0:T(8,128)S(1)} %shard_map.85.refs_5_), channel_id=1, source_target_pairs={{0,8},{1,9},{2,10},{3,11},{4,12},{5,13},{6,14},{7,15},{8,0},{9,1},... | collective-permute-start | bytes 786440 | tf_op jit(solution)/shard_map/ppermute | solution.py:52
  66.0 1.2 %shard_map.86 = (f32[256,1024]{1,0:T(8,128)}, f32[256,1024]{1,0:T(8,128)}) custom-call(f32[64,1024]{1,0:T(8,128)S(1)} %shard_map.76.refs_0_, f32[64,1024]{1,0:T(8,128)S(1)} %shard_map.79.refs_1_, f32[64,1024]{1,0:T(8,128)S(1)} %collective-permute-done.33.refs_2_, f32[64,1024]{1,0:T(8,128)S(1)} %collective-permute-done.34.refs_3_, ...), custom_call_target="tpu_custom_call" | custom-call | tf_op jit(solution)/shard_map/pallas_call | solution.py:160
  (106 shorter events, 18.7 us)
Async XLA Ops:
  4.9 6.8 %collective-permute-start.12 = (f32[128,1024]{1,0:T(8,128)S(1)}, f32[128,1024]{1,0:T(8,128)S(1)}, u32[]{:S(2)}, u32[]{:S(2)}) collective-permute-start(f32[128,1024]{1,0:T(8,128)S(1)} %get-tuple-element.80), channel_id=1, source_target_pairs={{0,8},{1,9},{2,10},{3,11},{4,12},{5,13},{6,14},{7,15},{8,0},{9,1},... | collective-permute-start | bytes 1572872 | tf_op jit(solution)/shard_map/ppermute | solution.py:52
  5.6 4.6 %collective-permute-start.5 = (f32[64,1024]{1,0:T(8,128)S(1)}, f32[64,1024]{1,0:T(8,128)S(1)}, u32[]{:S(2)}, u32[]{:S(2)}) collective-permute-start(f32[64,1024]{1,0:T(8,128)S(1)} %get-tuple-element.68), channel_id=1, source_target_pairs={{0,8},{1,9},{2,10},{3,11},{4,12},{5,13},{6,14},{7,15},{8,0},{9,1},... | collective-permute-start | bytes 786440 | tf_op jit(solution)/shard_map/ppermute | solution.py:52
  7.5 6.1 %collective-permute-start.1 = (f32[32,1024]{1,0:T(8,128)S(1)}, f32[32,1024]{1,0:T(8,128)S(1)}, u32[]{:S(2)}, u32[]{:S(2)}) collective-permute-start(f32[32,1024]{1,0:T(8,128)S(1)} %get-tuple-element.66), channel_id=1, source_target_pairs={{0,9},{1,11},{2,8},{3,10},{4,13},{5,15},{6,12},{7,14},{8,2},{9,0},... | collective-permute-start | bytes 393224 | tf_op jit(solution)/shard_map/ppermute | solution.py:52
  10.2 5.4 %collective-permute-start.6 = (f32[32,1024]{1,0:T(8,128)S(1)}, f32[32,1024]{1,0:T(8,128)S(1)}, u32[]{:S(2)}, u32[]{:S(2)}) collective-permute-start(f32[32,1024]{1,0:T(8,128)S(1)} %get-tuple-element.70), channel_id=1, source_target_pairs={{0,24},{1,25},{2,26},{3,27},{4,28},{5,29},{6,30},{7,31},{8,16},{9,... | collective-permute-start | bytes 393224 | tf_op jit(solution)/shard_map/ppermute | solution.py:52
  11.8 6.2 %collective-permute-start.17 = (f32[32,1024]{1,0:T(8,128)S(1)}, f32[32,1024]{1,0:T(8,128)S(1)}, u32[]{:S(2)}, u32[]{:S(2)}) collective-permute-start(f32[32,1024]{1,0:T(8,128)S(1)} %get-tuple-element.84), channel_id=1, source_target_pairs={{0,9},{1,25},{2,26},{3,10},{4,13},{5,29},{6,30},{7,14},{8,16},{9,0... | collective-permute-start | bytes 393224 | tf_op jit(solution)/shard_map/ppermute | solution.py:52
  12.1 6.9 %collective-permute-start.13 = (f32[32,1024]{1,0:T(8,128)S(1)}, f32[32,1024]{1,0:T(8,128)S(1)}, u32[]{:S(2)}, u32[]{:S(2)}) collective-permute-start(f32[32,1024]{1,0:T(8,128)S(1)} %get-tuple-element.82), channel_id=1, source_target_pairs={{0,9},{1,11},{2,8},{3,10},{4,13},{5,15},{6,12},{7,14},{8,2},{9,0},... | collective-permute-start | bytes 393224 | tf_op jit(solution)/shard_map/ppermute | solution.py:52
  13.6 6.2 %collective-permute-start.2 = (f32[32,1024]{1,0:T(8,128)S(1)}, f32[32,1024]{1,0:T(8,128)S(1)}, u32[]{:S(2)}, u32[]{:S(2)}) collective-permute-start(f32[32,1024]{1,0:T(8,128)S(1)} %shard_map.61), channel_id=1, source_target_pairs={{0,10},{1,25},{2,26},{3,9},{4,14},{5,29},{6,30},{7,13},{8,16},{9,3... | collective-permute-start | bytes 393224 | tf_op jit(solution)/shard_map/ppermute | solution.py:52
  15.6 5.0 %collective-permute-start.7 = (f32[32,1024]{1,0:T(8,128)S(1)}, f32[32,1024]{1,0:T(8,128)S(1)}, u32[]{:S(2)}, u32[]{:S(2)}) collective-permute-start(f32[32,1024]{1,0:T(8,128)S(1)} %shard_map.64), channel_id=1, source_target_pairs={{0,10},{1,8},{2,11},{3,9},{4,14},{5,12},{6,15},{7,13},{8,1},{9,3},... | collective-permute-start | bytes 393224 | tf_op jit(solution)/shard_map/ppermute | solution.py:52
  18.0 5.2 %collective-permute-start.18 = (f32[32,1024]{1,0:T(8,128)S(1)}, f32[32,1024]{1,0:T(8,128)S(1)}, u32[]{:S(2)}, u32[]{:S(2)}) collective-permute-start(f32[32,1024]{1,0:T(8,128)S(1)} %shard_map.71), channel_id=1, source_target_pairs={{0,24},{1,8},{2,11},{3,27},{4,28},{5,12},{6,15},{7,31},{8,1},{9,17... | collective-permute-start | bytes 393224 | tf_op jit(solution)/shard_map/ppermute | solution.py:52
  19.0 4.5 %collective-permute-start.14 = (f32[32,1024]{1,0:T(8,128)S(1)}, f32[32,1024]{1,0:T(8,128)S(1)}, u32[]{:S(2)}, u32[]{:S(2)}) collective-permute-start(f32[32,1024]{1,0:T(8,128)S(1)} %shard_map.69), channel_id=1, source_target_pairs={{0,10},{1,25},{2,26},{3,9},{4,14},{5,29},{6,30},{7,13},{8,16},{9,3... | collective-permute-start | bytes 393224 | tf_op jit(solution)/shard_map/ppermute | solution.py:52
  19.8 5.4 %collective-permute-start.3 = (f32[32,1024]{1,0:T(8,128)S(1)}, f32[32,1024]{1,0:T(8,128)S(1)}, u32[]{:S(2)}, u32[]{:S(2)}) collective-permute-start(f32[32,1024]{1,0:T(8,128)S(1)} %add.48), channel_id=1, source_target_pairs={{0,24},{1,8},{2,11},{3,27},{4,28},{5,12},{6,15},{7,31},{8,1},{9,17... | collective-permute-start | bytes 393224 | tf_op jit(solution)/shard_map/ppermute | solution.py:52
  20.6 5.1 %collective-permute-start.8 = (f32[32,1024]{1,0:T(8,128)S(1)}, f32[32,1024]{1,0:T(8,128)S(1)}, u32[]{:S(2)}, u32[]{:S(2)}) collective-permute-start(f32[32,1024]{1,0:T(8,128)S(1)} %add.50), channel_id=1, source_target_pairs={{0,9},{1,11},{2,8},{3,10},{4,13},{5,15},{6,12},{7,14},{8,2},{9,0},... | collective-permute-start | bytes 393224 | tf_op jit(solution)/shard_map/ppermute | solution.py:52
  23.2 5.4 %collective-permute-start.19 = (f32[32,1024]{1,0:T(8,128)S(1)}, f32[32,1024]{1,0:T(8,128)S(1)}, u32[]{:S(2)}, u32[]{:S(2)}) collective-permute-start(f32[32,1024]{1,0:T(8,128)S(1)} %add.54), channel_id=1, source_target_pairs={{0,10},{1,11},{2,8},{3,9},{4,14},{5,15},{6,12},{7,13},{8,2},{9,3},... | collective-permute-start | bytes 393224 | tf_op jit(solution)/shard_map/ppermute | solution.py:52
  23.5 5.3 %collective-permute-start.15 = (f32[32,1024]{1,0:T(8,128)S(1)}, f32[32,1024]{1,0:T(8,128)S(1)}, u32[]{:S(2)}, u32[]{:S(2)}) collective-permute-start(f32[32,1024]{1,0:T(8,128)S(1)} %add.52), channel_id=1, source_target_pairs={{0,24},{1,8},{2,11},{3,27},{4,28},{5,12},{6,15},{7,31},{8,1},{9,17... | collective-permute-start | bytes 393224 | tf_op jit(solution)/shard_map/ppermute | solution.py:52
  25.3 5.4 %collective-permute-start.4 = (f32[32,1024]{1,0:T(8,128)S(1)}, f32[32,1024]{1,0:T(8,128)S(1)}, u32[]{:S(2)}, u32[]{:S(2)}) collective-permute-start(f32[32,1024]{1,0:T(8,128)S(1)} %add.49.own_ref), channel_id=1, source_target_pairs={{0,9},{1,11},{2,8},{3,10},{4,13},{5,15},{6,12},{7,14},{8,2},{9,0},... | collective-permute-start | bytes 393224 | tf_op jit(solution)/shard_map/ppermute | solution.py:52
  25.8 5.6 %collective-permute-start.9 = (f32[32,1024]{1,0:T(8,128)S(1)}, f32[32,1024]{1,0:T(8,128)S(1)}, u32[]{:S(2)}, u32[]{:S(2)}) collective-permute-start(f32[32,1024]{1,0:T(8,128)S(1)} %add.51.own_ref), channel_id=1, source_target_pairs={{0,24},{1,25},{2,26},{3,27},{4,28},{5,29},{6,30},{7,31},{8,16},{9,... | collective-permute-start | bytes 393224 | tf_op jit(solution)/shard_map/ppermute | solution.py:52
  28.9 5.6 %collective-permute-start.16 = (f32[32,1024]{1,0:T(8,128)S(1)}, f32[32,1024]{1,0:T(8,128)S(1)}, u32[]{:S(2)}, u32[]{:S(2)}) collective-permute-start(f32[32,1024]{1,0:T(8,128)S(1)} %add.53.own_ref), channel_id=1, source_target_pairs={{0,9},{1,11},{2,8},{3,10},{4,13},{5,15},{6,12},{7,14},{8,2},{9,0},... | collective-permute-start | bytes 393224 | tf_op jit(solution)/shard_map/ppermute | solution.py:52
  38.8 5.2 %collective-permute-start.35 = (f32[128,1024]{1,0:T(8,128)S(1)}, f32[128,1024]{1,0:T(8,128)S(1)}, u32[]{:S(2)}, u32[]{:S(2)}) collective-permute-start(f32[128,1024]{1,0:T(8,128)S(1)} %get-tuple-element.99), channel_id=1, source_target_pairs={{0,8},{1,9},{2,10},{3,11},{4,12},{5,13},{6,14},{7,15},{8,0},{9,1},... | collective-permute-start | bytes 1572872 | tf_op jit(solution)/shard_map/ppermute | solution.py:52
  41.2 4.6 %collective-permute-start.24 = (f32[32,1024]{1,0:T(8,128)S(1)}, f32[32,1024]{1,0:T(8,128)S(1)}, u32[]{:S(2)}, u32[]{:S(2)}) collective-permute-start(f32[32,1024]{1,0:T(8,128)S(1)} %get-tuple-element.88), channel_id=1, source_target_pairs={{0,9},{1,11},{2,8},{3,10},{4,13},{5,15},{6,12},{7,14},{8,2},{9,0},... | collective-permute-start | bytes 393224 | tf_op jit(solution)/shard_map/ppermute | solution.py:52
  41.7 6.2 %collective-permute-start.29 = (f32[32,1024]{1,0:T(8,128)S(1)}, f32[32,1024]{1,0:T(8,128)S(1)}, u32[]{:S(2)}, u32[]{:S(2)}) collective-permute-start(f32[32,1024]{1,0:T(8,128)S(1)} %get-tuple-element.92), channel_id=1, source_target_pairs={{0,24},{1,25},{2,26},{3,27},{4,28},{5,29},{6,30},{7,31},{8,16},{9,... | collective-permute-start | bytes 393224 | tf_op jit(solution)/shard_map/ppermute | solution.py:52
  44.0 5.2 %collective-permute-start.40 = (f32[32,1024]{1,0:T(8,128)S(1)}, f32[32,1024]{1,0:T(8,128)S(1)}, u32[]{:S(2)}, u32[]{:S(2)}) collective-permute-start(f32[32,1024]{1,0:T(8,128)S(1)} %get-tuple-element.103), channel_id=1, source_target_pairs={{0,9},{1,25},{2,26},{3,10},{4,13},{5,29},{6,30},{7,14},{8,16},{9,0... | collective-permute-start | bytes 393224 | tf_op jit(solution)/shard_map/ppermute | solution.py:52
  44.5 5.7 %collective-permute-start.36 = (f32[32,1024]{1,0:T(8,128)S(1)}, f32[32,1024]{1,0:T(8,128)S(1)}, u32[]{:S(2)}, u32[]{:S(2)}) collective-permute-start(f32[32,1024]{1,0:T(8,128)S(1)} %get-tuple-element.101), channel_id=1, source_target_pairs={{0,9},{1,11},{2,8},{3,10},{4,13},{5,15},{6,12},{7,14},{8,2},{9,0},... | collective-permute-start | bytes 393224 | tf_op jit(solution)/shard_map/ppermute | solution.py:52
  45.8 6.2 %collective-permute-start.25 = (f32[32,1024]{1,0:T(8,128)S(1)}, f32[32,1024]{1,0:T(8,128)S(1)}, u32[]{:S(2)}, u32[]{:S(2)}) collective-permute-start(f32[32,1024]{1,0:T(8,128)S(1)} %shard_map.75), channel_id=1, source_target_pairs={{0,10},{1,25},{2,26},{3,9},{4,14},{5,29},{6,30},{7,13},{8,16},{9,3... | collective-permute-start | bytes 393224 | tf_op jit(solution)/shard_map/ppermute | solution.py:52
  49.3 4.8 %collective-permute-start.41 = (f32[32,1024]{1,0:T(8,128)S(1)}, f32[32,1024]{1,0:T(8,128)S(1)}, u32[]{:S(2)}, u32[]{:S(2)}) collective-permute-start(f32[32,1024]{1,0:T(8,128)S(1)} %shard_map.84), channel_id=1, source_target_pairs={{0,24},{1,8},{2,11},{3,27},{4,28},{5,12},{6,15},{7,31},{8,1},{9,17... | collective-permute-start | bytes 393224 | tf_op jit(solution)/shard_map/ppermute | solution.py:52
  50.2 5.3 %collective-permute-start.37 = (f32[32,1024]{1,0:T(8,128)S(1)}, f32[32,1024]{1,0:T(8,128)S(1)}, u32[]{:S(2)}, u32[]{:S(2)}) collective-permute-start(f32[32,1024]{1,0:T(8,128)S(1)} %shard_map.82), channel_id=1, source_target_pairs={{0,10},{1,25},{2,26},{3,9},{4,14},{5,29},{6,30},{7,13},{8,16},{9,3... | collective-permute-start | bytes 393224 | tf_op jit(solution)/shard_map/ppermute | solution.py:52
  52.0 4.5 %collective-permute-start.26 = (f32[32,1024]{1,0:T(8,128)S(1)}, f32[32,1024]{1,0:T(8,128)S(1)}, u32[]{:S(2)}, u32[]{:S(2)}) collective-permute-start(f32[32,1024]{1,0:T(8,128)S(1)} %add.56), channel_id=1, source_target_pairs={{0,24},{1,8},{2,11},{3,27},{4,28},{5,12},{6,15},{7,31},{8,1},{9,17... | collective-permute-start | bytes 393224 | tf_op jit(solution)/shard_map/ppermute | solution.py:52
  52.3 5.6 %collective-permute-start.31 = (f32[32,1024]{1,0:T(8,128)S(1)}, f32[32,1024]{1,0:T(8,128)S(1)}, u32[]{:S(2)}, u32[]{:S(2)}) collective-permute-start(f32[32,1024]{1,0:T(8,128)S(1)} %add.58), channel_id=1, source_target_pairs={{0,9},{1,11},{2,8},{3,10},{4,13},{5,15},{6,12},{7,14},{8,2},{9,0},... | collective-permute-start | bytes 393224 | tf_op jit(solution)/shard_map/ppermute | solution.py:52
  54.1 5.9 %collective-permute-start.42 = (f32[32,1024]{1,0:T(8,128)S(1)}, f32[32,1024]{1,0:T(8,128)S(1)}, u32[]{:S(2)}, u32[]{:S(2)}) collective-permute-start(f32[32,1024]{1,0:T(8,128)S(1)} %add.62), channel_id=1, source_target_pairs={{0,10},{1,11},{2,8},{3,9},{4,14},{5,15},{6,12},{7,13},{8,2},{9,3},... | collective-permute-start | bytes 393224 | tf_op jit(solution)/shard_map/ppermute | solution.py:52
  55.6 5.3 %collective-permute-start.38 = (f32[32,1024]{1,0:T(8,128)S(1)}, f32[32,1024]{1,0:T(8,128)S(1)}, u32[]{:S(2)}, u32[]{:S(2)}) collective-permute-start(f32[32,1024]{1,0:T(8,128)S(1)} %add.60), channel_id=1, source_target_pairs={{0,24},{1,8},{2,11},{3,27},{4,28},{5,12},{6,15},{7,31},{8,1},{9,17... | collective-permute-start | bytes 393224 | tf_op jit(solution)/shard_map/ppermute | solution.py:52
  56.6 5.3 %collective-permute-start.27 = (f32[32,1024]{1,0:T(8,128)S(1)}, f32[32,1024]{1,0:T(8,128)S(1)}, u32[]{:S(2)}, u32[]{:S(2)}) collective-permute-start(f32[32,1024]{1,0:T(8,128)S(1)} %add.57.own_ref), channel_id=1, source_target_pairs={{0,9},{1,11},{2,8},{3,10},{4,13},{5,15},{6,12},{7,14},{8,2},{9,0},... | collective-permute-start | bytes 393224 | tf_op jit(solution)/shard_map/ppermute | solution.py:52
  58.0 5.6 %collective-permute-start.32 = (f32[32,1024]{1,0:T(8,128)S(1)}, f32[32,1024]{1,0:T(8,128)S(1)}, u32[]{:S(2)}, u32[]{:S(2)}) collective-permute-start(f32[32,1024]{1,0:T(8,128)S(1)} %add.59.own_ref), channel_id=1, source_target_pairs={{0,24},{1,25},{2,26},{3,27},{4,28},{5,29},{6,30},{7,31},{8,16},{9,... | collective-permute-start | bytes 393224 | tf_op jit(solution)/shard_map/ppermute | solution.py:52
  60.9 4.9 %collective-permute-start.39 = (f32[32,1024]{1,0:T(8,128)S(1)}, f32[32,1024]{1,0:T(8,128)S(1)}, u32[]{:S(2)}, u32[]{:S(2)}) collective-permute-start(f32[32,1024]{1,0:T(8,128)S(1)} %add.61.own_ref), channel_id=1, source_target_pairs={{0,9},{1,11},{2,8},{3,10},{4,13},{5,15},{6,12},{7,14},{8,2},{9,0},... | collective-permute-start | bytes 393224 | tf_op jit(solution)/shard_map/ppermute | solution.py:52
  (14 other events, 42.4 us)

commit v9 on v8

--- a/solution.py
+++ b/solution.py
@@ -240,11 +240,16 @@
         moves += [(r_in.at[:, columns], r_ref.at[:, columns]), (x_in.at[0, :, columns], acts_refs[0].at[:, columns])]
     early = len(moves)
     later = [(source.at[i // 2], ref) for i, (source, ref) in enumerate(zip((x_in, g_in) * len(acts_refs), acts_refs))]
-    copies = start_copies(moves + [(e_in, e_ref)] + later[1:], sems)
+    copies = start_copies(moves, sems)
+    for i, (source, target) in enumerate([(e_in, e_ref)] + later[1:]):
+        copies.append(pltpu.make_async_copy(source, target, sems.at[early + i]))
 
     def arrived(i):
         copies[2 * i].wait()
         copies[2 * i + 1].wait()
+        if i == 0:
+            for copy in copies[early:]:
+                copy.start()
 
     hidden_of(r_ref, acts_refs[0], outs, arrived)
     for copy in copies[early:]:

time: 68.4 us -> 69 us (level)
  no operation moved by 1% of the time
where the time goes in v9:
time: 69 us; the launch traced here: 68.8 us
  starting transfers between devices  42.3 us (61%)
  waiting for transfers between devices  14.6 us (21%)
  Pallas kernels  10.7 us (16%)
  between operations  0.9 us (1%)
    ppermute x46, starting transfers between devices, from_partner(): return lax.ppermute(values, ('near', 'far'), pairs)  42.3 us
    ppermute x46, waiting for transfers between devices, from_partner(): return lax.ppermute(values, ('near', 'far'), pairs)  14.6 us
    pallas_call x2, Pallas kernels, shards(): pl.pallas_call(functools.partial(reduce_kernel, not first), out_shape=hal...  3.67 us
    pallas_call x1, Pallas kernels, shards(): pl.pallas_call(first_hidden_kernel, out_shape=hidden_shapes + [narrow] *...  2.66 us
    pallas_call x2, Pallas kernels, store(): pl.pallas_call(functools.partial(store_kernel, counted), out_shape=[jax.S...  1.99 us
  transfers between devices with their start and end apart: 46, of which 20 were waited for; matrix products, arithmetic and copies ran while one was open for 0% of the time, Pallas kernels for 4%

profile of v9, /device:TPU:0, one launch (start us, length us, event | category | flops | bytes accessed | tf_op | source)
XLA Modules:
  0.0 68.8 jit_solution(11980795500301413833)
XLA Ops:
  0.6 2.7 %hidden_0.1 = (f32[256,256]{1,0:T(8,128)S(1)}, bf16[256,256]{1,0:T(8,128)(2,1)S(1)}, bf16[256,256]{1,0:T(8,128)(2,1)S(1)}, bf16[256,256]{1,0:T(8,128)(2,1)S(1)},...) custom-call(bf16[2,256,1024]{2,1,0:T(8,128)(2,1)} %bitcast.6, ...), custom_call_target="tpu_custom_call" | custom-call | tf_op jit(solution)/shard_map/hidden_0/pallas_call | solution.py:328
  3.3 1.7 %shard_map.59 = (f32[64,1024]{1,0:T(8,128)S(1)}, f32[64,1024]{1,0:T(8,128)S(1)}, f32[64,1024]{1,0:T(8,128)S(1)}, f32[64,1024]{1,0:T(8,128)S(1)}, bf16[256,1024]{...) custom-call(bf16[256,1024]{1,0:T(8,128)(2,1)S(1)} %get-tuple-element.56.x_ref, ...), custom_call_target="tpu_custom_call" | custom-call | tf_op jit(solution)/shard_map/pallas_call | solution.py:343
  6.6 1.4 %collective-permute-done.got_ref = f32[64,1024]{1,0:T(8,128)S(1)} collective-permute-done((f32[64,1024]{1,0:T(8,128)S(1)}, f32[64,1024]{1,0:T(8,128)S(1)}, u32[]{:S(2)}, u32[]{:S(2)}) %collective-permute-start) | collective-permute-done | bytes 262176 | tf_op jit(solution)/shard_map/ppermute | solution.py:52
  8.1 2.7 %collective-permute-start.1 = (f32[32,1024]{1,0:T(8,128)S(1)}, f32[32,1024]{1,0:T(8,128)S(1)}, u32[]{:S(2)}, u32[]{:S(2)}) collective-permute-start(f32[32,1024]{1,0:T(8,128)S(1)} %get-tuple-element.66), channel_id=1, source_target_pairs={{0,9},{1,11},{2,8},{3,10},{4,13},{5,15},{6,12},{7,14},{8,2},{9,0},... | collective-permute-start | bytes 393224 | tf_op jit(solution)/shard_map/ppermute | solution.py:52
  10.8 1.5 %collective-permute-start.6 = (f32[32,1024]{1,0:T(8,128)S(1)}, f32[32,1024]{1,0:T(8,128)S(1)}, u32[]{:S(2)}, u32[]{:S(2)}) collective-permute-start(f32[32,1024]{1,0:T(8,128)S(1)} %get-tuple-element.70), channel_id=1, source_target_pairs={{0,24},{1,25},{2,26},{3,27},{4,28},{5,29},{6,30},{7,31},{8,16},{9,... | collective-permute-start | bytes 393224 | tf_op jit(solution)/shard_map/ppermute | solution.py:52
  12.7 1.5 %collective-permute-start.13 = (f32[32,1024]{1,0:T(8,128)S(1)}, f32[32,1024]{1,0:T(8,128)S(1)}, u32[]{:S(2)}, u32[]{:S(2)}) collective-permute-start(f32[32,1024]{1,0:T(8,128)S(1)} %get-tuple-element.82), channel_id=1, source_target_pairs={{0,9},{1,11},{2,8},{3,10},{4,13},{5,15},{6,12},{7,14},{8,2},{9,0},... | collective-permute-start | bytes 393224 | tf_op jit(solution)/shard_map/ppermute | solution.py:52
  14.2 1.4 %collective-permute-start.2 = (f32[32,1024]{1,0:T(8,128)S(1)}, f32[32,1024]{1,0:T(8,128)S(1)}, u32[]{:S(2)}, u32[]{:S(2)}) collective-permute-start(f32[32,1024]{1,0:T(8,128)S(1)} %shard_map.61), channel_id=1, source_target_pairs={{0,10},{1,25},{2,26},{3,9},{4,14},{5,29},{6,30},{7,13},{8,16},{9,3... | collective-permute-start | bytes 393224 | tf_op jit(solution)/shard_map/ppermute | solution.py:52
  16.2 2.3 %collective-permute-start.7 = (f32[32,1024]{1,0:T(8,128)S(1)}, f32[32,1024]{1,0:T(8,128)S(1)}, u32[]{:S(2)}, u32[]{:S(2)}) collective-permute-start(f32[32,1024]{1,0:T(8,128)S(1)} %shard_map.64), channel_id=1, source_target_pairs={{0,10},{1,8},{2,11},{3,9},{4,14},{5,12},{6,15},{7,13},{8,1},{9,3},... | collective-permute-start | bytes 393224 | tf_op jit(solution)/shard_map/ppermute | solution.py:52
  18.6 1.0 %collective-permute-start.18 = (f32[32,1024]{1,0:T(8,128)S(1)}, f32[32,1024]{1,0:T(8,128)S(1)}, u32[]{:S(2)}, u32[]{:S(2)}) collective-permute-start(f32[32,1024]{1,0:T(8,128)S(1)} %shard_map.71), channel_id=1, source_target_pairs={{0,24},{1,8},{2,11},{3,27},{4,28},{5,12},{6,15},{7,31},{8,1},{9,17... | collective-permute-start | bytes 393224 | tf_op jit(solution)/shard_map/ppermute | solution.py:52
  22.0 1.7 %collective-permute-done.18 = f32[32,1024]{1,0:T(8,128)S(1)} collective-permute-done((f32[32,1024]{1,0:T(8,128)S(1)}, f32[32,1024]{1,0:T(8,128)S(1)}, u32[]{:S(2)}, u32[]{:S(2)}) %collective-permute-start.18) | collective-permute-done | bytes 131104 | tf_op jit(solution)/shard_map/ppermute | solution.py:52
  24.1 1.8 %collective-permute-start.15 = (f32[32,1024]{1,0:T(8,128)S(1)}, f32[32,1024]{1,0:T(8,128)S(1)}, u32[]{:S(2)}, u32[]{:S(2)}) collective-permute-start(f32[32,1024]{1,0:T(8,128)S(1)} %add.52), channel_id=1, source_target_pairs={{0,24},{1,8},{2,11},{3,27},{4,28},{5,12},{6,15},{7,31},{8,1},{9,17... | collective-permute-start | bytes 393224 | tf_op jit(solution)/shard_map/ppermute | solution.py:52
  26.4 1.7 %collective-permute-start.9 = (f32[32,1024]{1,0:T(8,128)S(1)}, f32[32,1024]{1,0:T(8,128)S(1)}, u32[]{:S(2)}, u32[]{:S(2)}) collective-permute-start(f32[32,1024]{1,0:T(8,128)S(1)} %add.51.own_ref), channel_id=1, source_target_pairs={{0,24},{1,25},{2,26},{3,27},{4,28},{5,29},{6,30},{7,31},{8,16},{9,... | collective-permute-start | bytes 393224 | tf_op jit(solution)/shard_map/ppermute | solution.py:52
  28.0 1.1 %collective-permute-done.19 = f32[32,1024]{1,0:T(8,128)S(1)} collective-permute-done((f32[32,1024]{1,0:T(8,128)S(1)}, f32[32,1024]{1,0:T(8,128)S(1)}, u32[]{:S(2)}, u32[]{:S(2)}) %collective-permute-start.19) | collective-permute-done | bytes 131104 | tf_op jit(solution)/shard_map/ppermute | solution.py:52
  29.5 1.6 %collective-permute-start.16 = (f32[32,1024]{1,0:T(8,128)S(1)}, f32[32,1024]{1,0:T(8,128)S(1)}, u32[]{:S(2)}, u32[]{:S(2)}) collective-permute-start(f32[32,1024]{1,0:T(8,128)S(1)} %add.53.own_ref), channel_id=1, source_target_pairs={{0,9},{1,11},{2,8},{3,10},{4,13},{5,15},{6,12},{7,14},{8,2},{9,0},... | collective-permute-start | bytes 393224 | tf_op jit(solution)/shard_map/ppermute | solution.py:52
  32.1 1.5 %collective-permute-done.20.rest_ref = f32[32,1024]{1,0:T(8,128)S(1)} collective-permute-done((f32[32,1024]{1,0:T(8,128)S(1)}, f32[32,1024]{1,0:T(8,128)S(1)}, u32[]{:S(2)}, u32[]{:S(2)}) %collective-permute-start.20) | collective-permute-done | bytes 131104 | tf_op jit(solution)/shard_map/ppermute | solution.py:52
  33.8 1.2 %collective-permute-done.16.rest_ref = f32[32,1024]{1,0:T(8,128)S(1)} collective-permute-done((f32[32,1024]{1,0:T(8,128)S(1)}, f32[32,1024]{1,0:T(8,128)S(1)}, u32[]{:S(2)}, u32[]{:S(2)}) %collective-permute-start.16) | collective-permute-done | bytes 131104 | tf_op jit(solution)/shard_map/ppermute | solution.py:52
  36.7 2.0 %shard_map.73 = (f32[64,1024]{1,0:T(8,128)S(1)}, f32[64,1024]{1,0:T(8,128)S(1)}, f32[64,1024]{1,0:T(8,128)S(1)}, f32[64,1024]{1,0:T(8,128)S(1)}, bf16[256,1024]{...) custom-call(bf16[256,1024]{1,0:T(8,128)(2,1)S(1)} %get-tuple-element.54.x_ref, ...), custom_call_target="tpu_custom_call" | custom-call | tf_op jit(solution)/shard_map/pallas_call | solution.py:343
  40.3 1.4 %collective-permute-done.23.got_ref = f32[64,1024]{1,0:T(8,128)S(1)} collective-permute-done((f32[64,1024]{1,0:T(8,128)S(1)}, f32[64,1024]{1,0:T(8,128)S(1)}, u32[]{:S(2)}, u32[]{:S(2)}) %collective-permute-start.23) | collective-permute-done | bytes 262176 | tf_op jit(solution)/shard_map/ppermute | solution.py:52
  42.3 2.3 %collective-permute-start.29 = (f32[32,1024]{1,0:T(8,128)S(1)}, f32[32,1024]{1,0:T(8,128)S(1)}, u32[]{:S(2)}, u32[]{:S(2)}) collective-permute-start(f32[32,1024]{1,0:T(8,128)S(1)} %get-tuple-element.92), channel_id=1, source_target_pairs={{0,24},{1,25},{2,26},{3,27},{4,28},{5,29},{6,30},{7,31},{8,16},{9,... | collective-permute-start | bytes 393224 | tf_op jit(solution)/shard_map/ppermute | solution.py:52
  45.2 1.3 %collective-permute-start.36 = (f32[32,1024]{1,0:T(8,128)S(1)}, f32[32,1024]{1,0:T(8,128)S(1)}, u32[]{:S(2)}, u32[]{:S(2)}) collective-permute-start(f32[32,1024]{1,0:T(8,128)S(1)} %get-tuple-element.101), channel_id=1, source_target_pairs={{0,9},{1,11},{2,8},{3,10},{4,13},{5,15},{6,12},{7,14},{8,2},{9,0},... | collective-permute-start | bytes 393224 | tf_op jit(solution)/shard_map/ppermute | solution.py:52
  47.2 1.2 %collective-permute-done.29.right_ref = f32[32,1024]{1,0:T(8,128)S(1)} collective-permute-done((f32[32,1024]{1,0:T(8,128)S(1)}, f32[32,1024]{1,0:T(8,128)S(1)}, u32[]{:S(2)}, u32[]{:S(2)}) %collective-permute-start.29) | collective-permute-done | bytes 131104 | tf_op jit(solution)/shard_map/ppermute | solution.py:52
  48.4 1.4 %collective-permute-start.30 = (f32[32,1024]{1,0:T(8,128)S(1)}, f32[32,1024]{1,0:T(8,128)S(1)}, u32[]{:S(2)}, u32[]{:S(2)}) collective-permute-start(f32[32,1024]{1,0:T(8,128)S(1)} %shard_map.78), channel_id=1, source_target_pairs={{0,10},{1,8},{2,11},{3,9},{4,14},{5,12},{6,15},{7,13},{8,1},{9,3},... | collective-permute-start | bytes 393224 | tf_op jit(solution)/shard_map/ppermute | solution.py:52
  49.9 1.0 %collective-permute-start.41 = (f32[32,1024]{1,0:T(8,128)S(1)}, f32[32,1024]{1,0:T(8,128)S(1)}, u32[]{:S(2)}, u32[]{:S(2)}) collective-permute-start(f32[32,1024]{1,0:T(8,128)S(1)} %shard_map.84), channel_id=1, source_target_pairs={{0,24},{1,8},{2,11},{3,27},{4,28},{5,12},{6,15},{7,31},{8,1},{9,17... | collective-permute-start | bytes 393224 | tf_op jit(solution)/shard_map/ppermute | solution.py:52
  50.8 1.8 %collective-permute-start.37 = (f32[32,1024]{1,0:T(8,128)S(1)}, f32[32,1024]{1,0:T(8,128)S(1)}, u32[]{:S(2)}, u32[]{:S(2)}) collective-permute-start(f32[32,1024]{1,0:T(8,128)S(1)} %shard_map.82), channel_id=1, source_target_pairs={{0,10},{1,25},{2,26},{3,9},{4,14},{5,29},{6,30},{7,13},{8,16},{9,3... | collective-permute-start | bytes 393224 | tf_op jit(solution)/shard_map/ppermute | solution.py:52
  52.9 1.7 %collective-permute-start.31 = (f32[32,1024]{1,0:T(8,128)S(1)}, f32[32,1024]{1,0:T(8,128)S(1)}, u32[]{:S(2)}, u32[]{:S(2)}) collective-permute-start(f32[32,1024]{1,0:T(8,128)S(1)} %add.58), channel_id=1, source_target_pairs={{0,9},{1,11},{2,8},{3,10},{4,13},{5,15},{6,12},{7,14},{8,2},{9,0},... | collective-permute-start | bytes 393224 | tf_op jit(solution)/shard_map/ppermute | solution.py:52
  54.7 1.5 %collective-permute-start.42 = (f32[32,1024]{1,0:T(8,128)S(1)}, f32[32,1024]{1,0:T(8,128)S(1)}, u32[]{:S(2)}, u32[]{:S(2)}) collective-permute-start(f32[32,1024]{1,0:T(8,128)S(1)} %add.62), channel_id=1, source_target_pairs={{0,10},{1,11},{2,8},{3,9},{4,14},{5,15},{6,12},{7,13},{8,2},{9,3},... | collective-permute-start | bytes 393224 | tf_op jit(solution)/shard_map/ppermute | solution.py:52
  56.2 0.9 %collective-permute-start.38 = (f32[32,1024]{1,0:T(8,128)S(1)}, f32[32,1024]{1,0:T(8,128)S(1)}, u32[]{:S(2)}, u32[]{:S(2)}) collective-permute-start(f32[32,1024]{1,0:T(8,128)S(1)} %add.60), channel_id=1, source_target_pairs={{0,24},{1,8},{2,11},{3,27},{4,28},{5,12},{6,15},{7,31},{8,1},{9,17... | collective-permute-start | bytes 393224 | tf_op jit(solution)/shard_map/ppermute | solution.py:52
  57.2 0.9 %collective-permute-start.27 = (f32[32,1024]{1,0:T(8,128)S(1)}, f32[32,1024]{1,0:T(8,128)S(1)}, u32[]{:S(2)}, u32[]{:S(2)}) collective-permute-start(f32[32,1024]{1,0:T(8,128)S(1)} %add.57.own_ref), channel_id=1, source_target_pairs={{0,9},{1,11},{2,8},{3,10},{4,13},{5,15},{6,12},{7,14},{8,2},{9,0},... | collective-permute-start | bytes 393224 | tf_op jit(solution)/shard_map/ppermute | solution.py:52
  58.6 1.7 %collective-permute-start.32 = (f32[32,1024]{1,0:T(8,128)S(1)}, f32[32,1024]{1,0:T(8,128)S(1)}, u32[]{:S(2)}, u32[]{:S(2)}) collective-permute-start(f32[32,1024]{1,0:T(8,128)S(1)} %add.59.own_ref), channel_id=1, source_target_pairs={{0,24},{1,25},{2,26},{3,27},{4,28},{5,29},{6,30},{7,31},{8,16},{9,... | collective-permute-start | bytes 393224 | tf_op jit(solution)/shard_map/ppermute | solution.py:52
  60.5 1.0 %collective-permute-start.43 = (f32[32,1024]{1,0:T(8,128)S(1)}, f32[32,1024]{1,0:T(8,128)S(1)}, u32[]{:S(2)}, u32[]{:S(2)}) collective-permute-start(f32[32,1024]{1,0:T(8,128)S(1)} %add.63.own_ref), channel_id=1, source_target_pairs={{0,9},{1,25},{2,26},{3,10},{4,13},{5,29},{6,30},{7,14},{8,16},{9,0... | collective-permute-start | bytes 393224 | tf_op jit(solution)/shard_map/ppermute | solution.py:52
  65.0 1.1 %collective-permute-start.45 = (f32[64,1024]{1,0:T(8,128)S(1)}, f32[64,1024]{1,0:T(8,128)S(1)}, u32[]{:S(2)}, u32[]{:S(2)}) collective-permute-start(f32[64,1024]{1,0:T(8,128)S(1)} %shard_map.85.refs_5_), channel_id=1, source_target_pairs={{0,8},{1,9},{2,10},{3,11},{4,12},{5,13},{6,14},{7,15},{8,0},{9,1},... | collective-permute-start | bytes 786440 | tf_op jit(solution)/shard_map/ppermute | solution.py:52
  66.6 1.2 %shard_map.86 = (f32[256,1024]{1,0:T(8,128)}, f32[256,1024]{1,0:T(8,128)}) custom-call(f32[64,1024]{1,0:T(8,128)S(1)} %shard_map.76.refs_0_, f32[64,1024]{1,0:T(8,128)S(1)} %shard_map.79.refs_1_, f32[64,1024]{1,0:T(8,128)S(1)} %collective-permute-done.33.refs_2_, f32[64,1024]{1,0:T(8,128)S(1)} %collective-permute-done.34.refs_3_, ...), custom_call_target="tpu_custom_call" | custom-call | tf_op jit(solution)/shard_map/pallas_call | solution.py:160
  (106 shorter events, 18.7 us)
Async XLA Ops:
  5.5 6.8 %collective-permute-start.12 = (f32[128,1024]{1,0:T(8,128)S(1)}, f32[128,1024]{1,0:T(8,128)S(1)}, u32[]{:S(2)}, u32[]{:S(2)}) collective-permute-start(f32[128,1024]{1,0:T(8,128)S(1)} %get-tuple-element.80), channel_id=1, source_target_pairs={{0,8},{1,9},{2,10},{3,11},{4,12},{5,13},{6,14},{7,15},{8,0},{9,1},... | collective-permute-start | bytes 1572872 | tf_op jit(solution)/shard_map/ppermute | solution.py:52
  6.2 4.6 %collective-permute-start.5 = (f32[64,1024]{1,0:T(8,128)S(1)}, f32[64,1024]{1,0:T(8,128)S(1)}, u32[]{:S(2)}, u32[]{:S(2)}) collective-permute-start(f32[64,1024]{1,0:T(8,128)S(1)} %get-tuple-element.68), channel_id=1, source_target_pairs={{0,8},{1,9},{2,10},{3,11},{4,12},{5,13},{6,14},{7,15},{8,0},{9,1},... | collective-permute-start | bytes 786440 | tf_op jit(solution)/shard_map/ppermute | solution.py:52
  8.1 6.1 %collective-permute-start.1 = (f32[32,1024]{1,0:T(8,128)S(1)}, f32[32,1024]{1,0:T(8,128)S(1)}, u32[]{:S(2)}, u32[]{:S(2)}) collective-permute-start(f32[32,1024]{1,0:T(8,128)S(1)} %get-tuple-element.66), channel_id=1, source_target_pairs={{0,9},{1,11},{2,8},{3,10},{4,13},{5,15},{6,12},{7,14},{8,2},{9,0},... | collective-permute-start | bytes 393224 | tf_op jit(solution)/shard_map/ppermute | solution.py:52
  10.8 5.4 %collective-permute-start.6 = (f32[32,1024]{1,0:T(8,128)S(1)}, f32[32,1024]{1,0:T(8,128)S(1)}, u32[]{:S(2)}, u32[]{:S(2)}) collective-permute-start(f32[32,1024]{1,0:T(8,128)S(1)} %get-tuple-element.70), channel_id=1, source_target_pairs={{0,24},{1,25},{2,26},{3,27},{4,28},{5,29},{6,30},{7,31},{8,16},{9,... | collective-permute-start | bytes 393224 | tf_op jit(solution)/shard_map/ppermute | solution.py:52
  12.4 6.2 %collective-permute-start.17 = (f32[32,1024]{1,0:T(8,128)S(1)}, f32[32,1024]{1,0:T(8,128)S(1)}, u32[]{:S(2)}, u32[]{:S(2)}) collective-permute-start(f32[32,1024]{1,0:T(8,128)S(1)} %get-tuple-element.84), channel_id=1, source_target_pairs={{0,9},{1,25},{2,26},{3,10},{4,13},{5,29},{6,30},{7,14},{8,16},{9,0... | collective-permute-start | bytes 393224 | tf_op jit(solution)/shard_map/ppermute | solution.py:52
  12.7 6.9 %collective-permute-start.13 = (f32[32,1024]{1,0:T(8,128)S(1)}, f32[32,1024]{1,0:T(8,128)S(1)}, u32[]{:S(2)}, u32[]{:S(2)}) collective-permute-start(f32[32,1024]{1,0:T(8,128)S(1)} %get-tuple-element.82), channel_id=1, source_target_pairs={{0,9},{1,11},{2,8},{3,10},{4,13},{5,15},{6,12},{7,14},{8,2},{9,0},... | collective-permute-start | bytes 393224 | tf_op jit(solution)/shard_map/ppermute | solution.py:52
  14.2 6.2 %collective-permute-start.2 = (f32[32,1024]{1,0:T(8,128)S(1)}, f32[32,1024]{1,0:T(8,128)S(1)}, u32[]{:S(2)}, u32[]{:S(2)}) collective-permute-start(f32[32,1024]{1,0:T(8,128)S(1)} %shard_map.61), channel_id=1, source_target_pairs={{0,10},{1,25},{2,26},{3,9},{4,14},{5,29},{6,30},{7,13},{8,16},{9,3... | collective-permute-start | bytes 393224 | tf_op jit(solution)/shard_map/ppermute | solution.py:52
  16.2 5.0 %collective-permute-start.7 = (f32[32,1024]{1,0:T(8,128)S(1)}, f32[32,1024]{1,0:T(8,128)S(1)}, u32[]{:S(2)}, u32[]{:S(2)}) collective-permute-start(f32[32,1024]{1,0:T(8,128)S(1)} %shard_map.64), channel_id=1, source_target_pairs={{0,10},{1,8},{2,11},{3,9},{4,14},{5,12},{6,15},{7,13},{8,1},{9,3},... | collective-permute-start | bytes 393224 | tf_op jit(solution)/shard_map/ppermute | solution.py:52
  18.6 5.2 %collective-permute-start.18 = (f32[32,1024]{1,0:T(8,128)S(1)}, f32[32,1024]{1,0:T(8,128)S(1)}, u32[]{:S(2)}, u32[]{:S(2)}) collective-permute-start(f32[32,1024]{1,0:T(8,128)S(1)} %shard_map.71), channel_id=1, source_target_pairs={{0,24},{1,8},{2,11},{3,27},{4,28},{5,12},{6,15},{7,31},{8,1},{9,17... | collective-permute-start | bytes 393224 | tf_op jit(solution)/shard_map/ppermute | solution.py:52
  19.6 4.5 %collective-permute-start.14 = (f32[32,1024]{1,0:T(8,128)S(1)}, f32[32,1024]{1,0:T(8,128)S(1)}, u32[]{:S(2)}, u32[]{:S(2)}) collective-permute-start(f32[32,1024]{1,0:T(8,128)S(1)} %shard_map.69), channel_id=1, source_target_pairs={{0,10},{1,25},{2,26},{3,9},{4,14},{5,29},{6,30},{7,13},{8,16},{9,3... | collective-permute-start | bytes 393224 | tf_op jit(solution)/shard_map/ppermute | solution.py:52
  20.4 5.4 %collective-permute-start.3 = (f32[32,1024]{1,0:T(8,128)S(1)}, f32[32,1024]{1,0:T(8,128)S(1)}, u32[]{:S(2)}, u32[]{:S(2)}) collective-permute-start(f32[32,1024]{1,0:T(8,128)S(1)} %add.48), channel_id=1, source_target_pairs={{0,24},{1,8},{2,11},{3,27},{4,28},{5,12},{6,15},{7,31},{8,1},{9,17... | collective-permute-start | bytes 393224 | tf_op jit(solution)/shard_map/ppermute | solution.py:52
  21.2 5.1 %collective-permute-start.8 = (f32[32,1024]{1,0:T(8,128)S(1)}, f32[32,1024]{1,0:T(8,128)S(1)}, u32[]{:S(2)}, u32[]{:S(2)}) collective-permute-start(f32[32,1024]{1,0:T(8,128)S(1)} %add.50), channel_id=1, source_target_pairs={{0,9},{1,11},{2,8},{3,10},{4,13},{5,15},{6,12},{7,14},{8,2},{9,0},... | collective-permute-start | bytes 393224 | tf_op jit(solution)/shard_map/ppermute | solution.py:52
  23.8 5.4 %collective-permute-start.19 = (f32[32,1024]{1,0:T(8,128)S(1)}, f32[32,1024]{1,0:T(8,128)S(1)}, u32[]{:S(2)}, u32[]{:S(2)}) collective-permute-start(f32[32,1024]{1,0:T(8,128)S(1)} %add.54), channel_id=1, source_target_pairs={{0,10},{1,11},{2,8},{3,9},{4,14},{5,15},{6,12},{7,13},{8,2},{9,3},... | collective-permute-start | bytes 393224 | tf_op jit(solution)/shard_map/ppermute | solution.py:52
  24.1 5.3 %collective-permute-start.15 = (f32[32,1024]{1,0:T(8,128)S(1)}, f32[32,1024]{1,0:T(8,128)S(1)}, u32[]{:S(2)}, u32[]{:S(2)}) collective-permute-start(f32[32,1024]{1,0:T(8,128)S(1)} %add.52), channel_id=1, source_target_pairs={{0,24},{1,8},{2,11},{3,27},{4,28},{5,12},{6,15},{7,31},{8,1},{9,17... | collective-permute-start | bytes 393224 | tf_op jit(solution)/shard_map/ppermute | solution.py:52
  25.9 5.4 %collective-permute-start.4 = (f32[32,1024]{1,0:T(8,128)S(1)}, f32[32,1024]{1,0:T(8,128)S(1)}, u32[]{:S(2)}, u32[]{:S(2)}) collective-permute-start(f32[32,1024]{1,0:T(8,128)S(1)} %add.49.own_ref), channel_id=1, source_target_pairs={{0,9},{1,11},{2,8},{3,10},{4,13},{5,15},{6,12},{7,14},{8,2},{9,0},... | collective-permute-start | bytes 393224 | tf_op jit(solution)/shard_map/ppermute | solution.py:52
  26.4 5.6 %collective-permute-start.9 = (f32[32,1024]{1,0:T(8,128)S(1)}, f32[32,1024]{1,0:T(8,128)S(1)}, u32[]{:S(2)}, u32[]{:S(2)}) collective-permute-start(f32[32,1024]{1,0:T(8,128)S(1)} %add.51.own_ref), channel_id=1, source_target_pairs={{0,24},{1,25},{2,26},{3,27},{4,28},{5,29},{6,30},{7,31},{8,16},{9,... | collective-permute-start | bytes 393224 | tf_op jit(solution)/shard_map/ppermute | solution.py:52
  29.5 5.6 %collective-permute-start.16 = (f32[32,1024]{1,0:T(8,128)S(1)}, f32[32,1024]{1,0:T(8,128)S(1)}, u32[]{:S(2)}, u32[]{:S(2)}) collective-permute-start(f32[32,1024]{1,0:T(8,128)S(1)} %add.53.own_ref), channel_id=1, source_target_pairs={{0,9},{1,11},{2,8},{3,10},{4,13},{5,15},{6,12},{7,14},{8,2},{9,0},... | collective-permute-start | bytes 393224 | tf_op jit(solution)/shard_map/ppermute | solution.py:52
  39.4 5.2 %collective-permute-start.35 = (f32[128,1024]{1,0:T(8,128)S(1)}, f32[128,1024]{1,0:T(8,128)S(1)}, u32[]{:S(2)}, u32[]{:S(2)}) collective-permute-start(f32[128,1024]{1,0:T(8,128)S(1)} %get-tuple-element.99), channel_id=1, source_target_pairs={{0,8},{1,9},{2,10},{3,11},{4,12},{5,13},{6,14},{7,15},{8,0},{9,1},... | collective-permute-start | bytes 1572872 | tf_op jit(solution)/shard_map/ppermute | solution.py:52
  41.8 4.6 %collective-permute-start.24 = (f32[32,1024]{1,0:T(8,128)S(1)}, f32[32,1024]{1,0:T(8,128)S(1)}, u32[]{:S(2)}, u32[]{:S(2)}) collective-permute-start(f32[32,1024]{1,0:T(8,128)S(1)} %get-tuple-element.88), channel_id=1, source_target_pairs={{0,9},{1,11},{2,8},{3,10},{4,13},{5,15},{6,12},{7,14},{8,2},{9,0},... | collective-permute-start | bytes 393224 | tf_op jit(solution)/shard_map/ppermute | solution.py:52
  42.3 6.2 %collective-permute-start.29 = (f32[32,1024]{1,0:T(8,128)S(1)}, f32[32,1024]{1,0:T(8,128)S(1)}, u32[]{:S(2)}, u32[]{:S(2)}) collective-permute-start(f32[32,1024]{1,0:T(8,128)S(1)} %get-tuple-element.92), channel_id=1, source_target_pairs={{0,24},{1,25},{2,26},{3,27},{4,28},{5,29},{6,30},{7,31},{8,16},{9,... | collective-permute-start | bytes 393224 | tf_op jit(solution)/shard_map/ppermute | solution.py:52
  44.6 5.2 %collective-permute-start.40 = (f32[32,1024]{1,0:T(8,128)S(1)}, f32[32,1024]{1,0:T(8,128)S(1)}, u32[]{:S(2)}, u32[]{:S(2)}) collective-permute-start(f32[32,1024]{1,0:T(8,128)S(1)} %get-tuple-element.103), channel_id=1, source_target_pairs={{0,9},{1,25},{2,26},{3,10},{4,13},{5,29},{6,30},{7,14},{8,16},{9,0... | collective-permute-start | bytes 393224 | tf_op jit(solution)/shard_map/ppermute | solution.py:52
  45.2 5.7 %collective-permute-start.36 = (f32[32,1024]{1,0:T(8,128)S(1)}, f32[32,1024]{1,0:T(8,128)S(1)}, u32[]{:S(2)}, u32[]{:S(2)}) collective-permute-start(f32[32,1024]{1,0:T(8,128)S(1)} %get-tuple-element.101), channel_id=1, source_target_pairs={{0,9},{1,11},{2,8},{3,10},{4,13},{5,15},{6,12},{7,14},{8,2},{9,0},... | collective-permute-start | bytes 393224 | tf_op jit(solution)/shard_map/ppermute | solution.py:52
  46.4 6.2 %collective-permute-start.25 = (f32[32,1024]{1,0:T(8,128)S(1)}, f32[32,1024]{1,0:T(8,128)S(1)}, u32[]{:S(2)}, u32[]{:S(2)}) collective-permute-start(f32[32,1024]{1,0:T(8,128)S(1)} %shard_map.75), channel_id=1, source_target_pairs={{0,10},{1,25},{2,26},{3,9},{4,14},{5,29},{6,30},{7,13},{8,16},{9,3... | collective-permute-start | bytes 393224 | tf_op jit(solution)/shard_map/ppermute | solution.py:52
  49.9 4.8 %collective-permute-start.41 = (f32[32,1024]{1,0:T(8,128)S(1)}, f32[32,1024]{1,0:T(8,128)S(1)}, u32[]{:S(2)}, u32[]{:S(2)}) collective-permute-start(f32[32,1024]{1,0:T(8,128)S(1)} %shard_map.84), channel_id=1, source_target_pairs={{0,24},{1,8},{2,11},{3,27},{4,28},{5,12},{6,15},{7,31},{8,1},{9,17... | collective-permute-start | bytes 393224 | tf_op jit(solution)/shard_map/ppermute | solution.py:52
  50.8 5.3 %collective-permute-start.37 = (f32[32,1024]{1,0:T(8,128)S(1)}, f32[32,1024]{1,0:T(8,128)S(1)}, u32[]{:S(2)}, u32[]{:S(2)}) collective-permute-start(f32[32,1024]{1,0:T(8,128)S(1)} %shard_map.82), channel_id=1, source_target_pairs={{0,10},{1,25},{2,26},{3,9},{4,14},{5,29},{6,30},{7,13},{8,16},{9,3... | collective-permute-start | bytes 393224 | tf_op jit(solution)/shard_map/ppermute | solution.py:52
  52.6 4.5 %collective-permute-start.26 = (f32[32,1024]{1,0:T(8,128)S(1)}, f32[32,1024]{1,0:T(8,128)S(1)}, u32[]{:S(2)}, u32[]{:S(2)}) collective-permute-start(f32[32,1024]{1,0:T(8,128)S(1)} %add.56), channel_id=1, source_target_pairs={{0,24},{1,8},{2,11},{3,27},{4,28},{5,12},{6,15},{7,31},{8,1},{9,17... | collective-permute-start | bytes 393224 | tf_op jit(solution)/shard_map/ppermute | solution.py:52
  52.9 5.7 %collective-permute-start.31 = (f32[32,1024]{1,0:T(8,128)S(1)}, f32[32,1024]{1,0:T(8,128)S(1)}, u32[]{:S(2)}, u32[]{:S(2)}) collective-permute-start(f32[32,1024]{1,0:T(8,128)S(1)} %add.58), channel_id=1, source_target_pairs={{0,9},{1,11},{2,8},{3,10},{4,13},{5,15},{6,12},{7,14},{8,2},{9,0},... | collective-permute-start | bytes 393224 | tf_op jit(solution)/shard_map/ppermute | solution.py:52
  54.7 5.9 %collective-permute-start.42 = (f32[32,1024]{1,0:T(8,128)S(1)}, f32[32,1024]{1,0:T(8,128)S(1)}, u32[]{:S(2)}, u32[]{:S(2)}) collective-permute-start(f32[32,1024]{1,0:T(8,128)S(1)} %add.62), channel_id=1, source_target_pairs={{0,10},{1,11},{2,8},{3,9},{4,14},{5,15},{6,12},{7,13},{8,2},{9,3},... | collective-permute-start | bytes 393224 | tf_op jit(solution)/shard_map/ppermute | solution.py:52
  56.2 5.3 %collective-permute-start.38 = (f32[32,1024]{1,0:T(8,128)S(1)}, f32[32,1024]{1,0:T(8,128)S(1)}, u32[]{:S(2)}, u32[]{:S(2)}) collective-permute-start(f32[32,1024]{1,0:T(8,128)S(1)} %add.60), channel_id=1, source_target_pairs={{0,24},{1,8},{2,11},{3,27},{4,28},{5,12},{6,15},{7,31},{8,1},{9,17... | collective-permute-start | bytes 393224 | tf_op jit(solution)/shard_map/ppermute | solution.py:52
  57.2 5.3 %collective-permute-start.27 = (f32[32,1024]{1,0:T(8,128)S(1)}, f32[32,1024]{1,0:T(8,128)S(1)}, u32[]{:S(2)}, u32[]{:S(2)}) collective-permute-start(f32[32,1024]{1,0:T(8,128)S(1)} %add.57.own_ref), channel_id=1, source_target_pairs={{0,9},{1,11},{2,8},{3,10},{4,13},{5,15},{6,12},{7,14},{8,2},{9,0},... | collective-permute-start | bytes 393224 | tf_op jit(solution)/shard_map/ppermute | solution.py:52
  58.6 5.5 %collective-permute-start.32 = (f32[32,1024]{1,0:T(8,128)S(1)}, f32[32,1024]{1,0:T(8,128)S(1)}, u32[]{:S(2)}, u32[]{:S(2)}) collective-permute-start(f32[32,1024]{1,0:T(8,128)S(1)} %add.59.own_ref), channel_id=1, source_target_pairs={{0,24},{1,25},{2,26},{3,27},{4,28},{5,29},{6,30},{7,31},{8,16},{9,... | collective-permute-start | bytes 393224 | tf_op jit(solution)/shard_map/ppermute | solution.py:52
  61.5 4.8 %collective-permute-start.39 = (f32[32,1024]{1,0:T(8,128)S(1)}, f32[32,1024]{1,0:T(8,128)S(1)}, u32[]{:S(2)}, u32[]{:S(2)}) collective-permute-start(f32[32,1024]{1,0:T(8,128)S(1)} %add.61.own_ref), channel_id=1, source_target_pairs={{0,9},{1,11},{2,8},{3,10},{4,13},{5,15},{6,12},{7,14},{8,2},{9,0},... | collective-permute-start | bytes 393224 | tf_op jit(solution)/shard_map/ppermute | solution.py:52
  (14 other events, 42.5 us)
